TPU v7x, 128 devices: a whole 4x4x4 slice. The times are simulated.
128 devices in a mesh: gz: 8 (over x, z_hi), tile: 16 (over z_lo, y, core).
Axes of the slice: x: 4, y: 4, z: 4 (z_hi: 2, z_lo: 2; z = z_hi * 2 + z_lo), core: 2. Of those that a mesh axis runs over, the one named last changes fastest.
Arguments:
- disp: float32 [16, 2, 128, 5120], P('gz', None, 'tile'), may hold values from -6 to 6
- vel: float32 [16, 2, 128, 5120], P('gz', None, 'tile'), may hold values from -4 to 4
- stiff_class: int32 [16, 128, 5120], P('gz', 'tile'), may hold values from 0 to 7
- valid: int32 [16, 128, 5120], P('gz', 'tile'), may hold values 0 or 1
- class_table: float32 [8], replicated, may hold values from 0.3 to 3
- warp: float32 [16, 3, 2], P('gz'), may hold values from 0 to 1
- spring_z: float32 [16, 3], P('gz'), may hold values from 1.2 to 2
- skip_partner: int32 [16], replicated, may hold values from 0 to 15, as said below
Outputs:
- disp_out: float32 [16, 2, 128, 5120], P('gz', None, 'tile')
- vel_out: float32 [16, 2, 128, 5120], P('gz', None, 'tile')
Inputs may be any that keep to these rules, and one draw needn't show every extreme that they name: `skip_partner`: each section's partner lies in another z-block of 2 consecutive sections; the sections of one z-block have at most 1 partners inside any one other z-block, and exactly 1 inside some.
All inputs are finite; a program needn't handle non-finite values. No bound on the sum of `valid` on one device may be relied on, other than what follows from the above.
Results may differ from a plain program's by a relative error of at most 0.0003.
Values sent between devices are 32-bit elements; how exact they have to be, the bound alone decides.
A program may use at most 128 MiB of HBM per device.

v0:
```python
import jax
import jax.numpy as jnp
from jax import lax
from jax.sharding import PartitionSpec as P

ITERS = 3


DAMPING = 0.9
STEP = 0.1


def extended(block, sides, width):
    for axis, dim in sides:
        count = lax.axis_size(axis)
        forward = [(i, i + 1) for i in range(count - 1)]
        backward = [(target, source) for source, target in forward]
        low = lax.ppermute(
            lax.slice_in_dim(block, block.shape[dim] - width, None, axis=dim), axis, forward
        )
        high = lax.ppermute(lax.slice_in_dim(block, 0, width, axis=dim), axis, backward)
        block = jnp.concatenate([low, block, high], axis=dim)
    return block


def shift_left(field):
    return jnp.concatenate([field[..., 1:], jnp.zeros_like(field[..., :1])], axis=-1)


def shift_right(field):
    return jnp.concatenate([jnp.zeros_like(field[..., :1]), field[..., :-1]], axis=-1)


def warped(source, frac_row, frac_col):
    frac_row = frac_row[:, None, None, None]
    frac_col = frac_col[:, None, None, None]
    upper = source[:, :, 1:-1]
    lower = source[:, :, 2:]
    return (
        (1.0 - frac_row) * (1.0 - frac_col) * upper
        + (1.0 - frac_row) * frac_col * shift_left(upper)
        + frac_row * (1.0 - frac_col) * lower
        + frac_row * frac_col * shift_left(lower)
    )


def section_force(
    field_ext, stiff_ext, prev_ext, next_ext, partner_ext, warp, spring_z, has_prev, has_next
):
    center = field_ext[:, :, 1:-1]
    stiff_mid = stiff_ext[:, None, 1:-1]
    stiff_up = stiff_ext[:, None, :-2]
    stiff_down = stiff_ext[:, None, 2:]
    inplane = stiff_mid * (
        stiff_up * (field_ext[:, :, :-2] - center)
        + stiff_down * (field_ext[:, :, 2:] - center)
        + shift_right(stiff_mid) * (shift_right(center) - center)
        + shift_left(stiff_mid) * (shift_left(center) - center)
    )
    pull = (
        spring_z[:, 0][:, None, None, None]
        * has_prev[:, None, None, None]
        * (warped(prev_ext, warp[:, 0, 0], warp[:, 0, 1]) - center)
    )
    pull = pull + spring_z[:, 1][:, None, None, None] * has_next[:, None, None, None] * (
        warped(next_ext, warp[:, 1, 0], warp[:, 1, 1]) - center
    )
    pull = pull + spring_z[:, 2][:, None, None, None] * (
        warped(partner_ext, warp[:, 2, 0], warp[:, 2, 1]) - center
    )
    return inplane + pull


def body(disp, vel, stiff_class, valid, class_table, warp, spring_z, skip_partner):
    local_count = disp.shape[0]
    block_count = lax.axis_size("gz")
    block_index = lax.axis_index("gz")
    total = local_count * block_count
    alive = valid.astype(jnp.float32)
    kappa = jnp.zeros(stiff_class.shape, jnp.float32)
    for level in range(class_table.shape[0]):
        kappa = jnp.where(stiff_class == level, class_table[level], kappa)
    kappa = kappa * alive
    depth = 1
    coeffs = extended(jnp.stack([kappa, alive]), (("tile", 2),), depth)
    global_ids = block_index * local_count + jnp.arange(local_count, dtype=jnp.int32)
    has_prev = (global_ids > 0).astype(jnp.float32)
    has_next = (global_ids < total - 1).astype(jnp.float32)
    wanted = lax.dynamic_slice_in_dim(skip_partner, block_index * local_count, local_count, 0)
    field = disp
    velocity = vel
    for step in range(ITERS):
        field_ext = extended(field, (("tile", 2),), 1)
        vel_inner = velocity
        faces = extended(field_ext, (("gz", 0),), 1)
        piece = lax.all_gather(field_ext, "gz", axis=0, tiled=True)
        count = piece.shape[0]
        inside = (wanted >= 0) & (wanted < count)
        chosen = jnp.take(piece, jnp.clip(wanted, 0, count - 1), axis=0)
        partner_ext = jnp.where(inside[:, None, None, None], chosen, jnp.zeros_like(field_ext))
        force = section_force(
            field_ext,
            coeffs[0],
            faces[:-2],
            faces[2:],
            partner_ext,
            warp,
            spring_z,
            has_prev,
            has_next,
        )
        velocity = coeffs[1][:, None, 1:-1] * (DAMPING * vel_inner + STEP * force)
        field = field_ext[:, :, 1:-1] + STEP * velocity
    return (field, velocity)


def solution(mesh):
    placed = (
        P("gz", None, "tile", None),
        P("gz", None, "tile", None),
        P("gz", "tile", None),
        P("gz", "tile", None),
        P(),
        P("gz", None, None),
        P("gz", None),
        P(),
    )
    return jax.shard_map(
        body,
        mesh=mesh,
        in_specs=placed,
        out_specs=(P("gz", None, "tile", None), P("gz", None, "tile", None)),
        check_vma=False,
    )
```

profile of v0, /device:TPU:25, one launch (start us, length us, event | category | flops | bytes accessed | tf_op | source)
XLA Modules:
  0.0 398.7 jit_solution(12897192505926920959)
XLA Ops:
  8.6 3.8 collective-permute-start.2
  12.4 1.9 collective-permute-start.3
  15.9 6.3 %multiply_bitcast_fusion = f32[1,2,8,5120]{3,2,1,0:T(8,128)S(1)} fusion(s32[2,8,5120]{2,1,0:T(8,128)} %param.13, s32[2,8,5120]{2,1,0:T(8,128)} %param.12, f32[]{:T(128)} %bitcast.7, f32[]{:T(128)} %bitcast.6, f32[]{:T(128)} %bitcast.5, f32[]{:T(128)} %bitcast.4, f32[]{:T(128)} %bitcast.3, f32[]{:T(128)} %bitcast.2, f32[]{:T(128)} %bitcast.1, f32[]{:T(128)} %bitcast), kind=kLoop, calls=%fused_computation.137 | loop fusion | flops 1474560 | bytes 983072 | tf_op jit(solution)/shard_map/stack | solution.py:85
  25.4 5.8 %collective-permute-start = (f32[2,2,1,5120]{3,2,1,0:T(1,128)S(1)}, f32[2,2,1,5120]{3,2,1,0:T(1,128)S(1)}, u32[]{:S(2)}, u32[]{:S(2)}) collective-permute-start(f32[2,2,1,5120]{3,2,1,0:T(1,128)S(1)} %get-tuple-element.70), channel_id=1, source_target_pairs={{0,1},{1,2},{2,3},{3,4},{4,5},{5,6},{6,7},{7,8},{8,9},{9,10},{10,1... | collective-permute-start | bytes 245768 | tf_op jit(solution)/shard_map/ppermute | solution.py:18
  31.1 1.9 collective-permute-start.1
  34.9 4.1 %collective-permute-done.1 = f32[2,2,1,5120]{3,2,1,0:T(1,128)S(1)} collective-permute-done((f32[2,2,1,5120]{3,2,1,0:T(1,128)S(1)}, f32[2,2,1,5120]{3,2,1,0:T(1,128)S(1)}, u32[]{:S(2)}, u32[]{:S(2)}) %collective-permute-start.1) | collective-permute-done | bytes 81952 | tf_op jit(solution)/shard_map/ppermute | solution.py:21
  42.1 5.9 %collective-permute-start.4 = (f32[1,2,10,5120]{3,1,2,0:T(2,128)S(1)}, f32[1,2,10,5120]{3,1,2,0:T(2,128)S(1)}, u32[]{:S(2)}, u32[]{:S(2)}) collective-permute-start(f32[1,2,10,5120]{3,1,2,0:T(2,128)S(1)} %copy.52), channel_id=1, source_target_pairs={{0,16},{16,32},{32,48},{48,64},{64,80},{80,96},{96,112},{1,17},{17... | collective-permute-start | bytes 1228808 | tf_op jit(solution)/shard_map/ppermute | solution.py:18
  50.2 9.6 %collective-permute-done.5 = f32[1,2,10,5120]{3,1,2,0:T(2,128)S(1)} collective-permute-done((f32[1,2,10,5120]{3,1,2,0:T(2,128)S(1)}, f32[1,2,10,5120]{3,1,2,0:T(2,128)S(1)}, u32[]{:S(2)}, u32[]{:S(2)}) %collective-permute-start.5) | collective-permute-done | bytes 409632 | tf_op jit(solution)/shard_map/ppermute | solution.py:21
  60.0 5.3 %collective-permute-done.4 = f32[1,2,10,5120]{3,1,2,0:T(2,128)S(1)} collective-permute-done((f32[1,2,10,5120]{3,1,2,0:T(2,128)S(1)}, f32[1,2,10,5120]{3,1,2,0:T(2,128)S(1)}, u32[]{:S(2)}, u32[]{:S(2)}) %collective-permute-start.4) | collective-permute-done | bytes 409632 | tf_op jit(solution)/shard_map/ppermute | solution.py:18
  67.1 2.2 fusion.97
  69.3 65.5 %all-gather.4.cloned.1.call-done = f32[16,2,10,5120]{3,1,2,0:T(2,128)} async-done(((f32[2,2,10,5120]{3,1,2,0:T(2,128)}), f32[16,2,10,5120]{3,1,2,0:T(2,128)}) %all-gather.4.cloned.1.call-update) | async-done | bytes 6553616 | tf_op jit(solution)/shard_map/all_gather | solution.py:96
  134.9 5.1 %gather_fusion = f32[2,2,10,5120]{3,1,2,0:T(2,128)} fusion(f32[16,2,10,5120]{3,1,2,0:T(2,128)} %all-gather.4.cloned.1.call-done, s32[1024]{0:T(1024)S(1)} %pad_clamp_fusion), kind=kCustom, calls=%fused_computation.clone | custom fusion | bytes 1638408 | tf_op jit(solution)/shard_map/jit(_take)/gather | solution.py:99
  142.5 3.9 multiply_add_fusion.2
  146.5 3.5 collective-permute-start.6
  150.0 1.9 collective-permute-start.7
  151.9 5.9 %collective-permute-done.7 = f32[2,2,1,5120]{3,2,1,0:T(1,128)S(1)} collective-permute-done((f32[2,2,1,5120]{3,2,1,0:T(1,128)S(1)}, f32[2,2,1,5120]{3,2,1,0:T(1,128)S(1)}, u32[]{:S(2)}, u32[]{:S(2)}) %collective-permute-start.7) | collective-permute-done | bytes 81952 | tf_op jit(solution)/shard_map/ppermute | solution.py:21
  161.7 5.7 %collective-permute-start.8 = (f32[1,2,10,5120]{3,1,2,0:T(2,128)S(1)}, f32[1,2,10,5120]{3,1,2,0:T(2,128)S(1)}, u32[]{:S(2)}, u32[]{:S(2)}) collective-permute-start(f32[1,2,10,5120]{3,1,2,0:T(2,128)S(1)} %copy.58), channel_id=1, source_target_pairs={{0,16},{16,32},{32,48},{48,64},{64,80},{80,96},{96,112},{1,17},{17... | collective-permute-start | bytes 1228808 | tf_op jit(solution)/shard_map/ppermute | solution.py:18
  168.7 6.1 %collective-permute-done.9 = f32[1,2,10,5120]{3,1,2,0:T(2,128)S(1)} collective-permute-done((f32[1,2,10,5120]{3,1,2,0:T(2,128)S(1)}, f32[1,2,10,5120]{3,1,2,0:T(2,128)S(1)}, u32[]{:S(2)}, u32[]{:S(2)}) %collective-permute-start.9) | collective-permute-done | bytes 409632 | tf_op jit(solution)/shard_map/ppermute | solution.py:21
  174.9 13.3 %collective-permute-done.8 = f32[1,2,10,5120]{3,1,2,0:T(2,128)S(1)} collective-permute-done((f32[1,2,10,5120]{3,1,2,0:T(2,128)S(1)}, f32[1,2,10,5120]{3,1,2,0:T(2,128)S(1)}, u32[]{:S(2)}, u32[]{:S(2)}) %collective-permute-start.8) | collective-permute-done | bytes 409632 | tf_op jit(solution)/shard_map/ppermute | solution.py:18
  191.9 66.3 %all-gather.6.cloned.1.call-done = f32[16,2,10,5120]{3,1,2,0:T(2,128)} async-done(((f32[2,2,10,5120]{3,1,2,0:T(2,128)}), f32[16,2,10,5120]{3,1,2,0:T(2,128)}) %all-gather.6.cloned.1.call-update) | async-done | bytes 6553616 | tf_op jit(solution)/shard_map/all_gather | solution.py:96
  258.1 5.1 %gather_fusion.1 = f32[2,2,10,5120]{3,1,2,0:T(2,128)} fusion(f32[16,2,10,5120]{3,1,2,0:T(2,128)} %all-gather.6.cloned.1.call-done, s32[1024]{0:T(1024)S(1)} %pad_clamp_fusion), kind=kCustom, calls=%fused_computation.1.clone | custom fusion | bytes 1638408 | tf_op jit(solution)/shard_map/jit(_take)/gather | solution.py:99
  265.8 3.9 multiply_add_fusion.1
  269.7 3.5 collective-permute-start.10
  273.2 1.9 collective-permute-start.11
  275.2 5.9 %collective-permute-done.11 = f32[2,2,1,5120]{3,2,1,0:T(1,128)S(1)} collective-permute-done((f32[2,2,1,5120]{3,2,1,0:T(1,128)S(1)}, f32[2,2,1,5120]{3,2,1,0:T(1,128)S(1)}, u32[]{:S(2)}, u32[]{:S(2)}) %collective-permute-start.11) | collective-permute-done | bytes 81952 | tf_op jit(solution)/shard_map/ppermute | solution.py:21
  284.9 5.5 %collective-permute-start.12 = (f32[1,2,10,5120]{3,1,2,0:T(2,128)S(1)}, f32[1,2,10,5120]{3,1,2,0:T(2,128)S(1)}, u32[]{:S(2)}, u32[]{:S(2)}) collective-permute-start(f32[1,2,10,5120]{3,1,2,0:T(2,128)S(1)} %copy.64), channel_id=1, source_target_pairs={{0,16},{16,32},{32,48},{48,64},{64,80},{80,96},{96,112},{1,17},{17... | collective-permute-start | bytes 1228808 | tf_op jit(solution)/shard_map/ppermute | solution.py:18
  291.7 6.2 %collective-permute-done.13 = f32[1,2,10,5120]{3,1,2,0:T(2,128)S(1)} collective-permute-done((f32[1,2,10,5120]{3,1,2,0:T(2,128)S(1)}, f32[1,2,10,5120]{3,1,2,0:T(2,128)S(1)}, u32[]{:S(2)}, u32[]{:S(2)}) %collective-permute-start.13) | collective-permute-done | bytes 409632 | tf_op jit(solution)/shard_map/ppermute | solution.py:21
  298.1 13.4 %collective-permute-done.12 = f32[1,2,10,5120]{3,1,2,0:T(2,128)S(1)} collective-permute-done((f32[1,2,10,5120]{3,1,2,0:T(2,128)S(1)}, f32[1,2,10,5120]{3,1,2,0:T(2,128)S(1)}, u32[]{:S(2)}, u32[]{:S(2)}) %collective-permute-start.12) | collective-permute-done | bytes 409632 | tf_op jit(solution)/shard_map/ppermute | solution.py:18
  312.0 1.8 fusion.93
  315.3 66.1 %all-gather.8.cloned.1.call-done = f32[16,2,10,5120]{3,1,2,0:T(2,128)} async-done(((f32[2,2,10,5120]{3,1,2,0:T(2,128)}), f32[16,2,10,5120]{3,1,2,0:T(2,128)}) %all-gather.8.cloned.1.call-update) | async-done | bytes 6553616 | tf_op jit(solution)/shard_map/all_gather | solution.py:96
  381.3 4.4 %gather_fusion.2 = f32[2,2,10,5120]{3,1,2,0:T(2,128)S(1)} fusion(f32[16,2,10,5120]{3,1,2,0:T(2,128)} %all-gather.8.cloned.1.call-done, s32[1024]{0:T(1024)} %copy-done.49), kind=kCustom, calls=%fused_computation.2.clone | custom fusion | bytes 1638408 | tf_op jit(solution)/shard_map/jit(_take)/gather | solution.py:99
  388.1 4.1 %multiply_add_fusion = (f32[2,2,8,5120]{3,2,1,0:T(8,128)}, f32[2,2,8,5120]{3,2,1,0:T(8,128)}) fusion(f32[2,2,8,5120]{3,2,1,0:T(8,128)S(1)} %get-tuple-element.18, f32[2,2,8,5119]{3,2,1,0:T(8,128)S(1)} %get-tuple-element.39, f32[2]{0:T(128)S(1)} %get-tuple-element.86, f32[2,2,10,5120]{3,2,1,0:T(8,128)S(1)} %fusion, f32[2]{0:T(128)S(1)} %get-tuple-element.85, ...), kind=kLoop, calls=%fused_computation.132 | loop fusion | flops 8192000 | bytes 13925496 | tf_op jit(solution)/shard_map/add | solution.py:113
  (171 shorter events, 38.2 us)
Async XLA Ops:
  7.2 127.7 %all-gather.4.cloned.1.call-start = ((), (), s32[]{:S(2)}) async-start(), calls=%async_computation | async-start | bytes 7372800 | tf_op jit(solution)/shard_map/all_gather | solution.py:96
  8.6 13.6 %collective-permute-start.2 = (f32[2,2,1,5120]{3,2,1,0:T(1,128)S(1)}, f32[2,2,1,5120]{3,2,1,0:T(1,128)S(1)}, u32[]{:S(2)}, u32[]{:S(2)}) collective-permute-start(f32[2,2,1,5120]{3,2,1,0:T(1,128)S(1)} %get-tuple-element.72), channel_id=1, source_target_pairs={{0,1},{1,2},{2,3},{3,4},{4,5},{5,6},{6,7},{7,8},{8,9},{9,10},{10,1... | collective-permute-start | bytes 245768 | tf_op jit(solution)/shard_map/ppermute | solution.py:18
  12.4 9.9 %collective-permute-start.3 = (f32[2,2,1,5120]{3,2,1,0:T(1,128)S(1)}, f32[2,2,1,5120]{3,2,1,0:T(1,128)S(1)}, u32[]{:S(2)}, u32[]{:S(2)}) collective-permute-start(f32[2,2,1,5120]{3,2,1,0:T(1,128)S(1)} %get-tuple-element.73), channel_id=1, source_target_pairs={{1,0},{2,1},{3,2},{4,3},{5,4},{6,5},{7,6},{8,7},{9,8},{10,9},{11,1... | collective-permute-start | bytes 245768 | tf_op jit(solution)/shard_map/ppermute | solution.py:21
  23.6 9.5 %copy-start.50 = (s32[16]{0:T(128)S(1)}, s32[16]{0:T(128)}, u32[]{:S(2)}) copy-start(s32[16]{0:T(128)} %param.17) | copy-start | bytes 196
  23.6 9.6 %copy-start.32 = (f32[2,3]{1,0:T(2,128)S(1)}, f32[2,3]{1,0:T(2,128)}, u32[]{:S(2)}) copy-start(f32[2,3]{1,0:T(2,128)} %param.16) | copy-start | bytes 76
  23.6 9.8 %copy-start.31 = (f32[2,3,2]{1,2,0:T(2,128)S(1)}, f32[2,3,2]{1,2,0:T(2,128)}, u32[]{:S(2)}) copy-start(f32[2,3,2]{1,2,0:T(2,128)} %param.15) | copy-start | bytes 148
  23.6 10.0 %copy-start = (f32[2,2,8,5120]{3,2,1,0:T(8,128)S(1)}, f32[2,2,8,5120]{3,2,1,0:T(8,128)}, u32[]{:S(2)}) copy-start(f32[2,2,8,5120]{3,2,1,0:T(8,128)} %param.10) | copy-start | bytes 1966084
  25.2 233.0 %all-gather.6.cloned.1.call-start = ((), (), s32[]{:S(2)}) async-start(), calls=%async_computation.1 | async-start | bytes 7372800 | tf_op jit(solution)/shard_map/all_gather | solution.py:96
  25.4 9.6 %collective-permute-start = (f32[2,2,1,5120]{3,2,1,0:T(1,128)S(1)}, f32[2,2,1,5120]{3,2,1,0:T(1,128)S(1)}, u32[]{:S(2)}, u32[]{:S(2)}) collective-permute-start(f32[2,2,1,5120]{3,2,1,0:T(1,128)S(1)} %get-tuple-element.70), channel_id=1, source_target_pairs={{0,1},{1,2},{2,3},{3,4},{4,5},{5,6},{6,7},{7,8},{8,9},{9,10},{10,1... | collective-permute-start | bytes 245768 | tf_op jit(solution)/shard_map/ppermute | solution.py:18
  31.1 7.9 %collective-permute-start.1 = (f32[2,2,1,5120]{3,2,1,0:T(1,128)S(1)}, f32[2,2,1,5120]{3,2,1,0:T(1,128)S(1)}, u32[]{:S(2)}, u32[]{:S(2)}) collective-permute-start(f32[2,2,1,5120]{3,2,1,0:T(1,128)S(1)} %get-tuple-element.71), channel_id=1, source_target_pairs={{1,0},{2,1},{3,2},{4,3},{5,4},{6,5},{7,6},{8,7},{9,8},{10,9},{11,1... | collective-permute-start | bytes 245768 | tf_op jit(solution)/shard_map/ppermute | solution.py:21
  33.2 230.1 %copy-start.47 = (pred[2]{0:T(512)(128)(4,1)}, pred[2]{0:T(512)(128)(4,1)S(1)}, u32[]{:S(2)}) copy-start(pred[2]{0:T(512)(128)(4,1)S(1)} %get-tuple-element.22) | copy-start | bytes 10
  33.2 230.1 %copy-start.48 = (pred[2]{0:T(512)(128)(4,1)}, pred[2]{0:T(512)(128)(4,1)S(1)}, u32[]{:S(2)}) copy-start(pred[2]{0:T(512)(128)(4,1)S(1)} %get-tuple-element.96) | copy-start | bytes 10
  33.6 231.8 %copy-start.39 = (f32[2]{0:T(128)}, f32[2]{0:T(128)S(1)}, u32[]{:S(2)}) copy-start(f32[2]{0:T(128)S(1)} %get-tuple-element.76) | copy-start | bytes 28
  33.6 231.8 %copy-start.41 = (f32[2]{0:T(128)}, f32[2]{0:T(128)S(1)}, u32[]{:S(2)}) copy-start(f32[2]{0:T(128)S(1)} %get-tuple-element.77) | copy-start | bytes 28
  33.6 231.8 %copy-start.43 = (f32[2]{0:T(128)}, f32[2]{0:T(128)S(1)}, u32[]{:S(2)}) copy-start(f32[2]{0:T(128)S(1)} %get-tuple-element.78) | copy-start | bytes 28
  33.6 231.8 %copy-start.45 = (f32[2]{0:T(128)}, f32[2]{0:T(128)S(1)}, u32[]{:S(2)}) copy-start(f32[2]{0:T(128)S(1)} %get-tuple-element.79) | copy-start | bytes 28
  33.6 231.8 %copy-start.33 = (f32[2]{0:T(128)}, f32[2]{0:T(128)S(1)}, u32[]{:S(2)}) copy-start(f32[2]{0:T(128)S(1)} %get-tuple-element.98) | copy-start | bytes 28
  33.6 231.8 %copy-start.35 = (f32[2]{0:T(128)}, f32[2]{0:T(128)S(1)}, u32[]{:S(2)}) copy-start(f32[2]{0:T(128)S(1)} %get-tuple-element.99) | copy-start | bytes 28
  33.7 231.8 %copy-start.37 = (f32[2]{0:T(128)}, f32[2]{0:T(128)S(1)}, u32[]{:S(2)}) copy-start(f32[2]{0:T(128)S(1)} %get-tuple-element.100) | copy-start | bytes 28
  34.9 223.2 %copy-start.49 = (s32[1024]{0:T(1024)}, s32[1024]{0:T(1024)S(1)}, u32[]{:S(2)}) copy-start(s32[1024]{0:T(1024)S(1)} %pad_clamp_fusion) | copy-start | bytes 12292
  40.8 19.0 %collective-permute-start.5 = (f32[1,2,10,5120]{3,1,2,0:T(2,128)S(1)}, f32[1,2,10,5120]{3,1,2,0:T(2,128)S(1)}, u32[]{:S(2)}, u32[]{:S(2)}) collective-permute-start(f32[1,2,10,5120]{3,1,2,0:T(2,128)S(1)} %copy.54), channel_id=1, source_target_pairs={{16,0},{32,16},{48,32},{64,48},{80,64},{96,80},{112,96},{17,1},{33... | collective-permute-start | bytes 1228808 | tf_op jit(solution)/shard_map/ppermute | solution.py:21
  42.1 23.1 %collective-permute-start.4 = (f32[1,2,10,5120]{3,1,2,0:T(2,128)S(1)}, f32[1,2,10,5120]{3,1,2,0:T(2,128)S(1)}, u32[]{:S(2)}, u32[]{:S(2)}) collective-permute-start(f32[1,2,10,5120]{3,1,2,0:T(2,128)S(1)} %copy.52), channel_id=1, source_target_pairs={{0,16},{16,32},{32,48},{48,64},{64,80},{80,96},{96,112},{1,17},{17... | collective-permute-start | bytes 1228808 | tf_op jit(solution)/shard_map/ppermute | solution.py:18
  146.5 5.4 %collective-permute-start.6 = (f32[2,2,1,5120]{3,2,1,0:T(1,128)S(1)}, f32[2,2,1,5120]{3,2,1,0:T(1,128)S(1)}, u32[]{:S(2)}, u32[]{:S(2)}) collective-permute-start(f32[2,2,1,5120]{3,2,1,0:T(1,128)S(1)} %get-tuple-element.62), channel_id=1, source_target_pairs={{0,1},{1,2},{2,3},{3,4},{4,5},{5,6},{6,7},{7,8},{8,9},{9,10},{10,1... | collective-permute-start | bytes 245768 | tf_op jit(solution)/shard_map/ppermute | solution.py:18
  150.0 7.9 %collective-permute-start.7 = (f32[2,2,1,5120]{3,2,1,0:T(1,128)S(1)}, f32[2,2,1,5120]{3,2,1,0:T(1,128)S(1)}, u32[]{:S(2)}, u32[]{:S(2)}) collective-permute-start(f32[2,2,1,5120]{3,2,1,0:T(1,128)S(1)} %get-tuple-element.63), channel_id=1, source_target_pairs={{1,0},{2,1},{3,2},{4,3},{5,4},{6,5},{7,6},{8,7},{9,8},{10,9},{11,1... | collective-permute-start | bytes 245768 | tf_op jit(solution)/shard_map/ppermute | solution.py:21
  159.6 221.7 %all-gather.8.cloned.1.call-start = ((), (), s32[]{:S(2)}) async-start(), calls=%async_computation.2 | async-start | bytes 7372800 | tf_op jit(solution)/shard_map/all_gather | solution.py:96
  160.4 14.4 %collective-permute-start.9 = (f32[1,2,10,5120]{3,1,2,0:T(2,128)S(1)}, f32[1,2,10,5120]{3,1,2,0:T(2,128)S(1)}, u32[]{:S(2)}, u32[]{:S(2)}) collective-permute-start(f32[1,2,10,5120]{3,1,2,0:T(2,128)S(1)} %copy.60), channel_id=1, source_target_pairs={{16,0},{32,16},{48,32},{64,48},{80,64},{96,80},{112,96},{17,1},{33... | collective-permute-start | bytes 1228808 | tf_op jit(solution)/shard_map/ppermute | solution.py:21
  161.7 26.5 %collective-permute-start.8 = (f32[1,2,10,5120]{3,1,2,0:T(2,128)S(1)}, f32[1,2,10,5120]{3,1,2,0:T(2,128)S(1)}, u32[]{:S(2)}, u32[]{:S(2)}) collective-permute-start(f32[1,2,10,5120]{3,1,2,0:T(2,128)S(1)} %copy.58), channel_id=1, source_target_pairs={{0,16},{16,32},{32,48},{48,64},{64,80},{80,96},{96,112},{1,17},{17... | collective-permute-start | bytes 1228808 | tf_op jit(solution)/shard_map/ppermute | solution.py:18
  269.7 5.4 %collective-permute-start.10 = (f32[2,2,1,5120]{3,2,1,0:T(1,128)S(1)}, f32[2,2,1,5120]{3,2,1,0:T(1,128)S(1)}, u32[]{:S(2)}, u32[]{:S(2)}) collective-permute-start(f32[2,2,1,5120]{3,2,1,0:T(1,128)S(1)} %get-tuple-element.58), channel_id=1, source_target_pairs={{0,1},{1,2},{2,3},{3,4},{4,5},{5,6},{6,7},{7,8},{8,9},{9,10},{10,1... | collective-permute-start | bytes 245768 | tf_op jit(solution)/shard_map/ppermute | solution.py:18
  273.2 7.9 %collective-permute-start.11 = (f32[2,2,1,5120]{3,2,1,0:T(1,128)S(1)}, f32[2,2,1,5120]{3,2,1,0:T(1,128)S(1)}, u32[]{:S(2)}, u32[]{:S(2)}) collective-permute-start(f32[2,2,1,5120]{3,2,1,0:T(1,128)S(1)} %get-tuple-element.59), channel_id=1, source_target_pairs={{1,0},{2,1},{3,2},{4,3},{5,4},{6,5},{7,6},{8,7},{9,8},{10,9},{11,1... | collective-permute-start | bytes 245768 | tf_op jit(solution)/shard_map/ppermute | solution.py:21
  281.1 30.5 %copy-start.29 = (f32[2,2,1,5120]{3,2,1,0:T(1,128)}, f32[2,2,1,5120]{3,2,1,0:T(1,128)S(1)}, u32[]{:S(2)}) copy-start(f32[2,2,1,5120]{3,2,1,0:T(1,128)S(1)} %collective-permute-done.11) | copy-start | bytes 245764
  283.6 14.3 %collective-permute-start.13 = (f32[1,2,10,5120]{3,1,2,0:T(2,128)S(1)}, f32[1,2,10,5120]{3,1,2,0:T(2,128)S(1)}, u32[]{:S(2)}, u32[]{:S(2)}) collective-permute-start(f32[1,2,10,5120]{3,1,2,0:T(2,128)S(1)} %copy.66), channel_id=1, source_target_pairs={{16,0},{32,16},{48,32},{64,48},{80,64},{96,80},{112,96},{17,1},{33... | collective-permute-start | bytes 1228808 | tf_op jit(solution)/shard_map/ppermute | solution.py:21
  284.9 26.5 %collective-permute-start.12 = (f32[1,2,10,5120]{3,1,2,0:T(2,128)S(1)}, f32[1,2,10,5120]{3,1,2,0:T(2,128)S(1)}, u32[]{:S(2)}, u32[]{:S(2)}) collective-permute-start(f32[1,2,10,5120]{3,1,2,0:T(2,128)S(1)} %copy.64), channel_id=1, source_target_pairs={{0,16},{16,32},{32,48},{48,64},{64,80},{80,96},{96,112},{1,17},{17... | collective-permute-start | bytes 1228808 | tf_op jit(solution)/shard_map/ppermute | solution.py:18
  (36 other events, 74.4 us)
Sparse Core Ops, SparseCore 0:
  25.3 109.5 all-gather.3
  159.7 98.3 all-gather.5
  283.0 98.3 all-gather.7
where the time goes:
time: 401 us; the launch traced here: 399 us
  waiting for transfers between devices  268 us (67%)
  starting transfers between devices  45.3 us (11%)
  local copies, waits for them, and re-layouts  45.1 us (11%)
  other arithmetic  25.7 us (6%)
  between operations  14.7 us (4%)
    all_gather x3, waiting for transfers between devices, body(): piece = lax.all_gather(field_ext, 'gz', axis=0, tiled=True)  198 us
    ppermute x7, waiting for transfers between devices, extended(): lax.ppermute(lax.slice_in_dim(block, 0, width, axis=dim), axis, backward)  37.8 us
    ppermute x7, starting transfers between devices, extended(): lax.ppermute(lax.slice_in_dim(block, block.shape[dim] - width, None, axis...  33.7 us
    ppermute x7, waiting for transfers between devices, extended(): lax.ppermute(lax.slice_in_dim(block, block.shape[dim] - width, None, axis...  32 us
    gather x3, local copies, waits for them, and re-layouts, body(): chosen = jnp.take(piece, jnp.clip(wanted, 0, count - 1), axis=0)  14.6 us
    add x3, other arithmetic, body(): field = field_ext[:, :, 1:-1] + STEP * velocity  11.8 us
    ppermute x7, starting transfers between devices, extended(): lax.ppermute(lax.slice_in_dim(block, 0, width, axis=dim), axis, backward)  11.6 us
    slice x8, local copies, waits for them, and re-layouts, shift_left(): field[..., 1:]  9.86 us
  transfers between devices with their start and end apart: 17, of which 12 were waited for; matrix products, arithmetic and copies ran while one was open for 7% of the time, Pallas kernels for 0%

commit v1 on v0

v1 whole, which is shorter than its diff:
```python
import jax
import jax.numpy as jnp
from jax import lax
from jax.sharding import PartitionSpec as P

ITERS = 3


DAMPING = 0.9
STEP = 0.1


def shift_rows(block, axis, forward):
    count = lax.axis_size(axis)
    pairs = [(i, i + 1) for i in range(count - 1)]
    if not forward:
        pairs = [(t, s) for s, t in pairs]
    return lax.ppermute(block, axis, pairs)


def shift_left(field):
    return jnp.concatenate([field[..., 1:], jnp.zeros_like(field[..., :1])], axis=-1)


def shift_right(field):
    return jnp.concatenate([jnp.zeros_like(field[..., :1]), field[..., :-1]], axis=-1)


def warped9(source, frac_row, frac_col):
    upper = source[:, :-1]
    lower = source[:, 1:]
    return (
        (1.0 - frac_row) * (1.0 - frac_col) * upper
        + (1.0 - frac_row) * frac_col * shift_left(upper)
        + frac_row * (1.0 - frac_col) * lower
        + frac_row * frac_col * shift_left(lower)
    )


def body(disp, vel, stiff_class, valid, class_table, warp, spring_z, skip_partner):
    local_count = disp.shape[0]
    block_count = lax.axis_size("gz")
    block_index = lax.axis_index("gz")
    total = local_count * block_count
    alive = valid.astype(jnp.float32)
    kappa = jnp.zeros(stiff_class.shape, jnp.float32)
    for level in range(class_table.shape[0]):
        kappa = jnp.where(stiff_class == level, class_table[level], kappa)
    kappa = kappa * alive
    stiff = jnp.stack([kappa, alive])
    stiff_ext = jnp.concatenate(
        [
            shift_rows(stiff[:, :, -1:], "tile", True),
            stiff,
            shift_rows(stiff[:, :, :1], "tile", False),
        ],
        axis=2,
    )
    kap_ext = stiff_ext[0]
    alive_mid = alive
    global_ids = block_index * local_count + jnp.arange(local_count, dtype=jnp.int32)
    has_prev = (global_ids > 0).astype(jnp.float32)
    has_next = (global_ids < total - 1).astype(jnp.float32)

    mine = lax.dynamic_slice_in_dim(skip_partner, block_index * local_count, local_count, 0)
    src_block = mine // local_count
    wanted = skip_partner.reshape(block_count, local_count)
    hit = (wanted // local_count) == block_index
    send_sel = jnp.sum(jnp.where(hit, wanted % local_count, 0), axis=1)

    field = disp
    velocity = vel
    for step in range(ITERS):
        send = field[0][None]
        for l in range(1, local_count):
            send = jnp.where((send_sel == l)[:, None, None, None], field[l][None], send)
        recv = lax.all_to_all(send, "gz", 0, 0, tiled=True)
        partner8 = jnp.stack(
            [lax.dynamic_index_in_dim(recv, src_block[l], 0, keepdims=False) for l in range(local_count)]
        )
        prev_face = shift_rows(field[-1], "gz", True)
        next_face = shift_rows(field[0], "gz", False)
        up = shift_rows(field[:, :, -1:], "tile", True)
        down = shift_rows(field[:, :, :1], "tile", False)
        field_ext = jnp.concatenate([up, field, down], axis=2)
        firsts = jnp.concatenate(
            [prev_face[None, :, :1], next_face[None, :, :1], partner8[:, :, :1]], axis=0
        )
        below = shift_rows(firsts, "tile", False)
        prev9 = [jnp.concatenate([prev_face, below[0]], axis=1)] + [
            field_ext[l - 1, :, 1:] for l in range(1, local_count)
        ]
        next9 = [field_ext[l + 1, :, 1:] for l in range(local_count - 1)] + [
            jnp.concatenate([next_face, below[1]], axis=1)
        ]
        forces = []
        for l in range(local_count):
            center = field[l]
            k_mid = kap_ext[l, 1:-1][None]
            k_up = kap_ext[l, :-2][None]
            k_down = kap_ext[l, 2:][None]
            inplane = k_mid * (
                k_up * (field_ext[l, :, :-2] - center)
                + k_down * (field_ext[l, :, 2:] - center)
                + shift_right(k_mid) * (shift_right(center) - center)
                + shift_left(k_mid) * (shift_left(center) - center)
            )
            partner9 = jnp.concatenate([partner8[l], below[2 + l]], axis=1)
            pull = spring_z[l, 0] * has_prev[l] * (warped9(prev9[l], warp[l, 0, 0], warp[l, 0, 1]) - center)
            pull = pull + spring_z[l, 1] * has_next[l] * (
                warped9(next9[l], warp[l, 1, 0], warp[l, 1, 1]) - center
            )
            pull = pull + spring_z[l, 2] * (warped9(partner9, warp[l, 2, 0], warp[l, 2, 1]) - center)
            forces.append(inplane + pull)
        force = jnp.stack(forces)
        velocity = alive_mid[:, None] * (DAMPING * velocity + STEP * force)
        field = field + STEP * velocity
    return (field, velocity)


def solution(mesh):
    placed = (
        P("gz", None, "tile", None),
        P("gz", None, "tile", None),
        P("gz", "tile", None),
        P("gz", "tile", None),
        P(),
        P("gz", None, None),
        P("gz", None),
        P(),
    )
    return jax.shard_map(
        body,
        mesh=mesh,
        in_specs=placed,
        out_specs=(P("gz", None, "tile", None), P("gz", None, "tile", None)),
        check_vma=False,
    )
```

time: 401 us -> 262 us (0.65)
  waiting for transfers between devices: 268 us -> 64.3 us
  starting transfers between devices: 45.3 us -> 75.9 us
  between operations: 14.7 us -> 33.2 us
  other arithmetic: 25.7 us -> 35 us
  local copies, waits for them, and re-layouts: 45.1 us -> 51.4 us
    all_gather x3 -> x0, waiting for transfers between devices: 198 us -> none  [body(): piece = lax.all_gather(field_ext, 'gz', axis=0, tiled=True)]
    ppermute x14 -> x17, waiting for transfers between devices: 69.8 us -> 10 us  [shift_rows(): return lax.ppermute(block, axis, pairs)]
    all_to_all x0 -> x3, waiting for transfers between devices: none -> 54.3 us  [body(): recv = lax.all_to_all(send, 'gz', 0, 0, tiled=True)]
    all_to_all x0 -> x3, starting transfers between devices: none -> 18.2 us  [body(): recv = lax.all_to_all(send, 'gz', 0, 0, tiled=True)]
    another operation x2 -> x7, other arithmetic: 6.31 us -> 22.7 us  [the longest x6 17.7 us: body(): force = jnp.stack(forces)]
    gather x3 -> x0, local copies, waits for them, and re-layouts: 14.6 us -> none  [body(): chosen = jnp.take(piece, jnp.clip(wanted, 0, count - 1), axis=0)]
    ppermute x14 -> x17, starting transfers between devices: 45.2 us -> 57.7 us  [shift_rows(): return lax.ppermute(block, axis, pairs)]
    add x3, other arithmetic: 11.8 us -> 1.88 us  [body(): field = field + STEP * velocity]
  transfers between devices with their start and end apart: 17 -> 20, of which waited for: 12 -> 5; matrix products, arithmetic and copies ran while one was open for 7% -> 24% of each run, Pallas kernels for 0% -> 0%
where the time goes in v1:
time: 262 us; the launch traced here: 260 us
  starting transfers between devices  75.9 us (29%)
  waiting for transfers between devices  64.3 us (25%)
  local copies, waits for them, and re-layouts  51.4 us (20%)
  other arithmetic  35 us (13%)
  between operations  33.2 us (13%)
    ppermute x17, starting transfers between devices, shift_rows(): return lax.ppermute(block, axis, pairs)  57.7 us
    all_to_all x3, waiting for transfers between devices, body(): recv = lax.all_to_all(send, 'gz', 0, 0, tiled=True)  54.3 us
    all_to_all x3, starting transfers between devices, body(): recv = lax.all_to_all(send, 'gz', 0, 0, tiled=True)  18.2 us
    another operation x6, other arithmetic, body(): force = jnp.stack(forces)  17.7 us
    slice x18, local copies, waits for them, and re-layouts, shift_left(): field[..., 1:]  12.9 us
    slice x6, local copies, waits for them, and re-layouts, shift_right(): field[..., :-1]  11.9 us
    ppermute x17, waiting for transfers between devices, shift_rows(): return lax.ppermute(block, axis, pairs)  10 us
    select_n x3, other arithmetic, body(): send = jnp.where((send_sel == l)[:, None, None, None], field[l][None], send)  8.67 us
  transfers between devices with their start and end apart: 20, of which 5 were waited for; matrix products, arithmetic and copies ran while one was open for 24% of the time, Pallas kernels for 0%

profile of v1, /device:TPU:25, one launch (start us, length us, event | category | flops | bytes accessed | tf_op | source)
XLA Modules:
  0.0 259.8 jit_solution(14221218002234496024)
XLA Ops:
  0.6 2.0 slice_bitcast_fusion.8
  3.9 6.9 %collective-permute-start.4 = (f32[2,8,5120]{2,1,0:T(8,128)}, f32[2,8,5120]{2,1,0:T(8,128)}, u32[]{:S(2)}, u32[]{:S(2)}) collective-permute-start(f32[2,8,5120]{2,1,0:T(8,128)} %get-tuple-element.50), channel_id=1, source_target_pairs={{0,16},{16,32},{32,48},{48,64},{64,80},{80,96},{96,112},{1,17},{17... | collective-permute-start | bytes 983048 | tf_op jit(solution)/shard_map/ppermute | solution.py:18
  11.0 2.9 %broadcast_select_fusion.2 = f32[8,2,8,5120]{3,2,1,0:T(8,128)} fusion(f32[2,8,5120]{2,1,0:T(8,128)} %get-tuple-element.51, f32[2,8,5120]{2,1,0:T(8,128)} %get-tuple-element.50, pred[8]{0:T(512)(128)(4,1)S(1)} %broadcast_compare_fusion), kind=kLoop, calls=%fused_computation.14 | loop fusion | flops 655360 | bytes 3276808 | tf_op jit(solution)/shard_map/jit(_where)/select_n | solution.py:76
  13.9 7.0 %all-to-all-start = ((f32[8,2,8,5120]{3,2,1,0:T(8,128)}), f32[8,2,8,5120]{3,2,1,0:T(8,128)}, u32[]{:S(2)}, u32[]{:S(2)}) async-start(f32[8,2,8,5120]{3,2,1,0:T(8,128)} %broadcast_select_fusion.2), calls=%async_computation | async-start | bytes 5242880 | tf_op jit(solution)/shard_map/all_to_all | solution.py:77
  21.7 3.4 %collective-permute-start.3 = (f32[2,2,1,5120]{3,2,1,0:T(1,128)S(1)}, f32[2,2,1,5120]{3,2,1,0:T(1,128)S(1)}, u32[]{:S(2)}, u32[]{:S(2)}) collective-permute-start(f32[2,2,1,5120]{3,2,1,0:T(1,128)S(1)} %get-tuple-element.49), channel_id=1, source_target_pairs={{1,0},{2,1},{3,2},{4,3},{5,4},{6,5},{7,6},{8,7},{9,8},{10,9},{11,1... | collective-permute-start | bytes 245768 | tf_op jit(solution)/shard_map/ppermute | solution.py:18
  26.5 5.0 %multiply_bitcast_fusion = f32[1,2,8,5120]{3,2,1,0:T(8,128)S(1)} fusion(s32[2,8,5120]{2,1,0:T(8,128)S(1)} %copy-done.62, f32[]{:T(128)} %bitcast.7, f32[]{:T(128)} %bitcast.6, f32[]{:T(128)} %bitcast.5, f32[]{:T(128)} %bitcast.4, f32[]{:T(128)} %bitcast.3, f32[]{:T(128)} %bitcast.2, f32[]{:T(128)} %bitcast.1, f32[]{:T(128)} %bitcast, ...), kind=kLoop, calls=%fused_computation.301 | loop fusion | flops 1474560 | bytes 983072 | tf_op jit(solution)/shard_map/stack | solution.py:50
  33.6 5.8 %collective-permute-start = (f32[2,2,1,5120]{3,2,1,0:T(1,128)S(1)}, f32[2,2,1,5120]{3,2,1,0:T(1,128)S(1)}, u32[]{:S(2)}, u32[]{:S(2)}) collective-permute-start(f32[2,2,1,5120]{3,2,1,0:T(1,128)S(1)} %get-tuple-element.44), channel_id=1, source_target_pairs={{0,1},{1,2},{2,3},{3,4},{4,5},{5,6},{6,7},{7,8},{8,9},{9,10},{10,1... | collective-permute-start | bytes 245768 | tf_op jit(solution)/shard_map/ppermute | solution.py:18
  42.9 2.7 %fusion.234 = (f32[2,8,5119]{2,1,0:T(8,128)}, f32[2,8,5119]{2,1,0:T(8,128)}, f32[2,8,5119]{2,1,0:T(8,128)}, f32[2,8,5119]{2,1,0:T(8,128)}) fusion(f32[2,8,5120]{2,1,0:T(8,128)} %get-tuple-element.51, f32[2,8,5120]{2,1,0:T(8,128)} %get-tuple-element.50), kind=kLoop, calls=%fused_computation.380 | loop fusion | bytes 2620928 | tf_op jit(solution)/shard_map/slice | solution.py:26
  87.5 2.4 collective-permute-start.6
  93.8 2.4 collective-permute-done.6
  96.4 2.8 %fusion.85 = f32[1,2,8,5120]{3,2,1,0:T(8,128)S(1)} fusion(f32[2,8,5120]{2,1,0:T(8,128)S(1)} %bitcast.295, f32[2,1,5120]{2,1,0:T(1,128)S(1)} %get-tuple-element.75, f32[2,8,5120]{2,1,0:T(8,128)} %collective-permute-done.5, f32[2,1,5120]{2,1,0:T(1,128)S(1)} %get-tuple-element.76, f32[2,9,5120]{2,1,0:T(8,128)S(1)} %get-tuple-element.11, ...), kind=kLoop, calls=%fused_computation.137 | loop fusion | flops 4259840 | bytes 5898300 | tf_op jit(solution)/shard_map/stack | solution.py:115
  99.4 2.9 %fusion.101 = f32[1,2,8,5120]{3,2,1,0:T(8,128)S(1)} fusion(f32[2,8,5120]{2,1,0:T(8,128)S(1)} %bitcast.293, f32[2,1,5120]{2,1,0:T(1,128)S(1)} %get-tuple-element.77, f32[2,8,5120]{2,1,0:T(8,128)} %collective-permute-done.4, f32[2,1,5120]{2,1,0:T(1,128)S(1)} %get-tuple-element.74, f32[2,9,5120]{2,1,0:T(8,128)S(1)} %get-tuple-element.10, ...), kind=kLoop, calls=%fused_computation.153 | loop fusion | flops 4259840 | bytes 5898300 | tf_op jit(solution)/shard_map/stack | solution.py:115
  105.2 2.9 %broadcast_select_fusion.1 = f32[8,2,8,5120]{3,2,1,0:T(8,128)} fusion(f32[2,8,5120]{2,1,0:T(8,128)} %get-tuple-element.31, f32[2,8,5120]{2,1,0:T(8,128)} %get-tuple-element.30, pred[8]{0:T(512)(128)(4,1)S(1)} %broadcast_compare_fusion), kind=kLoop, calls=%fused_computation.13 | loop fusion | flops 655360 | bytes 3276808 | tf_op jit(solution)/shard_map/jit(_where)/select_n | solution.py:76
  108.1 6.5 %collective-permute-start.9 = (f32[2,8,5120]{2,1,0:T(8,128)}, f32[2,8,5120]{2,1,0:T(8,128)}, u32[]{:S(2)}, u32[]{:S(2)}) collective-permute-start(f32[2,8,5120]{2,1,0:T(8,128)} %get-tuple-element.30), channel_id=1, source_target_pairs={{0,16},{16,32},{32,48},{48,64},{64,80},{80,96},{96,112},{1,17},{17... | collective-permute-start | bytes 983048 | tf_op jit(solution)/shard_map/ppermute | solution.py:18
  115.3 2.1 fusion.232
  119.3 2.1 fusion.231
  121.4 6.8 %all-to-all-start.1 = ((f32[8,2,8,5120]{3,2,1,0:T(8,128)}), f32[8,2,8,5120]{3,2,1,0:T(8,128)}, u32[]{:S(2)}, u32[]{:S(2)}) async-start(f32[8,2,8,5120]{3,2,1,0:T(8,128)} %broadcast_select_fusion.1), calls=%async_computation.1 | async-start | bytes 5242880 | tf_op jit(solution)/shard_map/all_to_all | solution.py:77
  128.1 5.4 %collective-permute-start.7 = (f32[2,2,1,5120]{3,2,1,0:T(1,128)}, f32[2,2,1,5120]{3,2,1,0:T(1,128)}, u32[]{:S(2)}, u32[]{:S(2)}) collective-permute-start(f32[2,2,1,5120]{3,2,1,0:T(1,128)} %get-tuple-element.28), channel_id=1, source_target_pairs={{0,1},{1,2},{2,3},{3,4},{4,5},{5,6},{6,7},{7,8},{8,9},{9,10},{10,1... | collective-permute-start | bytes 245768 | tf_op jit(solution)/shard_map/ppermute | solution.py:18
  138.0 27.8 %all-to-all-done.1 = f32[8,2,8,5120]{3,2,1,0:T(8,128)} async-done(((f32[8,2,8,5120]{3,2,1,0:T(8,128)}), f32[8,2,8,5120]{3,2,1,0:T(8,128)}, u32[]{:S(2)}, u32[]{:S(2)}) %all-to-all-start.1) | async-done | bytes 2621472 | tf_op jit(solution)/shard_map/all_to_all | solution.py:77
  172.0 3.8 %collective-permute-done.11 = f32[4,2,1,5120]{3,2,1,0:T(1,128)S(1)} collective-permute-done((f32[4,2,1,5120]{3,2,1,0:T(1,128)S(1)}, f32[4,2,1,5120]{3,2,1,0:T(1,128)S(1)}, u32[]{:S(2)}, u32[]{:S(2)}) %collective-permute-start.11) | collective-permute-done | bytes 163872 | tf_op jit(solution)/shard_map/ppermute | solution.py:18
  176.0 2.9 %fusion.53 = f32[1,2,8,5120]{3,2,1,0:T(8,128)S(1)} fusion(f32[2,8,5120]{2,1,0:T(8,128)S(1)} %bitcast.303, f32[2,1,5120]{2,1,0:T(1,128)S(1)} %get-tuple-element.71, f32[2,8,5120]{2,1,0:T(8,128)} %collective-permute-done.10, f32[2,1,5120]{2,1,0:T(1,128)S(1)} %get-tuple-element.72, f32[2,2,8,5120]{3,2,1,0:T(8,128)S(1)} %multiply_add_fusion.2, ...), kind=kLoop, calls=%fused_computation.105 | loop fusion | flops 4341760 | bytes 5652540 | tf_op jit(solution)/shard_map/stack | solution.py:115
  179.0 3.0 %fusion.69 = f32[1,2,8,5120]{3,2,1,0:T(8,128)S(1)} fusion(f32[2,8,5120]{2,1,0:T(8,128)S(1)} %bitcast.301, f32[2,1,5120]{2,1,0:T(1,128)S(1)} %get-tuple-element.73, f32[2,8,5120]{2,1,0:T(8,128)} %collective-permute-done.9, f32[2,1,5120]{2,1,0:T(1,128)S(1)} %get-tuple-element.70, f32[2,2,8,5120]{3,2,1,0:T(8,128)S(1)} %multiply_add_fusion.2, ...), kind=kLoop, calls=%fused_computation.121 | loop fusion | flops 4341760 | bytes 5652540 | tf_op jit(solution)/shard_map/stack | solution.py:115
  184.9 2.9 %broadcast_select_fusion = f32[8,2,8,5120]{3,2,1,0:T(8,128)} fusion(f32[2,8,5120]{2,1,0:T(8,128)} %get-tuple-element.23, f32[2,8,5120]{2,1,0:T(8,128)} %get-tuple-element.22, pred[8]{0:T(512)(128)(4,1)S(1)} %broadcast_compare_fusion), kind=kLoop, calls=%fused_computation.12 | loop fusion | flops 655360 | bytes 3276808 | tf_op jit(solution)/shard_map/jit(_where)/select_n | solution.py:76
  187.8 6.2 %collective-permute-start.14 = (f32[2,8,5120]{2,1,0:T(8,128)}, f32[2,8,5120]{2,1,0:T(8,128)}, u32[]{:S(2)}, u32[]{:S(2)}) collective-permute-start(f32[2,8,5120]{2,1,0:T(8,128)} %get-tuple-element.22), channel_id=1, source_target_pairs={{0,16},{16,32},{32,48},{48,64},{64,80},{80,96},{96,112},{1,17},{17... | collective-permute-start | bytes 983048 | tf_op jit(solution)/shard_map/ppermute | solution.py:18
  194.8 2.1 fusion.230
  198.8 2.1 fusion.229
  200.9 4.4 %all-to-all-start.2 = ((f32[8,2,8,5120]{3,2,1,0:T(8,128)}), f32[8,2,8,5120]{3,2,1,0:T(8,128)}, u32[]{:S(2)}, u32[]{:S(2)}) async-start(f32[8,2,8,5120]{3,2,1,0:T(8,128)} %broadcast_select_fusion), calls=%async_computation.2 | async-start | bytes 5242880 | tf_op jit(solution)/shard_map/all_to_all | solution.py:77
  205.3 5.8 %collective-permute-start.12 = (f32[2,2,1,5120]{3,2,1,0:T(1,128)}, f32[2,2,1,5120]{3,2,1,0:T(1,128)}, u32[]{:S(2)}, u32[]{:S(2)}) collective-permute-start(f32[2,2,1,5120]{3,2,1,0:T(1,128)} %get-tuple-element.20), channel_id=1, source_target_pairs={{0,1},{1,2},{2,3},{3,4},{4,5},{5,6},{6,7},{7,8},{8,9},{9,10},{10,1... | collective-permute-start | bytes 245768 | tf_op jit(solution)/shard_map/ppermute | solution.py:18
  215.5 26.5 %all-to-all-done.2 = f32[8,2,8,5120]{3,2,1,0:T(8,128)} async-done(((f32[8,2,8,5120]{3,2,1,0:T(8,128)}), f32[8,2,8,5120]{3,2,1,0:T(8,128)}, u32[]{:S(2)}, u32[]{:S(2)}) %all-to-all-start.2) | async-done | bytes 2621472 | tf_op jit(solution)/shard_map/all_to_all | solution.py:77
  248.2 3.8 %collective-permute-done.16 = f32[4,2,1,5120]{3,2,1,0:T(1,128)S(1)} collective-permute-done((f32[4,2,1,5120]{3,2,1,0:T(1,128)S(1)}, f32[4,2,1,5120]{3,2,1,0:T(1,128)S(1)}, u32[]{:S(2)}, u32[]{:S(2)}) %collective-permute-start.16) | collective-permute-done | bytes 163872 | tf_op jit(solution)/shard_map/ppermute | solution.py:18
  252.2 2.9 %fusion.21 = f32[1,2,8,5120]{3,2,1,0:T(8,128)S(1)} fusion(f32[2,8,5120]{2,1,0:T(8,128)S(1)} %bitcast.299, f32[2,1,5120]{2,1,0:T(1,128)S(1)} %get-tuple-element.67, f32[2,8,5120]{2,1,0:T(8,128)} %collective-permute-done.15, f32[2,1,5120]{2,1,0:T(1,128)S(1)} %get-tuple-element.68, f32[2,2,8,5120]{3,2,1,0:T(8,128)S(1)} %multiply_add_fusion.1, ...), kind=kLoop, calls=%fused_computation.73 | loop fusion | flops 4341760 | bytes 5652540 | tf_op jit(solution)/shard_map/stack | solution.py:115
  255.2 3.1 %fusion.37 = f32[1,2,8,5120]{3,2,1,0:T(8,128)S(1)} fusion(f32[2,8,5120]{2,1,0:T(8,128)S(1)} %bitcast.297, f32[2,1,5120]{2,1,0:T(1,128)S(1)} %get-tuple-element.69, f32[2,8,5120]{2,1,0:T(8,128)} %collective-permute-done.14, f32[2,1,5120]{2,1,0:T(1,128)S(1)} %get-tuple-element.66, f32[2,2,8,5120]{3,2,1,0:T(8,128)S(1)} %multiply_add_fusion.1, ...), kind=kLoop, calls=%fused_computation.89 | loop fusion | flops 4341760 | bytes 5652540 | tf_op jit(solution)/shard_map/stack | solution.py:115
  (230 shorter events, 57.5 us)
Async XLA Ops:
  0.6 10.1 %copy-start.70 = (s32[16]{0:T(128)S(1)}, s32[16]{0:T(128)}, u32[]{:S(2)}) copy-start(s32[16]{0:T(128)} %param.15) | copy-start | bytes 196
  2.6 81.6 %collective-permute-start.5 = (f32[2,8,5120]{2,1,0:T(8,128)}, f32[2,8,5120]{2,1,0:T(8,128)}, u32[]{:S(2)}, u32[]{:S(2)}) collective-permute-start(f32[2,8,5120]{2,1,0:T(8,128)} %get-tuple-element.51), channel_id=1, source_target_pairs={{16,0},{32,16},{48,32},{64,48},{80,64},{96,80},{112,96},{17,1},{33... | collective-permute-start | bytes 983048 | tf_op jit(solution)/shard_map/ppermute | solution.py:18
  3.9 81.3 %collective-permute-start.4 = (f32[2,8,5120]{2,1,0:T(8,128)}, f32[2,8,5120]{2,1,0:T(8,128)}, u32[]{:S(2)}, u32[]{:S(2)}) collective-permute-start(f32[2,8,5120]{2,1,0:T(8,128)} %get-tuple-element.50), channel_id=1, source_target_pairs={{0,16},{16,32},{32,48},{48,64},{64,80},{80,96},{96,112},{1,17},{17... | collective-permute-start | bytes 983048 | tf_op jit(solution)/shard_map/ppermute | solution.py:18
  13.9 7.0 %copy-start = (f32[2,2,8,5120]{3,2,1,0:T(8,128)S(1)}, f32[2,2,8,5120]{3,2,1,0:T(8,128)}, u32[]{:S(2)}) copy-start(f32[2,2,8,5120]{3,2,1,0:T(8,128)} %param.8) | copy-start | bytes 1966084
  13.9 11.2 %copy-start.48 = (s32[2,8,5120]{2,1,0:T(8,128)S(1)}, s32[2,8,5120]{2,1,0:T(8,128)}, u32[]{:S(2)}) copy-start(s32[2,8,5120]{2,1,0:T(8,128)} %param.11) | copy-start | bytes 983044
  13.9 72.3 %all-to-all-start = ((f32[8,2,8,5120]{3,2,1,0:T(8,128)}), f32[8,2,8,5120]{3,2,1,0:T(8,128)}, u32[]{:S(2)}, u32[]{:S(2)}) async-start(f32[8,2,8,5120]{3,2,1,0:T(8,128)} %broadcast_select_fusion.2), calls=%async_computation | async-start | bytes 5242880 | tf_op jit(solution)/shard_map/all_to_all | solution.py:77
  20.9 5.6 %copy-start.62 = (s32[2,8,5120]{2,1,0:T(8,128)S(1)}, s32[2,8,5120]{2,1,0:T(8,128)}, u32[]{:S(2)}) copy-start(s32[2,8,5120]{2,1,0:T(8,128)} %param.10) | copy-start | bytes 983044
  21.7 58.9 %collective-permute-start.3 = (f32[2,2,1,5120]{3,2,1,0:T(1,128)S(1)}, f32[2,2,1,5120]{3,2,1,0:T(1,128)S(1)}, u32[]{:S(2)}, u32[]{:S(2)}) collective-permute-start(f32[2,2,1,5120]{3,2,1,0:T(1,128)S(1)} %get-tuple-element.49), channel_id=1, source_target_pairs={{1,0},{2,1},{3,2},{4,3},{5,4},{6,5},{7,6},{8,7},{9,8},{10,9},{11,1... | collective-permute-start | bytes 245768 | tf_op jit(solution)/shard_map/ppermute | solution.py:18
  31.7 44.9 %collective-permute-start.1 = (f32[2,2,1,5120]{3,2,1,0:T(1,128)S(1)}, f32[2,2,1,5120]{3,2,1,0:T(1,128)S(1)}, u32[]{:S(2)}, u32[]{:S(2)}) collective-permute-start(f32[2,2,1,5120]{3,2,1,0:T(1,128)S(1)} %get-tuple-element.45), channel_id=1, source_target_pairs={{1,0},{2,1},{3,2},{4,3},{5,4},{6,5},{7,6},{8,7},{9,8},{10,9},{11,1... | collective-permute-start | bytes 245768 | tf_op jit(solution)/shard_map/ppermute | solution.py:18
  33.6 44.9 %collective-permute-start = (f32[2,2,1,5120]{3,2,1,0:T(1,128)S(1)}, f32[2,2,1,5120]{3,2,1,0:T(1,128)S(1)}, u32[]{:S(2)}, u32[]{:S(2)}) collective-permute-start(f32[2,2,1,5120]{3,2,1,0:T(1,128)S(1)} %get-tuple-element.44), channel_id=1, source_target_pairs={{0,1},{1,2},{2,3},{3,4},{4,5},{5,6},{6,7},{7,8},{8,9},{9,10},{10,1... | collective-permute-start | bytes 245768 | tf_op jit(solution)/shard_map/ppermute | solution.py:18
  42.8 25.5 %copy-start.69 = (f32[2,3]{1,0:T(2,128)S(1)}, f32[2,3]{1,0:T(2,128)}, u32[]{:S(2)}) copy-start(f32[2,3]{1,0:T(2,128)} %param.14) | copy-start | bytes 76
  76.6 19.6 %collective-permute-start.2 = (f32[2,2,1,5120]{3,2,1,0:T(1,128)}, f32[2,2,1,5120]{3,2,1,0:T(1,128)S(1)}, u32[]{:S(2)}, u32[]{:S(2)}) collective-permute-start(f32[2,2,1,5120]{3,2,1,0:T(1,128)} %get-tuple-element.48), channel_id=1, source_target_pairs={{0,1},{1,2},{2,3},{3,4},{4,5},{5,6},{6,7},{7,8},{8,9},{9,10},{10,1... | collective-permute-start | bytes 245768 | tf_op jit(solution)/shard_map/ppermute | solution.py:18
  87.5 8.7 %collective-permute-start.6 = (f32[4,2,1,5120]{3,2,1,0:T(1,128)S(1)}, f32[4,2,1,5120]{3,2,1,0:T(1,128)S(1)}, u32[]{:S(2)}, u32[]{:S(2)}) collective-permute-start(f32[4,2,1,5120]{3,2,1,0:T(1,128)S(1)} %fusion.212), channel_id=1, source_target_pairs={{1,0},{2,1},{3,2},{4,3},{5,4},{6,5},{7,6},{8,7},{9,8},{10,9},{11,1... | collective-permute-start | bytes 491528 | tf_op jit(solution)/shard_map/ppermute | solution.py:18
  91.0 8.3 %copy-start.13 = (f32[8,5120]{1,0:T(8,128)}, f32[8,5120]{1,0:T(8,128)S(1)}, u32[]{:S(2)}) copy-start(f32[8,5120]{1,0:T(8,128)S(1)} %get-tuple-element.117) | copy-start | bytes 491524
  103.9 30.9 %collective-permute-start.10 = (f32[2,8,5120]{2,1,0:T(8,128)}, f32[2,8,5120]{2,1,0:T(8,128)}, u32[]{:S(2)}, u32[]{:S(2)}) collective-permute-start(f32[2,8,5120]{2,1,0:T(8,128)} %get-tuple-element.31), channel_id=1, source_target_pairs={{16,0},{32,16},{48,32},{64,48},{80,64},{96,80},{112,96},{17,1},{33... | collective-permute-start | bytes 983048 | tf_op jit(solution)/shard_map/ppermute | solution.py:18
  108.1 28.3 %collective-permute-start.9 = (f32[2,8,5120]{2,1,0:T(8,128)}, f32[2,8,5120]{2,1,0:T(8,128)}, u32[]{:S(2)}, u32[]{:S(2)}) collective-permute-start(f32[2,8,5120]{2,1,0:T(8,128)} %get-tuple-element.30), channel_id=1, source_target_pairs={{0,16},{16,32},{32,48},{48,64},{64,80},{80,96},{96,112},{1,17},{17... | collective-permute-start | bytes 983048 | tf_op jit(solution)/shard_map/ppermute | solution.py:18
  117.4 16.2 %collective-permute-start.8 = (f32[2,2,1,5120]{3,2,1,0:T(1,128)S(1)}, f32[2,2,1,5120]{3,2,1,0:T(1,128)S(1)}, u32[]{:S(2)}, u32[]{:S(2)}) collective-permute-start(f32[2,2,1,5120]{3,2,1,0:T(1,128)S(1)} %get-tuple-element.29), channel_id=1, source_target_pairs={{1,0},{2,1},{3,2},{4,3},{5,4},{6,5},{7,6},{8,7},{9,8},{10,9},{11,1... | collective-permute-start | bytes 245768 | tf_op jit(solution)/shard_map/ppermute | solution.py:18
  121.4 44.5 %all-to-all-start.1 = ((f32[8,2,8,5120]{3,2,1,0:T(8,128)}), f32[8,2,8,5120]{3,2,1,0:T(8,128)}, u32[]{:S(2)}, u32[]{:S(2)}) async-start(f32[8,2,8,5120]{3,2,1,0:T(8,128)} %broadcast_select_fusion.1), calls=%async_computation.1 | async-start | bytes 5242880 | tf_op jit(solution)/shard_map/all_to_all | solution.py:77
  128.1 47.7 %collective-permute-start.7 = (f32[2,2,1,5120]{3,2,1,0:T(1,128)}, f32[2,2,1,5120]{3,2,1,0:T(1,128)}, u32[]{:S(2)}, u32[]{:S(2)}) collective-permute-start(f32[2,2,1,5120]{3,2,1,0:T(1,128)} %get-tuple-element.28), channel_id=1, source_target_pairs={{0,1},{1,2},{2,3},{3,4},{4,5},{5,6},{6,7},{7,8},{8,9},{9,10},{10,1... | collective-permute-start | bytes 245768 | tf_op jit(solution)/shard_map/ppermute | solution.py:18
  167.1 8.7 %collective-permute-start.11 = (f32[4,2,1,5120]{3,2,1,0:T(1,128)S(1)}, f32[4,2,1,5120]{3,2,1,0:T(1,128)S(1)}, u32[]{:S(2)}, u32[]{:S(2)}) collective-permute-start(f32[4,2,1,5120]{3,2,1,0:T(1,128)S(1)} %fusion.211), channel_id=1, source_target_pairs={{1,0},{2,1},{3,2},{4,3},{5,4},{6,5},{7,6},{8,7},{9,8},{10,9},{11,1... | collective-permute-start | bytes 491528 | tf_op jit(solution)/shard_map/ppermute | solution.py:18
  170.4 5.5 %copy-start.17 = (f32[8,5120]{1,0:T(8,128)S(1)}, f32[8,5120]{1,0:T(8,128)}, u32[]{:S(2)}) copy-start(f32[8,5120]{1,0:T(8,128)} %get-tuple-element.114) | copy-start | bytes 491524
  170.4 5.5 %copy-start.20 = (f32[8,5120]{1,0:T(8,128)S(1)}, f32[8,5120]{1,0:T(8,128)}, u32[]{:S(2)}) copy-start(f32[8,5120]{1,0:T(8,128)} %get-tuple-element.115) | copy-start | bytes 491524
  170.4 5.5 %copy-start.32 = (f32[8,5120]{1,0:T(8,128)S(1)}, f32[8,5120]{1,0:T(8,128)}, u32[]{:S(2)}) copy-start(f32[8,5120]{1,0:T(8,128)} %get-tuple-element.33) | copy-start | bytes 491524
  170.4 5.5 %copy-start.35 = (f32[8,5120]{1,0:T(8,128)S(1)}, f32[8,5120]{1,0:T(8,128)}, u32[]{:S(2)}) copy-start(f32[8,5120]{1,0:T(8,128)} %get-tuple-element.34) | copy-start | bytes 491524
  170.4 5.5 %copy-start.38 = (f32[8,5120]{1,0:T(8,128)S(1)}, f32[8,5120]{1,0:T(8,128)}, u32[]{:S(2)}) copy-start(f32[8,5120]{1,0:T(8,128)} %get-tuple-element.35) | copy-start | bytes 491524
  170.4 5.5 %copy-start.55 = (f32[2,8,5119]{2,1,0:T(8,128)S(1)}, f32[2,8,5119]{2,1,0:T(8,128)}, u32[]{:S(2)}) copy-start(f32[2,8,5119]{2,1,0:T(8,128)} %get-tuple-element.58) | copy-start | bytes 982852
  183.7 28.6 %collective-permute-start.15 = (f32[2,8,5120]{2,1,0:T(8,128)}, f32[2,8,5120]{2,1,0:T(8,128)}, u32[]{:S(2)}, u32[]{:S(2)}) collective-permute-start(f32[2,8,5120]{2,1,0:T(8,128)} %get-tuple-element.23), channel_id=1, source_target_pairs={{16,0},{32,16},{48,32},{64,48},{80,64},{96,80},{112,96},{17,1},{33... | collective-permute-start | bytes 983048 | tf_op jit(solution)/shard_map/ppermute | solution.py:18
  187.8 26.1 %collective-permute-start.14 = (f32[2,8,5120]{2,1,0:T(8,128)}, f32[2,8,5120]{2,1,0:T(8,128)}, u32[]{:S(2)}, u32[]{:S(2)}) collective-permute-start(f32[2,8,5120]{2,1,0:T(8,128)} %get-tuple-element.22), channel_id=1, source_target_pairs={{0,16},{16,32},{32,48},{48,64},{64,80},{80,96},{96,112},{1,17},{17... | collective-permute-start | bytes 983048 | tf_op jit(solution)/shard_map/ppermute | solution.py:18
  196.9 14.2 %collective-permute-start.13 = (f32[2,2,1,5120]{3,2,1,0:T(1,128)S(1)}, f32[2,2,1,5120]{3,2,1,0:T(1,128)S(1)}, u32[]{:S(2)}, u32[]{:S(2)}) collective-permute-start(f32[2,2,1,5120]{3,2,1,0:T(1,128)S(1)} %get-tuple-element.21), channel_id=1, source_target_pairs={{1,0},{2,1},{3,2},{4,3},{5,4},{6,5},{7,6},{8,7},{9,8},{10,9},{11,1... | collective-permute-start | bytes 245768 | tf_op jit(solution)/shard_map/ppermute | solution.py:18
  200.9 41.1 %all-to-all-start.2 = ((f32[8,2,8,5120]{3,2,1,0:T(8,128)}), f32[8,2,8,5120]{3,2,1,0:T(8,128)}, u32[]{:S(2)}, u32[]{:S(2)}) async-start(f32[8,2,8,5120]{3,2,1,0:T(8,128)} %broadcast_select_fusion), calls=%async_computation.2 | async-start | bytes 5242880 | tf_op jit(solution)/shard_map/all_to_all | solution.py:77
  205.3 46.7 %collective-permute-start.12 = (f32[2,2,1,5120]{3,2,1,0:T(1,128)}, f32[2,2,1,5120]{3,2,1,0:T(1,128)}, u32[]{:S(2)}, u32[]{:S(2)}) collective-permute-start(f32[2,2,1,5120]{3,2,1,0:T(1,128)} %get-tuple-element.20), channel_id=1, source_target_pairs={{0,1},{1,2},{2,3},{3,4},{4,5},{5,6},{6,7},{7,8},{8,9},{9,10},{10,1... | collective-permute-start | bytes 245768 | tf_op jit(solution)/shard_map/ppermute | solution.py:18
  243.3 8.7 %collective-permute-start.16 = (f32[4,2,1,5120]{3,2,1,0:T(1,128)S(1)}, f32[4,2,1,5120]{3,2,1,0:T(1,128)S(1)}, u32[]{:S(2)}, u32[]{:S(2)}) collective-permute-start(f32[4,2,1,5120]{3,2,1,0:T(1,128)S(1)} %fusion.210), channel_id=1, source_target_pairs={{1,0},{2,1},{3,2},{4,3},{5,4},{6,5},{7,6},{8,7},{9,8},{10,9},{11,1... | collective-permute-start | bytes 491528 | tf_op jit(solution)/shard_map/ppermute | solution.py:18
  (59 other events, 205.4 us)

commit v2 on v1

--- a/solution.py
+++ b/solution.py
@@ -1,7 +1,13 @@
+import functools
+
 import jax
 import jax.numpy as jnp
 from jax import lax
+from jax.experimental import pallas as pl
+from jax.experimental.pallas import tpu as pltpu
 from jax.sharding import PartitionSpec as P
+
+MESH = pl.DeviceIdType.MESH
 
 ITERS = 3
 
@@ -35,6 +41,73 @@
         + frac_row * (1.0 - frac_col) * lower
         + frac_row * frac_col * shift_left(lower)
     )
+
+
+def gz_kernel(nb, send_ref, own_ref, recv_ref, prev_ref, next_ref, send_sems, recv_sems):
+    me = lax.axis_index("gz")
+    last = own_ref.shape[0] - 1
+    barrier = pltpu.get_barrier_semaphore()
+    for k in range(1, nb):
+        pl.semaphore_signal(
+            barrier, inc=1, device_id={"gz": lax.rem(me + k, nb)}, device_id_type=MESH
+        )
+    pl.semaphore_wait(barrier, nb - 1)
+    copies = []
+    for k in range(1, nb):
+        dest = lax.rem(me + k, nb)
+        copies.append(
+            pltpu.make_async_remote_copy(
+                src_ref=send_ref.at[dest],
+                dst_ref=recv_ref.at[me],
+                send_sem=send_sems.at[k],
+                recv_sem=recv_sems.at[k],
+                device_id={"gz": dest},
+                device_id_type=MESH,
+            )
+        )
+    copies.append(
+        pltpu.make_async_remote_copy(
+            src_ref=own_ref.at[last],
+            dst_ref=prev_ref,
+            send_sem=send_sems.at[nb],
+            recv_sem=recv_sems.at[nb],
+            device_id={"gz": lax.rem(me + 1, nb)},
+            device_id_type=MESH,
+        )
+    )
+    copies.append(
+        pltpu.make_async_remote_copy(
+            src_ref=own_ref.at[0],
+            dst_ref=next_ref,
+            send_sem=send_sems.at[nb + 1],
+            recv_sem=recv_sems.at[nb + 1],
+            device_id={"gz": lax.rem(me + nb - 1, nb)},
+            device_id_type=MESH,
+        )
+    )
+    for c in copies:
+        c.start()
+    for c in copies:
+        c.wait()
+
+
+def gz_exchange(send, own):
+    nb = send.shape[0]
+    face = own.shape[1:]
+    moved = 4 * (send.size + 2 * own[0].size)
+    return pl.pallas_call(
+        functools.partial(gz_kernel, nb),
+        out_shape=(
+            jax.ShapeDtypeStruct(send.shape, send.dtype),
+            jax.ShapeDtypeStruct(face, own.dtype),
+            jax.ShapeDtypeStruct(face, own.dtype),
+        ),
+        in_specs=[pl.BlockSpec(memory_space=pl.ANY)] * 2,
+        out_specs=[pl.BlockSpec(memory_space=pl.ANY)] * 3,
+        scratch_shapes=[pltpu.SemaphoreType.DMA((nb + 2,)), pltpu.SemaphoreType.DMA((nb + 2,))],
+        compiler_params=pltpu.CompilerParams(collective_id=0, has_side_effects=True),
+        cost_estimate=pl.CostEstimate(flops=0, bytes_accessed=2 * moved, transcendentals=0),
+    )(send, own)
 
 
 def body(disp, vel, stiff_class, valid, class_table, warp, spring_z, skip_partner):
@@ -74,12 +147,10 @@
         send = field[0][None]
         for l in range(1, local_count):
             send = jnp.where((send_sel == l)[:, None, None, None], field[l][None], send)
-        recv = lax.all_to_all(send, "gz", 0, 0, tiled=True)
+        recv, prev_face, next_face = gz_exchange(send, field)
         partner8 = jnp.stack(
             [lax.dynamic_index_in_dim(recv, src_block[l], 0, keepdims=False) for l in range(local_count)]
         )
-        prev_face = shift_rows(field[-1], "gz", True)
-        next_face = shift_rows(field[0], "gz", False)
         up = shift_rows(field[:, :, -1:], "tile", True)
         down = shift_rows(field[:, :, :1], "tile", False)
         field_ext = jnp.concatenate([up, field, down], axis=2)

time: 262 us -> 293 us (1.12)
  the two profiles are of different devices: /device:TPU:25 before, /device:TPU:34 now
where the time goes in v2:
time: 293 us; the launch traced here: 292 us
  Pallas kernels  154 us (53%)
  starting transfers between devices  40.7 us (14%)
  between operations  32.8 us (11%)
  local copies, waits for them, and re-layouts  28.3 us (10%)
  other arithmetic  26.1 us (9%)
  waiting for transfers between devices  9.25 us (3%)
    pallas_call x3, Pallas kernels, gz_exchange(): pl.pallas_call(functools.partial(gz_kernel, nb), out_shape=(jax.ShapeDtyp...  154 us
    ppermute x11, starting transfers between devices, shift_rows(): return lax.ppermute(block, axis, pairs)  40.7 us
    another operation x6, other arithmetic, body(): force = jnp.stack(forces)  9.65 us
    ppermute x11, waiting for transfers between devices, shift_rows(): return lax.ppermute(block, axis, pairs)  9.25 us
    slice x17, local copies, waits for them, and re-layouts, shift_left(): field[..., 1:]  7.01 us
  transfers between devices with their start and end apart: 11, of which 2 were waited for; matrix products, arithmetic and copies ran while one was open for 8% of the time, Pallas kernels for 0%

profile of v2, /device:TPU:34, one launch (start us, length us, event | category | flops | bytes accessed | tf_op | source)
XLA Modules:
  0.0 291.5 jit_solution(18204670111044736183)
XLA Ops:
  6.5 1.8 broadcast_select_fusion.2.send_ref
  8.4 55.9 %shard_map.95 = (f32[8,2,8,5120]{3,2,1,0:T(8,128)}, f32[2,8,5120]{2,1,0:T(8,128)}, f32[2,8,5120]{2,1,0:T(8,128)}) custom-call(f32[8,2,8,5120]{3,2,1,0:T(8,128)} %broadcast_select_fusion.2.send_ref, f32[2,2,8,5120]{3,2,1,0:T(8,128)} %own_ref.1), custom_call_target="tpu_custom_call" | custom-call | bytes 6553600 | tf_op jit(solution)/shard_map/pallas_call | solution.py:98
  68.1 4.1 %collective-permute-start.4 = (f32[4,2,1,5120]{3,2,1,0:T(1,128)S(1)}, f32[4,2,1,5120]{3,2,1,0:T(1,128)}, u32[]{:S(2)}, u32[]{:S(2)}) collective-permute-start(f32[4,2,1,5120]{3,2,1,0:T(1,128)S(1)} %fusion.212), channel_id=1, source_target_pairs={{1,0},{2,1},{3,2},{4,3},{5,4},{6,5},{7,6},{8,7},{9,8},{10,9},{11,1... | collective-permute-start | bytes 491528 | tf_op jit(solution)/shard_map/ppermute | solution.py:24
  72.9 3.3 %collective-permute-start.3 = (f32[2,2,1,5120]{3,2,1,0:T(1,128)}, f32[2,2,1,5120]{3,2,1,0:T(1,128)}, u32[]{:S(2)}, u32[]{:S(2)}) collective-permute-start(f32[2,2,1,5120]{3,2,1,0:T(1,128)} %get-tuple-element.67), channel_id=1, source_target_pairs={{1,0},{2,1},{3,2},{4,3},{5,4},{6,5},{7,6},{8,7},{9,8},{10,9},{11,1... | collective-permute-start | bytes 245768 | tf_op jit(solution)/shard_map/ppermute | solution.py:24
  76.2 1.9 collective-permute-start.2
  79.7 5.2 %multiply_bitcast_fusion = f32[1,2,8,5120]{3,2,1,0:T(8,128)S(1)} fusion(s32[2,8,5120]{2,1,0:T(8,128)S(1)} %copy-done.62, f32[]{:T(128)} %bitcast.7, f32[]{:T(128)} %bitcast.6, f32[]{:T(128)} %bitcast.5, f32[]{:T(128)} %bitcast.4, f32[]{:T(128)} %bitcast.3, f32[]{:T(128)} %bitcast.2, f32[]{:T(128)} %bitcast.1, f32[]{:T(128)} %bitcast, ...), kind=kLoop, calls=%fused_computation.301 | loop fusion | flops 1474560 | bytes 983072 | tf_op jit(solution)/shard_map/stack | solution.py:123
  85.7 5.7 %collective-permute-start.1 = (f32[2,2,1,5120]{3,2,1,0:T(1,128)}, f32[2,2,1,5120]{3,2,1,0:T(1,128)}, u32[]{:S(2)}, u32[]{:S(2)}) collective-permute-start(f32[2,2,1,5120]{3,2,1,0:T(1,128)} %get-tuple-element.63), channel_id=1, source_target_pairs={{1,0},{2,1},{3,2},{4,3},{5,4},{6,5},{7,6},{8,7},{9,8},{10,9},{11,1... | collective-permute-start | bytes 245768 | tf_op jit(solution)/shard_map/ppermute | solution.py:24
  91.4 1.9 collective-permute-start
  94.3 1.2 fusion.234
  107.3 1.9 slice.652
  130.8 1.3 dynamic-update-slice.1
  133.9 1.3 slice_bitcast_fusion.27
  135.5 1.6 fusion.85
  137.2 1.6 fusion.101
  140.8 1.8 broadcast_select_fusion.1.send_ref
  142.8 48.2 %shard_map.96 = (f32[8,2,8,5120]{3,2,1,0:T(8,128)}, f32[2,8,5120]{2,1,0:T(8,128)}, f32[2,8,5120]{2,1,0:T(8,128)}) custom-call(f32[8,2,8,5120]{3,2,1,0:T(8,128)} %broadcast_select_fusion.1.send_ref, f32[2,2,8,5120]{3,2,1,0:T(8,128)} %copy-done.3), custom_call_target="tpu_custom_call" | custom-call | bytes 6553600 | tf_op jit(solution)/shard_map/pallas_call | solution.py:98
  191.0 1.2 constant_dynamic-slice_fusion.2
  192.3 7.5 %collective-permute-start.6 = (f32[2,2,1,5120]{3,2,1,0:T(1,128)S(1)}, f32[2,2,1,5120]{3,2,1,0:T(1,128)S(1)}, u32[]{:S(2)}, u32[]{:S(2)}) collective-permute-start(f32[2,2,1,5120]{3,2,1,0:T(1,128)S(1)} %copy-done.63), channel_id=1, source_target_pairs={{1,0},{2,1},{3,2},{4,3},{5,4},{6,5},{7,6},{8,7},{9,8},{10,9},{11,1... | collective-permute-start | bytes 245768 | tf_op jit(solution)/shard_map/ppermute | solution.py:24
  200.2 1.9 collective-permute-start.7
  202.2 2.6 collective-permute-start.5
  205.8 4.3 %collective-permute-done.5 = f32[2,2,1,5120]{3,2,1,0:T(1,128)S(1)} collective-permute-done((f32[2,2,1,5120]{3,2,1,0:T(1,128)S(1)}, f32[2,2,1,5120]{3,2,1,0:T(1,128)S(1)}, u32[]{:S(2)}, u32[]{:S(2)}) %collective-permute-start.5) | collective-permute-done | bytes 81952 | tf_op jit(solution)/shard_map/ppermute | solution.py:24
  210.1 1.6 fusion.53
  211.7 1.6 fusion.69
  215.0 1.8 broadcast_select_fusion.send_ref
  216.9 50.4 %shard_map.97 = (f32[8,2,8,5120]{3,2,1,0:T(8,128)}, f32[2,8,5120]{2,1,0:T(8,128)}, f32[2,8,5120]{2,1,0:T(8,128)}) custom-call(f32[8,2,8,5120]{3,2,1,0:T(8,128)} %broadcast_select_fusion.send_ref, f32[2,2,8,5120]{3,2,1,0:T(8,128)} %copy-done.1), custom_call_target="tpu_custom_call" | custom-call | bytes 6553600 | tf_op jit(solution)/shard_map/pallas_call | solution.py:98
  268.6 6.4 %collective-permute-start.9 = (f32[2,2,1,5120]{3,2,1,0:T(1,128)S(1)}, f32[2,2,1,5120]{3,2,1,0:T(1,128)S(1)}, u32[]{:S(2)}, u32[]{:S(2)}) collective-permute-start(f32[2,2,1,5120]{3,2,1,0:T(1,128)S(1)} %get-tuple-element.39), channel_id=1, source_target_pairs={{1,0},{2,1},{3,2},{4,3},{5,4},{6,5},{7,6},{8,7},{9,8},{10,9},{11,1... | collective-permute-start | bytes 245768 | tf_op jit(solution)/shard_map/ppermute | solution.py:24
  275.5 3.3 %collective-permute-start.10 = (f32[4,2,1,5120]{3,2,1,0:T(1,128)S(1)}, f32[4,2,1,5120]{3,2,1,0:T(1,128)S(1)}, u32[]{:S(2)}, u32[]{:S(2)}) collective-permute-start(f32[4,2,1,5120]{3,2,1,0:T(1,128)S(1)} %fusion.210), channel_id=1, source_target_pairs={{1,0},{2,1},{3,2},{4,3},{5,4},{6,5},{7,6},{8,7},{9,8},{10,9},{11,1... | collective-permute-start | bytes 491528 | tf_op jit(solution)/shard_map/ppermute | solution.py:24
  278.8 1.9 collective-permute-start.8
  281.7 5.0 %collective-permute-done.8 = f32[2,2,1,5120]{3,2,1,0:T(1,128)S(1)} collective-permute-done((f32[2,2,1,5120]{3,2,1,0:T(1,128)S(1)}, f32[2,2,1,5120]{3,2,1,0:T(1,128)S(1)}, u32[]{:S(2)}, u32[]{:S(2)}) %collective-permute-start.8) | collective-permute-done | bytes 81952 | tf_op jit(solution)/shard_map/ppermute | solution.py:24
  286.7 1.6 fusion.21
  288.4 1.7 fusion.37
  290.1 1.5 multiply_add_fusion
  (205 shorter events, 25.8 us)
Async XLA Ops:
  64.2 7.9 %copy-start = (f32[2,2,8,5120]{3,2,1,0:T(8,128)S(1)}, f32[2,2,8,5120]{3,2,1,0:T(8,128)}, u32[]{:S(2)}) copy-start(f32[2,2,8,5120]{3,2,1,0:T(8,128)} %own_ref.1) | copy-start | bytes 1966084
  66.7 11.4 %copy-start.59 = (s32[2,8,5120]{2,1,0:T(8,128)S(1)}, s32[2,8,5120]{2,1,0:T(8,128)}, u32[]{:S(2)}) copy-start(s32[2,8,5120]{2,1,0:T(8,128)} %param.11) | copy-start | bytes 983044
  67.9 11.0 %copy-start.64 = (f32[8]{0:T(128)S(1)}, f32[8]{0:T(128)}, u32[]{:S(2)}) copy-start(f32[8]{0:T(128)} %param.12) | copy-start | bytes 100
  67.9 11.7 %copy-start.62 = (s32[2,8,5120]{2,1,0:T(8,128)S(1)}, s32[2,8,5120]{2,1,0:T(8,128)}, u32[]{:S(2)}) copy-start(s32[2,8,5120]{2,1,0:T(8,128)} %param.10) | copy-start | bytes 983044
  68.1 65.8 %collective-permute-start.4 = (f32[4,2,1,5120]{3,2,1,0:T(1,128)S(1)}, f32[4,2,1,5120]{3,2,1,0:T(1,128)}, u32[]{:S(2)}, u32[]{:S(2)}) collective-permute-start(f32[4,2,1,5120]{3,2,1,0:T(1,128)S(1)} %fusion.212), channel_id=1, source_target_pairs={{1,0},{2,1},{3,2},{4,3},{5,4},{6,5},{7,6},{8,7},{9,8},{10,9},{11,1... | collective-permute-start | bytes 491528 | tf_op jit(solution)/shard_map/ppermute | solution.py:24
  72.9 57.9 %collective-permute-start.3 = (f32[2,2,1,5120]{3,2,1,0:T(1,128)}, f32[2,2,1,5120]{3,2,1,0:T(1,128)}, u32[]{:S(2)}, u32[]{:S(2)}) collective-permute-start(f32[2,2,1,5120]{3,2,1,0:T(1,128)} %get-tuple-element.67), channel_id=1, source_target_pairs={{1,0},{2,1},{3,2},{4,3},{5,4},{6,5},{7,6},{8,7},{9,8},{10,9},{11,1... | collective-permute-start | bytes 245768 | tf_op jit(solution)/shard_map/ppermute | solution.py:24
  76.2 58.9 %collective-permute-start.2 = (f32[2,2,1,5120]{3,2,1,0:T(1,128)}, f32[2,2,1,5120]{3,2,1,0:T(1,128)S(1)}, u32[]{:S(2)}, u32[]{:S(2)}) collective-permute-start(f32[2,2,1,5120]{3,2,1,0:T(1,128)} %get-tuple-element.66), channel_id=1, source_target_pairs={{0,1},{1,2},{2,3},{3,4},{4,5},{5,6},{6,7},{7,8},{8,9},{9,10},{10,1... | collective-permute-start | bytes 245768 | tf_op jit(solution)/shard_map/ppermute | solution.py:24
  78.9 12.5 %copy-start.13 = (f32[1,2,8,5120]{3,2,1,0:T(8,128)}, f32[1,2,8,5120]{3,2,1,0:T(8,128)S(1)}, u32[]{:S(2)}) copy-start(f32[1,2,8,5120]{3,2,1,0:T(8,128)S(1)} %get-tuple-element.79) | copy-start | bytes 983044
  84.9 6.5 %copy-start.15 = (f32[1,2,8,5120]{3,2,1,0:T(8,128)}, f32[1,2,8,5120]{3,2,1,0:T(8,128)S(1)}, u32[]{:S(2)}) copy-start(f32[1,2,8,5120]{3,2,1,0:T(8,128)S(1)} %multiply_bitcast_fusion) | copy-start | bytes 983044
  84.9 8.5 %copy-start.45 = (f32[2,8,5120]{2,1,0:T(8,128)S(1)}, f32[2,8,5120]{2,1,0:T(8,128)}, u32[]{:S(2)}) copy-start(f32[2,8,5120]{2,1,0:T(8,128)} %get-tuple-element.12) | copy-start | bytes 983044
  85.7 43.0 %collective-permute-start.1 = (f32[2,2,1,5120]{3,2,1,0:T(1,128)}, f32[2,2,1,5120]{3,2,1,0:T(1,128)}, u32[]{:S(2)}, u32[]{:S(2)}) collective-permute-start(f32[2,2,1,5120]{3,2,1,0:T(1,128)} %get-tuple-element.63), channel_id=1, source_target_pairs={{1,0},{2,1},{3,2},{4,3},{5,4},{6,5},{7,6},{8,7},{9,8},{10,9},{11,1... | collective-permute-start | bytes 245768 | tf_op jit(solution)/shard_map/ppermute | solution.py:24
  91.4 37.2 %collective-permute-start = (f32[2,2,1,5120]{3,2,1,0:T(1,128)}, f32[2,2,1,5120]{3,2,1,0:T(1,128)}, u32[]{:S(2)}, u32[]{:S(2)}) collective-permute-start(f32[2,2,1,5120]{3,2,1,0:T(1,128)} %get-tuple-element.62), channel_id=1, source_target_pairs={{0,1},{1,2},{2,3},{3,4},{4,5},{5,6},{6,7},{7,8},{8,9},{9,10},{10,1... | collective-permute-start | bytes 245768 | tf_op jit(solution)/shard_map/ppermute | solution.py:24
  95.6 25.5 %copy-start.66 = (f32[2,3]{1,0:T(2,128)S(1)}, f32[2,3]{1,0:T(2,128)}, u32[]{:S(2)}) copy-start(f32[2,3]{1,0:T(2,128)} %param.14) | copy-start | bytes 76
  95.6 33.1 %copy-start.14 = (f32[1,2,8,5120]{3,2,1,0:T(8,128)S(1)}, f32[1,2,8,5120]{3,2,1,0:T(8,128)}, u32[]{:S(2)}) copy-start(f32[1,2,8,5120]{3,2,1,0:T(8,128)} %copy-done.13) | copy-start | bytes 983044
  95.6 33.1 %copy-start.16 = (f32[1,2,8,5120]{3,2,1,0:T(8,128)S(1)}, f32[1,2,8,5120]{3,2,1,0:T(8,128)}, u32[]{:S(2)}) copy-start(f32[1,2,8,5120]{3,2,1,0:T(8,128)} %copy-done.15) | copy-start | bytes 983044
  192.3 12.8 %collective-permute-start.6 = (f32[2,2,1,5120]{3,2,1,0:T(1,128)S(1)}, f32[2,2,1,5120]{3,2,1,0:T(1,128)S(1)}, u32[]{:S(2)}, u32[]{:S(2)}) collective-permute-start(f32[2,2,1,5120]{3,2,1,0:T(1,128)S(1)} %copy-done.63), channel_id=1, source_target_pairs={{1,0},{2,1},{3,2},{4,3},{5,4},{6,5},{7,6},{8,7},{9,8},{10,9},{11,1... | collective-permute-start | bytes 245768 | tf_op jit(solution)/shard_map/ppermute | solution.py:24
  199.9 5.2 %copy-start.4 = (f32[2,2,8,5120]{3,2,1,0:T(8,128)S(1)}, f32[2,2,8,5120]{3,2,1,0:T(8,128)}, u32[]{:S(2)}) copy-start(f32[2,2,8,5120]{3,2,1,0:T(8,128)} %copy-done.3) | copy-start | bytes 1966084
  200.2 5.5 %collective-permute-start.7 = (f32[4,2,1,5120]{3,2,1,0:T(1,128)S(1)}, f32[4,2,1,5120]{3,2,1,0:T(1,128)S(1)}, u32[]{:S(2)}, u32[]{:S(2)}) collective-permute-start(f32[4,2,1,5120]{3,2,1,0:T(1,128)S(1)} %fusion.211), channel_id=1, source_target_pairs={{1,0},{2,1},{3,2},{4,3},{5,4},{6,5},{7,6},{8,7},{9,8},{10,9},{11,1... | collective-permute-start | bytes 491528 | tf_op jit(solution)/shard_map/ppermute | solution.py:24
  202.2 7.9 %collective-permute-start.5 = (f32[2,2,1,5120]{3,2,1,0:T(1,128)S(1)}, f32[2,2,1,5120]{3,2,1,0:T(1,128)S(1)}, u32[]{:S(2)}, u32[]{:S(2)}) collective-permute-start(f32[2,2,1,5120]{3,2,1,0:T(1,128)S(1)} %get-tuple-element.46), channel_id=1, source_target_pairs={{0,1},{1,2},{2,3},{3,4},{4,5},{5,6},{6,7},{7,8},{8,9},{9,10},{10,1... | collective-permute-start | bytes 245768 | tf_op jit(solution)/shard_map/ppermute | solution.py:24
  205.2 4.9 %copy-start.21 = (f32[8,5120]{1,0:T(8,128)S(1)}, f32[8,5120]{1,0:T(8,128)}, u32[]{:S(2)}) copy-start(f32[8,5120]{1,0:T(8,128)} %copy-done.20) | copy-start | bytes 491524
  205.2 4.8 %copy-start.24 = (f32[8,5120]{1,0:T(8,128)S(1)}, f32[8,5120]{1,0:T(8,128)}, u32[]{:S(2)}) copy-start(f32[8,5120]{1,0:T(8,128)} %copy-done.23) | copy-start | bytes 491524
  205.2 4.8 %copy-start.36 = (f32[8,5120]{1,0:T(8,128)S(1)}, f32[8,5120]{1,0:T(8,128)}, u32[]{:S(2)}) copy-start(f32[8,5120]{1,0:T(8,128)} %get-tuple-element.51) | copy-start | bytes 491524
  205.2 4.8 %copy-start.39 = (f32[8,5120]{1,0:T(8,128)S(1)}, f32[8,5120]{1,0:T(8,128)}, u32[]{:S(2)}) copy-start(f32[8,5120]{1,0:T(8,128)} %get-tuple-element.52) | copy-start | bytes 491524
  268.6 12.5 %collective-permute-start.9 = (f32[2,2,1,5120]{3,2,1,0:T(1,128)S(1)}, f32[2,2,1,5120]{3,2,1,0:T(1,128)S(1)}, u32[]{:S(2)}, u32[]{:S(2)}) collective-permute-start(f32[2,2,1,5120]{3,2,1,0:T(1,128)S(1)} %get-tuple-element.39), channel_id=1, source_target_pairs={{1,0},{2,1},{3,2},{4,3},{5,4},{6,5},{7,6},{8,7},{9,8},{10,9},{11,1... | collective-permute-start | bytes 245768 | tf_op jit(solution)/shard_map/ppermute | solution.py:24
  275.1 5.9 %copy-start.2 = (f32[2,2,8,5120]{3,2,1,0:T(8,128)S(1)}, f32[2,2,8,5120]{3,2,1,0:T(8,128)}, u32[]{:S(2)}) copy-start(f32[2,2,8,5120]{3,2,1,0:T(8,128)} %copy-done.1) | copy-start | bytes 1966084
  275.5 6.2 %collective-permute-start.10 = (f32[4,2,1,5120]{3,2,1,0:T(1,128)S(1)}, f32[4,2,1,5120]{3,2,1,0:T(1,128)S(1)}, u32[]{:S(2)}, u32[]{:S(2)}) collective-permute-start(f32[4,2,1,5120]{3,2,1,0:T(1,128)S(1)} %fusion.210), channel_id=1, source_target_pairs={{1,0},{2,1},{3,2},{4,3},{5,4},{6,5},{7,6},{8,7},{9,8},{10,9},{11,1... | collective-permute-start | bytes 491528 | tf_op jit(solution)/shard_map/ppermute | solution.py:24
  278.8 7.9 %collective-permute-start.8 = (f32[2,2,1,5120]{3,2,1,0:T(1,128)S(1)}, f32[2,2,1,5120]{3,2,1,0:T(1,128)S(1)}, u32[]{:S(2)}, u32[]{:S(2)}) collective-permute-start(f32[2,2,1,5120]{3,2,1,0:T(1,128)S(1)} %get-tuple-element.38), channel_id=1, source_target_pairs={{0,1},{1,2},{2,3},{3,4},{4,5},{5,6},{6,7},{7,8},{8,9},{9,10},{10,1... | collective-permute-start | bytes 245768 | tf_op jit(solution)/shard_map/ppermute | solution.py:24
  281.1 5.5 %copy-start.22 = (f32[8,5120]{1,0:T(8,128)S(1)}, f32[8,5120]{1,0:T(8,128)}, u32[]{:S(2)}) copy-start(f32[8,5120]{1,0:T(8,128)} %copy-done.20) | copy-start | bytes 491524
  281.1 5.5 %copy-start.25 = (f32[8,5120]{1,0:T(8,128)S(1)}, f32[8,5120]{1,0:T(8,128)}, u32[]{:S(2)}) copy-start(f32[8,5120]{1,0:T(8,128)} %copy-done.23) | copy-start | bytes 491524
  281.2 5.5 %copy-start.37 = (f32[8,5120]{1,0:T(8,128)S(1)}, f32[8,5120]{1,0:T(8,128)}, u32[]{:S(2)}) copy-start(f32[8,5120]{1,0:T(8,128)} %get-tuple-element.51) | copy-start | bytes 491524
  281.2 5.5 %copy-start.40 = (f32[8,5120]{1,0:T(8,128)S(1)}, f32[8,5120]{1,0:T(8,128)}, u32[]{:S(2)}) copy-start(f32[8,5120]{1,0:T(8,128)} %get-tuple-element.52) | copy-start | bytes 491524
  281.2 5.5 %copy-start.43 = (f32[8,5120]{1,0:T(8,128)S(1)}, f32[8,5120]{1,0:T(8,128)}, u32[]{:S(2)}) copy-start(f32[8,5120]{1,0:T(8,128)} %get-tuple-element.53) | copy-start | bytes 491524
  (46 other events, 89.2 us)

commit v3 on v1

v3 whole, which is shorter than its diff:
```python
import jax
import jax.numpy as jnp
from jax import lax
from jax.experimental import pallas as pl
from jax.experimental.pallas import tpu as pltpu
from jax.sharding import PartitionSpec as P


ITERS = 3


DAMPING = 0.9
STEP = 0.1


def shift_rows(block, axis, forward):
    count = lax.axis_size(axis)
    pairs = [(i, i + 1) for i in range(count - 1)]
    if not forward:
        pairs = [(t, s) for s, t in pairs]
    return lax.ppermute(block, axis, pairs)


def shift_left(field):
    return jnp.concatenate([field[..., 1:], jnp.zeros_like(field[..., :1])], axis=-1)


def shift_right(field):
    return jnp.concatenate([jnp.zeros_like(field[..., :1]), field[..., :-1]], axis=-1)


def update_kernel(scal_ref, sel_ref, x_ref, v_ref, k_ref, alive_ref, part_ref, up_ref, down_ref,
                  prevf_ref, nextf_ref, below_ref, xo_ref, vo_ref, send_ref):
    L, ncomp, R, C = x_ref.shape
    rows = lax.broadcasted_iota(jnp.int32, (R, C), 0)
    cols = lax.broadcasted_iota(jnp.int32, (R, C), 1)
    first_row = rows == 0
    last_row = rows == R - 1

    def shl(a):
        return jnp.where(cols == C - 1, 0.0, pltpu.roll(a, C - 1, 1))

    def shr(a):
        return jnp.where(cols == 0, 0.0, pltpu.roll(a, 1, 1))

    def warp_of(src, row8, w):
        lower = jnp.where(last_row, row8, pltpu.roll(src, R - 1, 0))
        return w[0] * src + w[1] * shl(src) + w[2] * lower + w[3] * shl(lower)

    for l in range(L):
        ws = []
        for k in range(3):
            a = scal_ref[l, 3 + 2 * k]
            b = scal_ref[l, 4 + 2 * k]
            ws.append(((1.0 - a) * (1.0 - b), (1.0 - a) * b, a * (1.0 - b), a * b))
        k_up = k_ref[0, l]
        k_mid = k_ref[1, l]
        k_dn = k_ref[2, l]
        k_r = k_ref[3, l]
        k_l = k_ref[4, l]
        alive = alive_ref[l]
        for c in range(ncomp):
            x = x_ref[l, c]
            x_up = jnp.where(first_row, up_ref[pl.ds(l * ncomp + c, 1), :], pltpu.roll(x, 1, 0))
            x_dn = jnp.where(last_row, down_ref[pl.ds(l * ncomp + c, 1), :], pltpu.roll(x, R - 1, 0))
            inplane = k_mid * (
                k_up * (x_up - x) + k_dn * (x_dn - x) + k_r * (shr(x) - x) + k_l * (shl(x) - x)
            )
            if l == 0:
                prev_src, prev_row = prevf_ref[c], below_ref[pl.ds(c, 1), :]
            else:
                prev_src, prev_row = x_ref[l - 1, c], down_ref[pl.ds((l - 1) * ncomp + c, 1), :]
            if l == L - 1:
                next_src, next_row = nextf_ref[c], below_ref[pl.ds(ncomp + c, 1), :]
            else:
                next_src, next_row = x_ref[l + 1, c], down_ref[pl.ds((l + 1) * ncomp + c, 1), :]
            part_row = below_ref[pl.ds((2 + l) * ncomp + c, 1), :]
            pull = scal_ref[l, 0] * (warp_of(prev_src, prev_row, ws[0]) - x)
            pull = pull + scal_ref[l, 1] * (warp_of(next_src, next_row, ws[1]) - x)
            pull = pull + scal_ref[l, 2] * (warp_of(part_ref[l, c], part_row, ws[2]) - x)
            force = inplane + pull
            vel = alive * (DAMPING * v_ref[l, c] + STEP * force)
            vo_ref[l, c] = vel
            xo_ref[l, c] = x + STEP * vel
    for d in range(send_ref.shape[0]):
        send_ref[d] = xo_ref[sel_ref[d]]


def update(scal, sel, x, v, kst, alive, part, up, down, prevf, nextf, below):
    nb = sel.shape[0]
    vmem = pl.BlockSpec(memory_space=pltpu.VMEM)
    smem = pl.BlockSpec(memory_space=pltpu.SMEM)
    moved = 4 * (3 * x.size + kst.size + alive.size + part.size + 3 * x[0].size + nb * x[0].size)
    return pl.pallas_call(
        update_kernel,
        out_shape=(
            jax.ShapeDtypeStruct(x.shape, x.dtype),
            jax.ShapeDtypeStruct(x.shape, x.dtype),
            jax.ShapeDtypeStruct((nb,) + x.shape[1:], x.dtype),
        ),
        in_specs=[smem, smem] + [vmem] * 10,
        out_specs=[vmem] * 3,
        compiler_params=pltpu.CompilerParams(vmem_limit_bytes=48 * 1024 * 1024),
        cost_estimate=pl.CostEstimate(flops=80 * x.size, bytes_accessed=moved, transcendentals=0),
    )(scal, sel, x, v, kst, alive, part, up, down, prevf, nextf, below)


def body(disp, vel, stiff_class, valid, class_table, warp, spring_z, skip_partner):
    local_count = disp.shape[0]
    block_count = lax.axis_size("gz")
    block_index = lax.axis_index("gz")
    total = local_count * block_count
    alive = valid.astype(jnp.float32)
    kappa = jnp.zeros(stiff_class.shape, jnp.float32)
    for level in range(class_table.shape[0]):
        kappa = jnp.where(stiff_class == level, class_table[level], kappa)
    kappa = kappa * alive
    stiff = jnp.stack([kappa, alive])
    stiff_ext = jnp.concatenate(
        [
            shift_rows(stiff[:, :, -1:], "tile", True),
            stiff,
            shift_rows(stiff[:, :, :1], "tile", False),
        ],
        axis=2,
    )
    kap_ext = stiff_ext[0]
    alive_mid = alive
    global_ids = block_index * local_count + jnp.arange(local_count, dtype=jnp.int32)
    has_prev = (global_ids > 0).astype(jnp.float32)
    has_next = (global_ids < total - 1).astype(jnp.float32)

    mine = lax.dynamic_slice_in_dim(skip_partner, block_index * local_count, local_count, 0)
    src_block = mine // local_count
    wanted = skip_partner.reshape(block_count, local_count)
    hit = (wanted // local_count) == block_index
    send_sel = jnp.sum(jnp.where(hit, wanted % local_count, 0), axis=1)

    k_mid = kap_ext[:, 1:-1]
    kst = jnp.stack([kap_ext[:, :-2], k_mid, kap_ext[:, 2:], shift_right(k_mid), shift_left(k_mid)])
    scal = jnp.concatenate(
        [
            (spring_z[:, 0] * has_prev)[:, None],
            (spring_z[:, 1] * has_next)[:, None],
            spring_z[:, 2:3],
            warp.reshape(local_count, 6),
        ],
        axis=1,
    )
    ncomp = disp.shape[1]
    cols = disp.shape[3]

    field = disp
    velocity = vel
    send = field[0][None]
    for l in range(1, local_count):
        send = jnp.where((send_sel == l)[:, None, None, None], field[l][None], send)
    for _ in range(ITERS):
      recv = lax.all_to_all(send, "gz", 0, 0, tiled=True)
      partner8 = jnp.stack(
          [lax.dynamic_index_in_dim(recv, src_block[l], 0, keepdims=False) for l in range(local_count)]
      )
      prev_face = shift_rows(field[-1], "gz", True)
      next_face = shift_rows(field[0], "gz", False)
      up = shift_rows(field[:, :, -1:], "tile", True)
      down = shift_rows(field[:, :, :1], "tile", False)
      firsts = jnp.concatenate(
          [prev_face[None, :, :1], next_face[None, :, :1], partner8[:, :, :1]], axis=0
      )
      below = shift_rows(firsts, "tile", False)
      field, velocity, send = update(
          scal,
          send_sel,
          field,
          velocity,
          kst,
          alive_mid,
          partner8,
          up.reshape(local_count * ncomp, cols),
          down.reshape(local_count * ncomp, cols),
          prev_face,
          next_face,
          below.reshape((2 + local_count) * ncomp, cols),
      )
    return (field, velocity)


def solution(mesh):
    placed = (
        P("gz", None, "tile", None),
        P("gz", None, "tile", None),
        P("gz", "tile", None),
        P("gz", "tile", None),
        P(),
        P("gz", None, None),
        P("gz", None),
        P(),
    )
    return jax.shard_map(
        body,
        mesh=mesh,
        in_specs=placed,
        out_specs=(P("gz", None, "tile", None), P("gz", None, "tile", None)),
        check_vma=False,
    )
```

time: 262 us -> 251 us (0.958)
  the two profiles are of different devices: /device:TPU:25 before, /device:TPU:7 now
where the time goes in v3:
time: 251 us; the launch traced here: 249 us
  waiting for transfers between devices  116 us (46%)
  starting transfers between devices  70.7 us (28%)
  local copies, waits for them, and re-layouts  27.3 us (11%)
  other arithmetic  16.2 us (6%)
  Pallas kernels  14.3 us (6%)
  between operations  5.03 us (2%)
    ppermute x17, waiting for transfers between devices, shift_rows(): return lax.ppermute(block, axis, pairs)  94.3 us
    ppermute x17, starting transfers between devices, shift_rows(): return lax.ppermute(block, axis, pairs)  50.8 us
    all_to_all x3, waiting for transfers between devices, body(): recv = lax.all_to_all(send, 'gz', 0, 0, tiled=True)  21.7 us
    all_to_all x3, starting transfers between devices, body(): recv = lax.all_to_all(send, 'gz', 0, 0, tiled=True)  19.9 us
    pallas_call x3, Pallas kernels, update(): pl.pallas_call(update_kernel, out_shape=(jax.ShapeDtypeStruct(x.shape, x....  14.3 us
    unnamed x63, local copies, waits for them, and re-layouts  12.9 us
    ppermute x7, other arithmetic, shift_rows(): return lax.ppermute(block, axis, pairs)  5.74 us
    another operation x1, other arithmetic, body(): stiff = jnp.stack([kappa, alive])  5.14 us
  transfers between devices with their start and end apart: 20, of which 7 were waited for; matrix products, arithmetic and copies ran while one was open for 8% of the time, Pallas kernels for 0%

profile of v3, /device:TPU:7, one launch (start us, length us, event | category | flops | bytes accessed | tf_op | source)
XLA Modules:
  0.0 249.4 jit_solution(12662477865108941299)
XLA Ops:
  2.8 3.8 %collective-permute-start.2 = (f32[2,2,1,5120]{3,1,2,0:T(2,128)}, f32[2,2,1,5120]{3,1,2,0:T(2,128)}, u32[]{:S(2)}, u32[]{:S(2)}) collective-permute-start(f32[2,2,1,5120]{3,1,2,0:T(2,128)} %copy.22), channel_id=1, source_target_pairs={{0,1},{1,2},{2,3},{3,4},{4,5},{5,6},{6,7},{7,8},{8,9},{9,10},{10,1... | collective-permute-start | bytes 245768 | tf_op jit(solution)/shard_map/ppermute | solution.py:21
  9.3 5.1 %multiply_bitcast_fusion = f32[1,2,8,5120]{3,2,1,0:T(8,128)S(1)} fusion(s32[2,8,5120]{2,1,0:T(8,128)S(1)} %copy-done.22, f32[]{:T(128)} %bitcast.7, f32[]{:T(128)} %bitcast.6, f32[]{:T(128)} %bitcast.5, f32[]{:T(128)} %bitcast.4, f32[]{:T(128)} %bitcast.3, f32[]{:T(128)} %bitcast.2, f32[]{:T(128)} %bitcast.1, f32[]{:T(128)} %bitcast, ...), kind=kLoop, calls=%fused_computation.28 | loop fusion | flops 1474560 | bytes 983072 | tf_op jit(solution)/shard_map/stack | solution.py:118
  14.5 1.9 collective-permute-start
  16.5 2.4 collective-permute-start.1
  19.8 5.5 %collective-permute-start.4 = (f32[2,8,5120]{2,1,0:T(8,128)}, f32[2,8,5120]{2,1,0:T(8,128)S(1)}, u32[]{:S(2)}, u32[]{:S(2)}) collective-permute-start(f32[2,8,5120]{2,1,0:T(8,128)} %get-tuple-element.34), channel_id=1, source_target_pairs={{0,16},{16,32},{32,48},{48,64},{64,80},{80,96},{96,112},{1,17},{17... | collective-permute-start | bytes 983048 | tf_op jit(solution)/shard_map/ppermute | solution.py:21
  25.3 2.2 collective-permute-start.5
  27.7 2.9 %broadcast_select_fusion = f32[8,2,8,5120]{3,2,1,0:T(8,128)} fusion(f32[2,8,5120]{2,1,0:T(8,128)} %get-tuple-element.35, f32[2,8,5120]{2,1,0:T(8,128)} %get-tuple-element.34, pred[8]{0:T(512)(128)(4,1)S(1)} %broadcast_compare_fusion), kind=kLoop, calls=%fused_computation | loop fusion | flops 655360 | bytes 3276808 | tf_op jit(solution)/shard_map/jit(_where)/select_n | solution.py:157
  30.6 6.8 %all-to-all-start = ((f32[8,2,8,5120]{3,2,1,0:T(8,128)}), f32[8,2,8,5120]{3,2,1,0:T(8,128)}, u32[]{:S(2)}, u32[]{:S(2)}) async-start(f32[8,2,8,5120]{3,2,1,0:T(8,128)} %broadcast_select_fusion), calls=%async_computation | async-start | bytes 5242880 | tf_op jit(solution)/shard_map/all_to_all | solution.py:159
  42.8 2.4 collective-permute-start.3
  46.9 2.9 %collective-permute-done.3 = f32[2,2,1,5120]{3,1,2,0:T(2,128)} collective-permute-done((f32[2,2,1,5120]{3,1,2,0:T(2,128)}, f32[2,2,1,5120]{3,1,2,0:T(2,128)}, u32[]{:S(2)}, u32[]{:S(2)}) %collective-permute-start.3) | collective-permute-done | bytes 81952 | tf_op jit(solution)/shard_map/ppermute | solution.py:21
  52.1 21.7 %all-to-all-done = f32[8,2,8,5120]{3,2,1,0:T(8,128)} async-done(((f32[8,2,8,5120]{3,2,1,0:T(8,128)}), f32[8,2,8,5120]{3,2,1,0:T(8,128)}, u32[]{:S(2)}, u32[]{:S(2)}) %all-to-all-start) | async-done | bytes 2621472 | tf_op jit(solution)/shard_map/all_to_all | solution.py:159
  75.2 3.0 %collective-permute-start.6 = (f32[4,2,1,5120]{3,2,1,0:T(1,128)S(1)}, f32[4,2,1,5120]{3,2,1,0:T(1,128)}, u32[]{:S(2)}, u32[]{:S(2)}) collective-permute-start(f32[4,2,1,5120]{3,2,1,0:T(1,128)S(1)} %pad_maximum_fusion.6), channel_id=1, source_target_pairs={{1,0},{2,1},{3,2},{4,3},{5,4},{6,5},{7,6},{8,7},{9,8},{10,9},{11,1... | collective-permute-start | bytes 491528 | tf_op jit(solution)/shard_map/ppermute | solution.py:21
  78.3 3.7 %collective-permute-done.6 = f32[4,2,1,5120]{3,2,1,0:T(1,128)} collective-permute-done((f32[4,2,1,5120]{3,2,1,0:T(1,128)S(1)}, f32[4,2,1,5120]{3,2,1,0:T(1,128)}, u32[]{:S(2)}, u32[]{:S(2)}) %collective-permute-start.6) | collective-permute-done | bytes 163872 | tf_op jit(solution)/shard_map/ppermute | solution.py:21
  86.5 5.0 %shard_map.95 = (f32[2,2,8,5120]{3,2,1,0:T(8,128)S(1)}, f32[2,2,8,5120]{3,2,1,0:T(8,128)S(1)}, f32[8,2,8,5120]{3,2,1,0:T(8,128)}) custom-call(f32[2,9]{1,0:T(2,128)S(1)} %pad_maximum_fusion.11.scal_ref, s32[8]{0:T(128)S(1)} %fusion.9.sel_ref, f32[2,2,8,5120]{3,2,1,0:T(8,128)S(1)} %copy-done.2, f32[2,2,8,5120]{3,2,1,0:T(8,128)S(1)} %copy-done.3, ...), custom_call_target="tpu_custom_call" | custom-call | flops 13107200 | bytes 8192000 | tf_op jit(solution)/shard_map/pallas_call | solution.py:94
  91.5 2.9 %collective-permute-start.10 = (f32[2,8,5120]{2,1,0:T(8,128)S(1)}, f32[2,8,5120]{2,1,0:T(8,128)S(1)}, u32[]{:S(2)}, u32[]{:S(2)}) collective-permute-start(f32[2,8,5120]{2,1,0:T(8,128)S(1)} %get-tuple-element.28), channel_id=1, source_target_pairs={{16,0},{32,16},{48,32},{64,48},{80,64},{96,80},{112,96},{17,1},{33... | collective-permute-start | bytes 983048 | tf_op jit(solution)/shard_map/ppermute | solution.py:21
  94.6 1.9 collective-permute-start.8
  96.5 3.6 %collective-permute-start.7 = (f32[2,2,1,5120]{3,2,1,0:T(1,128)S(1)}, f32[2,2,1,5120]{3,2,1,0:T(1,128)S(1)}, u32[]{:S(2)}, u32[]{:S(2)}) collective-permute-start(f32[2,2,1,5120]{3,2,1,0:T(1,128)S(1)} %get-tuple-element.31), channel_id=1, source_target_pairs={{0,1},{1,2},{2,3},{3,4},{4,5},{5,6},{6,7},{7,8},{8,9},{9,10},{10,1... | collective-permute-start | bytes 245768 | tf_op jit(solution)/shard_map/ppermute | solution.py:21
  100.2 6.5 %all-to-all-start.1 = ((f32[8,2,8,5120]{3,2,1,0:T(8,128)}), f32[8,2,8,5120]{3,2,1,0:T(8,128)}, u32[]{:S(2)}, u32[]{:S(2)}) async-start(f32[8,2,8,5120]{3,2,1,0:T(8,128)} %get-tuple-element.12), calls=%async_computation.1 | async-start | bytes 5242880 | tf_op jit(solution)/shard_map/all_to_all | solution.py:159
  106.7 4.6 %collective-permute-start.9 = (f32[2,8,5120]{2,1,0:T(8,128)S(1)}, f32[2,8,5120]{2,1,0:T(8,128)S(1)}, u32[]{:S(2)}, u32[]{:S(2)}) collective-permute-start(f32[2,8,5120]{2,1,0:T(8,128)S(1)} %get-tuple-element.29), channel_id=1, source_target_pairs={{0,16},{16,32},{32,48},{48,64},{64,80},{80,96},{96,112},{1,17},{17... | collective-permute-start | bytes 983048 | tf_op jit(solution)/shard_map/ppermute | solution.py:21
  111.9 39.9 %collective-permute-done.9.prevf_ref = f32[2,8,5120]{2,1,0:T(8,128)S(1)} collective-permute-done((f32[2,8,5120]{2,1,0:T(8,128)S(1)}, f32[2,8,5120]{2,1,0:T(8,128)S(1)}, u32[]{:S(2)}, u32[]{:S(2)}) %collective-permute-start.9) | collective-permute-done | bytes 327712 | tf_op jit(solution)/shard_map/ppermute | solution.py:21
  153.4 2.1 collective-permute-start.11
  155.6 4.5 %collective-permute-done.11 = f32[4,2,1,5120]{3,2,1,0:T(1,128)} collective-permute-done((f32[4,2,1,5120]{3,2,1,0:T(1,128)S(1)}, f32[4,2,1,5120]{3,2,1,0:T(1,128)}, u32[]{:S(2)}, u32[]{:S(2)}) %collective-permute-start.11) | collective-permute-done | bytes 163872 | tf_op jit(solution)/shard_map/ppermute | solution.py:21
  163.6 5.0 %shard_map.96 = (f32[2,2,8,5120]{3,2,1,0:T(8,128)S(1)}, f32[2,2,8,5120]{3,2,1,0:T(8,128)S(1)}, f32[8,2,8,5120]{3,2,1,0:T(8,128)}) custom-call(f32[2,9]{1,0:T(2,128)S(1)} %pad_maximum_fusion.11.scal_ref, s32[8]{0:T(128)S(1)} %fusion.9.sel_ref, f32[2,2,8,5120]{3,2,1,0:T(8,128)S(1)} %get-tuple-element.10.x_ref, f32[2,2,8,5120]{3,2,1,0:T(8,128)S(1)} %copy-done.7, ...), custom_call_target="tpu_custom_call" | custom-call | flops 13107200 | bytes 8192000 | tf_op jit(solution)/shard_map/pallas_call | solution.py:94
  171.5 1.9 collective-permute-start.13
  173.4 3.6 %collective-permute-start.12 = (f32[2,2,1,5120]{3,2,1,0:T(1,128)S(1)}, f32[2,2,1,5120]{3,2,1,0:T(1,128)S(1)}, u32[]{:S(2)}, u32[]{:S(2)}) collective-permute-start(f32[2,2,1,5120]{3,2,1,0:T(1,128)S(1)} %get-tuple-element.27), channel_id=1, source_target_pairs={{0,1},{1,2},{2,3},{3,4},{4,5},{5,6},{6,7},{7,8},{8,9},{9,10},{10,1... | collective-permute-start | bytes 245768 | tf_op jit(solution)/shard_map/ppermute | solution.py:21
  177.1 6.7 %all-to-all-start.2 = ((f32[8,2,8,5120]{3,2,1,0:T(8,128)}), f32[8,2,8,5120]{3,2,1,0:T(8,128)}, u32[]{:S(2)}, u32[]{:S(2)}) async-start(f32[8,2,8,5120]{3,2,1,0:T(8,128)} %get-tuple-element.15), calls=%async_computation.2 | async-start | bytes 5242880 | tf_op jit(solution)/shard_map/all_to_all | solution.py:159
  183.7 4.8 %collective-permute-start.14 = (f32[2,8,5120]{2,1,0:T(8,128)S(1)}, f32[2,8,5120]{2,1,0:T(8,128)S(1)}, u32[]{:S(2)}, u32[]{:S(2)}) collective-permute-start(f32[2,8,5120]{2,1,0:T(8,128)S(1)} %get-tuple-element.25), channel_id=1, source_target_pairs={{0,16},{16,32},{32,48},{48,64},{64,80},{80,96},{96,112},{1,17},{17... | collective-permute-start | bytes 983048 | tf_op jit(solution)/shard_map/ppermute | solution.py:21
  190.5 38.4 %collective-permute-done.14.prevf_ref = f32[2,8,5120]{2,1,0:T(8,128)S(1)} collective-permute-done((f32[2,8,5120]{2,1,0:T(8,128)S(1)}, f32[2,8,5120]{2,1,0:T(8,128)S(1)}, u32[]{:S(2)}, u32[]{:S(2)}) %collective-permute-start.14) | collective-permute-done | bytes 327712 | tf_op jit(solution)/shard_map/ppermute | solution.py:21
  231.0 2.2 collective-permute-start.16
  233.3 4.7 %collective-permute-done.16 = f32[4,2,1,5120]{3,2,1,0:T(1,128)} collective-permute-done((f32[4,2,1,5120]{3,2,1,0:T(1,128)S(1)}, f32[4,2,1,5120]{3,2,1,0:T(1,128)}, u32[]{:S(2)}, u32[]{:S(2)}) %collective-permute-start.16) | collective-permute-done | bytes 163872 | tf_op jit(solution)/shard_map/ppermute | solution.py:21
  238.1 2.1 reduce.6
  245.1 4.3 %shard_map.97 = (f32[2,2,8,5120]{3,2,1,0:T(8,128)}, f32[2,2,8,5120]{3,2,1,0:T(8,128)}, f32[8,2,8,5120]{3,2,1,0:T(8,128)}) custom-call(f32[2,9]{1,0:T(2,128)S(1)} %pad_maximum_fusion.11.scal_ref, s32[8]{0:T(128)S(1)} %fusion.9.sel_ref, f32[2,2,8,5120]{3,2,1,0:T(8,128)S(1)} %get-tuple-element.13.x_ref, f32[2,2,8,5120]{3,2,1,0:T(8,128)S(1)} %copy-done.5, ...), custom_call_target="tpu_custom_call" | custom-call | flops 13107200 | bytes 8192000 | tf_op jit(solution)/shard_map/pallas_call | solution.py:94
  (130 shorter events, 35.3 us)
Async XLA Ops:
  0.6 18.2 %copy-start.2 = (f32[2,2,8,5120]{3,2,1,0:T(8,128)S(1)}, f32[2,2,8,5120]{3,2,1,0:T(8,128)}, u32[]{:S(2)}) copy-start(f32[2,2,8,5120]{3,2,1,0:T(8,128)} %x_ref.1) | copy-start | bytes 1966084
  0.6 8.6 %copy-start.21 = (s32[2,8,5120]{2,1,0:T(8,128)S(1)}, s32[2,8,5120]{2,1,0:T(8,128)}, u32[]{:S(2)}) copy-start(s32[2,8,5120]{2,1,0:T(8,128)} %param.11) | copy-start | bytes 983044
  0.7 8.6 %copy-start.22 = (s32[2,8,5120]{2,1,0:T(8,128)S(1)}, s32[2,8,5120]{2,1,0:T(8,128)}, u32[]{:S(2)}) copy-start(s32[2,8,5120]{2,1,0:T(8,128)} %param.10) | copy-start | bytes 983044
  2.8 42.9 %collective-permute-start.2 = (f32[2,2,1,5120]{3,1,2,0:T(2,128)}, f32[2,2,1,5120]{3,1,2,0:T(2,128)}, u32[]{:S(2)}, u32[]{:S(2)}) collective-permute-start(f32[2,2,1,5120]{3,1,2,0:T(2,128)} %copy.22), channel_id=1, source_target_pairs={{0,1},{1,2},{2,3},{3,4},{4,5},{5,6},{6,7},{7,8},{8,9},{9,10},{10,1... | collective-permute-start | bytes 245768 | tf_op jit(solution)/shard_map/ppermute | solution.py:21
  9.2 18.2 %copy-start.27 = (s32[16]{0:T(128)S(1)}, s32[16]{0:T(128)}, u32[]{:S(2)}) copy-start(s32[16]{0:T(128)} %param.15) | copy-start | bytes 196
  14.5 28.2 %collective-permute-start = (f32[2,2,1,5120]{3,2,1,0:T(1,128)S(1)}, f32[2,2,1,5120]{3,2,1,0:T(1,128)S(1)}, u32[]{:S(2)}, u32[]{:S(2)}) collective-permute-start(f32[2,2,1,5120]{3,2,1,0:T(1,128)S(1)} %get-tuple-element.38), channel_id=1, source_target_pairs={{0,1},{1,2},{2,3},{3,4},{4,5},{5,6},{6,7},{7,8},{8,9},{9,10},{10,1... | collective-permute-start | bytes 245768 | tf_op jit(solution)/shard_map/ppermute | solution.py:21
  16.5 28.7 %collective-permute-start.1 = (f32[2,2,1,5120]{3,2,1,0:T(1,128)S(1)}, f32[2,2,1,5120]{3,2,1,0:T(1,128)S(1)}, u32[]{:S(2)}, u32[]{:S(2)}) collective-permute-start(f32[2,2,1,5120]{3,2,1,0:T(1,128)S(1)} %get-tuple-element.39), channel_id=1, source_target_pairs={{1,0},{2,1},{3,2},{4,3},{5,4},{6,5},{7,6},{8,7},{9,8},{10,9},{11,1... | collective-permute-start | bytes 245768 | tf_op jit(solution)/shard_map/ppermute | solution.py:21
  19.8 31.0 %collective-permute-start.4 = (f32[2,8,5120]{2,1,0:T(8,128)}, f32[2,8,5120]{2,1,0:T(8,128)S(1)}, u32[]{:S(2)}, u32[]{:S(2)}) collective-permute-start(f32[2,8,5120]{2,1,0:T(8,128)} %get-tuple-element.34), channel_id=1, source_target_pairs={{0,16},{16,32},{32,48},{48,64},{64,80},{80,96},{96,112},{1,17},{17... | collective-permute-start | bytes 983048 | tf_op jit(solution)/shard_map/ppermute | solution.py:21
  25.3 26.2 %collective-permute-start.5 = (f32[2,8,5120]{2,1,0:T(8,128)}, f32[2,8,5120]{2,1,0:T(8,128)S(1)}, u32[]{:S(2)}, u32[]{:S(2)}) collective-permute-start(f32[2,8,5120]{2,1,0:T(8,128)} %get-tuple-element.35), channel_id=1, source_target_pairs={{16,0},{32,16},{48,32},{64,48},{80,64},{96,80},{112,96},{17,1},{33... | collective-permute-start | bytes 983048 | tf_op jit(solution)/shard_map/ppermute | solution.py:21
  30.6 9.9 %copy-start.25 = (f32[2,3]{1,0:T(2,128)S(1)}, f32[2,3]{1,0:T(2,128)}, u32[]{:S(2)}) copy-start(f32[2,3]{1,0:T(2,128)} %param.14) | copy-start | bytes 76
  30.6 10.0 %copy-start.26 = (f32[2,3,2]{1,2,0:T(2,128)S(1)}, f32[2,3,2]{1,2,0:T(2,128)}, u32[]{:S(2)}) copy-start(f32[2,3,2]{1,2,0:T(2,128)} %param.13) | copy-start | bytes 148
  30.6 43.2 %all-to-all-start = ((f32[8,2,8,5120]{3,2,1,0:T(8,128)}), f32[8,2,8,5120]{3,2,1,0:T(8,128)}, u32[]{:S(2)}, u32[]{:S(2)}) async-start(f32[8,2,8,5120]{3,2,1,0:T(8,128)} %broadcast_select_fusion), calls=%async_computation | async-start | bytes 5242880 | tf_op jit(solution)/shard_map/all_to_all | solution.py:159
  42.8 7.0 %collective-permute-start.3 = (f32[2,2,1,5120]{3,1,2,0:T(2,128)}, f32[2,2,1,5120]{3,1,2,0:T(2,128)}, u32[]{:S(2)}, u32[]{:S(2)}) collective-permute-start(f32[2,2,1,5120]{3,1,2,0:T(2,128)} %copy.23), channel_id=1, source_target_pairs={{1,0},{2,1},{3,2},{4,3},{5,4},{6,5},{7,6},{8,7},{9,8},{10,9},{11,1... | collective-permute-start | bytes 245768 | tf_op jit(solution)/shard_map/ppermute | solution.py:21
  45.8 32.5 %copy-start = (f32[5,2,8,5120]{3,2,1,0:T(8,128)}, f32[5,2,8,5120]{3,2,1,0:T(8,128)S(1)}, u32[]{:S(2)}) copy-start(f32[5,2,8,5120]{3,2,1,0:T(8,128)S(1)} %bitcast_dynamic-update-slice_fusion.k_ref) | copy-start | bytes 4915204
  50.7 24.5 %copy-start.8 = (f32[2,8,5120]{2,1,0:T(8,128)}, f32[2,8,5120]{2,1,0:T(8,128)S(1)}, u32[]{:S(2)}) copy-start(f32[2,8,5120]{2,1,0:T(8,128)S(1)} %collective-permute-done.4.prevf_ref) | copy-start | bytes 983044
  51.4 23.8 %copy-start.10 = (f32[2,8,5120]{2,1,0:T(8,128)}, f32[2,8,5120]{2,1,0:T(8,128)S(1)}, u32[]{:S(2)}) copy-start(f32[2,8,5120]{2,1,0:T(8,128)S(1)} %collective-permute-done.5.nextf_ref) | copy-start | bytes 983044
  75.2 6.7 %collective-permute-start.6 = (f32[4,2,1,5120]{3,2,1,0:T(1,128)S(1)}, f32[4,2,1,5120]{3,2,1,0:T(1,128)}, u32[]{:S(2)}, u32[]{:S(2)}) collective-permute-start(f32[4,2,1,5120]{3,2,1,0:T(1,128)S(1)} %pad_maximum_fusion.6), channel_id=1, source_target_pairs={{1,0},{2,1},{3,2},{4,3},{5,4},{6,5},{7,6},{8,7},{9,8},{10,9},{11,1... | collective-permute-start | bytes 491528 | tf_op jit(solution)/shard_map/ppermute | solution.py:21
  91.5 8.7 %copy-start.6 = (f32[2,2,8,5120]{3,2,1,0:T(8,128)}, f32[2,2,8,5120]{3,2,1,0:T(8,128)S(1)}, u32[]{:S(2)}) copy-start(f32[2,2,8,5120]{3,2,1,0:T(8,128)S(1)} %get-tuple-element.11.v_ref) | copy-start | bytes 1966084
  91.5 20.4 %collective-permute-start.10 = (f32[2,8,5120]{2,1,0:T(8,128)S(1)}, f32[2,8,5120]{2,1,0:T(8,128)S(1)}, u32[]{:S(2)}, u32[]{:S(2)}) collective-permute-start(f32[2,8,5120]{2,1,0:T(8,128)S(1)} %get-tuple-element.28), channel_id=1, source_target_pairs={{16,0},{32,16},{48,32},{64,48},{80,64},{96,80},{112,96},{17,1},{33... | collective-permute-start | bytes 983048 | tf_op jit(solution)/shard_map/ppermute | solution.py:21
  94.6 16.7 %collective-permute-start.8 = (f32[2,2,1,5120]{3,2,1,0:T(1,128)S(1)}, f32[2,2,1,5120]{3,2,1,0:T(1,128)S(1)}, u32[]{:S(2)}, u32[]{:S(2)}) collective-permute-start(f32[2,2,1,5120]{3,2,1,0:T(1,128)S(1)} %get-tuple-element.30), channel_id=1, source_target_pairs={{1,0},{2,1},{3,2},{4,3},{5,4},{6,5},{7,6},{8,7},{9,8},{10,9},{11,1... | collective-permute-start | bytes 245768 | tf_op jit(solution)/shard_map/ppermute | solution.py:21
  96.5 15.1 %collective-permute-start.7 = (f32[2,2,1,5120]{3,2,1,0:T(1,128)S(1)}, f32[2,2,1,5120]{3,2,1,0:T(1,128)S(1)}, u32[]{:S(2)}, u32[]{:S(2)}) collective-permute-start(f32[2,2,1,5120]{3,2,1,0:T(1,128)S(1)} %get-tuple-element.31), channel_id=1, source_target_pairs={{0,1},{1,2},{2,3},{3,4},{4,5},{5,6},{6,7},{7,8},{8,9},{9,10},{10,1... | collective-permute-start | bytes 245768 | tf_op jit(solution)/shard_map/ppermute | solution.py:21
  100.2 51.8 %all-to-all-start.1 = ((f32[8,2,8,5120]{3,2,1,0:T(8,128)}), f32[8,2,8,5120]{3,2,1,0:T(8,128)}, u32[]{:S(2)}, u32[]{:S(2)}) async-start(f32[8,2,8,5120]{3,2,1,0:T(8,128)} %get-tuple-element.12), calls=%async_computation.1 | async-start | bytes 5242880 | tf_op jit(solution)/shard_map/all_to_all | solution.py:159
  106.7 45.2 %collective-permute-start.9 = (f32[2,8,5120]{2,1,0:T(8,128)S(1)}, f32[2,8,5120]{2,1,0:T(8,128)S(1)}, u32[]{:S(2)}, u32[]{:S(2)}) collective-permute-start(f32[2,8,5120]{2,1,0:T(8,128)S(1)} %get-tuple-element.29), channel_id=1, source_target_pairs={{0,16},{16,32},{32,48},{48,64},{64,80},{80,96},{96,112},{1,17},{17... | collective-permute-start | bytes 983048 | tf_op jit(solution)/shard_map/ppermute | solution.py:21
  111.9 43.7 %copy-start.14 = (f32[2,8,5120]{2,1,0:T(8,128)}, f32[2,8,5120]{2,1,0:T(8,128)S(1)}, u32[]{:S(2)}) copy-start(f32[2,8,5120]{2,1,0:T(8,128)S(1)} %collective-permute-done.10.nextf_ref) | copy-start | bytes 983044
  153.4 6.7 %collective-permute-start.11 = (f32[4,2,1,5120]{3,2,1,0:T(1,128)S(1)}, f32[4,2,1,5120]{3,2,1,0:T(1,128)}, u32[]{:S(2)}, u32[]{:S(2)}) collective-permute-start(f32[4,2,1,5120]{3,2,1,0:T(1,128)S(1)} %pad_maximum_fusion.7), channel_id=1, source_target_pairs={{1,0},{2,1},{3,2},{4,3},{5,4},{6,5},{7,6},{8,7},{9,8},{10,9},{11,1... | collective-permute-start | bytes 491528 | tf_op jit(solution)/shard_map/ppermute | solution.py:21
  169.4 20.3 %collective-permute-start.15 = (f32[2,8,5120]{2,1,0:T(8,128)S(1)}, f32[2,8,5120]{2,1,0:T(8,128)S(1)}, u32[]{:S(2)}, u32[]{:S(2)}) collective-permute-start(f32[2,8,5120]{2,1,0:T(8,128)S(1)} %get-tuple-element.24), channel_id=1, source_target_pairs={{16,0},{32,16},{48,32},{64,48},{80,64},{96,80},{112,96},{17,1},{33... | collective-permute-start | bytes 983048 | tf_op jit(solution)/shard_map/ppermute | solution.py:21
  171.5 17.0 %collective-permute-start.13 = (f32[2,2,1,5120]{3,2,1,0:T(1,128)S(1)}, f32[2,2,1,5120]{3,2,1,0:T(1,128)S(1)}, u32[]{:S(2)}, u32[]{:S(2)}) collective-permute-start(f32[2,2,1,5120]{3,2,1,0:T(1,128)S(1)} %get-tuple-element.26), channel_id=1, source_target_pairs={{1,0},{2,1},{3,2},{4,3},{5,4},{6,5},{7,6},{8,7},{9,8},{10,9},{11,1... | collective-permute-start | bytes 245768 | tf_op jit(solution)/shard_map/ppermute | solution.py:21
  173.4 15.4 %collective-permute-start.12 = (f32[2,2,1,5120]{3,2,1,0:T(1,128)S(1)}, f32[2,2,1,5120]{3,2,1,0:T(1,128)S(1)}, u32[]{:S(2)}, u32[]{:S(2)}) collective-permute-start(f32[2,2,1,5120]{3,2,1,0:T(1,128)S(1)} %get-tuple-element.27), channel_id=1, source_target_pairs={{0,1},{1,2},{2,3},{3,4},{4,5},{5,6},{6,7},{7,8},{8,9},{9,10},{10,1... | collective-permute-start | bytes 245768 | tf_op jit(solution)/shard_map/ppermute | solution.py:21
  177.1 52.6 %all-to-all-start.2 = ((f32[8,2,8,5120]{3,2,1,0:T(8,128)}), f32[8,2,8,5120]{3,2,1,0:T(8,128)}, u32[]{:S(2)}, u32[]{:S(2)}) async-start(f32[8,2,8,5120]{3,2,1,0:T(8,128)} %get-tuple-element.15), calls=%async_computation.2 | async-start | bytes 5242880 | tf_op jit(solution)/shard_map/all_to_all | solution.py:159
  183.7 45.2 %collective-permute-start.14 = (f32[2,8,5120]{2,1,0:T(8,128)S(1)}, f32[2,8,5120]{2,1,0:T(8,128)S(1)}, u32[]{:S(2)}, u32[]{:S(2)}) collective-permute-start(f32[2,8,5120]{2,1,0:T(8,128)S(1)} %get-tuple-element.25), channel_id=1, source_target_pairs={{0,16},{16,32},{32,48},{48,64},{64,80},{80,96},{96,112},{1,17},{17... | collective-permute-start | bytes 983048 | tf_op jit(solution)/shard_map/ppermute | solution.py:21
  230.8 10.3 %copy-start.1 = (f32[5,2,8,5120]{3,2,1,0:T(8,128)S(1)}, f32[5,2,8,5120]{3,2,1,0:T(8,128)}, u32[]{:S(2)}) copy-start(f32[5,2,8,5120]{3,2,1,0:T(8,128)} %copy-done) | copy-start | bytes 4915204
  231.0 7.0 %collective-permute-start.16 = (f32[4,2,1,5120]{3,2,1,0:T(1,128)S(1)}, f32[4,2,1,5120]{3,2,1,0:T(1,128)}, u32[]{:S(2)}, u32[]{:S(2)}) collective-permute-start(f32[4,2,1,5120]{3,2,1,0:T(1,128)S(1)} %pad_maximum_fusion.8), channel_id=1, source_target_pairs={{1,0},{2,1},{3,2},{4,3},{5,4},{6,5},{7,6},{8,7},{9,8},{10,9},{11,1... | collective-permute-start | bytes 491528 | tf_op jit(solution)/shard_map/ppermute | solution.py:21
  (16 other events, 23.6 us)

commit v4 on v3

--- a/solution.py
+++ b/solution.py
@@ -30,7 +30,8 @@
 
 
 def update_kernel(scal_ref, sel_ref, x_ref, v_ref, k_ref, alive_ref, part_ref, up_ref, down_ref,
-                  prevf_ref, nextf_ref, below_ref, xo_ref, vo_ref, send_ref):
+                  prevf_ref, nextf_ref, below_ref, xo_ref, vo_ref, send_ref, lastf_ref, firstf_ref,
+                  top_ref, bot_ref):
     L, ncomp, R, C = x_ref.shape
     rows = lax.broadcasted_iota(jnp.int32, (R, C), 0)
     cols = lax.broadcasted_iota(jnp.int32, (R, C), 1)
@@ -81,7 +82,14 @@
             force = inplane + pull
             vel = alive * (DAMPING * v_ref[l, c] + STEP * force)
             vo_ref[l, c] = vel
-            xo_ref[l, c] = x + STEP * vel
+            new = x + STEP * vel
+            xo_ref[l, c] = new
+            if l == L - 1:
+                lastf_ref[c] = new
+            if l == 0:
+                firstf_ref[c] = new
+            top_ref[pl.ds(l * ncomp + c, 1), :] = new[0:1]
+            bot_ref[pl.ds(l * ncomp + c, 1), :] = new[R - 1 : R]
     for d in range(send_ref.shape[0]):
         send_ref[d] = xo_ref[sel_ref[d]]
 
@@ -97,9 +105,13 @@
             jax.ShapeDtypeStruct(x.shape, x.dtype),
             jax.ShapeDtypeStruct(x.shape, x.dtype),
             jax.ShapeDtypeStruct((nb,) + x.shape[1:], x.dtype),
+            jax.ShapeDtypeStruct(x.shape[1:], x.dtype),
+            jax.ShapeDtypeStruct(x.shape[1:], x.dtype),
+            jax.ShapeDtypeStruct((x.shape[0] * x.shape[1], x.shape[3]), x.dtype),
+            jax.ShapeDtypeStruct((x.shape[0] * x.shape[1], x.shape[3]), x.dtype),
         ),
         in_specs=[smem, smem] + [vmem] * 10,
-        out_specs=[vmem] * 3,
+        out_specs=[vmem] * 7,
         compiler_params=pltpu.CompilerParams(vmem_limit_bytes=48 * 1024 * 1024),
         cost_estimate=pl.CostEstimate(flops=80 * x.size, bytes_accessed=moved, transcendentals=0),
     )(scal, sel, x, v, kst, alive, part, up, down, prevf, nextf, below)
@@ -155,20 +167,24 @@
     send = field[0][None]
     for l in range(1, local_count):
         send = jnp.where((send_sel == l)[:, None, None, None], field[l][None], send)
+    last_face = field[-1]
+    first_face = field[0]
+    top_rows = field[:, :, 0].reshape(local_count * ncomp, cols)
+    bot_rows = field[:, :, -1].reshape(local_count * ncomp, cols)
     for _ in range(ITERS):
       recv = lax.all_to_all(send, "gz", 0, 0, tiled=True)
       partner8 = jnp.stack(
           [lax.dynamic_index_in_dim(recv, src_block[l], 0, keepdims=False) for l in range(local_count)]
       )
-      prev_face = shift_rows(field[-1], "gz", True)
-      next_face = shift_rows(field[0], "gz", False)
-      up = shift_rows(field[:, :, -1:], "tile", True)
-      down = shift_rows(field[:, :, :1], "tile", False)
+      prev_face = shift_rows(last_face, "gz", True)
+      next_face = shift_rows(first_face, "gz", False)
+      up = shift_rows(bot_rows, "tile", True)
+      down = shift_rows(top_rows, "tile", False)
       firsts = jnp.concatenate(
-          [prev_face[None, :, :1], next_face[None, :, :1], partner8[:, :, :1]], axis=0
+          [prev_face[:, 0], next_face[:, 0]] + [partner8[l, :, 0] for l in range(local_count)], axis=0
       )
       below = shift_rows(firsts, "tile", False)
-      field, velocity, send = update(
+      field, velocity, send, last_face, first_face, top_rows, bot_rows = update(
           scal,
           send_sel,
           field,
@@ -176,11 +192,11 @@
           kst,
           alive_mid,
           partner8,
-          up.reshape(local_count * ncomp, cols),
-          down.reshape(local_count * ncomp, cols),
+          up,
+          down,
           prev_face,
           next_face,
-          below.reshape((2 + local_count) * ncomp, cols),
+          below,
       )
     return (field, velocity)
 

time: 251 us -> 236 us (0.940)
  the two profiles are of different devices: /device:TPU:7 before, /device:TPU:25 now
where the time goes in v4:
time: 236 us; the launch traced here: 235 us
  waiting for transfers between devices  98.7 us (42%)
  starting transfers between devices  65.4 us (28%)
  local copies, waits for them, and re-layouts  37.6 us (16%)
  Pallas kernels  14.6 us (6%)
  other arithmetic  13.3 us (6%)
  between operations  4.94 us (2%)
    all_to_all x3, waiting for transfers between devices, body(): recv = lax.all_to_all(send, 'gz', 0, 0, tiled=True)  85.1 us
    ppermute x17, starting transfers between devices, shift_rows(): return lax.ppermute(block, axis, pairs)  49.6 us
    all_to_all x3, starting transfers between devices, body(): recv = lax.all_to_all(send, 'gz', 0, 0, tiled=True)  15.8 us
    pallas_call x3, Pallas kernels, update(): pl.pallas_call(update_kernel, out_shape=(jax.ShapeDtypeStruct(x.shape, x....  14.6 us
    ppermute x17, waiting for transfers between devices, shift_rows(): return lax.ppermute(block, axis, pairs)  13.6 us
    pallas_call x6, local copies, waits for them, and re-layouts, update(): pl.pallas_call(update_kernel, out_shape=(jax.ShapeDtypeStruct(x.shape, x....  12.2 us
    another operation x1, other arithmetic, body(): stiff = jnp.stack([kappa, alive])  6.2 us
  transfers between devices with their start and end apart: 20, of which 6 were waited for; matrix products, arithmetic and copies ran while one was open for 19% of the time, Pallas kernels for 0%

profile of v4, /device:TPU:25, one launch (start us, length us, event | category | flops | bytes accessed | tf_op | source)
XLA Modules:
  0.0 234.5 jit_solution(9720530808671773514)
XLA Ops:
  0.6 1.8 slice_reduce_fusion
  3.2 3.8 %collective-permute-start.2 = (f32[4,5120]{1,0:T(4,128)}, f32[4,5120]{1,0:T(4,128)S(1)}, u32[]{:S(2)}, u32[]{:S(2)}) collective-permute-start(f32[4,5120]{1,0:T(4,128)} %reshape_squeeze.6), channel_id=1, source_target_pairs={{0,1},{1,2},{2,3},{3,4},{4,5},{5,6},{6,7},{7,8},{8,9},{9,10},{10,1... | collective-permute-start | bytes 245768 | tf_op jit(solution)/shard_map/ppermute | solution.py:21
  7.0 1.6 fusion.13
  9.6 6.2 %multiply_bitcast_fusion = f32[1,2,8,5120]{3,2,1,0:T(8,128)S(1)} fusion(s32[2,8,5120]{2,1,0:T(8,128)} %param.10, f32[]{:T(128)} %bitcast.7, f32[]{:T(128)} %bitcast.6, f32[]{:T(128)} %bitcast.5, f32[]{:T(128)} %bitcast.4, f32[]{:T(128)} %bitcast.3, f32[]{:T(128)} %bitcast.2, f32[]{:T(128)} %bitcast.1, f32[]{:T(128)} %bitcast, s32[2,8,5120]{2,1,0:T(8,128)} %param.11), kind=kLoop, calls=%fused_computation.18 | loop fusion | flops 1474560 | bytes 983072 | tf_op jit(solution)/shard_map/stack | solution.py:130
  15.9 1.9 collective-permute-start
  17.9 2.4 %collective-permute-start.1 = (f32[2,2,1,5120]{3,2,1,0:T(1,128)S(1)}, f32[2,2,1,5120]{3,2,1,0:T(1,128)S(1)}, u32[]{:S(2)}, u32[]{:S(2)}) collective-permute-start(f32[2,2,1,5120]{3,2,1,0:T(1,128)S(1)} %get-tuple-element.53), channel_id=1, source_target_pairs={{1,0},{2,1},{3,2},{4,3},{5,4},{6,5},{7,6},{8,7},{9,8},{10,9},{11,1... | collective-permute-start | bytes 245768 | tf_op jit(solution)/shard_map/ppermute | solution.py:21
  23.6 6.6 %collective-permute-start.4 = (f32[2,8,5120]{2,0,1:T(2,128)}, f32[2,8,5120]{2,0,1:T(2,128)}, u32[]{:S(2)}, u32[]{:S(2)}) collective-permute-start(f32[2,8,5120]{2,0,1:T(2,128)} %bitcast.61), channel_id=1, source_target_pairs={{0,16},{16,32},{32,48},{48,64},{64,80},{80,96},{96,112},{1,17},{17... | collective-permute-start | bytes 983048 | tf_op jit(solution)/shard_map/ppermute | solution.py:21
  30.4 3.5 %broadcast_select_fusion = f32[8,2,8,5120]{3,1,2,0:T(2,128)} fusion(pred[8]{0:T(512)(128)(4,1)S(1)} %broadcast_compare_fusion, f32[2,8,5120]{2,0,1:T(2,128)} %bitcast.60, f32[2,8,5120]{2,0,1:T(2,128)} %bitcast.61), kind=kLoop, calls=%fused_computation | loop fusion | flops 655360 | bytes 3276808 | tf_op jit(solution)/shard_map/jit(_where)/select_n | solution.py:169
  33.9 7.0 %all-to-all-start = ((f32[8,2,8,5120]{3,1,2,0:T(2,128)}), f32[8,2,8,5120]{3,1,2,0:T(2,128)}, u32[]{:S(2)}, u32[]{:S(2)}) async-start(f32[8,2,8,5120]{3,1,2,0:T(2,128)} %broadcast_select_fusion), calls=%async_computation | async-start | bytes 5242880 | tf_op jit(solution)/shard_map/all_to_all | solution.py:175
  46.4 3.1 %collective-permute-start.3 = (f32[4,5120]{1,0:T(4,128)}, f32[4,5120]{1,0:T(4,128)S(1)}, u32[]{:S(2)}, u32[]{:S(2)}) collective-permute-start(f32[4,5120]{1,0:T(4,128)} %reshape_squeeze.7), channel_id=1, source_target_pairs={{1,0},{2,1},{3,2},{4,3},{5,4},{6,5},{7,6},{8,7},{9,8},{10,9},{11,1... | collective-permute-start | bytes 245768 | tf_op jit(solution)/shard_map/ppermute | solution.py:21
  54.2 24.6 %all-to-all-done = f32[8,2,8,5120]{3,1,2,0:T(2,128)} async-done(((f32[8,2,8,5120]{3,1,2,0:T(2,128)}), f32[8,2,8,5120]{3,1,2,0:T(2,128)}, u32[]{:S(2)}, u32[]{:S(2)}) %all-to-all-start) | async-done | bytes 2621472 | tf_op jit(solution)/shard_map/all_to_all | solution.py:175
  79.7 3.6 %collective-permute-start.6 = (f32[8,5120]{1,0:T(8,128)S(1)}, f32[8,5120]{1,0:T(8,128)S(1)}, u32[]{:S(2)}, u32[]{:S(2)}) collective-permute-start(f32[8,5120]{1,0:T(8,128)S(1)} %pad_maximum_fusion.6), channel_id=1, source_target_pairs={{1,0},{2,1},{3,2},{4,3},{5,4},{6,5},{7,6},{8,7},{9,8},{10,9},{11,1... | collective-permute-start | bytes 491528 | tf_op jit(solution)/shard_map/ppermute | solution.py:21
  84.9 3.5 %collective-permute-done.6.below_ref = f32[8,5120]{1,0:T(8,128)S(1)} collective-permute-done((f32[8,5120]{1,0:T(8,128)S(1)}, f32[8,5120]{1,0:T(8,128)S(1)}, u32[]{:S(2)}, u32[]{:S(2)}) %collective-permute-start.6) | collective-permute-done | bytes 163872 | tf_op jit(solution)/shard_map/ppermute | solution.py:21
  88.4 5.0 %shard_map.95 = (f32[2,2,8,5120]{3,2,1,0:T(8,128)S(1)}, f32[2,2,8,5120]{3,2,1,0:T(8,128)S(1)}, f32[8,2,8,5120]{3,2,1,0:T(8,128)}, f32[2,8,5120]{2,1,0:T(8,128)S(...) custom-call(f32[2,9]{1,0:T(2,128)S(1)} %pad_maximum_fusion.11.scal_ref, ...), custom_call_target="tpu_custom_call" | custom-call | flops 13107200 | bytes 8192000 | tf_op jit(solution)/shard_map/pallas_call | solution.py:102
  96.1 5.5 %collective-permute-start.9 = (f32[2,8,5120]{2,0,1:T(2,128)S(1)}, f32[2,8,5120]{2,0,1:T(2,128)S(1)}, u32[]{:S(2)}, u32[]{:S(2)}) collective-permute-start(f32[2,8,5120]{2,0,1:T(2,128)S(1)} %copy.35), channel_id=1, source_target_pairs={{0,16},{16,32},{32,48},{48,64},{64,80},{80,96},{96,112},{1,17},{17... | collective-permute-start | bytes 983048 | tf_op jit(solution)/shard_map/ppermute | solution.py:21
  101.6 5.2 %copy.34 = f32[8,2,8,5120]{3,1,2,0:T(2,128)} copy(f32[8,2,8,5120]{3,2,1,0:T(8,128)} %get-tuple-element.20) | data formatting | bytes 5242880 | tf_op jit(solution)/shard_map/pallas_call | solution.py:102
  106.9 4.4 %all-to-all-start.1 = ((f32[8,2,8,5120]{3,1,2,0:T(2,128)}), f32[8,2,8,5120]{3,1,2,0:T(2,128)}, u32[]{:S(2)}, u32[]{:S(2)}) async-start(f32[8,2,8,5120]{3,1,2,0:T(2,128)} %copy.34), calls=%async_computation.1 | async-start | bytes 5242880 | tf_op jit(solution)/shard_map/all_to_all | solution.py:175
  111.3 2.3 collective-permute-start.7
  113.6 2.0 collective-permute-start.8
  115.9 32.5 %all-to-all-done.1 = f32[8,2,8,5120]{3,1,2,0:T(2,128)} async-done(((f32[8,2,8,5120]{3,1,2,0:T(2,128)}), f32[8,2,8,5120]{3,1,2,0:T(2,128)}, u32[]{:S(2)}, u32[]{:S(2)}) %all-to-all-start.1) | async-done | bytes 2621472 | tf_op jit(solution)/shard_map/all_to_all | solution.py:175
  149.3 2.1 collective-permute-start.11
  153.1 4.9 %collective-permute-done.11.below_ref = f32[8,5120]{1,0:T(8,128)S(1)} collective-permute-done((f32[8,5120]{1,0:T(8,128)S(1)}, f32[8,5120]{1,0:T(8,128)S(1)}, u32[]{:S(2)}, u32[]{:S(2)}) %collective-permute-start.11) | collective-permute-done | bytes 163872 | tf_op jit(solution)/shard_map/ppermute | solution.py:21
  158.1 5.0 %shard_map.96 = (f32[2,2,8,5120]{3,2,1,0:T(8,128)S(1)}, f32[2,2,8,5120]{3,2,1,0:T(8,128)S(1)}, f32[8,2,8,5120]{3,2,1,0:T(8,128)}, f32[2,8,5120]{2,1,0:T(8,128)S(...) custom-call(f32[2,9]{1,0:T(2,128)S(1)} %pad_maximum_fusion.11.scal_ref, ...), custom_call_target="tpu_custom_call" | custom-call | flops 13107200 | bytes 8192000 | tf_op jit(solution)/shard_map/pallas_call | solution.py:102
  166.4 6.2 %collective-permute-start.14 = (f32[2,8,5120]{2,0,1:T(2,128)}, f32[2,8,5120]{2,0,1:T(2,128)}, u32[]{:S(2)}, u32[]{:S(2)}) collective-permute-start(f32[2,8,5120]{2,0,1:T(2,128)} %copy.41), channel_id=1, source_target_pairs={{0,16},{16,32},{32,48},{48,64},{64,80},{80,96},{96,112},{1,17},{17... | collective-permute-start | bytes 983048 | tf_op jit(solution)/shard_map/ppermute | solution.py:21
  172.6 5.3 %copy.40 = f32[8,2,8,5120]{3,1,2,0:T(2,128)} copy(f32[8,2,8,5120]{3,2,1,0:T(8,128)} %get-tuple-element.27) | data formatting | bytes 5242880 | tf_op jit(solution)/shard_map/pallas_call | solution.py:102
  177.9 4.4 %all-to-all-start.2 = ((f32[8,2,8,5120]{3,1,2,0:T(2,128)}), f32[8,2,8,5120]{3,1,2,0:T(2,128)}, u32[]{:S(2)}, u32[]{:S(2)}) async-start(f32[8,2,8,5120]{3,1,2,0:T(2,128)} %copy.40), calls=%async_computation.2 | async-start | bytes 5242880 | tf_op jit(solution)/shard_map/all_to_all | solution.py:175
  182.3 2.3 collective-permute-start.12
  184.6 2.0 collective-permute-start.13
  191.4 28.0 %all-to-all-done.2 = f32[8,2,8,5120]{3,1,2,0:T(2,128)} async-done(((f32[8,2,8,5120]{3,1,2,0:T(2,128)}), f32[8,2,8,5120]{3,1,2,0:T(2,128)}, u32[]{:S(2)}, u32[]{:S(2)}) %all-to-all-start.2) | async-done | bytes 2621472 | tf_op jit(solution)/shard_map/all_to_all | solution.py:175
  221.1 1.9 collective-permute-start.16
  224.7 5.2 %collective-permute-done.16.below_ref = f32[8,5120]{1,0:T(8,128)S(1)} collective-permute-done((f32[8,5120]{1,0:T(8,128)S(1)}, f32[8,5120]{1,0:T(8,128)S(1)}, u32[]{:S(2)}, u32[]{:S(2)}) %collective-permute-start.16) | collective-permute-done | bytes 163872 | tf_op jit(solution)/shard_map/ppermute | solution.py:21
  229.9 4.6 %shard_map.97 = (f32[2,2,8,5120]{3,2,1,0:T(8,128)}, f32[2,2,8,5120]{3,2,1,0:T(8,128)}, f32[8,2,8,5120]{3,2,1,0:T(8,128)}, f32[2,8,5120]{2,1,0:T(8,128)}, f32[2,8...) custom-call(f32[2,9]{1,0:T(2,128)S(1)} %pad_maximum_fusion.11.scal_ref, s32[8]{0:T(128)S(1)} %fusion.6.sel_ref, ...), custom_call_target="tpu_custom_call" | custom-call | flops 13107200 | bytes 8192000 | tf_op jit(solution)/shard_map/pallas_call | solution.py:102
  (95 shorter events, 31.1 us)
Async XLA Ops:
  0.6 19.7 %copy-start.2 = (f32[2,2,8,5120]{3,2,1,0:T(8,128)S(1)}, f32[2,2,8,5120]{3,2,1,0:T(8,128)}, u32[]{:S(2)}) copy-start(f32[2,2,8,5120]{3,2,1,0:T(8,128)} %x_ref.1) | copy-start | bytes 1966084
  3.2 81.7 %collective-permute-start.2 = (f32[4,5120]{1,0:T(4,128)}, f32[4,5120]{1,0:T(4,128)S(1)}, u32[]{:S(2)}, u32[]{:S(2)}) collective-permute-start(f32[4,5120]{1,0:T(4,128)} %reshape_squeeze.6), channel_id=1, source_target_pairs={{0,1},{1,2},{2,3},{3,4},{4,5},{5,6},{6,7},{7,8},{8,9},{9,10},{10,1... | collective-permute-start | bytes 245768 | tf_op jit(solution)/shard_map/ppermute | solution.py:21
  8.6 21.6 %copy-start.11 = (s32[16]{0:T(128)S(1)}, s32[16]{0:T(128)}, u32[]{:S(2)}) copy-start(s32[16]{0:T(128)} %param.15) | copy-start | bytes 196
  15.9 30.5 %collective-permute-start = (f32[2,2,1,5120]{3,2,1,0:T(1,128)S(1)}, f32[2,2,1,5120]{3,2,1,0:T(1,128)S(1)}, u32[]{:S(2)}, u32[]{:S(2)}) collective-permute-start(f32[2,2,1,5120]{3,2,1,0:T(1,128)S(1)} %get-tuple-element.52), channel_id=1, source_target_pairs={{0,1},{1,2},{2,3},{3,4},{4,5},{5,6},{6,7},{7,8},{8,9},{9,10},{10,1... | collective-permute-start | bytes 245768 | tf_op jit(solution)/shard_map/ppermute | solution.py:21
  17.9 31.7 %collective-permute-start.1 = (f32[2,2,1,5120]{3,2,1,0:T(1,128)S(1)}, f32[2,2,1,5120]{3,2,1,0:T(1,128)S(1)}, u32[]{:S(2)}, u32[]{:S(2)}) collective-permute-start(f32[2,2,1,5120]{3,2,1,0:T(1,128)S(1)} %get-tuple-element.53), channel_id=1, source_target_pairs={{1,0},{2,1},{3,2},{4,3},{5,4},{6,5},{7,6},{8,7},{9,8},{10,9},{11,1... | collective-permute-start | bytes 245768 | tf_op jit(solution)/shard_map/ppermute | solution.py:21
  21.3 28.8 %collective-permute-start.5 = (f32[2,8,5120]{2,0,1:T(2,128)}, f32[2,8,5120]{2,0,1:T(2,128)}, u32[]{:S(2)}, u32[]{:S(2)}) collective-permute-start(f32[2,8,5120]{2,0,1:T(2,128)} %bitcast.60), channel_id=1, source_target_pairs={{16,0},{32,16},{48,32},{64,48},{80,64},{96,80},{112,96},{17,1},{33... | collective-permute-start | bytes 983048 | tf_op jit(solution)/shard_map/ppermute | solution.py:21
  23.6 27.9 %collective-permute-start.4 = (f32[2,8,5120]{2,0,1:T(2,128)}, f32[2,8,5120]{2,0,1:T(2,128)}, u32[]{:S(2)}, u32[]{:S(2)}) collective-permute-start(f32[2,8,5120]{2,0,1:T(2,128)} %bitcast.61), channel_id=1, source_target_pairs={{0,16},{16,32},{32,48},{48,64},{64,80},{80,96},{96,112},{1,17},{17... | collective-permute-start | bytes 983048 | tf_op jit(solution)/shard_map/ppermute | solution.py:21
  33.9 10.2 %copy-start.9 = (f32[2,3]{1,0:T(2,128)S(1)}, f32[2,3]{1,0:T(2,128)}, u32[]{:S(2)}) copy-start(f32[2,3]{1,0:T(2,128)} %param.14) | copy-start | bytes 76
  33.9 10.3 %copy-start.10 = (f32[2,3,2]{1,2,0:T(2,128)S(1)}, f32[2,3,2]{1,2,0:T(2,128)}, u32[]{:S(2)}) copy-start(f32[2,3,2]{1,2,0:T(2,128)} %param.13) | copy-start | bytes 148
  33.9 44.8 %all-to-all-start = ((f32[8,2,8,5120]{3,1,2,0:T(2,128)}), f32[8,2,8,5120]{3,1,2,0:T(2,128)}, u32[]{:S(2)}, u32[]{:S(2)}) async-start(f32[8,2,8,5120]{3,1,2,0:T(2,128)} %broadcast_select_fusion), calls=%async_computation | async-start | bytes 5242880 | tf_op jit(solution)/shard_map/all_to_all | solution.py:175
  46.4 38.5 %collective-permute-start.3 = (f32[4,5120]{1,0:T(4,128)}, f32[4,5120]{1,0:T(4,128)S(1)}, u32[]{:S(2)}, u32[]{:S(2)}) collective-permute-start(f32[4,5120]{1,0:T(4,128)} %reshape_squeeze.7), channel_id=1, source_target_pairs={{1,0},{2,1},{3,2},{4,3},{5,4},{6,5},{7,6},{8,7},{9,8},{10,9},{11,1... | collective-permute-start | bytes 245768 | tf_op jit(solution)/shard_map/ppermute | solution.py:21
  50.1 34.8 %copy-start = (f32[5,2,8,5120]{3,2,1,0:T(8,128)}, f32[5,2,8,5120]{3,2,1,0:T(8,128)S(1)}, u32[]{:S(2)}) copy-start(f32[5,2,8,5120]{3,2,1,0:T(8,128)S(1)} %bitcast_dynamic-update-slice_fusion.k_ref) | copy-start | bytes 4915204
  78.7 9.7 %copy-start.3 = (f32[2,2,8,5120]{3,2,1,0:T(8,128)S(1)}, f32[2,2,8,5120]{3,2,1,0:T(8,128)}, u32[]{:S(2)}) copy-start(f32[2,2,8,5120]{3,2,1,0:T(8,128)} %v_ref.1) | copy-start | bytes 1966084
  79.7 8.7 %collective-permute-start.6 = (f32[8,5120]{1,0:T(8,128)S(1)}, f32[8,5120]{1,0:T(8,128)S(1)}, u32[]{:S(2)}, u32[]{:S(2)}) collective-permute-start(f32[8,5120]{1,0:T(8,128)S(1)} %pad_maximum_fusion.6), channel_id=1, source_target_pairs={{1,0},{2,1},{3,2},{4,3},{5,4},{6,5},{7,6},{8,7},{9,8},{10,9},{11,1... | collective-permute-start | bytes 491528 | tf_op jit(solution)/shard_map/ppermute | solution.py:21
  93.4 0.8 copy-start.6
  94.5 21.1 %collective-permute-start.10 = (f32[2,8,5120]{2,0,1:T(2,128)S(1)}, f32[2,8,5120]{2,0,1:T(2,128)S(1)}, u32[]{:S(2)}, u32[]{:S(2)}) collective-permute-start(f32[2,8,5120]{2,0,1:T(2,128)S(1)} %copy.36), channel_id=1, source_target_pairs={{16,0},{32,16},{48,32},{64,48},{80,64},{96,80},{112,96},{17,1},{33... | collective-permute-start | bytes 983048 | tf_op jit(solution)/shard_map/ppermute | solution.py:21
  96.1 19.6 %collective-permute-start.9 = (f32[2,8,5120]{2,0,1:T(2,128)S(1)}, f32[2,8,5120]{2,0,1:T(2,128)S(1)}, u32[]{:S(2)}, u32[]{:S(2)}) collective-permute-start(f32[2,8,5120]{2,0,1:T(2,128)S(1)} %copy.35), channel_id=1, source_target_pairs={{0,16},{16,32},{32,48},{48,64},{64,80},{80,96},{96,112},{1,17},{17... | collective-permute-start | bytes 983048 | tf_op jit(solution)/shard_map/ppermute | solution.py:21
  106.9 41.6 %all-to-all-start.1 = ((f32[8,2,8,5120]{3,1,2,0:T(2,128)}), f32[8,2,8,5120]{3,1,2,0:T(2,128)}, u32[]{:S(2)}, u32[]{:S(2)}) async-start(f32[8,2,8,5120]{3,1,2,0:T(2,128)} %copy.34), calls=%async_computation.1 | async-start | bytes 5242880 | tf_op jit(solution)/shard_map/all_to_all | solution.py:175
  111.3 41.9 %collective-permute-start.7 = (f32[4,5120]{1,0:T(4,128)}, f32[4,5120]{1,0:T(4,128)S(1)}, u32[]{:S(2)}, u32[]{:S(2)}) collective-permute-start(f32[4,5120]{1,0:T(4,128)} %get-tuple-element.21), channel_id=1, source_target_pairs={{0,1},{1,2},{2,3},{3,4},{4,5},{5,6},{6,7},{7,8},{8,9},{9,10},{10,1... | collective-permute-start | bytes 245768 | tf_op jit(solution)/shard_map/ppermute | solution.py:21
  113.6 39.6 %collective-permute-start.8 = (f32[4,5120]{1,0:T(4,128)S(1)}, f32[4,5120]{1,0:T(4,128)S(1)}, u32[]{:S(2)}, u32[]{:S(2)}) collective-permute-start(f32[4,5120]{1,0:T(4,128)S(1)} %get-tuple-element.22), channel_id=1, source_target_pairs={{1,0},{2,1},{3,2},{4,3},{5,4},{6,5},{7,6},{8,7},{9,8},{10,9},{11,1... | collective-permute-start | bytes 245768 | tf_op jit(solution)/shard_map/ppermute | solution.py:21
  115.7 42.3 %copy-start.7 = (f32[2,2,8,5120]{3,2,1,0:T(8,128)S(1)}, f32[2,2,8,5120]{3,2,1,0:T(8,128)}, u32[]{:S(2)}) copy-start(f32[2,2,8,5120]{3,2,1,0:T(8,128)} %copy-done.6) | copy-start | bytes 1966084
  149.3 8.8 %collective-permute-start.11 = (f32[8,5120]{1,0:T(8,128)S(1)}, f32[8,5120]{1,0:T(8,128)S(1)}, u32[]{:S(2)}, u32[]{:S(2)}) collective-permute-start(f32[8,5120]{1,0:T(8,128)S(1)} %pad_maximum_fusion.7), channel_id=1, source_target_pairs={{1,0},{2,1},{3,2},{4,3},{5,4},{6,5},{7,6},{8,7},{9,8},{10,9},{11,1... | collective-permute-start | bytes 491528 | tf_op jit(solution)/shard_map/ppermute | solution.py:21
  163.0 0.8 copy-start.4
  164.1 22.5 %collective-permute-start.15 = (f32[2,8,5120]{2,0,1:T(2,128)S(1)}, f32[2,8,5120]{2,0,1:T(2,128)S(1)}, u32[]{:S(2)}, u32[]{:S(2)}) collective-permute-start(f32[2,8,5120]{2,0,1:T(2,128)S(1)} %copy.42), channel_id=1, source_target_pairs={{16,0},{32,16},{48,32},{64,48},{80,64},{96,80},{112,96},{17,1},{33... | collective-permute-start | bytes 983048 | tf_op jit(solution)/shard_map/ppermute | solution.py:21
  166.4 21.0 %collective-permute-start.14 = (f32[2,8,5120]{2,0,1:T(2,128)}, f32[2,8,5120]{2,0,1:T(2,128)}, u32[]{:S(2)}, u32[]{:S(2)}) collective-permute-start(f32[2,8,5120]{2,0,1:T(2,128)} %copy.41), channel_id=1, source_target_pairs={{0,16},{16,32},{32,48},{48,64},{64,80},{80,96},{96,112},{1,17},{17... | collective-permute-start | bytes 983048 | tf_op jit(solution)/shard_map/ppermute | solution.py:21
  177.9 41.5 %all-to-all-start.2 = ((f32[8,2,8,5120]{3,1,2,0:T(2,128)}), f32[8,2,8,5120]{3,1,2,0:T(2,128)}, u32[]{:S(2)}, u32[]{:S(2)}) async-start(f32[8,2,8,5120]{3,1,2,0:T(2,128)} %copy.40), calls=%async_computation.2 | async-start | bytes 5242880 | tf_op jit(solution)/shard_map/all_to_all | solution.py:175
  182.3 42.4 %collective-permute-start.12 = (f32[4,5120]{1,0:T(4,128)}, f32[4,5120]{1,0:T(4,128)S(1)}, u32[]{:S(2)}, u32[]{:S(2)}) collective-permute-start(f32[4,5120]{1,0:T(4,128)} %get-tuple-element.28), channel_id=1, source_target_pairs={{0,1},{1,2},{2,3},{3,4},{4,5},{5,6},{6,7},{7,8},{8,9},{9,10},{10,1... | collective-permute-start | bytes 245768 | tf_op jit(solution)/shard_map/ppermute | solution.py:21
  184.6 40.1 %collective-permute-start.13 = (f32[4,5120]{1,0:T(4,128)S(1)}, f32[4,5120]{1,0:T(4,128)S(1)}, u32[]{:S(2)}, u32[]{:S(2)}) collective-permute-start(f32[4,5120]{1,0:T(4,128)S(1)} %get-tuple-element.29), channel_id=1, source_target_pairs={{1,0},{2,1},{3,2},{4,3},{5,4},{6,5},{7,6},{8,7},{9,8},{10,9},{11,1... | collective-permute-start | bytes 245768 | tf_op jit(solution)/shard_map/ppermute | solution.py:21
  186.6 0.7 copy-start.8
  187.4 42.5 %copy-start.1 = (f32[5,2,8,5120]{3,2,1,0:T(8,128)S(1)}, f32[5,2,8,5120]{3,2,1,0:T(8,128)}, u32[]{:S(2)}) copy-start(f32[5,2,8,5120]{3,2,1,0:T(8,128)} %copy-done) | copy-start | bytes 4915204
  219.4 10.5 %copy-start.5 = (f32[2,2,8,5120]{3,2,1,0:T(8,128)S(1)}, f32[2,2,8,5120]{3,2,1,0:T(8,128)}, u32[]{:S(2)}) copy-start(f32[2,2,8,5120]{3,2,1,0:T(8,128)} %copy-done.4) | copy-start | bytes 1966084
  221.1 8.7 %collective-permute-start.16 = (f32[8,5120]{1,0:T(8,128)S(1)}, f32[8,5120]{1,0:T(8,128)S(1)}, u32[]{:S(2)}, u32[]{:S(2)}) collective-permute-start(f32[8,5120]{1,0:T(8,128)S(1)} %pad_maximum_fusion.8), channel_id=1, source_target_pairs={{1,0},{2,1},{3,2},{4,3},{5,4},{6,5},{7,6},{8,7},{9,8},{10,9},{11,1... | collective-permute-start | bytes 491528 | tf_op jit(solution)/shard_map/ppermute | solution.py:21

commit v5 on v4

--- a/solution.py
+++ b/solution.py
@@ -68,30 +68,31 @@
                 k_up * (x_up - x) + k_dn * (x_dn - x) + k_r * (shr(x) - x) + k_l * (shl(x) - x)
             )
             if l == 0:
-                prev_src, prev_row = prevf_ref[c], below_ref[pl.ds(c, 1), :]
+                prev_src, prev_row = prevf_ref[pl.ds(c * R, R), :], below_ref[pl.ds(c, 1), :]
             else:
                 prev_src, prev_row = x_ref[l - 1, c], down_ref[pl.ds((l - 1) * ncomp + c, 1), :]
             if l == L - 1:
-                next_src, next_row = nextf_ref[c], below_ref[pl.ds(ncomp + c, 1), :]
+                next_src, next_row = nextf_ref[pl.ds(c * R, R), :], below_ref[pl.ds(ncomp + c, 1), :]
             else:
                 next_src, next_row = x_ref[l + 1, c], down_ref[pl.ds((l + 1) * ncomp + c, 1), :]
             part_row = below_ref[pl.ds((2 + l) * ncomp + c, 1), :]
             pull = scal_ref[l, 0] * (warp_of(prev_src, prev_row, ws[0]) - x)
             pull = pull + scal_ref[l, 1] * (warp_of(next_src, next_row, ws[1]) - x)
-            pull = pull + scal_ref[l, 2] * (warp_of(part_ref[l, c], part_row, ws[2]) - x)
+            pull = pull + scal_ref[l, 2] * (warp_of(part_ref[l, pl.ds(c * R, R), :], part_row, ws[2]) - x)
             force = inplane + pull
             vel = alive * (DAMPING * v_ref[l, c] + STEP * force)
             vo_ref[l, c] = vel
             new = x + STEP * vel
             xo_ref[l, c] = new
             if l == L - 1:
-                lastf_ref[c] = new
+                lastf_ref[pl.ds(c * R, R), :] = new
             if l == 0:
-                firstf_ref[c] = new
+                firstf_ref[pl.ds(c * R, R), :] = new
             top_ref[pl.ds(l * ncomp + c, 1), :] = new[0:1]
             bot_ref[pl.ds(l * ncomp + c, 1), :] = new[R - 1 : R]
     for d in range(send_ref.shape[0]):
-        send_ref[d] = xo_ref[sel_ref[d]]
+        for c in range(ncomp):
+            send_ref[d, pl.ds(c * R, R), :] = xo_ref[sel_ref[d], c]
 
 
 def update(scal, sel, x, v, kst, alive, part, up, down, prevf, nextf, below):
@@ -104,9 +105,9 @@
         out_shape=(
             jax.ShapeDtypeStruct(x.shape, x.dtype),
             jax.ShapeDtypeStruct(x.shape, x.dtype),
-            jax.ShapeDtypeStruct((nb,) + x.shape[1:], x.dtype),
-            jax.ShapeDtypeStruct(x.shape[1:], x.dtype),
-            jax.ShapeDtypeStruct(x.shape[1:], x.dtype),
+            jax.ShapeDtypeStruct((nb, x.shape[1] * x.shape[2], x.shape[3]), x.dtype),
+            jax.ShapeDtypeStruct((x.shape[1] * x.shape[2], x.shape[3]), x.dtype),
+            jax.ShapeDtypeStruct((x.shape[1] * x.shape[2], x.shape[3]), x.dtype),
             jax.ShapeDtypeStruct((x.shape[0] * x.shape[1], x.shape[3]), x.dtype),
             jax.ShapeDtypeStruct((x.shape[0] * x.shape[1], x.shape[3]), x.dtype),
         ),
@@ -161,43 +162,59 @@
     )
     ncomp = disp.shape[1]
     cols = disp.shape[3]
-
-    field = disp
-    velocity = vel
-    send = field[0][None]
-    for l in range(1, local_count):
-        send = jnp.where((send_sel == l)[:, None, None, None], field[l][None], send)
-    last_face = field[-1]
-    first_face = field[0]
-    top_rows = field[:, :, 0].reshape(local_count * ncomp, cols)
-    bot_rows = field[:, :, -1].reshape(local_count * ncomp, cols)
+    rows = disp.shape[2]
+
+    states = []
+    for c in range(ncomp):
+        field = disp[:, c : c + 1]
+        send = field[0][None]
+        for l in range(1, local_count):
+            send = jnp.where((send_sel == l)[:, None, None, None], field[l][None], send)
+        states.append(
+            dict(
+                field=field,
+                velocity=vel[:, c : c + 1],
+                send=send.reshape(block_count, rows, cols),
+                last_face=field[-1].reshape(rows, cols),
+                first_face=field[0].reshape(rows, cols),
+                top_rows=field[:, :, 0].reshape(local_count, cols),
+                bot_rows=field[:, :, -1].reshape(local_count, cols),
+            )
+        )
     for _ in range(ITERS):
-      recv = lax.all_to_all(send, "gz", 0, 0, tiled=True)
-      partner8 = jnp.stack(
-          [lax.dynamic_index_in_dim(recv, src_block[l], 0, keepdims=False) for l in range(local_count)]
-      )
-      prev_face = shift_rows(last_face, "gz", True)
-      next_face = shift_rows(first_face, "gz", False)
-      up = shift_rows(bot_rows, "tile", True)
-      down = shift_rows(top_rows, "tile", False)
-      firsts = jnp.concatenate(
-          [prev_face[:, 0], next_face[:, 0]] + [partner8[l, :, 0] for l in range(local_count)], axis=0
-      )
-      below = shift_rows(firsts, "tile", False)
-      field, velocity, send, last_face, first_face, top_rows, bot_rows = update(
-          scal,
-          send_sel,
-          field,
-          velocity,
-          kst,
-          alive_mid,
-          partner8,
-          up,
-          down,
-          prev_face,
-          next_face,
-          below,
-      )
+      for c in range(ncomp):
+        st = states[c]
+        recv = lax.all_to_all(st["send"], "gz", 0, 0, tiled=True)
+        partner8 = jnp.stack(
+            [lax.dynamic_index_in_dim(recv, src_block[l], 0, keepdims=False) for l in range(local_count)]
+        )
+        prev_face = shift_rows(st["last_face"], "gz", True)
+        next_face = shift_rows(st["first_face"], "gz", False)
+        up = shift_rows(st["bot_rows"], "tile", True)
+        down = shift_rows(st["top_rows"], "tile", False)
+        firsts = jnp.concatenate(
+            [prev_face[::rows], next_face[::rows]] + [partner8[l, ::rows] for l in range(local_count)],
+            axis=0,
+        )
+        below = shift_rows(firsts, "tile", False)
+        outs = update(
+            scal,
+            send_sel,
+            st["field"],
+            st["velocity"],
+            kst,
+            alive_mid,
+            partner8,
+            up,
+            down,
+            prev_face,
+            next_face,
+            below,
+        )
+        keys = ("field", "velocity", "send", "last_face", "first_face", "top_rows", "bot_rows")
+        states[c] = dict(zip(keys, outs))
+    field = jnp.concatenate([st["field"] for st in states], axis=1)
+    velocity = jnp.concatenate([st["velocity"] for st in states], axis=1)
     return (field, velocity)
 
 

time: 236 us -> 258 us (1.093); the launches traced: 235 us -> 254 us
  starting transfers between devices: 65.4 us -> 139 us
  waiting for transfers between devices: 98.7 us -> 35.5 us
  Pallas kernels: 14.6 us -> 18.4 us
    all_to_all x3 -> x6, waiting for transfers between devices: 85.1 us -> 29.5 us  [body(): recv = lax.all_to_all(st['send'], 'gz', 0, 0, tiled=True)]
    ppermute x17 -> x32, starting transfers between devices: 49.6 us -> 102 us  [shift_rows(): return lax.ppermute(block, axis, pairs)]
    all_to_all x3 -> x6, starting transfers between devices: 15.8 us -> 37.1 us  [body(): recv = lax.all_to_all(st['send'], 'gz', 0, 0, tiled=True)]
    unnamed x31 -> x103, local copies, waits for them, and re-layouts: 4.6 us -> 18.4 us
    pallas_call x6 -> x0, local copies, waits for them, and re-layouts: 12.2 us -> none  [update(): pl.pallas_call(update_kernel, out_shape=(jax.ShapeDtypeStruct(x.shape, x....]
    ppermute x17 -> x32, waiting for transfers between devices: 13.6 us -> 5.98 us  [shift_rows(): return lax.ppermute(block, axis, pairs)]
    concatenate x3 -> x8, other arithmetic: 1.03 us -> 5.47 us  [the longest x6 3.71 us: body(): jnp.concatenate([prev_face[::rows], next_face[::rows]] + [partner8[l, ::r...]
    ppermute x6 -> x0, local copies, waits for them, and re-layouts: 3.95 us -> none  [shift_rows(): return lax.ppermute(block, axis, pairs)]
  transfers between devices with their start and end apart: 20 -> 38, of which waited for: 6 -> 4; matrix products, arithmetic and copies ran while one was open for 19% -> 14% of each run, Pallas kernels for 0% -> 6%
where the time goes in v5:
time: 258 us; the launch traced here: 254 us
  starting transfers between devices  139 us (54%)
  local copies, waits for them, and re-layouts  39.2 us (15%)
  waiting for transfers between devices  35.5 us (14%)
  Pallas kernels  18.4 us (7%)
  other arithmetic  15.7 us (6%)
  between operations  5.56 us (2%)
    ppermute x32, starting transfers between devices, shift_rows(): return lax.ppermute(block, axis, pairs)  102 us
    all_to_all x6, starting transfers between devices, body(): recv = lax.all_to_all(st['send'], 'gz', 0, 0, tiled=True)  37.1 us
    all_to_all x6, waiting for transfers between devices, body(): recv = lax.all_to_all(st['send'], 'gz', 0, 0, tiled=True)  29.5 us
    pallas_call x6, Pallas kernels, update(): pl.pallas_call(update_kernel, out_shape=(jax.ShapeDtypeStruct(x.shape, x....  18.4 us
    unnamed x103, local copies, waits for them, and re-layouts  18.4 us
    squeeze x6, local copies, waits for them, and re-layouts, body(): partner8[l, ::rows]  6.21 us
    ppermute x32, waiting for transfers between devices, shift_rows(): return lax.ppermute(block, axis, pairs)  5.98 us
    dynamic_slice x5, local copies, waits for them, and re-layouts, body(): lax.dynamic_index_in_dim(recv, src_block[l], 0, keepdims=False)  5.47 us
  transfers between devices with their start and end apart: 38, of which 4 were waited for; matrix products, arithmetic and copies ran while one was open for 14% of the time, Pallas kernels for 6%

profile of v5, /device:TPU:25, one launch (start us, length us, event | category | flops | bytes accessed | tf_op | source)
XLA Modules:
  0.0 253.8 jit_solution(11869240947422121164)
XLA Ops:
  2.7 5.5 %collective-permute-start.4 = (f32[8,5120]{1,0:T(8,128)}, f32[8,5120]{1,0:T(8,128)S(1)}, u32[]{:S(2)}, u32[]{:S(2)}) collective-permute-start(f32[8,5120]{1,0:T(8,128)} %get-tuple-element.94), channel_id=1, source_target_pairs={{0,16},{16,32},{32,48},{48,64},{64,80},{80,96},{96,112},{1,17},{17... | collective-permute-start | bytes 491528 | tf_op jit(solution)/shard_map/ppermute | solution.py:21
  11.6 5.2 %multiply_bitcast_fusion = f32[1,2,8,5120]{3,2,1,0:T(8,128)S(1)} fusion(s32[2,8,5120]{2,1,0:T(8,128)S(1)} %copy-done.41, f32[]{:T(128)} %bitcast.7, f32[]{:T(128)} %bitcast.6, f32[]{:T(128)} %bitcast.5, f32[]{:T(128)} %bitcast.4, f32[]{:T(128)} %bitcast.3, f32[]{:T(128)} %bitcast.2, f32[]{:T(128)} %bitcast.1, f32[]{:T(128)} %bitcast, ...), kind=kLoop, calls=%fused_computation.22 | loop fusion | flops 1474560 | bytes 983072 | tf_op jit(solution)/shard_map/stack | solution.py:131
  17.5 3.1 %collective-permute-start = (f32[2,2,1,5120]{3,2,1,0:T(1,128)}, f32[2,2,1,5120]{3,2,1,0:T(1,128)S(1)}, u32[]{:S(2)}, u32[]{:S(2)}) collective-permute-start(f32[2,2,1,5120]{3,2,1,0:T(1,128)} %get-tuple-element.104), channel_id=1, source_target_pairs={{0,1},{1,2},{2,3},{3,4},{4,5},{5,6},{6,7},{7,8},{8,9},{9,10},{10,1... | collective-permute-start | bytes 245768 | tf_op jit(solution)/shard_map/ppermute | solution.py:21
  22.8 3.0 %broadcast_select_fusion.1 = (f32[8,8,5120]{2,1,0:T(8,128)}, f32[8,8,5120]{2,1,0:T(8,128)}) fusion(f32[8,5120]{1,0:T(8,128)} %get-tuple-element.96, f32[8,5120]{1,0:T(8,128)} %get-tuple-element.94, pred[8]{0:T(512)(128)(4,1)S(1)} %broadcast_compare_fusion, f32[8,5120]{1,0:T(8,128)} %get-tuple-element.95, f32[8,5120]{1,0:T(8,128)} %get-tuple-element.97), kind=kLoop, calls=%fused_computation.7 | loop fusion | flops 655360 | bytes 3276808 | tf_op jit(solution)/shard_map/jit(_where)/select_n | solution.py:172
  25.8 10.8 %all-to-all-start.3 = ((f32[8,8,5120]{2,1,0:T(8,128)}), f32[8,8,5120]{2,1,0:T(8,128)}, u32[]{:S(2)}, u32[]{:S(2)}) async-start(f32[8,8,5120]{2,1,0:T(8,128)} %get-tuple-element.112), calls=%async_computation.3 | async-start | bytes 2621440 | tf_op jit(solution)/shard_map/all_to_all | solution.py:187
  45.3 4.8 %collective-permute-start.19 = (f32[8,5120]{1,0:T(8,128)}, f32[8,5120]{1,0:T(8,128)S(1)}, u32[]{:S(2)}, u32[]{:S(2)}) collective-permute-start(f32[8,5120]{1,0:T(8,128)} %get-tuple-element.97), channel_id=1, source_target_pairs={{0,16},{16,32},{32,48},{48,64},{64,80},{80,96},{96,112},{1,17},{17... | collective-permute-start | bytes 491528 | tf_op jit(solution)/shard_map/ppermute | solution.py:21
  50.2 2.7 %collective-permute-start.18 = (f32[2,5120]{1,0:T(2,128)}, f32[2,5120]{1,0:T(2,128)S(1)}, u32[]{:S(2)}, u32[]{:S(2)}) collective-permute-start(f32[2,5120]{1,0:T(2,128)} %bitcast.72), channel_id=1, source_target_pairs={{1,0},{2,1},{3,2},{4,3},{5,4},{6,5},{7,6},{8,7},{9,8},{10,9},{11,1... | collective-permute-start | bytes 122888 | tf_op jit(solution)/shard_map/ppermute | solution.py:21
  53.5 5.2 %collective-permute-start.2 = (f32[2,5120]{1,0:T(2,128)}, f32[2,5120]{1,0:T(2,128)}, u32[]{:S(2)}, u32[]{:S(2)}) collective-permute-start(f32[2,5120]{1,0:T(2,128)} %bitcast.75), channel_id=1, source_target_pairs={{0,1},{1,2},{2,3},{3,4},{4,5},{5,6},{6,7},{7,8},{8,9},{9,10},{10,1... | collective-permute-start | bytes 122888 | tf_op jit(solution)/shard_map/ppermute | solution.py:21
  66.2 5.2 %all-to-all-start = ((f32[8,8,5120]{2,1,0:T(8,128)}), f32[8,8,5120]{2,1,0:T(8,128)}, u32[]{:S(2)}, u32[]{:S(2)}) async-start(f32[8,8,5120]{2,1,0:T(8,128)} %get-tuple-element.111), calls=%async_computation | async-start | bytes 2621440 | tf_op jit(solution)/shard_map/all_to_all | solution.py:187
  77.9 13.9 %all-to-all-done = f32[8,8,5120]{2,1,0:T(8,128)} async-done(((f32[8,8,5120]{2,1,0:T(8,128)}), f32[8,8,5120]{2,1,0:T(8,128)}, u32[]{:S(2)}, u32[]{:S(2)}) %all-to-all-start) | async-done | bytes 1310752 | tf_op jit(solution)/shard_map/all_to_all | solution.py:187
  94.1 3.0 %collective-permute-start.6 = (f32[4,5120]{1,0:T(4,128)}, f32[4,5120]{1,0:T(4,128)S(1)}, u32[]{:S(2)}, u32[]{:S(2)}) collective-permute-start(f32[4,5120]{1,0:T(4,128)} %pad_maximum_fusion.13), channel_id=1, source_target_pairs={{1,0},{2,1},{3,2},{4,3},{5,4},{6,5},{7,6},{8,7},{9,8},{10,9},{11,1... | collective-permute-start | bytes 245768 | tf_op jit(solution)/shard_map/ppermute | solution.py:21
  99.0 3.2 %shard_map.98 = (f32[2,1,8,5120]{3,2,1,0:T(8,128)S(1)}, f32[2,1,8,5120]{3,2,1,0:T(8,128)S(1)}, f32[8,8,5120]{2,1,0:T(8,128)}, f32[8,5120]{1,0:T(8,128)S(1)}, f32...) custom-call(f32[2,9]{1,0:T(2,128)S(1)} %pad_maximum_fusion.19.scal_ref, s32[8]{0:T(128)S(1)} %fusion.6.sel_ref, ...), custom_call_target="tpu_custom_call" | custom-call | flops 6553600 | bytes 5079040 | tf_op jit(solution)/shard_map/pallas_call | solution.py:103
  104.9 4.3 %all-to-all-start.4 = ((f32[8,8,5120]{2,1,0:T(8,128)}), f32[8,8,5120]{2,1,0:T(8,128)}, u32[]{:S(2)}, u32[]{:S(2)}) async-start(f32[8,8,5120]{2,1,0:T(8,128)} %get-tuple-element.51), calls=%async_computation.4 | async-start | bytes 2621440 | tf_op jit(solution)/shard_map/all_to_all | solution.py:187
  110.4 4.7 %collective-permute-start.24 = (f32[8,5120]{1,0:T(8,128)S(1)}, f32[8,5120]{1,0:T(8,128)S(1)}, u32[]{:S(2)}, u32[]{:S(2)}) collective-permute-start(f32[8,5120]{1,0:T(8,128)S(1)} %copy-done.38), channel_id=1, source_target_pairs={{0,16},{16,32},{32,48},{48,64},{64,80},{80,96},{96,112},{1,17},{17... | collective-permute-start | bytes 491528 | tf_op jit(solution)/shard_map/ppermute | solution.py:21
  116.5 3.2 %shard_map.95 = (f32[2,1,8,5120]{3,2,1,0:T(8,128)S(1)}, f32[2,1,8,5120]{3,2,1,0:T(8,128)S(1)}, f32[8,8,5120]{2,1,0:T(8,128)}, f32[8,5120]{1,0:T(8,128)S(1)}, f32...) custom-call(f32[2,9]{1,0:T(2,128)S(1)} %pad_maximum_fusion.19.scal_ref, s32[8]{0:T(128)S(1)} %fusion.6.sel_ref, ...), custom_call_target="tpu_custom_call" | custom-call | flops 6553600 | bytes 5079040 | tf_op jit(solution)/shard_map/pallas_call | solution.py:103
  121.1 5.5 %collective-permute-start.9 = (f32[8,5120]{1,0:T(8,128)S(1)}, f32[8,5120]{1,0:T(8,128)S(1)}, u32[]{:S(2)}, u32[]{:S(2)}) collective-permute-start(f32[8,5120]{1,0:T(8,128)S(1)} %get-tuple-element.39), channel_id=1, source_target_pairs={{0,16},{16,32},{32,48},{48,64},{64,80},{80,96},{96,112},{1,17},{17... | collective-permute-start | bytes 491528 | tf_op jit(solution)/shard_map/ppermute | solution.py:21
  127.9 5.7 %collective-permute-start.22 = (f32[2,5120]{1,0:T(2,128)}, f32[2,5120]{1,0:T(2,128)S(1)}, u32[]{:S(2)}, u32[]{:S(2)}) collective-permute-start(f32[2,5120]{1,0:T(2,128)} %get-tuple-element.52), channel_id=1, source_target_pairs={{0,1},{1,2},{2,3},{3,4},{4,5},{5,6},{6,7},{7,8},{8,9},{9,10},{10,1... | collective-permute-start | bytes 122888 | tf_op jit(solution)/shard_map/ppermute | solution.py:21
  135.6 5.8 %collective-permute-start.7 = (f32[2,5120]{1,0:T(2,128)}, f32[2,5120]{1,0:T(2,128)}, u32[]{:S(2)}, u32[]{:S(2)}) collective-permute-start(f32[2,5120]{1,0:T(2,128)} %get-tuple-element.37), channel_id=1, source_target_pairs={{0,1},{1,2},{2,3},{3,4},{4,5},{5,6},{6,7},{7,8},{8,9},{9,10},{10,1... | collective-permute-start | bytes 122888 | tf_op jit(solution)/shard_map/ppermute | solution.py:21
  144.0 8.2 %all-to-all-start.1 = ((f32[8,8,5120]{2,1,0:T(8,128)}), f32[8,8,5120]{2,1,0:T(8,128)}, u32[]{:S(2)}, u32[]{:S(2)}) async-start(f32[8,8,5120]{2,1,0:T(8,128)} %get-tuple-element.36), calls=%async_computation.1 | async-start | bytes 2621440 | tf_op jit(solution)/shard_map/all_to_all | solution.py:187
  156.4 12.3 %all-to-all-done.1 = f32[8,8,5120]{2,1,0:T(8,128)} async-done(((f32[8,8,5120]{2,1,0:T(8,128)}), f32[8,8,5120]{2,1,0:T(8,128)}, u32[]{:S(2)}, u32[]{:S(2)}) %all-to-all-start.1) | async-done | bytes 1310752 | tf_op jit(solution)/shard_map/all_to_all | solution.py:187
  178.6 2.8 %shard_map.99 = (f32[2,1,8,5120]{3,2,1,0:T(8,128)S(1)}, f32[2,1,8,5120]{3,2,1,0:T(8,128)S(1)}, f32[8,8,5120]{2,1,0:T(8,128)}, f32[8,5120]{1,0:T(8,128)}, f32[8,5...) custom-call(f32[2,9]{1,0:T(2,128)S(1)} %pad_maximum_fusion.19.scal_ref, s32[8]{0:T(128)S(1)} %fusion.6.sel_ref, ...), custom_call_target="tpu_custom_call" | custom-call | flops 6553600 | bytes 5079040 | tf_op jit(solution)/shard_map/pallas_call | solution.py:103
  181.4 4.3 %all-to-all-start.5 = ((f32[8,8,5120]{2,1,0:T(8,128)}), f32[8,8,5120]{2,1,0:T(8,128)}, u32[]{:S(2)}, u32[]{:S(2)}) async-start(f32[8,8,5120]{2,1,0:T(8,128)} %get-tuple-element.58), calls=%async_computation.5 | async-start | bytes 2621440 | tf_op jit(solution)/shard_map/all_to_all | solution.py:187
  186.9 4.7 %collective-permute-start.29 = (f32[8,5120]{1,0:T(8,128)}, f32[8,5120]{1,0:T(8,128)S(1)}, u32[]{:S(2)}, u32[]{:S(2)}) collective-permute-start(f32[8,5120]{1,0:T(8,128)} %get-tuple-element.61), channel_id=1, source_target_pairs={{0,16},{16,32},{32,48},{48,64},{64,80},{80,96},{96,112},{1,17},{17... | collective-permute-start | bytes 491528 | tf_op jit(solution)/shard_map/ppermute | solution.py:21
  193.0 3.0 %shard_map.96 = (f32[2,1,8,5120]{3,2,1,0:T(8,128)S(1)}, f32[2,1,8,5120]{3,2,1,0:T(8,128)S(1)}, f32[8,8,5120]{2,1,0:T(8,128)}, f32[8,5120]{1,0:T(8,128)}, f32[8,5...) custom-call(f32[2,9]{1,0:T(2,128)S(1)} %pad_maximum_fusion.19.scal_ref, s32[8]{0:T(128)S(1)} %fusion.6.sel_ref, ...), custom_call_target="tpu_custom_call" | custom-call | flops 6553600 | bytes 5079040 | tf_op jit(solution)/shard_map/pallas_call | solution.py:103
  196.7 5.5 %collective-permute-start.14 = (f32[8,5120]{1,0:T(8,128)}, f32[8,5120]{1,0:T(8,128)S(1)}, u32[]{:S(2)}, u32[]{:S(2)}) collective-permute-start(f32[8,5120]{1,0:T(8,128)} %get-tuple-element.46), channel_id=1, source_target_pairs={{0,16},{16,32},{32,48},{48,64},{64,80},{80,96},{96,112},{1,17},{17... | collective-permute-start | bytes 491528 | tf_op jit(solution)/shard_map/ppermute | solution.py:21
  203.5 3.2 %all-to-all-done.5 = f32[8,8,5120]{2,1,0:T(8,128)} async-done(((f32[8,8,5120]{2,1,0:T(8,128)}), f32[8,8,5120]{2,1,0:T(8,128)}, u32[]{:S(2)}, u32[]{:S(2)}) %all-to-all-start.5) | async-done | bytes 1310752 | tf_op jit(solution)/shard_map/all_to_all | solution.py:187
  206.8 4.4 %all-to-all-start.2 = ((f32[8,8,5120]{2,1,0:T(8,128)}), f32[8,8,5120]{2,1,0:T(8,128)}, u32[]{:S(2)}, u32[]{:S(2)}) async-start(f32[8,8,5120]{2,1,0:T(8,128)} %get-tuple-element.43), calls=%async_computation.2 | async-start | bytes 2621440 | tf_op jit(solution)/shard_map/all_to_all | solution.py:187
  211.2 8.5 %collective-permute-start.27 = (f32[2,5120]{1,0:T(2,128)}, f32[2,5120]{1,0:T(2,128)}, u32[]{:S(2)}, u32[]{:S(2)}) collective-permute-start(f32[2,5120]{1,0:T(2,128)} %get-tuple-element.59), channel_id=1, source_target_pairs={{0,1},{1,2},{2,3},{3,4},{4,5},{5,6},{6,7},{7,8},{8,9},{9,10},{10,1... | collective-permute-start | bytes 122888 | tf_op jit(solution)/shard_map/ppermute | solution.py:21
  221.7 5.8 %collective-permute-start.12 = (f32[2,5120]{1,0:T(2,128)}, f32[2,5120]{1,0:T(2,128)}, u32[]{:S(2)}, u32[]{:S(2)}) collective-permute-start(f32[2,5120]{1,0:T(2,128)} %get-tuple-element.44), channel_id=1, source_target_pairs={{0,1},{1,2},{2,3},{3,4},{4,5},{5,6},{6,7},{7,8},{8,9},{9,10},{10,1... | collective-permute-start | bytes 122888 | tf_op jit(solution)/shard_map/ppermute | solution.py:21
  239.9 5.9 %collective-permute-done.16.below_ref = f32[4,5120]{1,0:T(4,128)S(1)} collective-permute-done((f32[4,5120]{1,0:T(4,128)S(1)}, f32[4,5120]{1,0:T(4,128)S(1)}, u32[]{:S(2)}, u32[]{:S(2)}) %collective-permute-start.16) | collective-permute-done | bytes 81952 | tf_op jit(solution)/shard_map/ppermute | solution.py:21
  245.8 3.0 %shard_map.97 = (f32[2,1,8,5120]{3,2,1,0:T(8,128)S(1)}, f32[2,1,8,5120]{3,2,1,0:T(8,128)S(1)}, f32[8,8,5120]{2,1,0:T(8,128)}, f32[8,5120]{1,0:T(8,128)}, f32[8,5...) custom-call(f32[2,9]{1,0:T(2,128)S(1)} %pad_maximum_fusion.19.scal_ref, s32[8]{0:T(128)S(1)} %fusion.6.sel_ref, ...), custom_call_target="tpu_custom_call" | custom-call | flops 6553600 | bytes 5079040 | tf_op jit(solution)/shard_map/pallas_call | solution.py:103
  248.9 3.2 %shard_map.100 = (f32[2,1,8,5120]{3,2,1,0:T(8,128)S(1)}, f32[2,1,8,5120]{3,2,1,0:T(8,128)S(1)}, f32[8,8,5120]{2,1,0:T(8,128)}, f32[8,5120]{1,0:T(8,128)}, f32[8,...) custom-call(f32[2,9]{1,0:T(2,128)S(1)} %pad_maximum_fusion.19.scal_ref, s32[8]{0:T(128)S(1)} %fusion.6.sel_ref, ...), custom_call_target="tpu_custom_call" | custom-call | flops 6553600 | bytes 5079040 | tf_op jit(solution)/shard_map/pallas_call | solution.py:103
  (214 shorter events, 78.5 us)
Async XLA Ops:
  2.7 50.7 %collective-permute-start.4 = (f32[8,5120]{1,0:T(8,128)}, f32[8,5120]{1,0:T(8,128)S(1)}, u32[]{:S(2)}, u32[]{:S(2)}) collective-permute-start(f32[8,5120]{1,0:T(8,128)} %get-tuple-element.94), channel_id=1, source_target_pairs={{0,16},{16,32},{32,48},{48,64},{64,80},{80,96},{96,112},{1,17},{17... | collective-permute-start | bytes 491528 | tf_op jit(solution)/shard_map/ppermute | solution.py:21
  8.2 50.5 %collective-permute-start.20 = (f32[8,5120]{1,0:T(8,128)}, f32[8,5120]{1,0:T(8,128)}, u32[]{:S(2)}, u32[]{:S(2)}) collective-permute-start(f32[8,5120]{1,0:T(8,128)} %get-tuple-element.95), channel_id=1, source_target_pairs={{16,0},{32,16},{48,32},{64,48},{80,64},{96,80},{112,96},{17,1},{33... | collective-permute-start | bytes 491528 | tf_op jit(solution)/shard_map/ppermute | solution.py:21
  9.5 52.5 %collective-permute-start.5 = (f32[8,5120]{1,0:T(8,128)}, f32[8,5120]{1,0:T(8,128)}, u32[]{:S(2)}, u32[]{:S(2)}) collective-permute-start(f32[8,5120]{1,0:T(8,128)} %get-tuple-element.96), channel_id=1, source_target_pairs={{16,0},{32,16},{48,32},{64,48},{80,64},{96,80},{112,96},{17,1},{33... | collective-permute-start | bytes 491528 | tf_op jit(solution)/shard_map/ppermute | solution.py:21
  17.5 27.8 %collective-permute-start = (f32[2,2,1,5120]{3,2,1,0:T(1,128)}, f32[2,2,1,5120]{3,2,1,0:T(1,128)S(1)}, u32[]{:S(2)}, u32[]{:S(2)}) collective-permute-start(f32[2,2,1,5120]{3,2,1,0:T(1,128)} %get-tuple-element.104), channel_id=1, source_target_pairs={{0,1},{1,2},{2,3},{3,4},{4,5},{5,6},{6,7},{7,8},{8,9},{9,10},{10,1... | collective-permute-start | bytes 245768 | tf_op jit(solution)/shard_map/ppermute | solution.py:21
  20.6 29.5 %collective-permute-start.1 = (f32[2,2,1,5120]{3,2,1,0:T(1,128)S(1)}, f32[2,2,1,5120]{3,2,1,0:T(1,128)S(1)}, u32[]{:S(2)}, u32[]{:S(2)}) collective-permute-start(f32[2,2,1,5120]{3,2,1,0:T(1,128)S(1)} %get-tuple-element.105), channel_id=1, source_target_pairs={{1,0},{2,1},{3,2},{4,3},{5,4},{6,5},{7,6},{8,7},{9,8},{10,9},{11,1... | collective-permute-start | bytes 245768 | tf_op jit(solution)/shard_map/ppermute | solution.py:21
  25.8 40.4 %all-to-all-start.3 = ((f32[8,8,5120]{2,1,0:T(8,128)}), f32[8,8,5120]{2,1,0:T(8,128)}, u32[]{:S(2)}, u32[]{:S(2)}) async-start(f32[8,8,5120]{2,1,0:T(8,128)} %get-tuple-element.112), calls=%async_computation.3 | async-start | bytes 2621440 | tf_op jit(solution)/shard_map/all_to_all | solution.py:187
  50.2 43.4 %collective-permute-start.18 = (f32[2,5120]{1,0:T(2,128)}, f32[2,5120]{1,0:T(2,128)S(1)}, u32[]{:S(2)}, u32[]{:S(2)}) collective-permute-start(f32[2,5120]{1,0:T(2,128)} %bitcast.72), channel_id=1, source_target_pairs={{1,0},{2,1},{3,2},{4,3},{5,4},{6,5},{7,6},{8,7},{9,8},{10,9},{11,1... | collective-permute-start | bytes 122888 | tf_op jit(solution)/shard_map/ppermute | solution.py:21
  53.5 63.0 %collective-permute-start.2 = (f32[2,5120]{1,0:T(2,128)}, f32[2,5120]{1,0:T(2,128)}, u32[]{:S(2)}, u32[]{:S(2)}) collective-permute-start(f32[2,5120]{1,0:T(2,128)} %bitcast.75), channel_id=1, source_target_pairs={{0,1},{1,2},{2,3},{3,4},{4,5},{5,6},{6,7},{7,8},{8,9},{9,10},{10,1... | collective-permute-start | bytes 122888 | tf_op jit(solution)/shard_map/ppermute | solution.py:21
  58.7 38.5 %collective-permute-start.17 = (f32[2,5120]{1,0:T(2,128)}, f32[2,5120]{1,0:T(2,128)}, u32[]{:S(2)}, u32[]{:S(2)}) collective-permute-start(f32[2,5120]{1,0:T(2,128)} %bitcast.73), channel_id=1, source_target_pairs={{0,1},{1,2},{2,3},{3,4},{4,5},{5,6},{6,7},{7,8},{8,9},{9,10},{10,1... | collective-permute-start | bytes 122888 | tf_op jit(solution)/shard_map/ppermute | solution.py:21
  62.0 54.4 %collective-permute-start.3 = (f32[2,5120]{1,0:T(2,128)}, f32[2,5120]{1,0:T(2,128)}, u32[]{:S(2)}, u32[]{:S(2)}) collective-permute-start(f32[2,5120]{1,0:T(2,128)} %bitcast.74), channel_id=1, source_target_pairs={{1,0},{2,1},{3,2},{4,3},{5,4},{6,5},{7,6},{8,7},{9,8},{10,9},{11,1... | collective-permute-start | bytes 122888 | tf_op jit(solution)/shard_map/ppermute | solution.py:21
  66.2 25.6 %all-to-all-start = ((f32[8,8,5120]{2,1,0:T(8,128)}), f32[8,8,5120]{2,1,0:T(8,128)}, u32[]{:S(2)}, u32[]{:S(2)}) async-start(f32[8,8,5120]{2,1,0:T(8,128)} %get-tuple-element.111), calls=%async_computation | async-start | bytes 2621440 | tf_op jit(solution)/shard_map/all_to_all | solution.py:187
  73.9 23.3 %collective-permute-start.21 = (f32[4,5120]{1,0:T(4,128)}, f32[4,5120]{1,0:T(4,128)}, u32[]{:S(2)}, u32[]{:S(2)}) collective-permute-start(f32[4,5120]{1,0:T(4,128)} %pad_maximum_fusion.16), channel_id=1, source_target_pairs={{1,0},{2,1},{3,2},{4,3},{5,4},{6,5},{7,6},{8,7},{9,8},{10,9},{11,1... | collective-permute-start | bytes 245768 | tf_op jit(solution)/shard_map/ppermute | solution.py:21
  94.1 22.3 %collective-permute-start.6 = (f32[4,5120]{1,0:T(4,128)}, f32[4,5120]{1,0:T(4,128)S(1)}, u32[]{:S(2)}, u32[]{:S(2)}) collective-permute-start(f32[4,5120]{1,0:T(4,128)} %pad_maximum_fusion.13), channel_id=1, source_target_pairs={{1,0},{2,1},{3,2},{4,3},{5,4},{6,5},{7,6},{8,7},{9,8},{10,9},{11,1... | collective-permute-start | bytes 245768 | tf_op jit(solution)/shard_map/ppermute | solution.py:21
  104.9 38.5 %all-to-all-start.4 = ((f32[8,8,5120]{2,1,0:T(8,128)}), f32[8,8,5120]{2,1,0:T(8,128)}, u32[]{:S(2)}, u32[]{:S(2)}) async-start(f32[8,8,5120]{2,1,0:T(8,128)} %get-tuple-element.51), calls=%async_computation.4 | async-start | bytes 2621440 | tf_op jit(solution)/shard_map/all_to_all | solution.py:187
  110.4 23.3 %collective-permute-start.24 = (f32[8,5120]{1,0:T(8,128)S(1)}, f32[8,5120]{1,0:T(8,128)S(1)}, u32[]{:S(2)}, u32[]{:S(2)}) collective-permute-start(f32[8,5120]{1,0:T(8,128)S(1)} %copy-done.38), channel_id=1, source_target_pairs={{0,16},{16,32},{32,48},{48,64},{64,80},{80,96},{96,112},{1,17},{17... | collective-permute-start | bytes 491528 | tf_op jit(solution)/shard_map/ppermute | solution.py:21
  115.1 20.5 %collective-permute-start.25 = (f32[8,5120]{1,0:T(8,128)S(1)}, f32[8,5120]{1,0:T(8,128)S(1)}, u32[]{:S(2)}, u32[]{:S(2)}) collective-permute-start(f32[8,5120]{1,0:T(8,128)S(1)} %copy-done.36), channel_id=1, source_target_pairs={{16,0},{32,16},{48,32},{64,48},{80,64},{96,80},{112,96},{17,1},{33... | collective-permute-start | bytes 491528 | tf_op jit(solution)/shard_map/ppermute | solution.py:21
  121.1 20.3 %collective-permute-start.9 = (f32[8,5120]{1,0:T(8,128)S(1)}, f32[8,5120]{1,0:T(8,128)S(1)}, u32[]{:S(2)}, u32[]{:S(2)}) collective-permute-start(f32[8,5120]{1,0:T(8,128)S(1)} %get-tuple-element.39), channel_id=1, source_target_pairs={{0,16},{16,32},{32,48},{48,64},{64,80},{80,96},{96,112},{1,17},{17... | collective-permute-start | bytes 491528 | tf_op jit(solution)/shard_map/ppermute | solution.py:21
  127.9 42.6 %collective-permute-start.22 = (f32[2,5120]{1,0:T(2,128)}, f32[2,5120]{1,0:T(2,128)S(1)}, u32[]{:S(2)}, u32[]{:S(2)}) collective-permute-start(f32[2,5120]{1,0:T(2,128)} %get-tuple-element.52), channel_id=1, source_target_pairs={{0,1},{1,2},{2,3},{3,4},{4,5},{5,6},{6,7},{7,8},{8,9},{9,10},{10,1... | collective-permute-start | bytes 122888 | tf_op jit(solution)/shard_map/ppermute | solution.py:21
  133.7 39.3 %collective-permute-start.23 = (f32[2,5120]{1,0:T(2,128)}, f32[2,5120]{1,0:T(2,128)S(1)}, u32[]{:S(2)}, u32[]{:S(2)}) collective-permute-start(f32[2,5120]{1,0:T(2,128)} %get-tuple-element.53), channel_id=1, source_target_pairs={{1,0},{2,1},{3,2},{4,3},{5,4},{6,5},{7,6},{8,7},{9,8},{10,9},{11,1... | collective-permute-start | bytes 122888 | tf_op jit(solution)/shard_map/ppermute | solution.py:21
  135.6 57.3 %collective-permute-start.7 = (f32[2,5120]{1,0:T(2,128)}, f32[2,5120]{1,0:T(2,128)}, u32[]{:S(2)}, u32[]{:S(2)}) collective-permute-start(f32[2,5120]{1,0:T(2,128)} %get-tuple-element.37), channel_id=1, source_target_pairs={{0,1},{1,2},{2,3},{3,4},{4,5},{5,6},{6,7},{7,8},{8,9},{9,10},{10,1... | collective-permute-start | bytes 122888 | tf_op jit(solution)/shard_map/ppermute | solution.py:21
  141.4 51.5 %collective-permute-start.8 = (f32[2,5120]{1,0:T(2,128)}, f32[2,5120]{1,0:T(2,128)}, u32[]{:S(2)}, u32[]{:S(2)}) collective-permute-start(f32[2,5120]{1,0:T(2,128)} %get-tuple-element.38), channel_id=1, source_target_pairs={{1,0},{2,1},{3,2},{4,3},{5,4},{6,5},{7,6},{8,7},{9,8},{10,9},{11,1... | collective-permute-start | bytes 122888 | tf_op jit(solution)/shard_map/ppermute | solution.py:21
  144.0 24.7 %all-to-all-start.1 = ((f32[8,8,5120]{2,1,0:T(8,128)}), f32[8,8,5120]{2,1,0:T(8,128)}, u32[]{:S(2)}, u32[]{:S(2)}) async-start(f32[8,8,5120]{2,1,0:T(8,128)} %get-tuple-element.36), calls=%async_computation.1 | async-start | bytes 2621440 | tf_op jit(solution)/shard_map/all_to_all | solution.py:187
  153.4 20.2 %collective-permute-start.26 = (f32[4,5120]{1,0:T(4,128)S(1)}, f32[4,5120]{1,0:T(4,128)S(1)}, u32[]{:S(2)}, u32[]{:S(2)}) collective-permute-start(f32[4,5120]{1,0:T(4,128)S(1)} %pad_maximum_fusion.17), channel_id=1, source_target_pairs={{1,0},{2,1},{3,2},{4,3},{5,4},{6,5},{7,6},{8,7},{9,8},{10,9},{11,1... | collective-permute-start | bytes 245768 | tf_op jit(solution)/shard_map/ppermute | solution.py:21
  171.1 21.8 %collective-permute-start.11 = (f32[4,5120]{1,0:T(4,128)}, f32[4,5120]{1,0:T(4,128)S(1)}, u32[]{:S(2)}, u32[]{:S(2)}) collective-permute-start(f32[4,5120]{1,0:T(4,128)} %pad_maximum_fusion.14), channel_id=1, source_target_pairs={{1,0},{2,1},{3,2},{4,3},{5,4},{6,5},{7,6},{8,7},{9,8},{10,9},{11,1... | collective-permute-start | bytes 245768 | tf_op jit(solution)/shard_map/ppermute | solution.py:21
  181.4 25.4 %all-to-all-start.5 = ((f32[8,8,5120]{2,1,0:T(8,128)}), f32[8,8,5120]{2,1,0:T(8,128)}, u32[]{:S(2)}, u32[]{:S(2)}) async-start(f32[8,8,5120]{2,1,0:T(8,128)} %get-tuple-element.58), calls=%async_computation.5 | async-start | bytes 2621440 | tf_op jit(solution)/shard_map/all_to_all | solution.py:187
  186.9 32.9 %collective-permute-start.29 = (f32[8,5120]{1,0:T(8,128)}, f32[8,5120]{1,0:T(8,128)S(1)}, u32[]{:S(2)}, u32[]{:S(2)}) collective-permute-start(f32[8,5120]{1,0:T(8,128)} %get-tuple-element.61), channel_id=1, source_target_pairs={{0,16},{16,32},{32,48},{48,64},{64,80},{80,96},{96,112},{1,17},{17... | collective-permute-start | bytes 491528 | tf_op jit(solution)/shard_map/ppermute | solution.py:21
  191.6 30.1 %collective-permute-start.30 = (f32[8,5120]{1,0:T(8,128)}, f32[8,5120]{1,0:T(8,128)}, u32[]{:S(2)}, u32[]{:S(2)}) collective-permute-start(f32[8,5120]{1,0:T(8,128)} %get-tuple-element.62), channel_id=1, source_target_pairs={{16,0},{32,16},{48,32},{64,48},{80,64},{96,80},{112,96},{17,1},{33... | collective-permute-start | bytes 491528 | tf_op jit(solution)/shard_map/ppermute | solution.py:21
  196.7 31.7 %collective-permute-start.14 = (f32[8,5120]{1,0:T(8,128)}, f32[8,5120]{1,0:T(8,128)S(1)}, u32[]{:S(2)}, u32[]{:S(2)}) collective-permute-start(f32[8,5120]{1,0:T(8,128)} %get-tuple-element.46), channel_id=1, source_target_pairs={{0,16},{16,32},{32,48},{48,64},{64,80},{80,96},{96,112},{1,17},{17... | collective-permute-start | bytes 491528 | tf_op jit(solution)/shard_map/ppermute | solution.py:21
  202.2 28.1 %collective-permute-start.15 = (f32[8,5120]{1,0:T(8,128)}, f32[8,5120]{1,0:T(8,128)S(1)}, u32[]{:S(2)}, u32[]{:S(2)}) collective-permute-start(f32[8,5120]{1,0:T(8,128)} %get-tuple-element.47), channel_id=1, source_target_pairs={{16,0},{32,16},{48,32},{64,48},{80,64},{96,80},{112,96},{17,1},{33... | collective-permute-start | bytes 491528 | tf_op jit(solution)/shard_map/ppermute | solution.py:21
  206.8 28.7 %all-to-all-start.2 = ((f32[8,8,5120]{2,1,0:T(8,128)}), f32[8,8,5120]{2,1,0:T(8,128)}, u32[]{:S(2)}, u32[]{:S(2)}) async-start(f32[8,8,5120]{2,1,0:T(8,128)} %get-tuple-element.43), calls=%async_computation.2 | async-start | bytes 2621440 | tf_op jit(solution)/shard_map/all_to_all | solution.py:187
  211.2 37.6 %collective-permute-start.27 = (f32[2,5120]{1,0:T(2,128)}, f32[2,5120]{1,0:T(2,128)}, u32[]{:S(2)}, u32[]{:S(2)}) collective-permute-start(f32[2,5120]{1,0:T(2,128)} %get-tuple-element.59), channel_id=1, source_target_pairs={{0,1},{1,2},{2,3},{3,4},{4,5},{5,6},{6,7},{7,8},{8,9},{9,10},{10,1... | collective-permute-start | bytes 122888 | tf_op jit(solution)/shard_map/ppermute | solution.py:21
  219.7 29.1 %collective-permute-start.28 = (f32[2,5120]{1,0:T(2,128)}, f32[2,5120]{1,0:T(2,128)}, u32[]{:S(2)}, u32[]{:S(2)}) collective-permute-start(f32[2,5120]{1,0:T(2,128)} %get-tuple-element.60), channel_id=1, source_target_pairs={{1,0},{2,1},{3,2},{4,3},{5,4},{6,5},{7,6},{8,7},{9,8},{10,9},{11,1... | collective-permute-start | bytes 122888 | tf_op jit(solution)/shard_map/ppermute | solution.py:21
  (57 other events, 412.9 us)

commit v6 on v4

--- a/solution.py
+++ b/solution.py
@@ -29,7 +29,7 @@
     return jnp.concatenate([jnp.zeros_like(field[..., :1]), field[..., :-1]], axis=-1)
 
 
-def update_kernel(scal_ref, sel_ref, x_ref, v_ref, k_ref, alive_ref, part_ref, up_ref, down_ref,
+def update_kernel(scal_ref, sel_ref, src_ref, x_ref, v_ref, k_ref, alive_ref, part_ref, up_ref, down_ref,
                   prevf_ref, nextf_ref, below_ref, xo_ref, vo_ref, send_ref, lastf_ref, firstf_ref,
                   top_ref, bot_ref):
     L, ncomp, R, C = x_ref.shape
@@ -68,33 +68,36 @@
                 k_up * (x_up - x) + k_dn * (x_dn - x) + k_r * (shr(x) - x) + k_l * (shl(x) - x)
             )
             if l == 0:
-                prev_src, prev_row = prevf_ref[c], below_ref[pl.ds(c, 1), :]
+                prev_src, prev_row = prevf_ref[pl.ds(c * R, R), :], below_ref[pl.ds(c, 1), :]
             else:
                 prev_src, prev_row = x_ref[l - 1, c], down_ref[pl.ds((l - 1) * ncomp + c, 1), :]
             if l == L - 1:
-                next_src, next_row = nextf_ref[c], below_ref[pl.ds(ncomp + c, 1), :]
+                next_src, next_row = nextf_ref[pl.ds(c * R, R), :], below_ref[pl.ds(ncomp + c, 1), :]
             else:
                 next_src, next_row = x_ref[l + 1, c], down_ref[pl.ds((l + 1) * ncomp + c, 1), :]
             part_row = below_ref[pl.ds((2 + l) * ncomp + c, 1), :]
             pull = scal_ref[l, 0] * (warp_of(prev_src, prev_row, ws[0]) - x)
             pull = pull + scal_ref[l, 1] * (warp_of(next_src, next_row, ws[1]) - x)
-            pull = pull + scal_ref[l, 2] * (warp_of(part_ref[l, c], part_row, ws[2]) - x)
+            pull = pull + scal_ref[l, 2] * (
+                warp_of(part_ref[src_ref[l], pl.ds(c * R, R), :], part_row, ws[2]) - x
+            )
             force = inplane + pull
             vel = alive * (DAMPING * v_ref[l, c] + STEP * force)
             vo_ref[l, c] = vel
             new = x + STEP * vel
             xo_ref[l, c] = new
             if l == L - 1:
-                lastf_ref[c] = new
+                lastf_ref[pl.ds(c * R, R), :] = new
             if l == 0:
-                firstf_ref[c] = new
+                firstf_ref[pl.ds(c * R, R), :] = new
             top_ref[pl.ds(l * ncomp + c, 1), :] = new[0:1]
             bot_ref[pl.ds(l * ncomp + c, 1), :] = new[R - 1 : R]
     for d in range(send_ref.shape[0]):
-        send_ref[d] = xo_ref[sel_ref[d]]
-
-
-def update(scal, sel, x, v, kst, alive, part, up, down, prevf, nextf, below):
+        for c in range(ncomp):
+            send_ref[d, pl.ds(c * R, R), :] = xo_ref[sel_ref[d], c]
+
+
+def update(scal, sel, src, x, v, kst, alive, part, up, down, prevf, nextf, below):
     nb = sel.shape[0]
     vmem = pl.BlockSpec(memory_space=pltpu.VMEM)
     smem = pl.BlockSpec(memory_space=pltpu.SMEM)
@@ -104,17 +107,17 @@
         out_shape=(
             jax.ShapeDtypeStruct(x.shape, x.dtype),
             jax.ShapeDtypeStruct(x.shape, x.dtype),
-            jax.ShapeDtypeStruct((nb,) + x.shape[1:], x.dtype),
-            jax.ShapeDtypeStruct(x.shape[1:], x.dtype),
-            jax.ShapeDtypeStruct(x.shape[1:], x.dtype),
+            jax.ShapeDtypeStruct((nb, x.shape[1] * x.shape[2], x.shape[3]), x.dtype),
+            jax.ShapeDtypeStruct((x.shape[1] * x.shape[2], x.shape[3]), x.dtype),
+            jax.ShapeDtypeStruct((x.shape[1] * x.shape[2], x.shape[3]), x.dtype),
             jax.ShapeDtypeStruct((x.shape[0] * x.shape[1], x.shape[3]), x.dtype),
             jax.ShapeDtypeStruct((x.shape[0] * x.shape[1], x.shape[3]), x.dtype),
         ),
-        in_specs=[smem, smem] + [vmem] * 10,
+        in_specs=[smem, smem, smem] + [vmem] * 10,
         out_specs=[vmem] * 7,
         compiler_params=pltpu.CompilerParams(vmem_limit_bytes=48 * 1024 * 1024),
         cost_estimate=pl.CostEstimate(flops=80 * x.size, bytes_accessed=moved, transcendentals=0),
-    )(scal, sel, x, v, kst, alive, part, up, down, prevf, nextf, below)
+    )(scal, sel, src, x, v, kst, alive, part, up, down, prevf, nextf, below)
 
 
 def body(disp, vel, stiff_class, valid, class_table, warp, spring_z, skip_partner):
@@ -147,6 +150,8 @@
     wanted = skip_partner.reshape(block_count, local_count)
     hit = (wanted // local_count) == block_index
     send_sel = jnp.sum(jnp.where(hit, wanted % local_count, 0), axis=1)
+    send_sel = jnp.clip(send_sel, 0, local_count - 1)
+    src_block = jnp.clip(src_block, 0, block_count - 1)
 
     k_mid = kap_ext[:, 1:-1]
     kst = jnp.stack([kap_ext[:, :-2], k_mid, kap_ext[:, 2:], shift_right(k_mid), shift_left(k_mid)])
@@ -167,31 +172,36 @@
     send = field[0][None]
     for l in range(1, local_count):
         send = jnp.where((send_sel == l)[:, None, None, None], field[l][None], send)
-    last_face = field[-1]
-    first_face = field[0]
+    plane = ncomp * disp.shape[2]
+    send = send.reshape(block_count, plane, cols)
+    last_face = field[-1].reshape(plane, cols)
+    first_face = field[0].reshape(plane, cols)
     top_rows = field[:, :, 0].reshape(local_count * ncomp, cols)
     bot_rows = field[:, :, -1].reshape(local_count * ncomp, cols)
     for _ in range(ITERS):
       recv = lax.all_to_all(send, "gz", 0, 0, tiled=True)
-      partner8 = jnp.stack(
-          [lax.dynamic_index_in_dim(recv, src_block[l], 0, keepdims=False) for l in range(local_count)]
+      heads = recv[:, :: disp.shape[2]]
+      partner_heads = jnp.stack(
+          [lax.dynamic_index_in_dim(heads, src_block[l], 0, keepdims=False) for l in range(local_count)]
       )
       prev_face = shift_rows(last_face, "gz", True)
       next_face = shift_rows(first_face, "gz", False)
       up = shift_rows(bot_rows, "tile", True)
       down = shift_rows(top_rows, "tile", False)
+      rows = disp.shape[2]
       firsts = jnp.concatenate(
-          [prev_face[:, 0], next_face[:, 0]] + [partner8[l, :, 0] for l in range(local_count)], axis=0
+          [prev_face[::rows], next_face[::rows]] + [partner_heads[l] for l in range(local_count)], axis=0
       )
       below = shift_rows(firsts, "tile", False)
       field, velocity, send, last_face, first_face, top_rows, bot_rows = update(
           scal,
           send_sel,
+          src_block,
           field,
           velocity,
           kst,
           alive_mid,
-          partner8,
+          recv,
           up,
           down,
           prev_face,

time: 236 us -> 256 us (1.085)
  starting transfers between devices: 65.4 us -> 73.8 us
  waiting for transfers between devices: 98.7 us -> 107 us
  Pallas kernels: 14.6 us -> 18.5 us
    ppermute x17, waiting for transfers between devices: 13.6 us -> 82.3 us  [shift_rows(): return lax.ppermute(block, axis, pairs)]
    all_to_all x3, waiting for transfers between devices: 85.1 us -> 24.8 us  [body(): recv = lax.all_to_all(send, 'gz', 0, 0, tiled=True)]
    slice x1 -> x9, local copies, waits for them, and re-layouts: 0.04 us -> 20.6 us  [the longest x3 15 us: body(): heads = recv[:, ::disp.shape[2]]]
    pallas_call x6 -> x0, local copies, waits for them, and re-layouts: 12.2 us -> none  [update(): pl.pallas_call(update_kernel, out_shape=(jax.ShapeDtypeStruct(x.shape, x....]
    squeeze x9 -> x3, local copies, waits for them, and re-layouts: 6.91 us -> 1.62 us  [body(): lax.dynamic_index_in_dim(heads, src_block[l], 0, keepdims=False)]
    ppermute x17, starting transfers between devices: 49.6 us -> 54.2 us  [shift_rows(): return lax.ppermute(block, axis, pairs)]
    ppermute x6 -> x0, local copies, waits for them, and re-layouts: 3.95 us -> none  [shift_rows(): return lax.ppermute(block, axis, pairs)]
    pallas_call x3, Pallas kernels: 14.6 us -> 18.5 us  [update(): pl.pallas_call(update_kernel, out_shape=(jax.ShapeDtypeStruct(x.shape, x....]
  transfers between devices with their start and end apart: 20 -> 20, of which waited for: 6 -> 6; matrix products, arithmetic and copies ran while one was open for 19% -> 11% of each run, Pallas kernels for 0% -> 0%
where the time goes in v6:
time: 256 us; the launch traced here: 252 us
  waiting for transfers between devices  107 us (42%)
  starting transfers between devices  73.8 us (29%)
  local copies, waits for them, and re-layouts  37.1 us (14%)
  Pallas kernels  18.5 us (7%)
  other arithmetic  10.8 us (4%)
  between operations  4.75 us (2%)
    ppermute x17, waiting for transfers between devices, shift_rows(): return lax.ppermute(block, axis, pairs)  82.3 us
    ppermute x17, starting transfers between devices, shift_rows(): return lax.ppermute(block, axis, pairs)  54.2 us
    all_to_all x3, waiting for transfers between devices, body(): recv = lax.all_to_all(send, 'gz', 0, 0, tiled=True)  24.8 us
    all_to_all x3, starting transfers between devices, body(): recv = lax.all_to_all(send, 'gz', 0, 0, tiled=True)  19.6 us
    pallas_call x3, Pallas kernels, update(): pl.pallas_call(update_kernel, out_shape=(jax.ShapeDtypeStruct(x.shape, x....  18.5 us
    slice x3, local copies, waits for them, and re-layouts, body(): heads = recv[:, ::disp.shape[2]]  15 us
    unnamed x51, local copies, waits for them, and re-layouts  6.58 us
    another operation x1, other arithmetic, body(): stiff = jnp.stack([kappa, alive])  5.24 us
  transfers between devices with their start and end apart: 20, of which 6 were waited for; matrix products, arithmetic and copies ran while one was open for 11% of the time, Pallas kernels for 0%

profile of v6, /device:TPU:25, one launch (start us, length us, event | category | flops | bytes accessed | tf_op | source)
XLA Modules:
  0.0 252.1 jit_solution(8192018491630033576)
XLA Ops:
  0.7 1.9 slice_reduce_fusion
  3.3 3.8 %collective-permute-start.2 = (f32[4,5120]{1,0:T(4,128)}, f32[4,5120]{1,0:T(4,128)S(1)}, u32[]{:S(2)}, u32[]{:S(2)}) collective-permute-start(f32[4,5120]{1,0:T(4,128)} %reshape_squeeze.8), channel_id=1, source_target_pairs={{0,1},{1,2},{2,3},{3,4},{4,5},{5,6},{6,7},{7,8},{8,9},{9,10},{10,1... | collective-permute-start | bytes 245768 | tf_op jit(solution)/shard_map/ppermute | solution.py:21
  9.7 5.2 %multiply_bitcast_fusion = f32[1,2,8,5120]{3,2,1,0:T(8,128)S(1)} fusion(s32[2,8,5120]{2,1,0:T(8,128)S(1)} %copy-done.19, f32[]{:T(128)} %bitcast.7, f32[]{:T(128)} %bitcast.6, f32[]{:T(128)} %bitcast.5, f32[]{:T(128)} %bitcast.4, f32[]{:T(128)} %bitcast.3, f32[]{:T(128)} %bitcast.2, f32[]{:T(128)} %bitcast.1, f32[]{:T(128)} %bitcast, ...), kind=kLoop, calls=%fused_computation.15 | loop fusion | flops 1474560 | bytes 983072 | tf_op jit(solution)/shard_map/stack | solution.py:133
  15.0 1.9 collective-permute-start
  17.0 2.4 collective-permute-start.1
  20.3 5.9 %collective-permute-start.4 = (f32[16,5120]{1,0:T(8,128)}, f32[16,5120]{1,0:T(8,128)}, u32[]{:S(2)}, u32[]{:S(2)}) collective-permute-start(f32[16,5120]{1,0:T(8,128)} %get-tuple-element.36), channel_id=1, source_target_pairs={{0,16},{16,32},{32,48},{48,64},{64,80},{80,96},{96,112},{1,17},{17... | collective-permute-start | bytes 983048 | tf_op jit(solution)/shard_map/ppermute | solution.py:21
  27.7 2.9 %broadcast_select_fusion = f32[8,16,5120]{2,1,0:T(8,128)} fusion(f32[16,5120]{1,0:T(8,128)} %get-tuple-element.37, f32[16,5120]{1,0:T(8,128)} %get-tuple-element.36, pred[8]{0:T(512)(128)(4,1)S(1)} %broadcast_compare_fusion), kind=kLoop, calls=%fused_computation | loop fusion | flops 655360 | bytes 3276808 | tf_op jit(solution)/shard_map/jit(_where)/select_n | solution.py:174
  30.6 7.2 %all-to-all-start = ((f32[8,16,5120]{2,1,0:T(8,128)}), f32[8,16,5120]{2,1,0:T(8,128)}, u32[]{:S(2)}, u32[]{:S(2)}) async-start(f32[8,16,5120]{2,1,0:T(8,128)} %broadcast_select_fusion), calls=%async_computation | async-start | bytes 5242880 | tf_op jit(solution)/shard_map/all_to_all | solution.py:182
  43.2 3.1 %collective-permute-start.3 = (f32[4,5120]{1,0:T(4,128)}, f32[4,5120]{1,0:T(4,128)S(1)}, u32[]{:S(2)}, u32[]{:S(2)}) collective-permute-start(f32[4,5120]{1,0:T(4,128)} %reshape_squeeze.9), channel_id=1, source_target_pairs={{1,0},{2,1},{3,2},{4,3},{5,4},{6,5},{7,6},{8,7},{9,8},{10,9},{11,1... | collective-permute-start | bytes 245768 | tf_op jit(solution)/shard_map/ppermute | solution.py:21
  50.8 24.8 %all-to-all-done.part_ref = f32[8,16,5120]{2,1,0:T(8,128)} async-done(((f32[8,16,5120]{2,1,0:T(8,128)}), f32[8,16,5120]{2,1,0:T(8,128)}, u32[]{:S(2)}, u32[]{:S(2)}) %all-to-all-start) | async-done | bytes 2621472 | tf_op jit(solution)/shard_map/all_to_all | solution.py:182
  75.7 5.4 %slice.135 = f32[8,2,5120]{2,1,0:T(2,128)} slice(f32[8,16,5120]{2,1,0:T(8,128)} %all-to-all-done.part_ref), slice={[0:8:1], [0:16:8], [0:5120:1]} | slice | bytes 655360 | tf_op jit(solution)/shard_map/slice | solution.py:183
  82.7 3.6 %collective-permute-start.6 = (f32[8,5120]{1,0:T(8,128)S(1)}, f32[8,5120]{1,0:T(8,128)S(1)}, u32[]{:S(2)}, u32[]{:S(2)}) collective-permute-start(f32[8,5120]{1,0:T(8,128)S(1)} %pad_maximum_fusion.3), channel_id=1, source_target_pairs={{1,0},{2,1},{3,2},{4,3},{5,4},{6,5},{7,6},{8,7},{9,8},{10,9},{11,1... | collective-permute-start | bytes 491528 | tf_op jit(solution)/shard_map/ppermute | solution.py:21
  87.3 4.1 %collective-permute-done.6.below_ref = f32[8,5120]{1,0:T(8,128)S(1)} collective-permute-done((f32[8,5120]{1,0:T(8,128)S(1)}, f32[8,5120]{1,0:T(8,128)S(1)}, u32[]{:S(2)}, u32[]{:S(2)}) %collective-permute-start.6) | collective-permute-done | bytes 163872 | tf_op jit(solution)/shard_map/ppermute | solution.py:21
  91.5 6.2 %shard_map.95 = (f32[2,2,8,5120]{3,2,1,0:T(8,128)S(1)}, f32[2,2,8,5120]{3,2,1,0:T(8,128)S(1)}, f32[8,16,5120]{2,1,0:T(8,128)}, f32[16,5120]{1,0:T(8,128)S(1)}, f...) custom-call(f32[2,9]{1,0:T(2,128)S(1)} %pad_maximum_fusion.8.scal_ref, ...), custom_call_target="tpu_custom_call" | custom-call | flops 13107200 | bytes 10158080 | tf_op jit(solution)/shard_map/pallas_call | solution.py:105
  101.4 4.5 %all-to-all-start.1 = ((f32[8,16,5120]{2,1,0:T(8,128)}), f32[8,16,5120]{2,1,0:T(8,128)}, u32[]{:S(2)}, u32[]{:S(2)}) async-start(f32[8,16,5120]{2,1,0:T(8,128)} %get-tuple-element.20), calls=%async_computation.1 | async-start | bytes 5242880 | tf_op jit(solution)/shard_map/all_to_all | solution.py:182
  106.0 4.9 %collective-permute-start.9 = (f32[16,5120]{1,0:T(8,128)S(1)}, f32[16,5120]{1,0:T(8,128)S(1)}, u32[]{:S(2)}, u32[]{:S(2)}) collective-permute-start(f32[16,5120]{1,0:T(8,128)S(1)} %copy-done.15), channel_id=1, source_target_pairs={{0,16},{16,32},{32,48},{48,64},{64,80},{80,96},{96,112},{1,17},{17... | collective-permute-start | bytes 983048 | tf_op jit(solution)/shard_map/ppermute | solution.py:21
  112.2 34.5 %collective-permute-done.9.prevf_ref = f32[16,5120]{1,0:T(8,128)S(1)} collective-permute-done((f32[16,5120]{1,0:T(8,128)S(1)}, f32[16,5120]{1,0:T(8,128)S(1)}, u32[]{:S(2)}, u32[]{:S(2)}) %collective-permute-start.9) | collective-permute-done | bytes 327712 | tf_op jit(solution)/shard_map/ppermute | solution.py:21
  146.9 4.2 %slice.140 = f32[8,2,5120]{2,1,0:T(2,128)S(1)} slice(f32[8,16,5120]{2,1,0:T(8,128)} %all-to-all-done.1.part_ref), slice={[0:8:1], [0:16:8], [0:5120:1]} | slice | bytes 655360 | tf_op jit(solution)/shard_map/slice | solution.py:183
  151.3 1.9 collective-permute-start.11
  153.2 5.8 %collective-permute-start.7 = (f32[4,5120]{1,0:T(4,128)S(1)}, f32[4,5120]{1,0:T(4,128)S(1)}, u32[]{:S(2)}, u32[]{:S(2)}) collective-permute-start(f32[4,5120]{1,0:T(4,128)S(1)} %copy-done.17), channel_id=1, source_target_pairs={{0,1},{1,2},{2,3},{3,4},{4,5},{5,6},{6,7},{7,8},{8,9},{9,10},{10,1... | collective-permute-start | bytes 245768 | tf_op jit(solution)/shard_map/ppermute | solution.py:21
  159.0 1.9 collective-permute-start.8
  160.9 5.9 %collective-permute-done.8.down_ref = f32[4,5120]{1,0:T(4,128)S(1)} collective-permute-done((f32[4,5120]{1,0:T(4,128)S(1)}, f32[4,5120]{1,0:T(4,128)S(1)}, u32[]{:S(2)}, u32[]{:S(2)}) %collective-permute-start.8) | collective-permute-done | bytes 81952 | tf_op jit(solution)/shard_map/ppermute | solution.py:21
  167.8 6.1 %shard_map.96 = (f32[2,2,8,5120]{3,2,1,0:T(8,128)S(1)}, f32[2,2,8,5120]{3,2,1,0:T(8,128)S(1)}, f32[8,16,5120]{2,1,0:T(8,128)}, f32[16,5120]{1,0:T(8,128)S(1)}, f...) custom-call(f32[2,9]{1,0:T(2,128)S(1)} %pad_maximum_fusion.8.scal_ref, ...), custom_call_target="tpu_custom_call" | custom-call | flops 13107200 | bytes 10158080 | tf_op jit(solution)/shard_map/pallas_call | solution.py:105
  175.3 7.9 %all-to-all-start.2 = ((f32[8,16,5120]{2,1,0:T(8,128)}), f32[8,16,5120]{2,1,0:T(8,128)}, u32[]{:S(2)}, u32[]{:S(2)}) async-start(f32[8,16,5120]{2,1,0:T(8,128)} %get-tuple-element.27), calls=%async_computation.2 | async-start | bytes 5242880 | tf_op jit(solution)/shard_map/all_to_all | solution.py:182
  183.2 5.6 %collective-permute-start.14 = (f32[16,5120]{1,0:T(8,128)}, f32[16,5120]{1,0:T(8,128)}, u32[]{:S(2)}, u32[]{:S(2)}) collective-permute-start(f32[16,5120]{1,0:T(8,128)} %copy-done.13), channel_id=1, source_target_pairs={{0,16},{16,32},{32,48},{48,64},{64,80},{80,96},{96,112},{1,17},{17... | collective-permute-start | bytes 983048 | tf_op jit(solution)/shard_map/ppermute | solution.py:21
  190.1 31.9 %collective-permute-done.14.prevf_ref = f32[16,5120]{1,0:T(8,128)} collective-permute-done((f32[16,5120]{1,0:T(8,128)}, f32[16,5120]{1,0:T(8,128)}, u32[]{:S(2)}, u32[]{:S(2)}) %collective-permute-start.14) | collective-permute-done | bytes 327712 | tf_op jit(solution)/shard_map/ppermute | solution.py:21
  224.1 5.4 %slice.143 = f32[8,2,5120]{2,1,0:T(2,128)} slice(f32[8,16,5120]{2,1,0:T(8,128)} %all-to-all-done.2.part_ref), slice={[0:8:1], [0:16:8], [0:5120:1]} | slice | bytes 655360 | tf_op jit(solution)/shard_map/slice | solution.py:183
  230.3 1.9 collective-permute-start.16
  232.2 5.8 %collective-permute-start.12 = (f32[4,5120]{1,0:T(4,128)S(1)}, f32[4,5120]{1,0:T(4,128)S(1)}, u32[]{:S(2)}, u32[]{:S(2)}) collective-permute-start(f32[4,5120]{1,0:T(4,128)S(1)} %get-tuple-element.28), channel_id=1, source_target_pairs={{0,1},{1,2},{2,3},{3,4},{4,5},{5,6},{6,7},{7,8},{8,9},{9,10},{10,1... | collective-permute-start | bytes 245768 | tf_op jit(solution)/shard_map/ppermute | solution.py:21
  238.0 1.9 collective-permute-start.13
  239.9 5.9 %collective-permute-done.13.down_ref = f32[4,5120]{1,0:T(4,128)S(1)} collective-permute-done((f32[4,5120]{1,0:T(4,128)S(1)}, f32[4,5120]{1,0:T(4,128)S(1)}, u32[]{:S(2)}, u32[]{:S(2)}) %collective-permute-start.13) | collective-permute-done | bytes 81952 | tf_op jit(solution)/shard_map/ppermute | solution.py:21
  245.9 6.3 %shard_map.97 = (f32[2,2,8,5120]{3,2,1,0:T(8,128)}, f32[2,2,8,5120]{3,2,1,0:T(8,128)}, f32[8,16,5120]{2,1,0:T(8,128)}, f32[16,5120]{1,0:T(8,128)}, f32[16,5120]{...) custom-call(f32[2,9]{1,0:T(2,128)S(1)} %pad_maximum_fusion.8.scal_ref, s32[8]{0:T(128)S(1)} %broadcast_clamp_fusion.sel_ref, ...), custom_call_target="tpu_custom_call" | custom-call | flops 13107200 | bytes 10158080 | tf_op jit(solution)/shard_map/pallas_call | solution.py:105
  (98 shorter events, 26.8 us)
Async XLA Ops:
  0.6 18.8 %copy-start.2 = (f32[2,2,8,5120]{3,2,1,0:T(8,128)S(1)}, f32[2,2,8,5120]{3,2,1,0:T(8,128)}, u32[]{:S(2)}) copy-start(f32[2,2,8,5120]{3,2,1,0:T(8,128)} %x_ref.1) | copy-start | bytes 1966084
  0.6 9.0 %copy-start.18 = (s32[2,8,5120]{2,1,0:T(8,128)S(1)}, s32[2,8,5120]{2,1,0:T(8,128)}, u32[]{:S(2)}) copy-start(s32[2,8,5120]{2,1,0:T(8,128)} %param.11) | copy-start | bytes 983044
  3.3 84.1 %collective-permute-start.2 = (f32[4,5120]{1,0:T(4,128)}, f32[4,5120]{1,0:T(4,128)S(1)}, u32[]{:S(2)}, u32[]{:S(2)}) collective-permute-start(f32[4,5120]{1,0:T(4,128)} %reshape_squeeze.8), channel_id=1, source_target_pairs={{0,1},{1,2},{2,3},{3,4},{4,5},{5,6},{6,7},{7,8},{8,9},{9,10},{10,1... | collective-permute-start | bytes 245768 | tf_op jit(solution)/shard_map/ppermute | solution.py:21
  9.7 17.8 %copy-start.22 = (s32[16]{0:T(128)S(1)}, s32[16]{0:T(128)}, u32[]{:S(2)}) copy-start(s32[16]{0:T(128)} %param.15) | copy-start | bytes 196
  15.0 28.1 %collective-permute-start = (f32[2,2,1,5120]{3,2,1,0:T(1,128)S(1)}, f32[2,2,1,5120]{3,2,1,0:T(1,128)S(1)}, u32[]{:S(2)}, u32[]{:S(2)}) collective-permute-start(f32[2,2,1,5120]{3,2,1,0:T(1,128)S(1)} %get-tuple-element.40), channel_id=1, source_target_pairs={{0,1},{1,2},{2,3},{3,4},{4,5},{5,6},{6,7},{7,8},{8,9},{9,10},{10,1... | collective-permute-start | bytes 245768 | tf_op jit(solution)/shard_map/ppermute | solution.py:21
  17.0 29.3 %collective-permute-start.1 = (f32[2,2,1,5120]{3,2,1,0:T(1,128)S(1)}, f32[2,2,1,5120]{3,2,1,0:T(1,128)S(1)}, u32[]{:S(2)}, u32[]{:S(2)}) collective-permute-start(f32[2,2,1,5120]{3,2,1,0:T(1,128)S(1)} %get-tuple-element.41), channel_id=1, source_target_pairs={{1,0},{2,1},{3,2},{4,3},{5,4},{6,5},{7,6},{8,7},{9,8},{10,9},{11,1... | collective-permute-start | bytes 245768 | tf_op jit(solution)/shard_map/ppermute | solution.py:21
  20.3 27.3 %collective-permute-start.4 = (f32[16,5120]{1,0:T(8,128)}, f32[16,5120]{1,0:T(8,128)}, u32[]{:S(2)}, u32[]{:S(2)}) collective-permute-start(f32[16,5120]{1,0:T(8,128)} %get-tuple-element.36), channel_id=1, source_target_pairs={{0,16},{16,32},{32,48},{48,64},{64,80},{80,96},{96,112},{1,17},{17... | collective-permute-start | bytes 983048 | tf_op jit(solution)/shard_map/ppermute | solution.py:21
  26.2 23.0 %collective-permute-start.5 = (f32[16,5120]{1,0:T(8,128)}, f32[16,5120]{1,0:T(8,128)}, u32[]{:S(2)}, u32[]{:S(2)}) collective-permute-start(f32[16,5120]{1,0:T(8,128)} %get-tuple-element.37), channel_id=1, source_target_pairs={{16,0},{32,16},{48,32},{64,48},{80,64},{96,80},{112,96},{17,1},{33... | collective-permute-start | bytes 983048 | tf_op jit(solution)/shard_map/ppermute | solution.py:21
  30.6 10.3 %copy-start.20 = (f32[2,3]{1,0:T(2,128)S(1)}, f32[2,3]{1,0:T(2,128)}, u32[]{:S(2)}) copy-start(f32[2,3]{1,0:T(2,128)} %param.14) | copy-start | bytes 76
  30.6 10.3 %copy-start.21 = (f32[2,3,2]{1,2,0:T(2,128)S(1)}, f32[2,3,2]{1,2,0:T(2,128)}, u32[]{:S(2)}) copy-start(f32[2,3,2]{1,2,0:T(2,128)} %param.13) | copy-start | bytes 148
  30.6 45.0 %all-to-all-start = ((f32[8,16,5120]{2,1,0:T(8,128)}), f32[8,16,5120]{2,1,0:T(8,128)}, u32[]{:S(2)}, u32[]{:S(2)}) async-start(f32[8,16,5120]{2,1,0:T(8,128)} %broadcast_select_fusion), calls=%async_computation | async-start | bytes 5242880 | tf_op jit(solution)/shard_map/all_to_all | solution.py:182
  43.2 44.2 %collective-permute-start.3 = (f32[4,5120]{1,0:T(4,128)}, f32[4,5120]{1,0:T(4,128)S(1)}, u32[]{:S(2)}, u32[]{:S(2)}) collective-permute-start(f32[4,5120]{1,0:T(4,128)} %reshape_squeeze.9), channel_id=1, source_target_pairs={{1,0},{2,1},{3,2},{4,3},{5,4},{6,5},{7,6},{8,7},{9,8},{10,9},{11,1... | collective-permute-start | bytes 245768 | tf_op jit(solution)/shard_map/ppermute | solution.py:21
  47.4 44.1 %copy-start.3 = (f32[2,2,8,5120]{3,2,1,0:T(8,128)S(1)}, f32[2,2,8,5120]{3,2,1,0:T(8,128)}, u32[]{:S(2)}) copy-start(f32[2,2,8,5120]{3,2,1,0:T(8,128)} %v_ref.1) | copy-start | bytes 1966084
  82.7 8.7 %collective-permute-start.6 = (f32[8,5120]{1,0:T(8,128)S(1)}, f32[8,5120]{1,0:T(8,128)S(1)}, u32[]{:S(2)}, u32[]{:S(2)}) collective-permute-start(f32[8,5120]{1,0:T(8,128)S(1)} %pad_maximum_fusion.3), channel_id=1, source_target_pairs={{1,0},{2,1},{3,2},{4,3},{5,4},{6,5},{7,6},{8,7},{9,8},{10,9},{11,1... | collective-permute-start | bytes 491528 | tf_op jit(solution)/shard_map/ppermute | solution.py:21
  101.4 9.4 %copy-start.12 = (f32[16,5120]{1,0:T(8,128)S(1)}, f32[16,5120]{1,0:T(8,128)}, u32[]{:S(2)}) copy-start(f32[16,5120]{1,0:T(8,128)} %copy-done.11) | copy-start | bytes 983044
  101.4 51.8 %copy-start.17 = (f32[4,5120]{1,0:T(4,128)S(1)}, f32[4,5120]{1,0:T(4,128)}, u32[]{:S(2)}) copy-start(f32[4,5120]{1,0:T(4,128)} %copy-done.16) | copy-start | bytes 245764
  101.4 45.5 %all-to-all-start.1 = ((f32[8,16,5120]{2,1,0:T(8,128)}), f32[8,16,5120]{2,1,0:T(8,128)}, u32[]{:S(2)}, u32[]{:S(2)}) async-start(f32[8,16,5120]{2,1,0:T(8,128)} %get-tuple-element.20), calls=%async_computation.1 | async-start | bytes 5242880 | tf_op jit(solution)/shard_map/all_to_all | solution.py:182
  105.9 60.9 %copy-start.5 = (f32[2,2,8,5120]{3,2,1,0:T(8,128)S(1)}, f32[2,2,8,5120]{3,2,1,0:T(8,128)}, u32[]{:S(2)}) copy-start(f32[2,2,8,5120]{3,2,1,0:T(8,128)} %copy-done.4) | copy-start | bytes 1966084
  105.9 60.9 %copy-start.7 = (f32[2,2,8,5120]{3,2,1,0:T(8,128)S(1)}, f32[2,2,8,5120]{3,2,1,0:T(8,128)}, u32[]{:S(2)}) copy-start(f32[2,2,8,5120]{3,2,1,0:T(8,128)} %copy-done.6) | copy-start | bytes 1966084
  106.0 40.7 %collective-permute-start.9 = (f32[16,5120]{1,0:T(8,128)S(1)}, f32[16,5120]{1,0:T(8,128)S(1)}, u32[]{:S(2)}, u32[]{:S(2)}) collective-permute-start(f32[16,5120]{1,0:T(8,128)S(1)} %copy-done.15), channel_id=1, source_target_pairs={{0,16},{16,32},{32,48},{48,64},{64,80},{80,96},{96,112},{1,17},{17... | collective-permute-start | bytes 983048 | tf_op jit(solution)/shard_map/ppermute | solution.py:21
  110.9 35.9 %collective-permute-start.10 = (f32[16,5120]{1,0:T(8,128)S(1)}, f32[16,5120]{1,0:T(8,128)S(1)}, u32[]{:S(2)}, u32[]{:S(2)}) collective-permute-start(f32[16,5120]{1,0:T(8,128)S(1)} %copy-done.12), channel_id=1, source_target_pairs={{16,0},{32,16},{48,32},{64,48},{80,64},{96,80},{112,96},{17,1},{33... | collective-permute-start | bytes 983048 | tf_op jit(solution)/shard_map/ppermute | solution.py:21
  146.8 20.1 %copy-start.8 = (f32[16,5120]{1,0:T(8,128)}, f32[16,5120]{1,0:T(8,128)S(1)}, u32[]{:S(2)}) copy-start(f32[16,5120]{1,0:T(8,128)S(1)} %collective-permute-done.10.nextf_ref) | copy-start | bytes 983044
  151.3 15.6 %collective-permute-start.11 = (f32[8,5120]{1,0:T(8,128)S(1)}, f32[8,5120]{1,0:T(8,128)S(1)}, u32[]{:S(2)}, u32[]{:S(2)}) collective-permute-start(f32[8,5120]{1,0:T(8,128)S(1)} %pad_maximum_fusion.4), channel_id=1, source_target_pairs={{1,0},{2,1},{3,2},{4,3},{5,4},{6,5},{7,6},{8,7},{9,8},{10,9},{11,1... | collective-permute-start | bytes 491528 | tf_op jit(solution)/shard_map/ppermute | solution.py:21
  153.2 7.7 %collective-permute-start.7 = (f32[4,5120]{1,0:T(4,128)S(1)}, f32[4,5120]{1,0:T(4,128)S(1)}, u32[]{:S(2)}, u32[]{:S(2)}) collective-permute-start(f32[4,5120]{1,0:T(4,128)S(1)} %copy-done.17), channel_id=1, source_target_pairs={{0,1},{1,2},{2,3},{3,4},{4,5},{5,6},{6,7},{7,8},{8,9},{9,10},{10,1... | collective-permute-start | bytes 245768 | tf_op jit(solution)/shard_map/ppermute | solution.py:21
  159.0 7.9 %collective-permute-start.8 = (f32[4,5120]{1,0:T(4,128)S(1)}, f32[4,5120]{1,0:T(4,128)S(1)}, u32[]{:S(2)}, u32[]{:S(2)}) collective-permute-start(f32[4,5120]{1,0:T(4,128)S(1)} %get-tuple-element.22), channel_id=1, source_target_pairs={{1,0},{2,1},{3,2},{4,3},{5,4},{6,5},{7,6},{8,7},{9,8},{10,9},{11,1... | collective-permute-start | bytes 245768 | tf_op jit(solution)/shard_map/ppermute | solution.py:21
  175.3 70.5 %copy-start.1 = (f32[5,2,8,5120]{3,2,1,0:T(8,128)S(1)}, f32[5,2,8,5120]{3,2,1,0:T(8,128)}, u32[]{:S(2)}) copy-start(f32[5,2,8,5120]{3,2,1,0:T(8,128)} %copy-done) | copy-start | bytes 4915204
  175.3 48.7 %all-to-all-start.2 = ((f32[8,16,5120]{2,1,0:T(8,128)}), f32[8,16,5120]{2,1,0:T(8,128)}, u32[]{:S(2)}, u32[]{:S(2)}) async-start(f32[8,16,5120]{2,1,0:T(8,128)} %get-tuple-element.27), calls=%async_computation.2 | async-start | bytes 5242880 | tf_op jit(solution)/shard_map/all_to_all | solution.py:182
  183.2 38.7 %collective-permute-start.14 = (f32[16,5120]{1,0:T(8,128)}, f32[16,5120]{1,0:T(8,128)}, u32[]{:S(2)}, u32[]{:S(2)}) collective-permute-start(f32[16,5120]{1,0:T(8,128)} %copy-done.13), channel_id=1, source_target_pairs={{0,16},{16,32},{32,48},{48,64},{64,80},{80,96},{96,112},{1,17},{17... | collective-permute-start | bytes 983048 | tf_op jit(solution)/shard_map/ppermute | solution.py:21
  188.8 34.2 %collective-permute-start.15 = (f32[16,5120]{1,0:T(8,128)}, f32[16,5120]{1,0:T(8,128)}, u32[]{:S(2)}, u32[]{:S(2)}) collective-permute-start(f32[16,5120]{1,0:T(8,128)} %copy-done.10), channel_id=1, source_target_pairs={{16,0},{32,16},{48,32},{64,48},{80,64},{96,80},{112,96},{17,1},{33... | collective-permute-start | bytes 983048 | tf_op jit(solution)/shard_map/ppermute | solution.py:21
  230.3 15.6 %collective-permute-start.16 = (f32[8,5120]{1,0:T(8,128)S(1)}, f32[8,5120]{1,0:T(8,128)S(1)}, u32[]{:S(2)}, u32[]{:S(2)}) collective-permute-start(f32[8,5120]{1,0:T(8,128)S(1)} %pad_maximum_fusion.5), channel_id=1, source_target_pairs={{1,0},{2,1},{3,2},{4,3},{5,4},{6,5},{7,6},{8,7},{9,8},{10,9},{11,1... | collective-permute-start | bytes 491528 | tf_op jit(solution)/shard_map/ppermute | solution.py:21
  232.2 7.7 %collective-permute-start.12 = (f32[4,5120]{1,0:T(4,128)S(1)}, f32[4,5120]{1,0:T(4,128)S(1)}, u32[]{:S(2)}, u32[]{:S(2)}) collective-permute-start(f32[4,5120]{1,0:T(4,128)S(1)} %get-tuple-element.28), channel_id=1, source_target_pairs={{0,1},{1,2},{2,3},{3,4},{4,5},{5,6},{6,7},{7,8},{8,9},{9,10},{10,1... | collective-permute-start | bytes 245768 | tf_op jit(solution)/shard_map/ppermute | solution.py:21
  238.0 7.9 %collective-permute-start.13 = (f32[4,5120]{1,0:T(4,128)S(1)}, f32[4,5120]{1,0:T(4,128)S(1)}, u32[]{:S(2)}, u32[]{:S(2)}) collective-permute-start(f32[4,5120]{1,0:T(4,128)S(1)} %get-tuple-element.29), channel_id=1, source_target_pairs={{1,0},{2,1},{3,2},{4,3},{5,4},{6,5},{7,6},{8,7},{9,8},{10,9},{11,1... | collective-permute-start | bytes 245768 | tf_op jit(solution)/shard_map/ppermute | solution.py:21
  (11 other events, 23.9 us)

commit v7 on v6

--- a/solution.py
+++ b/solution.py
@@ -29,7 +29,7 @@
     return jnp.concatenate([jnp.zeros_like(field[..., :1]), field[..., :-1]], axis=-1)
 
 
-def update_kernel(scal_ref, sel_ref, src_ref, x_ref, v_ref, k_ref, alive_ref, part_ref, up_ref, down_ref,
+def update_kernel(scal_ref, sel_ref, x_ref, v_ref, k_ref, alive_ref, part_ref, up_ref, down_ref,
                   prevf_ref, nextf_ref, below_ref, xo_ref, vo_ref, send_ref, lastf_ref, firstf_ref,
                   top_ref, bot_ref):
     L, ncomp, R, C = x_ref.shape
@@ -78,9 +78,7 @@
             part_row = below_ref[pl.ds((2 + l) * ncomp + c, 1), :]
             pull = scal_ref[l, 0] * (warp_of(prev_src, prev_row, ws[0]) - x)
             pull = pull + scal_ref[l, 1] * (warp_of(next_src, next_row, ws[1]) - x)
-            pull = pull + scal_ref[l, 2] * (
-                warp_of(part_ref[src_ref[l], pl.ds(c * R, R), :], part_row, ws[2]) - x
-            )
+            pull = pull + scal_ref[l, 2] * (warp_of(part_ref[l, pl.ds(c * R, R), :], part_row, ws[2]) - x)
             force = inplane + pull
             vel = alive * (DAMPING * v_ref[l, c] + STEP * force)
             vo_ref[l, c] = vel
@@ -97,7 +95,7 @@
             send_ref[d, pl.ds(c * R, R), :] = xo_ref[sel_ref[d], c]
 
 
-def update(scal, sel, src, x, v, kst, alive, part, up, down, prevf, nextf, below):
+def update(scal, sel, x, v, kst, alive, part, up, down, prevf, nextf, below):
     nb = sel.shape[0]
     vmem = pl.BlockSpec(memory_space=pltpu.VMEM)
     smem = pl.BlockSpec(memory_space=pltpu.SMEM)
@@ -113,11 +111,11 @@
             jax.ShapeDtypeStruct((x.shape[0] * x.shape[1], x.shape[3]), x.dtype),
             jax.ShapeDtypeStruct((x.shape[0] * x.shape[1], x.shape[3]), x.dtype),
         ),
-        in_specs=[smem, smem, smem] + [vmem] * 10,
+        in_specs=[smem, smem] + [vmem] * 10,
         out_specs=[vmem] * 7,
         compiler_params=pltpu.CompilerParams(vmem_limit_bytes=48 * 1024 * 1024),
         cost_estimate=pl.CostEstimate(flops=80 * x.size, bytes_accessed=moved, transcendentals=0),
-    )(scal, sel, src, x, v, kst, alive, part, up, down, prevf, nextf, below)
+    )(scal, sel, x, v, kst, alive, part, up, down, prevf, nextf, below)
 
 
 def body(disp, vel, stiff_class, valid, class_table, warp, spring_z, skip_partner):
@@ -150,8 +148,6 @@
     wanted = skip_partner.reshape(block_count, local_count)
     hit = (wanted // local_count) == block_index
     send_sel = jnp.sum(jnp.where(hit, wanted % local_count, 0), axis=1)
-    send_sel = jnp.clip(send_sel, 0, local_count - 1)
-    src_block = jnp.clip(src_block, 0, block_count - 1)
 
     k_mid = kap_ext[:, 1:-1]
     kst = jnp.stack([kap_ext[:, :-2], k_mid, kap_ext[:, 2:], shift_right(k_mid), shift_left(k_mid)])
@@ -180,28 +176,27 @@
     bot_rows = field[:, :, -1].reshape(local_count * ncomp, cols)
     for _ in range(ITERS):
       recv = lax.all_to_all(send, "gz", 0, 0, tiled=True)
-      heads = recv[:, :: disp.shape[2]]
-      partner_heads = jnp.stack(
-          [lax.dynamic_index_in_dim(heads, src_block[l], 0, keepdims=False) for l in range(local_count)]
+      partner8 = jnp.stack(
+          [lax.dynamic_index_in_dim(recv, src_block[l], 0, keepdims=False) for l in range(local_count)]
       )
       prev_face = shift_rows(last_face, "gz", True)
       next_face = shift_rows(first_face, "gz", False)
       up = shift_rows(bot_rows, "tile", True)
       down = shift_rows(top_rows, "tile", False)
       rows = disp.shape[2]
+      heads = [prev_face, next_face] + [partner8[l] for l in range(local_count)]
       firsts = jnp.concatenate(
-          [prev_face[::rows], next_face[::rows]] + [partner_heads[l] for l in range(local_count)], axis=0
+          [h[c * rows : c * rows + 1] for h in heads for c in range(ncomp)], axis=0
       )
       below = shift_rows(firsts, "tile", False)
       field, velocity, send, last_face, first_face, top_rows, bot_rows = update(
           scal,
           send_sel,
-          src_block,
           field,
           velocity,
           kst,
           alive_mid,
-          recv,
+          partner8,
           up,
           down,
           prev_face,

time: 256 us -> 236 us (0.922)
  the two profiles are of different devices: /device:TPU:25 before, /device:TPU:97 now
where the time goes in v7:
time: 236 us; the launch traced here: 235 us
  waiting for transfers between devices  104 us (44%)
  starting transfers between devices  70.1 us (30%)
  local copies, waits for them, and re-layouts  28.9 us (12%)
  Pallas kernels  16 us (7%)
  other arithmetic  10.9 us (5%)
  between operations  4.75 us (2%)
    ppermute x17, waiting for transfers between devices, shift_rows(): return lax.ppermute(block, axis, pairs)  87.8 us
    ppermute x17, starting transfers between devices, shift_rows(): return lax.ppermute(block, axis, pairs)  48.1 us
    all_to_all x3, starting transfers between devices, body(): recv = lax.all_to_all(send, 'gz', 0, 0, tiled=True)  22 us
    all_to_all x3, waiting for transfers between devices, body(): recv = lax.all_to_all(send, 'gz', 0, 0, tiled=True)  16.4 us
    pallas_call x3, Pallas kernels, update(): pl.pallas_call(update_kernel, out_shape=(jax.ShapeDtypeStruct(x.shape, x....  16 us
    slice x9, local copies, waits for them, and re-layouts, body(): h[c * rows:c * rows + 1]  9.56 us
    another operation x1, other arithmetic, body(): stiff = jnp.stack([kappa, alive])  6.28 us
    unnamed x45, local copies, waits for them, and re-layouts  5.56 us
  transfers between devices with their start and end apart: 20, of which 8 were waited for; matrix products, arithmetic and copies ran while one was open for 14% of the time, Pallas kernels for 0%

profile of v7, /device:TPU:97, one launch (start us, length us, event | category | flops | bytes accessed | tf_op | source)
XLA Modules:
  0.0 234.8 jit_solution(9988721257394903760)
XLA Ops:
  3.2 3.8 %collective-permute-start.2 = (f32[4,5120]{1,0:T(4,128)}, f32[4,5120]{1,0:T(4,128)S(1)}, u32[]{:S(2)}, u32[]{:S(2)}) collective-permute-start(f32[4,5120]{1,0:T(4,128)} %reshape_squeeze.8), channel_id=1, source_target_pairs={{0,1},{1,2},{2,3},{3,4},{4,5},{5,6},{6,7},{7,8},{8,9},{9,10},{10,1... | collective-permute-start | bytes 245768 | tf_op jit(solution)/shard_map/ppermute | solution.py:21
  9.6 6.3 %multiply_bitcast_fusion = f32[1,2,8,5120]{3,2,1,0:T(8,128)S(1)} fusion(s32[2,8,5120]{2,1,0:T(8,128)} %param.10, f32[]{:T(128)} %bitcast.7, f32[]{:T(128)} %bitcast.6, f32[]{:T(128)} %bitcast.5, f32[]{:T(128)} %bitcast.4, f32[]{:T(128)} %bitcast.3, f32[]{:T(128)} %bitcast.2, f32[]{:T(128)} %bitcast.1, f32[]{:T(128)} %bitcast, s32[2,8,5120]{2,1,0:T(8,128)} %param.11), kind=kLoop, calls=%fused_computation.18 | loop fusion | flops 1474560 | bytes 983072 | tf_op jit(solution)/shard_map/stack | solution.py:131
  16.0 1.9 collective-permute-start
  17.9 2.4 %collective-permute-start.1 = (f32[2,2,1,5120]{3,2,1,0:T(1,128)S(1)}, f32[2,2,1,5120]{3,2,1,0:T(1,128)S(1)}, u32[]{:S(2)}, u32[]{:S(2)}) collective-permute-start(f32[2,2,1,5120]{3,2,1,0:T(1,128)S(1)} %get-tuple-element.59), channel_id=1, source_target_pairs={{1,0},{2,1},{3,2},{4,3},{5,4},{6,5},{7,6},{8,7},{9,8},{10,9},{11,1... | collective-permute-start | bytes 245768 | tf_op jit(solution)/shard_map/ppermute | solution.py:21
  21.2 3.1 %collective-permute-start.4 = (f32[16,5120]{1,0:T(8,128)}, f32[16,5120]{1,0:T(8,128)}, u32[]{:S(2)}, u32[]{:S(2)}) collective-permute-start(f32[16,5120]{1,0:T(8,128)} %get-tuple-element.54), channel_id=1, source_target_pairs={{0,16},{16,32},{32,48},{48,64},{64,80},{80,96},{96,112},{1,17},{17... | collective-permute-start | bytes 983048 | tf_op jit(solution)/shard_map/ppermute | solution.py:21
  24.4 4.4 %collective-permute-start.5 = (f32[16,5120]{1,0:T(8,128)}, f32[16,5120]{1,0:T(8,128)}, u32[]{:S(2)}, u32[]{:S(2)}) collective-permute-start(f32[16,5120]{1,0:T(8,128)} %get-tuple-element.55), channel_id=1, source_target_pairs={{16,0},{32,16},{48,32},{64,48},{80,64},{96,80},{112,96},{17,1},{33... | collective-permute-start | bytes 983048 | tf_op jit(solution)/shard_map/ppermute | solution.py:21
  29.0 2.9 %broadcast_select_fusion = f32[8,16,5120]{2,1,0:T(8,128)} fusion(f32[16,5120]{1,0:T(8,128)} %get-tuple-element.55, f32[16,5120]{1,0:T(8,128)} %get-tuple-element.54, pred[8]{0:T(512)(128)(4,1)S(1)} %broadcast_compare_fusion), kind=kLoop, calls=%fused_computation | loop fusion | flops 655360 | bytes 3276808 | tf_op jit(solution)/shard_map/jit(_where)/select_n | solution.py:170
  31.9 6.6 %all-to-all-start = ((f32[8,16,5120]{2,1,0:T(8,128)}), f32[8,16,5120]{2,1,0:T(8,128)}, u32[]{:S(2)}, u32[]{:S(2)}) async-start(f32[8,16,5120]{2,1,0:T(8,128)} %broadcast_select_fusion), calls=%async_computation | async-start | bytes 5242880 | tf_op jit(solution)/shard_map/all_to_all | solution.py:178
  43.9 5.2 %collective-permute-start.3 = (f32[4,5120]{1,0:T(4,128)}, f32[4,5120]{1,0:T(4,128)S(1)}, u32[]{:S(2)}, u32[]{:S(2)}) collective-permute-start(f32[4,5120]{1,0:T(4,128)} %reshape_squeeze.9), channel_id=1, source_target_pairs={{1,0},{2,1},{3,2},{4,3},{5,4},{6,5},{7,6},{8,7},{9,8},{10,9},{11,1... | collective-permute-start | bytes 245768 | tf_op jit(solution)/shard_map/ppermute | solution.py:21
  52.2 16.4 %all-to-all-done = f32[8,16,5120]{2,1,0:T(8,128)} async-done(((f32[8,16,5120]{2,1,0:T(8,128)}), f32[8,16,5120]{2,1,0:T(8,128)}, u32[]{:S(2)}, u32[]{:S(2)}) %all-to-all-start) | async-done | bytes 2621472 | tf_op jit(solution)/shard_map/all_to_all | solution.py:178
  72.1 5.7 %collective-permute-start.6 = (f32[8,5120]{1,0:T(8,128)}, f32[8,5120]{1,0:T(8,128)S(1)}, u32[]{:S(2)}, u32[]{:S(2)}) collective-permute-start(f32[8,5120]{1,0:T(8,128)} %concatenate.25), channel_id=1, source_target_pairs={{1,0},{2,1},{3,2},{4,3},{5,4},{6,5},{7,6},{8,7},{9,8},{10,9},{11,1... | collective-permute-start | bytes 491528 | tf_op jit(solution)/shard_map/ppermute | solution.py:21
  79.0 7.5 %collective-permute-done.6.below_ref = f32[8,5120]{1,0:T(8,128)S(1)} collective-permute-done((f32[8,5120]{1,0:T(8,128)}, f32[8,5120]{1,0:T(8,128)S(1)}, u32[]{:S(2)}, u32[]{:S(2)}) %collective-permute-start.6) | collective-permute-done | bytes 163872 | tf_op jit(solution)/shard_map/ppermute | solution.py:21
  86.5 5.5 %shard_map.95 = (f32[2,2,8,5120]{3,2,1,0:T(8,128)S(1)}, f32[2,2,8,5120]{3,2,1,0:T(8,128)S(1)}, f32[8,16,5120]{2,1,0:T(8,128)}, f32[16,5120]{1,0:T(8,128)}, f32[1...) custom-call(f32[2,9]{1,0:T(2,128)S(1)} %pad_maximum_fusion.8.scal_ref, s32[8]{0:T(128)S(1)} %fusion.6.sel_ref, ...), custom_call_target="tpu_custom_call" | custom-call | flops 13107200 | bytes 8192000 | tf_op jit(solution)/shard_map/pallas_call | solution.py:103
  96.9 7.4 %all-to-all-start.1 = ((f32[8,16,5120]{2,1,0:T(8,128)}), f32[8,16,5120]{2,1,0:T(8,128)}, u32[]{:S(2)}, u32[]{:S(2)}) async-start(f32[8,16,5120]{2,1,0:T(8,128)} %get-tuple-element.20), calls=%async_computation.1 | async-start | bytes 5242880 | tf_op jit(solution)/shard_map/all_to_all | solution.py:178
  104.3 2.5 %collective-permute-start.7 = (f32[4,5120]{1,0:T(4,128)S(1)}, f32[4,5120]{1,0:T(4,128)S(1)}, u32[]{:S(2)}, u32[]{:S(2)}) collective-permute-start(f32[4,5120]{1,0:T(4,128)S(1)} %copy-done.16), channel_id=1, source_target_pairs={{0,1},{1,2},{2,3},{3,4},{4,5},{5,6},{6,7},{7,8},{8,9},{9,10},{10,1... | collective-permute-start | bytes 245768 | tf_op jit(solution)/shard_map/ppermute | solution.py:21
  106.9 1.9 collective-permute-start.8
  108.8 2.1 collective-permute-start.10
  110.9 11.6 %collective-permute-done.9.prevf_ref = f32[16,5120]{1,0:T(8,128)S(1)} collective-permute-done((f32[16,5120]{1,0:T(8,128)}, f32[16,5120]{1,0:T(8,128)S(1)}, u32[]{:S(2)}, u32[]{:S(2)}) %collective-permute-start.9) | collective-permute-done | bytes 327712 | tf_op jit(solution)/shard_map/ppermute | solution.py:21
  122.5 25.6 %collective-permute-done.10.nextf_ref = f32[16,5120]{1,0:T(8,128)S(1)} collective-permute-done((f32[16,5120]{1,0:T(8,128)S(1)}, f32[16,5120]{1,0:T(8,128)S(1)}, u32[]{:S(2)}, u32[]{:S(2)}) %collective-permute-start.10) | collective-permute-done | bytes 327712 | tf_op jit(solution)/shard_map/ppermute | solution.py:21
  150.3 2.4 %collective-permute-start.11 = (f32[8,5120]{1,0:T(8,128)S(1)}, f32[8,5120]{1,0:T(8,128)S(1)}, u32[]{:S(2)}, u32[]{:S(2)}) collective-permute-start(f32[8,5120]{1,0:T(8,128)S(1)} %concatenate.26), channel_id=1, source_target_pairs={{1,0},{2,1},{3,2},{4,3},{5,4},{6,5},{7,6},{8,7},{9,8},{10,9},{11,1... | collective-permute-start | bytes 491528 | tf_op jit(solution)/shard_map/ppermute | solution.py:21
  153.8 3.2 %collective-permute-done.11.below_ref = f32[8,5120]{1,0:T(8,128)S(1)} collective-permute-done((f32[8,5120]{1,0:T(8,128)S(1)}, f32[8,5120]{1,0:T(8,128)S(1)}, u32[]{:S(2)}, u32[]{:S(2)}) %collective-permute-start.11) | collective-permute-done | bytes 163872 | tf_op jit(solution)/shard_map/ppermute | solution.py:21
  157.0 5.2 %shard_map.96 = (f32[2,2,8,5120]{3,2,1,0:T(8,128)S(1)}, f32[2,2,8,5120]{3,2,1,0:T(8,128)S(1)}, f32[8,16,5120]{2,1,0:T(8,128)}, f32[16,5120]{1,0:T(8,128)}, f32[1...) custom-call(f32[2,9]{1,0:T(2,128)S(1)} %pad_maximum_fusion.8.scal_ref, s32[8]{0:T(128)S(1)} %fusion.6.sel_ref, ...), custom_call_target="tpu_custom_call" | custom-call | flops 13107200 | bytes 8192000 | tf_op jit(solution)/shard_map/pallas_call | solution.py:103
  163.0 1.9 collective-permute-start.14
  164.9 7.9 %all-to-all-start.2 = ((f32[8,16,5120]{2,1,0:T(8,128)}), f32[8,16,5120]{2,1,0:T(8,128)}, u32[]{:S(2)}, u32[]{:S(2)}) async-start(f32[8,16,5120]{2,1,0:T(8,128)} %get-tuple-element.27), calls=%async_computation.2 | async-start | bytes 5242880 | tf_op jit(solution)/shard_map/all_to_all | solution.py:178
  172.9 2.4 %collective-permute-start.12 = (f32[4,5120]{1,0:T(4,128)}, f32[4,5120]{1,0:T(4,128)S(1)}, u32[]{:S(2)}, u32[]{:S(2)}) collective-permute-start(f32[4,5120]{1,0:T(4,128)} %get-tuple-element.28), channel_id=1, source_target_pairs={{0,1},{1,2},{2,3},{3,4},{4,5},{5,6},{6,7},{7,8},{8,9},{9,10},{10,1... | collective-permute-start | bytes 245768 | tf_op jit(solution)/shard_map/ppermute | solution.py:21
  175.3 2.0 collective-permute-start.13
  177.3 2.1 collective-permute-start.15
  179.4 11.1 %collective-permute-done.14.prevf_ref = f32[16,5120]{1,0:T(8,128)} collective-permute-done((f32[16,5120]{1,0:T(8,128)}, f32[16,5120]{1,0:T(8,128)}, u32[]{:S(2)}, u32[]{:S(2)}) %collective-permute-start.14) | collective-permute-done | bytes 327712 | tf_op jit(solution)/shard_map/ppermute | solution.py:21
  192.1 25.5 %collective-permute-done.15.nextf_ref = f32[16,5120]{1,0:T(8,128)S(1)} collective-permute-done((f32[16,5120]{1,0:T(8,128)}, f32[16,5120]{1,0:T(8,128)S(1)}, u32[]{:S(2)}, u32[]{:S(2)}) %collective-permute-start.15) | collective-permute-done | bytes 327712 | tf_op jit(solution)/shard_map/ppermute | solution.py:21
  222.5 2.4 %collective-permute-start.16 = (f32[8,5120]{1,0:T(8,128)}, f32[8,5120]{1,0:T(8,128)S(1)}, u32[]{:S(2)}, u32[]{:S(2)}) collective-permute-start(f32[8,5120]{1,0:T(8,128)} %concatenate.27), channel_id=1, source_target_pairs={{1,0},{2,1},{3,2},{4,3},{5,4},{6,5},{7,6},{8,7},{9,8},{10,9},{11,1... | collective-permute-start | bytes 491528 | tf_op jit(solution)/shard_map/ppermute | solution.py:21
  226.2 3.3 %collective-permute-done.16.below_ref = f32[8,5120]{1,0:T(8,128)S(1)} collective-permute-done((f32[8,5120]{1,0:T(8,128)}, f32[8,5120]{1,0:T(8,128)S(1)}, u32[]{:S(2)}, u32[]{:S(2)}) %collective-permute-start.16) | collective-permute-done | bytes 163872 | tf_op jit(solution)/shard_map/ppermute | solution.py:21
  229.5 5.3 %shard_map.97 = (f32[2,2,8,5120]{3,2,1,0:T(8,128)}, f32[2,2,8,5120]{3,2,1,0:T(8,128)}, f32[8,16,5120]{2,1,0:T(8,128)}, f32[16,5120]{1,0:T(8,128)}, f32[16,5120]{...) custom-call(f32[2,9]{1,0:T(2,128)S(1)} %pad_maximum_fusion.8.scal_ref, s32[8]{0:T(128)S(1)} %fusion.6.sel_ref, ...), custom_call_target="tpu_custom_call" | custom-call | flops 13107200 | bytes 8192000 | tf_op jit(solution)/shard_map/pallas_call | solution.py:103
  (94 shorter events, 32.5 us)
Async XLA Ops:
  0.6 19.7 %copy-start.2 = (f32[2,2,8,5120]{3,2,1,0:T(8,128)S(1)}, f32[2,2,8,5120]{3,2,1,0:T(8,128)}, u32[]{:S(2)}) copy-start(f32[2,2,8,5120]{3,2,1,0:T(8,128)} %x_ref.1) | copy-start | bytes 1966084
  0.6 28.1 %copy-start.19 = (s32[16]{0:T(128)S(1)}, s32[16]{0:T(128)}, u32[]{:S(2)}) copy-start(s32[16]{0:T(128)} %param.15) | copy-start | bytes 196
  3.2 75.8 %collective-permute-start.2 = (f32[4,5120]{1,0:T(4,128)}, f32[4,5120]{1,0:T(4,128)S(1)}, u32[]{:S(2)}, u32[]{:S(2)}) collective-permute-start(f32[4,5120]{1,0:T(4,128)} %reshape_squeeze.8), channel_id=1, source_target_pairs={{0,1},{1,2},{2,3},{3,4},{4,5},{5,6},{6,7},{7,8},{8,9},{9,10},{10,1... | collective-permute-start | bytes 245768 | tf_op jit(solution)/shard_map/ppermute | solution.py:21
  16.0 27.9 %collective-permute-start = (f32[2,2,1,5120]{3,2,1,0:T(1,128)S(1)}, f32[2,2,1,5120]{3,2,1,0:T(1,128)S(1)}, u32[]{:S(2)}, u32[]{:S(2)}) collective-permute-start(f32[2,2,1,5120]{3,2,1,0:T(1,128)S(1)} %get-tuple-element.58), channel_id=1, source_target_pairs={{0,1},{1,2},{2,3},{3,4},{4,5},{5,6},{6,7},{7,8},{8,9},{9,10},{10,1... | collective-permute-start | bytes 245768 | tf_op jit(solution)/shard_map/ppermute | solution.py:21
  17.9 31.2 %collective-permute-start.1 = (f32[2,2,1,5120]{3,2,1,0:T(1,128)S(1)}, f32[2,2,1,5120]{3,2,1,0:T(1,128)S(1)}, u32[]{:S(2)}, u32[]{:S(2)}) collective-permute-start(f32[2,2,1,5120]{3,2,1,0:T(1,128)S(1)} %get-tuple-element.59), channel_id=1, source_target_pairs={{1,0},{2,1},{3,2},{4,3},{5,4},{6,5},{7,6},{8,7},{9,8},{10,9},{11,1... | collective-permute-start | bytes 245768 | tf_op jit(solution)/shard_map/ppermute | solution.py:21
  21.2 28.5 %collective-permute-start.4 = (f32[16,5120]{1,0:T(8,128)}, f32[16,5120]{1,0:T(8,128)}, u32[]{:S(2)}, u32[]{:S(2)}) collective-permute-start(f32[16,5120]{1,0:T(8,128)} %get-tuple-element.54), channel_id=1, source_target_pairs={{0,16},{16,32},{32,48},{48,64},{64,80},{80,96},{96,112},{1,17},{17... | collective-permute-start | bytes 983048 | tf_op jit(solution)/shard_map/ppermute | solution.py:21
  24.4 26.8 %collective-permute-start.5 = (f32[16,5120]{1,0:T(8,128)}, f32[16,5120]{1,0:T(8,128)}, u32[]{:S(2)}, u32[]{:S(2)}) collective-permute-start(f32[16,5120]{1,0:T(8,128)} %get-tuple-element.55), channel_id=1, source_target_pairs={{16,0},{32,16},{48,32},{64,48},{80,64},{96,80},{112,96},{17,1},{33... | collective-permute-start | bytes 983048 | tf_op jit(solution)/shard_map/ppermute | solution.py:21
  31.9 9.8 %copy-start.17 = (f32[2,3]{1,0:T(2,128)S(1)}, f32[2,3]{1,0:T(2,128)}, u32[]{:S(2)}) copy-start(f32[2,3]{1,0:T(2,128)} %param.14) | copy-start | bytes 76
  31.9 9.9 %copy-start.18 = (f32[2,3,2]{1,2,0:T(2,128)S(1)}, f32[2,3,2]{1,2,0:T(2,128)}, u32[]{:S(2)}) copy-start(f32[2,3,2]{1,2,0:T(2,128)} %param.13) | copy-start | bytes 148
  31.9 36.8 %all-to-all-start = ((f32[8,16,5120]{2,1,0:T(8,128)}), f32[8,16,5120]{2,1,0:T(8,128)}, u32[]{:S(2)}, u32[]{:S(2)}) async-start(f32[8,16,5120]{2,1,0:T(8,128)} %broadcast_select_fusion), calls=%async_computation | async-start | bytes 5242880 | tf_op jit(solution)/shard_map/all_to_all | solution.py:178
  43.9 35.1 %collective-permute-start.3 = (f32[4,5120]{1,0:T(4,128)}, f32[4,5120]{1,0:T(4,128)S(1)}, u32[]{:S(2)}, u32[]{:S(2)}) collective-permute-start(f32[4,5120]{1,0:T(4,128)} %reshape_squeeze.9), channel_id=1, source_target_pairs={{1,0},{2,1},{3,2},{4,3},{5,4},{6,5},{7,6},{8,7},{9,8},{10,9},{11,1... | collective-permute-start | bytes 245768 | tf_op jit(solution)/shard_map/ppermute | solution.py:21
  49.5 37.0 %copy-start.3 = (f32[2,2,8,5120]{3,2,1,0:T(8,128)S(1)}, f32[2,2,8,5120]{3,2,1,0:T(8,128)}, u32[]{:S(2)}) copy-start(f32[2,2,8,5120]{3,2,1,0:T(8,128)} %v_ref.1) | copy-start | bytes 1966084
  49.7 36.8 %copy-start = (f32[5,2,8,5120]{3,2,1,0:T(8,128)}, f32[5,2,8,5120]{3,2,1,0:T(8,128)S(1)}, u32[]{:S(2)}) copy-start(f32[5,2,8,5120]{3,2,1,0:T(8,128)S(1)} %bitcast_dynamic-update-slice_fusion.k_ref) | copy-start | bytes 4915204
  72.1 14.4 %collective-permute-start.6 = (f32[8,5120]{1,0:T(8,128)}, f32[8,5120]{1,0:T(8,128)S(1)}, u32[]{:S(2)}, u32[]{:S(2)}) collective-permute-start(f32[8,5120]{1,0:T(8,128)} %concatenate.25), channel_id=1, source_target_pairs={{1,0},{2,1},{3,2},{4,3},{5,4},{6,5},{7,6},{8,7},{9,8},{10,9},{11,1... | collective-permute-start | bytes 491528 | tf_op jit(solution)/shard_map/ppermute | solution.py:21
  95.0 27.5 %collective-permute-start.9 = (f32[16,5120]{1,0:T(8,128)}, f32[16,5120]{1,0:T(8,128)S(1)}, u32[]{:S(2)}, u32[]{:S(2)}) collective-permute-start(f32[16,5120]{1,0:T(8,128)} %get-tuple-element.23), channel_id=1, source_target_pairs={{0,16},{16,32},{32,48},{48,64},{64,80},{80,96},{96,112},{1,17},{17... | collective-permute-start | bytes 983048 | tf_op jit(solution)/shard_map/ppermute | solution.py:21
  96.9 7.4 %copy-start.16 = (f32[4,5120]{1,0:T(4,128)S(1)}, f32[4,5120]{1,0:T(4,128)}, u32[]{:S(2)}) copy-start(f32[4,5120]{1,0:T(4,128)} %copy-done.15) | copy-start | bytes 245764
  96.9 11.9 %copy-start.14 = (f32[16,5120]{1,0:T(8,128)S(1)}, f32[16,5120]{1,0:T(8,128)}, u32[]{:S(2)}) copy-start(f32[16,5120]{1,0:T(8,128)} %copy-done.13) | copy-start | bytes 983044
  96.9 51.9 %all-to-all-start.1 = ((f32[8,16,5120]{2,1,0:T(8,128)}), f32[8,16,5120]{2,1,0:T(8,128)}, u32[]{:S(2)}, u32[]{:S(2)}) async-start(f32[8,16,5120]{2,1,0:T(8,128)} %get-tuple-element.20), calls=%async_computation.1 | async-start | bytes 5242880 | tf_op jit(solution)/shard_map/all_to_all | solution.py:178
  104.3 52.7 %copy-start.5 = (f32[2,2,8,5120]{3,2,1,0:T(8,128)S(1)}, f32[2,2,8,5120]{3,2,1,0:T(8,128)}, u32[]{:S(2)}) copy-start(f32[2,2,8,5120]{3,2,1,0:T(8,128)} %copy-done.4) | copy-start | bytes 1966084
  104.3 52.7 %copy-start.7 = (f32[2,2,8,5120]{3,2,1,0:T(8,128)S(1)}, f32[2,2,8,5120]{3,2,1,0:T(8,128)}, u32[]{:S(2)}) copy-start(f32[2,2,8,5120]{3,2,1,0:T(8,128)} %copy-done.6) | copy-start | bytes 1966084
  104.3 49.5 %collective-permute-start.7 = (f32[4,5120]{1,0:T(4,128)S(1)}, f32[4,5120]{1,0:T(4,128)S(1)}, u32[]{:S(2)}, u32[]{:S(2)}) collective-permute-start(f32[4,5120]{1,0:T(4,128)S(1)} %copy-done.16), channel_id=1, source_target_pairs={{0,1},{1,2},{2,3},{3,4},{4,5},{5,6},{6,7},{7,8},{8,9},{9,10},{10,1... | collective-permute-start | bytes 245768 | tf_op jit(solution)/shard_map/ppermute | solution.py:21
  106.9 47.0 %collective-permute-start.8 = (f32[4,5120]{1,0:T(4,128)S(1)}, f32[4,5120]{1,0:T(4,128)S(1)}, u32[]{:S(2)}, u32[]{:S(2)}) collective-permute-start(f32[4,5120]{1,0:T(4,128)S(1)} %get-tuple-element.22), channel_id=1, source_target_pairs={{1,0},{2,1},{3,2},{4,3},{5,4},{6,5},{7,6},{8,7},{9,8},{10,9},{11,1... | collective-permute-start | bytes 245768 | tf_op jit(solution)/shard_map/ppermute | solution.py:21
  108.8 39.2 %collective-permute-start.10 = (f32[16,5120]{1,0:T(8,128)S(1)}, f32[16,5120]{1,0:T(8,128)S(1)}, u32[]{:S(2)}, u32[]{:S(2)}) collective-permute-start(f32[16,5120]{1,0:T(8,128)S(1)} %copy-done.14), channel_id=1, source_target_pairs={{16,0},{32,16},{48,32},{64,48},{80,64},{96,80},{112,96},{17,1},{33... | collective-permute-start | bytes 983048 | tf_op jit(solution)/shard_map/ppermute | solution.py:21
  150.3 6.8 %collective-permute-start.11 = (f32[8,5120]{1,0:T(8,128)S(1)}, f32[8,5120]{1,0:T(8,128)S(1)}, u32[]{:S(2)}, u32[]{:S(2)}) collective-permute-start(f32[8,5120]{1,0:T(8,128)S(1)} %concatenate.26), channel_id=1, source_target_pairs={{1,0},{2,1},{3,2},{4,3},{5,4},{6,5},{7,6},{8,7},{9,8},{10,9},{11,1... | collective-permute-start | bytes 491528 | tf_op jit(solution)/shard_map/ppermute | solution.py:21
  163.0 27.5 %collective-permute-start.14 = (f32[16,5120]{1,0:T(8,128)}, f32[16,5120]{1,0:T(8,128)}, u32[]{:S(2)}, u32[]{:S(2)}) collective-permute-start(f32[16,5120]{1,0:T(8,128)} %get-tuple-element.30), channel_id=1, source_target_pairs={{0,16},{16,32},{32,48},{48,64},{64,80},{80,96},{96,112},{1,17},{17... | collective-permute-start | bytes 983048 | tf_op jit(solution)/shard_map/ppermute | solution.py:21
  164.9 54.1 %all-to-all-start.2 = ((f32[8,16,5120]{2,1,0:T(8,128)}), f32[8,16,5120]{2,1,0:T(8,128)}, u32[]{:S(2)}, u32[]{:S(2)}) async-start(f32[8,16,5120]{2,1,0:T(8,128)} %get-tuple-element.27), calls=%async_computation.2 | async-start | bytes 5242880 | tf_op jit(solution)/shard_map/all_to_all | solution.py:178
  172.9 56.7 %copy-start.1 = (f32[5,2,8,5120]{3,2,1,0:T(8,128)S(1)}, f32[5,2,8,5120]{3,2,1,0:T(8,128)}, u32[]{:S(2)}) copy-start(f32[5,2,8,5120]{3,2,1,0:T(8,128)} %copy-done) | copy-start | bytes 4915204
  172.9 53.3 %collective-permute-start.12 = (f32[4,5120]{1,0:T(4,128)}, f32[4,5120]{1,0:T(4,128)S(1)}, u32[]{:S(2)}, u32[]{:S(2)}) collective-permute-start(f32[4,5120]{1,0:T(4,128)} %get-tuple-element.28), channel_id=1, source_target_pairs={{0,1},{1,2},{2,3},{3,4},{4,5},{5,6},{6,7},{7,8},{8,9},{9,10},{10,1... | collective-permute-start | bytes 245768 | tf_op jit(solution)/shard_map/ppermute | solution.py:21
  175.3 50.9 %collective-permute-start.13 = (f32[4,5120]{1,0:T(4,128)S(1)}, f32[4,5120]{1,0:T(4,128)S(1)}, u32[]{:S(2)}, u32[]{:S(2)}) collective-permute-start(f32[4,5120]{1,0:T(4,128)S(1)} %get-tuple-element.29), channel_id=1, source_target_pairs={{1,0},{2,1},{3,2},{4,3},{5,4},{6,5},{7,6},{8,7},{9,8},{10,9},{11,1... | collective-permute-start | bytes 245768 | tf_op jit(solution)/shard_map/ppermute | solution.py:21
  177.3 40.3 %collective-permute-start.15 = (f32[16,5120]{1,0:T(8,128)}, f32[16,5120]{1,0:T(8,128)S(1)}, u32[]{:S(2)}, u32[]{:S(2)}) collective-permute-start(f32[16,5120]{1,0:T(8,128)} %copy-done.12), channel_id=1, source_target_pairs={{16,0},{32,16},{48,32},{64,48},{80,64},{96,80},{112,96},{17,1},{33... | collective-permute-start | bytes 983048 | tf_op jit(solution)/shard_map/ppermute | solution.py:21
  222.5 7.0 %copy-start.9 = (f32[16,5120]{1,0:T(8,128)S(1)}, f32[16,5120]{1,0:T(8,128)}, u32[]{:S(2)}) copy-start(f32[16,5120]{1,0:T(8,128)} %copy-done.8) | copy-start | bytes 983044
  222.5 7.0 %collective-permute-start.16 = (f32[8,5120]{1,0:T(8,128)}, f32[8,5120]{1,0:T(8,128)S(1)}, u32[]{:S(2)}, u32[]{:S(2)}) collective-permute-start(f32[8,5120]{1,0:T(8,128)} %concatenate.27), channel_id=1, source_target_pairs={{1,0},{2,1},{3,2},{4,3},{5,4},{6,5},{7,6},{8,7},{9,8},{10,9},{11,1... | collective-permute-start | bytes 491528 | tf_op jit(solution)/shard_map/ppermute | solution.py:21
  (8 other events, 12.0 us)

commit v8 on v7

--- a/solution.py
+++ b/solution.py
@@ -184,10 +184,14 @@
       up = shift_rows(bot_rows, "tile", True)
       down = shift_rows(top_rows, "tile", False)
       rows = disp.shape[2]
-      heads = [prev_face, next_face] + [partner8[l] for l in range(local_count)]
-      firsts = jnp.concatenate(
-          [h[c * rows : c * rows + 1] for h in heads for c in range(ncomp)], axis=0
-      )
+      heads = [prev_face[c * rows : c * rows + 1] for c in range(ncomp)]
+      heads += [next_face[c * rows : c * rows + 1] for c in range(ncomp)]
+      heads += [
+          lax.dynamic_slice(recv, (src_block[l], c * rows, 0), (1, 1, cols))[0]
+          for l in range(local_count)
+          for c in range(ncomp)
+      ]
+      firsts = jnp.concatenate(heads, axis=0)
       below = shift_rows(firsts, "tile", False)
       field, velocity, send, last_face, first_face, top_rows, bot_rows = update(
           scal,

time: 236 us -> 236 us (level)
    slice x9 -> x6, local copies, waits for them, and re-layouts: 9.56 us -> 4.75 us  [the longest x3 3.06 us: body(): heads = [prev_face[c * rows:c * rows + 1] for c in range(ncomp)]]
    squeeze x0 -> x3, local copies, waits for them, and re-layouts: none -> 4.81 us  [body(): lax.dynamic_slice(recv, (src_block[l], c * rows, 0), (1, 1, cols))[0]]
where the time goes in v8:
time: 236 us; the launch traced here: 235 us
  waiting for transfers between devices  104 us (44%)
  starting transfers between devices  70.1 us (30%)
  local copies, waits for them, and re-layouts  28.9 us (12%)
  Pallas kernels  16 us (7%)
  other arithmetic  10.9 us (5%)
  between operations  4.75 us (2%)
    ppermute x17, waiting for transfers between devices, shift_rows(): return lax.ppermute(block, axis, pairs)  87.8 us
    ppermute x17, starting transfers between devices, shift_rows(): return lax.ppermute(block, axis, pairs)  48.1 us
    all_to_all x3, starting transfers between devices, body(): recv = lax.all_to_all(send, 'gz', 0, 0, tiled=True)  22 us
    all_to_all x3, waiting for transfers between devices, body(): recv = lax.all_to_all(send, 'gz', 0, 0, tiled=True)  16.4 us
    pallas_call x3, Pallas kernels, update(): pl.pallas_call(update_kernel, out_shape=(jax.ShapeDtypeStruct(x.shape, x....  16 us
    another operation x1, other arithmetic, body(): stiff = jnp.stack([kappa, alive])  6.28 us
    unnamed x45, local copies, waits for them, and re-layouts  5.56 us
    squeeze x3, local copies, waits for them, and re-layouts, body(): lax.dynamic_slice(recv, (src_block[l], c * rows, 0), (1, 1, cols))[0]  4.81 us
  transfers between devices with their start and end apart: 20, of which 8 were waited for; matrix products, arithmetic and copies ran while one was open for 14% of the time, Pallas kernels for 0%

profile of v8, /device:TPU:97, one launch (start us, length us, event | category | flops | bytes accessed | tf_op | source)
XLA Modules:
  0.0 234.8 jit_solution(4826237222631539008)
XLA Ops:
  3.2 3.8 %collective-permute-start.2 = (f32[4,5120]{1,0:T(4,128)}, f32[4,5120]{1,0:T(4,128)S(1)}, u32[]{:S(2)}, u32[]{:S(2)}) collective-permute-start(f32[4,5120]{1,0:T(4,128)} %reshape_squeeze.8), channel_id=1, source_target_pairs={{0,1},{1,2},{2,3},{3,4},{4,5},{5,6},{6,7},{7,8},{8,9},{9,10},{10,1... | collective-permute-start | bytes 245768 | tf_op jit(solution)/shard_map/ppermute | solution.py:21
  9.6 6.3 %multiply_bitcast_fusion = f32[1,2,8,5120]{3,2,1,0:T(8,128)S(1)} fusion(s32[2,8,5120]{2,1,0:T(8,128)} %param.10, f32[]{:T(128)} %bitcast.7, f32[]{:T(128)} %bitcast.6, f32[]{:T(128)} %bitcast.5, f32[]{:T(128)} %bitcast.4, f32[]{:T(128)} %bitcast.3, f32[]{:T(128)} %bitcast.2, f32[]{:T(128)} %bitcast.1, f32[]{:T(128)} %bitcast, s32[2,8,5120]{2,1,0:T(8,128)} %param.11), kind=kLoop, calls=%fused_computation.18 | loop fusion | flops 1474560 | bytes 983072 | tf_op jit(solution)/shard_map/stack | solution.py:131
  16.0 1.9 collective-permute-start
  17.9 2.4 %collective-permute-start.1 = (f32[2,2,1,5120]{3,2,1,0:T(1,128)S(1)}, f32[2,2,1,5120]{3,2,1,0:T(1,128)S(1)}, u32[]{:S(2)}, u32[]{:S(2)}) collective-permute-start(f32[2,2,1,5120]{3,2,1,0:T(1,128)S(1)} %get-tuple-element.59), channel_id=1, source_target_pairs={{1,0},{2,1},{3,2},{4,3},{5,4},{6,5},{7,6},{8,7},{9,8},{10,9},{11,1... | collective-permute-start | bytes 245768 | tf_op jit(solution)/shard_map/ppermute | solution.py:21
  21.2 3.1 %collective-permute-start.4 = (f32[16,5120]{1,0:T(8,128)}, f32[16,5120]{1,0:T(8,128)}, u32[]{:S(2)}, u32[]{:S(2)}) collective-permute-start(f32[16,5120]{1,0:T(8,128)} %get-tuple-element.54), channel_id=1, source_target_pairs={{0,16},{16,32},{32,48},{48,64},{64,80},{80,96},{96,112},{1,17},{17... | collective-permute-start | bytes 983048 | tf_op jit(solution)/shard_map/ppermute | solution.py:21
  24.4 4.4 %collective-permute-start.5 = (f32[16,5120]{1,0:T(8,128)}, f32[16,5120]{1,0:T(8,128)}, u32[]{:S(2)}, u32[]{:S(2)}) collective-permute-start(f32[16,5120]{1,0:T(8,128)} %get-tuple-element.55), channel_id=1, source_target_pairs={{16,0},{32,16},{48,32},{64,48},{80,64},{96,80},{112,96},{17,1},{33... | collective-permute-start | bytes 983048 | tf_op jit(solution)/shard_map/ppermute | solution.py:21
  29.0 2.9 %broadcast_select_fusion = f32[8,16,5120]{2,1,0:T(8,128)} fusion(f32[16,5120]{1,0:T(8,128)} %get-tuple-element.55, f32[16,5120]{1,0:T(8,128)} %get-tuple-element.54, pred[8]{0:T(512)(128)(4,1)S(1)} %broadcast_compare_fusion), kind=kLoop, calls=%fused_computation | loop fusion | flops 655360 | bytes 3276808 | tf_op jit(solution)/shard_map/jit(_where)/select_n | solution.py:170
  31.9 6.6 %all-to-all-start = ((f32[8,16,5120]{2,1,0:T(8,128)}), f32[8,16,5120]{2,1,0:T(8,128)}, u32[]{:S(2)}, u32[]{:S(2)}) async-start(f32[8,16,5120]{2,1,0:T(8,128)} %broadcast_select_fusion), calls=%async_computation | async-start | bytes 5242880 | tf_op jit(solution)/shard_map/all_to_all | solution.py:178
  43.9 5.2 %collective-permute-start.3 = (f32[4,5120]{1,0:T(4,128)}, f32[4,5120]{1,0:T(4,128)S(1)}, u32[]{:S(2)}, u32[]{:S(2)}) collective-permute-start(f32[4,5120]{1,0:T(4,128)} %reshape_squeeze.9), channel_id=1, source_target_pairs={{1,0},{2,1},{3,2},{4,3},{5,4},{6,5},{7,6},{8,7},{9,8},{10,9},{11,1... | collective-permute-start | bytes 245768 | tf_op jit(solution)/shard_map/ppermute | solution.py:21
  52.2 16.4 %all-to-all-done = f32[8,16,5120]{2,1,0:T(8,128)} async-done(((f32[8,16,5120]{2,1,0:T(8,128)}), f32[8,16,5120]{2,1,0:T(8,128)}, u32[]{:S(2)}, u32[]{:S(2)}) %all-to-all-start) | async-done | bytes 2621472 | tf_op jit(solution)/shard_map/all_to_all | solution.py:178
  72.1 5.7 %collective-permute-start.6 = (f32[8,5120]{1,0:T(8,128)}, f32[8,5120]{1,0:T(8,128)S(1)}, u32[]{:S(2)}, u32[]{:S(2)}) collective-permute-start(f32[8,5120]{1,0:T(8,128)} %concatenate.25), channel_id=1, source_target_pairs={{1,0},{2,1},{3,2},{4,3},{5,4},{6,5},{7,6},{8,7},{9,8},{10,9},{11,1... | collective-permute-start | bytes 491528 | tf_op jit(solution)/shard_map/ppermute | solution.py:21
  79.0 7.5 %collective-permute-done.6.below_ref = f32[8,5120]{1,0:T(8,128)S(1)} collective-permute-done((f32[8,5120]{1,0:T(8,128)}, f32[8,5120]{1,0:T(8,128)S(1)}, u32[]{:S(2)}, u32[]{:S(2)}) %collective-permute-start.6) | collective-permute-done | bytes 163872 | tf_op jit(solution)/shard_map/ppermute | solution.py:21
  86.5 5.5 %shard_map.95 = (f32[2,2,8,5120]{3,2,1,0:T(8,128)S(1)}, f32[2,2,8,5120]{3,2,1,0:T(8,128)S(1)}, f32[8,16,5120]{2,1,0:T(8,128)}, f32[16,5120]{1,0:T(8,128)}, f32[1...) custom-call(f32[2,9]{1,0:T(2,128)S(1)} %pad_maximum_fusion.8.scal_ref, s32[8]{0:T(128)S(1)} %fusion.6.sel_ref, ...), custom_call_target="tpu_custom_call" | custom-call | flops 13107200 | bytes 8192000 | tf_op jit(solution)/shard_map/pallas_call | solution.py:103
  96.9 7.4 %all-to-all-start.1 = ((f32[8,16,5120]{2,1,0:T(8,128)}), f32[8,16,5120]{2,1,0:T(8,128)}, u32[]{:S(2)}, u32[]{:S(2)}) async-start(f32[8,16,5120]{2,1,0:T(8,128)} %get-tuple-element.20), calls=%async_computation.1 | async-start | bytes 5242880 | tf_op jit(solution)/shard_map/all_to_all | solution.py:178
  104.3 2.5 %collective-permute-start.7 = (f32[4,5120]{1,0:T(4,128)S(1)}, f32[4,5120]{1,0:T(4,128)S(1)}, u32[]{:S(2)}, u32[]{:S(2)}) collective-permute-start(f32[4,5120]{1,0:T(4,128)S(1)} %copy-done.16), channel_id=1, source_target_pairs={{0,1},{1,2},{2,3},{3,4},{4,5},{5,6},{6,7},{7,8},{8,9},{9,10},{10,1... | collective-permute-start | bytes 245768 | tf_op jit(solution)/shard_map/ppermute | solution.py:21
  106.9 1.9 collective-permute-start.8
  108.8 2.1 collective-permute-start.10
  110.9 11.6 %collective-permute-done.9.prevf_ref = f32[16,5120]{1,0:T(8,128)S(1)} collective-permute-done((f32[16,5120]{1,0:T(8,128)}, f32[16,5120]{1,0:T(8,128)S(1)}, u32[]{:S(2)}, u32[]{:S(2)}) %collective-permute-start.9) | collective-permute-done | bytes 327712 | tf_op jit(solution)/shard_map/ppermute | solution.py:21
  122.5 25.6 %collective-permute-done.10.nextf_ref = f32[16,5120]{1,0:T(8,128)S(1)} collective-permute-done((f32[16,5120]{1,0:T(8,128)S(1)}, f32[16,5120]{1,0:T(8,128)S(1)}, u32[]{:S(2)}, u32[]{:S(2)}) %collective-permute-start.10) | collective-permute-done | bytes 327712 | tf_op jit(solution)/shard_map/ppermute | solution.py:21
  150.3 2.4 %collective-permute-start.11 = (f32[8,5120]{1,0:T(8,128)S(1)}, f32[8,5120]{1,0:T(8,128)S(1)}, u32[]{:S(2)}, u32[]{:S(2)}) collective-permute-start(f32[8,5120]{1,0:T(8,128)S(1)} %concatenate.26), channel_id=1, source_target_pairs={{1,0},{2,1},{3,2},{4,3},{5,4},{6,5},{7,6},{8,7},{9,8},{10,9},{11,1... | collective-permute-start | bytes 491528 | tf_op jit(solution)/shard_map/ppermute | solution.py:21
  153.8 3.2 %collective-permute-done.11.below_ref = f32[8,5120]{1,0:T(8,128)S(1)} collective-permute-done((f32[8,5120]{1,0:T(8,128)S(1)}, f32[8,5120]{1,0:T(8,128)S(1)}, u32[]{:S(2)}, u32[]{:S(2)}) %collective-permute-start.11) | collective-permute-done | bytes 163872 | tf_op jit(solution)/shard_map/ppermute | solution.py:21
  157.0 5.2 %shard_map.96 = (f32[2,2,8,5120]{3,2,1,0:T(8,128)S(1)}, f32[2,2,8,5120]{3,2,1,0:T(8,128)S(1)}, f32[8,16,5120]{2,1,0:T(8,128)}, f32[16,5120]{1,0:T(8,128)}, f32[1...) custom-call(f32[2,9]{1,0:T(2,128)S(1)} %pad_maximum_fusion.8.scal_ref, s32[8]{0:T(128)S(1)} %fusion.6.sel_ref, ...), custom_call_target="tpu_custom_call" | custom-call | flops 13107200 | bytes 8192000 | tf_op jit(solution)/shard_map/pallas_call | solution.py:103
  163.0 1.9 collective-permute-start.14
  164.9 7.9 %all-to-all-start.2 = ((f32[8,16,5120]{2,1,0:T(8,128)}), f32[8,16,5120]{2,1,0:T(8,128)}, u32[]{:S(2)}, u32[]{:S(2)}) async-start(f32[8,16,5120]{2,1,0:T(8,128)} %get-tuple-element.27), calls=%async_computation.2 | async-start | bytes 5242880 | tf_op jit(solution)/shard_map/all_to_all | solution.py:178
  172.9 2.4 %collective-permute-start.12 = (f32[4,5120]{1,0:T(4,128)}, f32[4,5120]{1,0:T(4,128)S(1)}, u32[]{:S(2)}, u32[]{:S(2)}) collective-permute-start(f32[4,5120]{1,0:T(4,128)} %get-tuple-element.28), channel_id=1, source_target_pairs={{0,1},{1,2},{2,3},{3,4},{4,5},{5,6},{6,7},{7,8},{8,9},{9,10},{10,1... | collective-permute-start | bytes 245768 | tf_op jit(solution)/shard_map/ppermute | solution.py:21
  175.3 2.0 collective-permute-start.13
  177.3 2.1 collective-permute-start.15
  179.4 11.1 %collective-permute-done.14.prevf_ref = f32[16,5120]{1,0:T(8,128)} collective-permute-done((f32[16,5120]{1,0:T(8,128)}, f32[16,5120]{1,0:T(8,128)}, u32[]{:S(2)}, u32[]{:S(2)}) %collective-permute-start.14) | collective-permute-done | bytes 327712 | tf_op jit(solution)/shard_map/ppermute | solution.py:21
  192.1 25.5 %collective-permute-done.15.nextf_ref = f32[16,5120]{1,0:T(8,128)S(1)} collective-permute-done((f32[16,5120]{1,0:T(8,128)}, f32[16,5120]{1,0:T(8,128)S(1)}, u32[]{:S(2)}, u32[]{:S(2)}) %collective-permute-start.15) | collective-permute-done | bytes 327712 | tf_op jit(solution)/shard_map/ppermute | solution.py:21
  222.5 2.4 %collective-permute-start.16 = (f32[8,5120]{1,0:T(8,128)}, f32[8,5120]{1,0:T(8,128)S(1)}, u32[]{:S(2)}, u32[]{:S(2)}) collective-permute-start(f32[8,5120]{1,0:T(8,128)} %concatenate.27), channel_id=1, source_target_pairs={{1,0},{2,1},{3,2},{4,3},{5,4},{6,5},{7,6},{8,7},{9,8},{10,9},{11,1... | collective-permute-start | bytes 491528 | tf_op jit(solution)/shard_map/ppermute | solution.py:21
  226.2 3.3 %collective-permute-done.16.below_ref = f32[8,5120]{1,0:T(8,128)S(1)} collective-permute-done((f32[8,5120]{1,0:T(8,128)}, f32[8,5120]{1,0:T(8,128)S(1)}, u32[]{:S(2)}, u32[]{:S(2)}) %collective-permute-start.16) | collective-permute-done | bytes 163872 | tf_op jit(solution)/shard_map/ppermute | solution.py:21
  229.5 5.3 %shard_map.97 = (f32[2,2,8,5120]{3,2,1,0:T(8,128)}, f32[2,2,8,5120]{3,2,1,0:T(8,128)}, f32[8,16,5120]{2,1,0:T(8,128)}, f32[16,5120]{1,0:T(8,128)}, f32[16,5120]{...) custom-call(f32[2,9]{1,0:T(2,128)S(1)} %pad_maximum_fusion.8.scal_ref, s32[8]{0:T(128)S(1)} %fusion.6.sel_ref, ...), custom_call_target="tpu_custom_call" | custom-call | flops 13107200 | bytes 8192000 | tf_op jit(solution)/shard_map/pallas_call | solution.py:103
  (94 shorter events, 32.5 us)
Async XLA Ops:
  0.6 19.7 %copy-start.2 = (f32[2,2,8,5120]{3,2,1,0:T(8,128)S(1)}, f32[2,2,8,5120]{3,2,1,0:T(8,128)}, u32[]{:S(2)}) copy-start(f32[2,2,8,5120]{3,2,1,0:T(8,128)} %x_ref.1) | copy-start | bytes 1966084
  0.6 28.1 %copy-start.19 = (s32[16]{0:T(128)S(1)}, s32[16]{0:T(128)}, u32[]{:S(2)}) copy-start(s32[16]{0:T(128)} %param.15) | copy-start | bytes 196
  3.2 75.8 %collective-permute-start.2 = (f32[4,5120]{1,0:T(4,128)}, f32[4,5120]{1,0:T(4,128)S(1)}, u32[]{:S(2)}, u32[]{:S(2)}) collective-permute-start(f32[4,5120]{1,0:T(4,128)} %reshape_squeeze.8), channel_id=1, source_target_pairs={{0,1},{1,2},{2,3},{3,4},{4,5},{5,6},{6,7},{7,8},{8,9},{9,10},{10,1... | collective-permute-start | bytes 245768 | tf_op jit(solution)/shard_map/ppermute | solution.py:21
  16.0 27.9 %collective-permute-start = (f32[2,2,1,5120]{3,2,1,0:T(1,128)S(1)}, f32[2,2,1,5120]{3,2,1,0:T(1,128)S(1)}, u32[]{:S(2)}, u32[]{:S(2)}) collective-permute-start(f32[2,2,1,5120]{3,2,1,0:T(1,128)S(1)} %get-tuple-element.58), channel_id=1, source_target_pairs={{0,1},{1,2},{2,3},{3,4},{4,5},{5,6},{6,7},{7,8},{8,9},{9,10},{10,1... | collective-permute-start | bytes 245768 | tf_op jit(solution)/shard_map/ppermute | solution.py:21
  17.9 31.2 %collective-permute-start.1 = (f32[2,2,1,5120]{3,2,1,0:T(1,128)S(1)}, f32[2,2,1,5120]{3,2,1,0:T(1,128)S(1)}, u32[]{:S(2)}, u32[]{:S(2)}) collective-permute-start(f32[2,2,1,5120]{3,2,1,0:T(1,128)S(1)} %get-tuple-element.59), channel_id=1, source_target_pairs={{1,0},{2,1},{3,2},{4,3},{5,4},{6,5},{7,6},{8,7},{9,8},{10,9},{11,1... | collective-permute-start | bytes 245768 | tf_op jit(solution)/shard_map/ppermute | solution.py:21
  21.2 28.5 %collective-permute-start.4 = (f32[16,5120]{1,0:T(8,128)}, f32[16,5120]{1,0:T(8,128)}, u32[]{:S(2)}, u32[]{:S(2)}) collective-permute-start(f32[16,5120]{1,0:T(8,128)} %get-tuple-element.54), channel_id=1, source_target_pairs={{0,16},{16,32},{32,48},{48,64},{64,80},{80,96},{96,112},{1,17},{17... | collective-permute-start | bytes 983048 | tf_op jit(solution)/shard_map/ppermute | solution.py:21
  24.4 26.8 %collective-permute-start.5 = (f32[16,5120]{1,0:T(8,128)}, f32[16,5120]{1,0:T(8,128)}, u32[]{:S(2)}, u32[]{:S(2)}) collective-permute-start(f32[16,5120]{1,0:T(8,128)} %get-tuple-element.55), channel_id=1, source_target_pairs={{16,0},{32,16},{48,32},{64,48},{80,64},{96,80},{112,96},{17,1},{33... | collective-permute-start | bytes 983048 | tf_op jit(solution)/shard_map/ppermute | solution.py:21
  31.9 9.8 %copy-start.17 = (f32[2,3]{1,0:T(2,128)S(1)}, f32[2,3]{1,0:T(2,128)}, u32[]{:S(2)}) copy-start(f32[2,3]{1,0:T(2,128)} %param.14) | copy-start | bytes 76
  31.9 9.9 %copy-start.18 = (f32[2,3,2]{1,2,0:T(2,128)S(1)}, f32[2,3,2]{1,2,0:T(2,128)}, u32[]{:S(2)}) copy-start(f32[2,3,2]{1,2,0:T(2,128)} %param.13) | copy-start | bytes 148
  31.9 36.8 %all-to-all-start = ((f32[8,16,5120]{2,1,0:T(8,128)}), f32[8,16,5120]{2,1,0:T(8,128)}, u32[]{:S(2)}, u32[]{:S(2)}) async-start(f32[8,16,5120]{2,1,0:T(8,128)} %broadcast_select_fusion), calls=%async_computation | async-start | bytes 5242880 | tf_op jit(solution)/shard_map/all_to_all | solution.py:178
  43.9 35.1 %collective-permute-start.3 = (f32[4,5120]{1,0:T(4,128)}, f32[4,5120]{1,0:T(4,128)S(1)}, u32[]{:S(2)}, u32[]{:S(2)}) collective-permute-start(f32[4,5120]{1,0:T(4,128)} %reshape_squeeze.9), channel_id=1, source_target_pairs={{1,0},{2,1},{3,2},{4,3},{5,4},{6,5},{7,6},{8,7},{9,8},{10,9},{11,1... | collective-permute-start | bytes 245768 | tf_op jit(solution)/shard_map/ppermute | solution.py:21
  49.5 37.0 %copy-start.3 = (f32[2,2,8,5120]{3,2,1,0:T(8,128)S(1)}, f32[2,2,8,5120]{3,2,1,0:T(8,128)}, u32[]{:S(2)}) copy-start(f32[2,2,8,5120]{3,2,1,0:T(8,128)} %v_ref.1) | copy-start | bytes 1966084
  49.7 36.8 %copy-start = (f32[5,2,8,5120]{3,2,1,0:T(8,128)}, f32[5,2,8,5120]{3,2,1,0:T(8,128)S(1)}, u32[]{:S(2)}) copy-start(f32[5,2,8,5120]{3,2,1,0:T(8,128)S(1)} %bitcast_dynamic-update-slice_fusion.k_ref) | copy-start | bytes 4915204
  72.1 14.4 %collective-permute-start.6 = (f32[8,5120]{1,0:T(8,128)}, f32[8,5120]{1,0:T(8,128)S(1)}, u32[]{:S(2)}, u32[]{:S(2)}) collective-permute-start(f32[8,5120]{1,0:T(8,128)} %concatenate.25), channel_id=1, source_target_pairs={{1,0},{2,1},{3,2},{4,3},{5,4},{6,5},{7,6},{8,7},{9,8},{10,9},{11,1... | collective-permute-start | bytes 491528 | tf_op jit(solution)/shard_map/ppermute | solution.py:21
  95.0 27.5 %collective-permute-start.9 = (f32[16,5120]{1,0:T(8,128)}, f32[16,5120]{1,0:T(8,128)S(1)}, u32[]{:S(2)}, u32[]{:S(2)}) collective-permute-start(f32[16,5120]{1,0:T(8,128)} %get-tuple-element.23), channel_id=1, source_target_pairs={{0,16},{16,32},{32,48},{48,64},{64,80},{80,96},{96,112},{1,17},{17... | collective-permute-start | bytes 983048 | tf_op jit(solution)/shard_map/ppermute | solution.py:21
  96.9 7.4 %copy-start.16 = (f32[4,5120]{1,0:T(4,128)S(1)}, f32[4,5120]{1,0:T(4,128)}, u32[]{:S(2)}) copy-start(f32[4,5120]{1,0:T(4,128)} %copy-done.15) | copy-start | bytes 245764
  96.9 11.9 %copy-start.14 = (f32[16,5120]{1,0:T(8,128)S(1)}, f32[16,5120]{1,0:T(8,128)}, u32[]{:S(2)}) copy-start(f32[16,5120]{1,0:T(8,128)} %copy-done.13) | copy-start | bytes 983044
  96.9 51.9 %all-to-all-start.1 = ((f32[8,16,5120]{2,1,0:T(8,128)}), f32[8,16,5120]{2,1,0:T(8,128)}, u32[]{:S(2)}, u32[]{:S(2)}) async-start(f32[8,16,5120]{2,1,0:T(8,128)} %get-tuple-element.20), calls=%async_computation.1 | async-start | bytes 5242880 | tf_op jit(solution)/shard_map/all_to_all | solution.py:178
  104.3 52.7 %copy-start.5 = (f32[2,2,8,5120]{3,2,1,0:T(8,128)S(1)}, f32[2,2,8,5120]{3,2,1,0:T(8,128)}, u32[]{:S(2)}) copy-start(f32[2,2,8,5120]{3,2,1,0:T(8,128)} %copy-done.4) | copy-start | bytes 1966084
  104.3 52.7 %copy-start.7 = (f32[2,2,8,5120]{3,2,1,0:T(8,128)S(1)}, f32[2,2,8,5120]{3,2,1,0:T(8,128)}, u32[]{:S(2)}) copy-start(f32[2,2,8,5120]{3,2,1,0:T(8,128)} %copy-done.6) | copy-start | bytes 1966084
  104.3 49.5 %collective-permute-start.7 = (f32[4,5120]{1,0:T(4,128)S(1)}, f32[4,5120]{1,0:T(4,128)S(1)}, u32[]{:S(2)}, u32[]{:S(2)}) collective-permute-start(f32[4,5120]{1,0:T(4,128)S(1)} %copy-done.16), channel_id=1, source_target_pairs={{0,1},{1,2},{2,3},{3,4},{4,5},{5,6},{6,7},{7,8},{8,9},{9,10},{10,1... | collective-permute-start | bytes 245768 | tf_op jit(solution)/shard_map/ppermute | solution.py:21
  106.9 47.0 %collective-permute-start.8 = (f32[4,5120]{1,0:T(4,128)S(1)}, f32[4,5120]{1,0:T(4,128)S(1)}, u32[]{:S(2)}, u32[]{:S(2)}) collective-permute-start(f32[4,5120]{1,0:T(4,128)S(1)} %get-tuple-element.22), channel_id=1, source_target_pairs={{1,0},{2,1},{3,2},{4,3},{5,4},{6,5},{7,6},{8,7},{9,8},{10,9},{11,1... | collective-permute-start | bytes 245768 | tf_op jit(solution)/shard_map/ppermute | solution.py:21
  108.8 39.2 %collective-permute-start.10 = (f32[16,5120]{1,0:T(8,128)S(1)}, f32[16,5120]{1,0:T(8,128)S(1)}, u32[]{:S(2)}, u32[]{:S(2)}) collective-permute-start(f32[16,5120]{1,0:T(8,128)S(1)} %copy-done.14), channel_id=1, source_target_pairs={{16,0},{32,16},{48,32},{64,48},{80,64},{96,80},{112,96},{17,1},{33... | collective-permute-start | bytes 983048 | tf_op jit(solution)/shard_map/ppermute | solution.py:21
  150.3 6.8 %collective-permute-start.11 = (f32[8,5120]{1,0:T(8,128)S(1)}, f32[8,5120]{1,0:T(8,128)S(1)}, u32[]{:S(2)}, u32[]{:S(2)}) collective-permute-start(f32[8,5120]{1,0:T(8,128)S(1)} %concatenate.26), channel_id=1, source_target_pairs={{1,0},{2,1},{3,2},{4,3},{5,4},{6,5},{7,6},{8,7},{9,8},{10,9},{11,1... | collective-permute-start | bytes 491528 | tf_op jit(solution)/shard_map/ppermute | solution.py:21
  163.0 27.5 %collective-permute-start.14 = (f32[16,5120]{1,0:T(8,128)}, f32[16,5120]{1,0:T(8,128)}, u32[]{:S(2)}, u32[]{:S(2)}) collective-permute-start(f32[16,5120]{1,0:T(8,128)} %get-tuple-element.30), channel_id=1, source_target_pairs={{0,16},{16,32},{32,48},{48,64},{64,80},{80,96},{96,112},{1,17},{17... | collective-permute-start | bytes 983048 | tf_op jit(solution)/shard_map/ppermute | solution.py:21
  164.9 54.1 %all-to-all-start.2 = ((f32[8,16,5120]{2,1,0:T(8,128)}), f32[8,16,5120]{2,1,0:T(8,128)}, u32[]{:S(2)}, u32[]{:S(2)}) async-start(f32[8,16,5120]{2,1,0:T(8,128)} %get-tuple-element.27), calls=%async_computation.2 | async-start | bytes 5242880 | tf_op jit(solution)/shard_map/all_to_all | solution.py:178
  172.9 56.7 %copy-start.1 = (f32[5,2,8,5120]{3,2,1,0:T(8,128)S(1)}, f32[5,2,8,5120]{3,2,1,0:T(8,128)}, u32[]{:S(2)}) copy-start(f32[5,2,8,5120]{3,2,1,0:T(8,128)} %copy-done) | copy-start | bytes 4915204
  172.9 53.3 %collective-permute-start.12 = (f32[4,5120]{1,0:T(4,128)}, f32[4,5120]{1,0:T(4,128)S(1)}, u32[]{:S(2)}, u32[]{:S(2)}) collective-permute-start(f32[4,5120]{1,0:T(4,128)} %get-tuple-element.28), channel_id=1, source_target_pairs={{0,1},{1,2},{2,3},{3,4},{4,5},{5,6},{6,7},{7,8},{8,9},{9,10},{10,1... | collective-permute-start | bytes 245768 | tf_op jit(solution)/shard_map/ppermute | solution.py:21
  175.3 50.9 %collective-permute-start.13 = (f32[4,5120]{1,0:T(4,128)S(1)}, f32[4,5120]{1,0:T(4,128)S(1)}, u32[]{:S(2)}, u32[]{:S(2)}) collective-permute-start(f32[4,5120]{1,0:T(4,128)S(1)} %get-tuple-element.29), channel_id=1, source_target_pairs={{1,0},{2,1},{3,2},{4,3},{5,4},{6,5},{7,6},{8,7},{9,8},{10,9},{11,1... | collective-permute-start | bytes 245768 | tf_op jit(solution)/shard_map/ppermute | solution.py:21
  177.3 40.3 %collective-permute-start.15 = (f32[16,5120]{1,0:T(8,128)}, f32[16,5120]{1,0:T(8,128)S(1)}, u32[]{:S(2)}, u32[]{:S(2)}) collective-permute-start(f32[16,5120]{1,0:T(8,128)} %copy-done.12), channel_id=1, source_target_pairs={{16,0},{32,16},{48,32},{64,48},{80,64},{96,80},{112,96},{17,1},{33... | collective-permute-start | bytes 983048 | tf_op jit(solution)/shard_map/ppermute | solution.py:21
  222.5 7.0 %copy-start.9 = (f32[16,5120]{1,0:T(8,128)S(1)}, f32[16,5120]{1,0:T(8,128)}, u32[]{:S(2)}) copy-start(f32[16,5120]{1,0:T(8,128)} %copy-done.8) | copy-start | bytes 983044
  222.5 7.0 %collective-permute-start.16 = (f32[8,5120]{1,0:T(8,128)}, f32[8,5120]{1,0:T(8,128)S(1)}, u32[]{:S(2)}, u32[]{:S(2)}) collective-permute-start(f32[8,5120]{1,0:T(8,128)} %concatenate.27), channel_id=1, source_target_pairs={{1,0},{2,1},{3,2},{4,3},{5,4},{6,5},{7,6},{8,7},{9,8},{10,9},{11,1... | collective-permute-start | bytes 491528 | tf_op jit(solution)/shard_map/ppermute | solution.py:21
  (8 other events, 12.0 us)

commit v9 on v8

--- a/solution.py
+++ b/solution.py
@@ -45,15 +45,18 @@
         return jnp.where(cols == 0, 0.0, pltpu.roll(a, 1, 1))
 
     def warp_of(src, row8, w):
-        lower = jnp.where(last_row, row8, pltpu.roll(src, R - 1, 0))
-        return w[0] * src + w[1] * shl(src) + w[2] * lower + w[3] * shl(lower)
+        a, b = w
+        across = (1.0 - b) * src + b * shl(src)
+        across8 = (1.0 - b) * row8 + b * jnp.where(cols[0:1] == C - 1, 0.0, pltpu.roll(row8, C - 1, 1))
+        lower = jnp.where(last_row, across8, pltpu.roll(across, R - 1, 0))
+        return (1.0 - a) * across + a * lower
 
     for l in range(L):
         ws = []
         for k in range(3):
             a = scal_ref[l, 3 + 2 * k]
             b = scal_ref[l, 4 + 2 * k]
-            ws.append(((1.0 - a) * (1.0 - b), (1.0 - a) * b, a * (1.0 - b), a * b))
+            ws.append((a, b))
         k_up = k_ref[0, l]
         k_mid = k_ref[1, l]
         k_dn = k_ref[2, l]

time: 236 us -> 236 us (level)
  no operation moved by 1% of the time
where the time goes in v9:
time: 236 us; the launch traced here: 235 us
  waiting for transfers between devices  104 us (44%)
  starting transfers between devices  70.1 us (30%)
  local copies, waits for them, and re-layouts  28.9 us (12%)
  Pallas kernels  16.2 us (7%)
  other arithmetic  10.9 us (5%)
  between operations  4.75 us (2%)
    ppermute x17, waiting for transfers between devices, shift_rows(): return lax.ppermute(block, axis, pairs)  87.8 us
    ppermute x17, starting transfers between devices, shift_rows(): return lax.ppermute(block, axis, pairs)  48.1 us
    all_to_all x3, starting transfers between devices, body(): recv = lax.all_to_all(send, 'gz', 0, 0, tiled=True)  22 us
    all_to_all x3, waiting for transfers between devices, body(): recv = lax.all_to_all(send, 'gz', 0, 0, tiled=True)  16.4 us
    pallas_call x3, Pallas kernels, update(): pl.pallas_call(update_kernel, out_shape=(jax.ShapeDtypeStruct(x.shape, x....  16.2 us
    another operation x1, other arithmetic, body(): stiff = jnp.stack([kappa, alive])  6.28 us
    unnamed x45, local copies, waits for them, and re-layouts  5.56 us
    squeeze x3, local copies, waits for them, and re-layouts, body(): lax.dynamic_slice(recv, (src_block[l], c * rows, 0), (1, 1, cols))[0]  4.81 us
  transfers between devices with their start and end apart: 20, of which 8 were waited for; matrix products, arithmetic and copies ran while one was open for 14% of the time, Pallas kernels for 0%

profile of v9, /device:TPU:97, one launch (start us, length us, event | category | flops | bytes accessed | tf_op | source)
XLA Modules:
  0.0 235.0 jit_solution(7750060558112631823)
XLA Ops:
  3.2 3.8 %collective-permute-start.2 = (f32[4,5120]{1,0:T(4,128)}, f32[4,5120]{1,0:T(4,128)S(1)}, u32[]{:S(2)}, u32[]{:S(2)}) collective-permute-start(f32[4,5120]{1,0:T(4,128)} %reshape_squeeze.8), channel_id=1, source_target_pairs={{0,1},{1,2},{2,3},{3,4},{4,5},{5,6},{6,7},{7,8},{8,9},{9,10},{10,1... | collective-permute-start | bytes 245768 | tf_op jit(solution)/shard_map/ppermute | solution.py:21
  9.6 6.3 %multiply_bitcast_fusion = f32[1,2,8,5120]{3,2,1,0:T(8,128)S(1)} fusion(s32[2,8,5120]{2,1,0:T(8,128)} %param.10, f32[]{:T(128)} %bitcast.7, f32[]{:T(128)} %bitcast.6, f32[]{:T(128)} %bitcast.5, f32[]{:T(128)} %bitcast.4, f32[]{:T(128)} %bitcast.3, f32[]{:T(128)} %bitcast.2, f32[]{:T(128)} %bitcast.1, f32[]{:T(128)} %bitcast, s32[2,8,5120]{2,1,0:T(8,128)} %param.11), kind=kLoop, calls=%fused_computation.18 | loop fusion | flops 1474560 | bytes 983072 | tf_op jit(solution)/shard_map/stack | solution.py:134
  16.0 1.9 collective-permute-start
  17.9 2.4 %collective-permute-start.1 = (f32[2,2,1,5120]{3,2,1,0:T(1,128)S(1)}, f32[2,2,1,5120]{3,2,1,0:T(1,128)S(1)}, u32[]{:S(2)}, u32[]{:S(2)}) collective-permute-start(f32[2,2,1,5120]{3,2,1,0:T(1,128)S(1)} %get-tuple-element.59), channel_id=1, source_target_pairs={{1,0},{2,1},{3,2},{4,3},{5,4},{6,5},{7,6},{8,7},{9,8},{10,9},{11,1... | collective-permute-start | bytes 245768 | tf_op jit(solution)/shard_map/ppermute | solution.py:21
  21.2 3.1 %collective-permute-start.4 = (f32[16,5120]{1,0:T(8,128)}, f32[16,5120]{1,0:T(8,128)}, u32[]{:S(2)}, u32[]{:S(2)}) collective-permute-start(f32[16,5120]{1,0:T(8,128)} %get-tuple-element.54), channel_id=1, source_target_pairs={{0,16},{16,32},{32,48},{48,64},{64,80},{80,96},{96,112},{1,17},{17... | collective-permute-start | bytes 983048 | tf_op jit(solution)/shard_map/ppermute | solution.py:21
  24.4 4.4 %collective-permute-start.5 = (f32[16,5120]{1,0:T(8,128)}, f32[16,5120]{1,0:T(8,128)}, u32[]{:S(2)}, u32[]{:S(2)}) collective-permute-start(f32[16,5120]{1,0:T(8,128)} %get-tuple-element.55), channel_id=1, source_target_pairs={{16,0},{32,16},{48,32},{64,48},{80,64},{96,80},{112,96},{17,1},{33... | collective-permute-start | bytes 983048 | tf_op jit(solution)/shard_map/ppermute | solution.py:21
  29.0 2.9 %broadcast_select_fusion = f32[8,16,5120]{2,1,0:T(8,128)} fusion(f32[16,5120]{1,0:T(8,128)} %get-tuple-element.55, f32[16,5120]{1,0:T(8,128)} %get-tuple-element.54, pred[8]{0:T(512)(128)(4,1)S(1)} %broadcast_compare_fusion), kind=kLoop, calls=%fused_computation | loop fusion | flops 655360 | bytes 3276808 | tf_op jit(solution)/shard_map/jit(_where)/select_n | solution.py:173
  31.9 6.6 %all-to-all-start = ((f32[8,16,5120]{2,1,0:T(8,128)}), f32[8,16,5120]{2,1,0:T(8,128)}, u32[]{:S(2)}, u32[]{:S(2)}) async-start(f32[8,16,5120]{2,1,0:T(8,128)} %broadcast_select_fusion), calls=%async_computation | async-start | bytes 5242880 | tf_op jit(solution)/shard_map/all_to_all | solution.py:181
  43.9 5.2 %collective-permute-start.3 = (f32[4,5120]{1,0:T(4,128)}, f32[4,5120]{1,0:T(4,128)S(1)}, u32[]{:S(2)}, u32[]{:S(2)}) collective-permute-start(f32[4,5120]{1,0:T(4,128)} %reshape_squeeze.9), channel_id=1, source_target_pairs={{1,0},{2,1},{3,2},{4,3},{5,4},{6,5},{7,6},{8,7},{9,8},{10,9},{11,1... | collective-permute-start | bytes 245768 | tf_op jit(solution)/shard_map/ppermute | solution.py:21
  52.2 16.4 %all-to-all-done = f32[8,16,5120]{2,1,0:T(8,128)} async-done(((f32[8,16,5120]{2,1,0:T(8,128)}), f32[8,16,5120]{2,1,0:T(8,128)}, u32[]{:S(2)}, u32[]{:S(2)}) %all-to-all-start) | async-done | bytes 2621472 | tf_op jit(solution)/shard_map/all_to_all | solution.py:181
  72.1 5.7 %collective-permute-start.6 = (f32[8,5120]{1,0:T(8,128)}, f32[8,5120]{1,0:T(8,128)S(1)}, u32[]{:S(2)}, u32[]{:S(2)}) collective-permute-start(f32[8,5120]{1,0:T(8,128)} %concatenate.25), channel_id=1, source_target_pairs={{1,0},{2,1},{3,2},{4,3},{5,4},{6,5},{7,6},{8,7},{9,8},{10,9},{11,1... | collective-permute-start | bytes 491528 | tf_op jit(solution)/shard_map/ppermute | solution.py:21
  79.0 7.5 %collective-permute-done.6.below_ref = f32[8,5120]{1,0:T(8,128)S(1)} collective-permute-done((f32[8,5120]{1,0:T(8,128)}, f32[8,5120]{1,0:T(8,128)S(1)}, u32[]{:S(2)}, u32[]{:S(2)}) %collective-permute-start.6) | collective-permute-done | bytes 163872 | tf_op jit(solution)/shard_map/ppermute | solution.py:21
  86.5 5.5 %shard_map.95 = (f32[2,2,8,5120]{3,2,1,0:T(8,128)S(1)}, f32[2,2,8,5120]{3,2,1,0:T(8,128)S(1)}, f32[8,16,5120]{2,1,0:T(8,128)}, f32[16,5120]{1,0:T(8,128)}, f32[1...) custom-call(f32[2,9]{1,0:T(2,128)S(1)} %pad_maximum_fusion.8.scal_ref, s32[8]{0:T(128)S(1)} %fusion.6.sel_ref, ...), custom_call_target="tpu_custom_call" | custom-call | flops 13107200 | bytes 8192000 | tf_op jit(solution)/shard_map/pallas_call | solution.py:106
  97.0 7.4 %all-to-all-start.1 = ((f32[8,16,5120]{2,1,0:T(8,128)}), f32[8,16,5120]{2,1,0:T(8,128)}, u32[]{:S(2)}, u32[]{:S(2)}) async-start(f32[8,16,5120]{2,1,0:T(8,128)} %get-tuple-element.20), calls=%async_computation.1 | async-start | bytes 5242880 | tf_op jit(solution)/shard_map/all_to_all | solution.py:181
  104.4 2.5 %collective-permute-start.7 = (f32[4,5120]{1,0:T(4,128)S(1)}, f32[4,5120]{1,0:T(4,128)S(1)}, u32[]{:S(2)}, u32[]{:S(2)}) collective-permute-start(f32[4,5120]{1,0:T(4,128)S(1)} %copy-done.16), channel_id=1, source_target_pairs={{0,1},{1,2},{2,3},{3,4},{4,5},{5,6},{6,7},{7,8},{8,9},{9,10},{10,1... | collective-permute-start | bytes 245768 | tf_op jit(solution)/shard_map/ppermute | solution.py:21
  106.9 1.9 collective-permute-start.8
  108.9 2.1 collective-permute-start.10
  110.9 11.6 %collective-permute-done.9.prevf_ref = f32[16,5120]{1,0:T(8,128)S(1)} collective-permute-done((f32[16,5120]{1,0:T(8,128)}, f32[16,5120]{1,0:T(8,128)S(1)}, u32[]{:S(2)}, u32[]{:S(2)}) %collective-permute-start.9) | collective-permute-done | bytes 327712 | tf_op jit(solution)/shard_map/ppermute | solution.py:21
  122.5 25.6 %collective-permute-done.10.nextf_ref = f32[16,5120]{1,0:T(8,128)S(1)} collective-permute-done((f32[16,5120]{1,0:T(8,128)S(1)}, f32[16,5120]{1,0:T(8,128)S(1)}, u32[]{:S(2)}, u32[]{:S(2)}) %collective-permute-start.10) | collective-permute-done | bytes 327712 | tf_op jit(solution)/shard_map/ppermute | solution.py:21
  150.3 2.4 %collective-permute-start.11 = (f32[8,5120]{1,0:T(8,128)S(1)}, f32[8,5120]{1,0:T(8,128)S(1)}, u32[]{:S(2)}, u32[]{:S(2)}) collective-permute-start(f32[8,5120]{1,0:T(8,128)S(1)} %concatenate.26), channel_id=1, source_target_pairs={{1,0},{2,1},{3,2},{4,3},{5,4},{6,5},{7,6},{8,7},{9,8},{10,9},{11,1... | collective-permute-start | bytes 491528 | tf_op jit(solution)/shard_map/ppermute | solution.py:21
  153.9 3.2 %collective-permute-done.11.below_ref = f32[8,5120]{1,0:T(8,128)S(1)} collective-permute-done((f32[8,5120]{1,0:T(8,128)S(1)}, f32[8,5120]{1,0:T(8,128)S(1)}, u32[]{:S(2)}, u32[]{:S(2)}) %collective-permute-start.11) | collective-permute-done | bytes 163872 | tf_op jit(solution)/shard_map/ppermute | solution.py:21
  157.1 5.3 %shard_map.96 = (f32[2,2,8,5120]{3,2,1,0:T(8,128)S(1)}, f32[2,2,8,5120]{3,2,1,0:T(8,128)S(1)}, f32[8,16,5120]{2,1,0:T(8,128)}, f32[16,5120]{1,0:T(8,128)}, f32[1...) custom-call(f32[2,9]{1,0:T(2,128)S(1)} %pad_maximum_fusion.8.scal_ref, s32[8]{0:T(128)S(1)} %fusion.6.sel_ref, ...), custom_call_target="tpu_custom_call" | custom-call | flops 13107200 | bytes 8192000 | tf_op jit(solution)/shard_map/pallas_call | solution.py:106
  163.1 1.9 collective-permute-start.14
  165.0 7.9 %all-to-all-start.2 = ((f32[8,16,5120]{2,1,0:T(8,128)}), f32[8,16,5120]{2,1,0:T(8,128)}, u32[]{:S(2)}, u32[]{:S(2)}) async-start(f32[8,16,5120]{2,1,0:T(8,128)} %get-tuple-element.27), calls=%async_computation.2 | async-start | bytes 5242880 | tf_op jit(solution)/shard_map/all_to_all | solution.py:181
  173.0 2.4 %collective-permute-start.12 = (f32[4,5120]{1,0:T(4,128)}, f32[4,5120]{1,0:T(4,128)S(1)}, u32[]{:S(2)}, u32[]{:S(2)}) collective-permute-start(f32[4,5120]{1,0:T(4,128)} %get-tuple-element.28), channel_id=1, source_target_pairs={{0,1},{1,2},{2,3},{3,4},{4,5},{5,6},{6,7},{7,8},{8,9},{9,10},{10,1... | collective-permute-start | bytes 245768 | tf_op jit(solution)/shard_map/ppermute | solution.py:21
  175.4 2.0 collective-permute-start.13
  177.4 2.1 collective-permute-start.15
  179.5 11.1 %collective-permute-done.14.prevf_ref = f32[16,5120]{1,0:T(8,128)} collective-permute-done((f32[16,5120]{1,0:T(8,128)}, f32[16,5120]{1,0:T(8,128)}, u32[]{:S(2)}, u32[]{:S(2)}) %collective-permute-start.14) | collective-permute-done | bytes 327712 | tf_op jit(solution)/shard_map/ppermute | solution.py:21
  192.2 25.5 %collective-permute-done.15.nextf_ref = f32[16,5120]{1,0:T(8,128)S(1)} collective-permute-done((f32[16,5120]{1,0:T(8,128)}, f32[16,5120]{1,0:T(8,128)S(1)}, u32[]{:S(2)}, u32[]{:S(2)}) %collective-permute-start.15) | collective-permute-done | bytes 327712 | tf_op jit(solution)/shard_map/ppermute | solution.py:21
  222.7 2.4 %collective-permute-start.16 = (f32[8,5120]{1,0:T(8,128)}, f32[8,5120]{1,0:T(8,128)S(1)}, u32[]{:S(2)}, u32[]{:S(2)}) collective-permute-start(f32[8,5120]{1,0:T(8,128)} %concatenate.27), channel_id=1, source_target_pairs={{1,0},{2,1},{3,2},{4,3},{5,4},{6,5},{7,6},{8,7},{9,8},{10,9},{11,1... | collective-permute-start | bytes 491528 | tf_op jit(solution)/shard_map/ppermute | solution.py:21
  226.3 3.3 %collective-permute-done.16.below_ref = f32[8,5120]{1,0:T(8,128)S(1)} collective-permute-done((f32[8,5120]{1,0:T(8,128)}, f32[8,5120]{1,0:T(8,128)S(1)}, u32[]{:S(2)}, u32[]{:S(2)}) %collective-permute-start.16) | collective-permute-done | bytes 163872 | tf_op jit(solution)/shard_map/ppermute | solution.py:21
  229.6 5.3 %shard_map.97 = (f32[2,2,8,5120]{3,2,1,0:T(8,128)}, f32[2,2,8,5120]{3,2,1,0:T(8,128)}, f32[8,16,5120]{2,1,0:T(8,128)}, f32[16,5120]{1,0:T(8,128)}, f32[16,5120]{...) custom-call(f32[2,9]{1,0:T(2,128)S(1)} %pad_maximum_fusion.8.scal_ref, s32[8]{0:T(128)S(1)} %fusion.6.sel_ref, ...), custom_call_target="tpu_custom_call" | custom-call | flops 13107200 | bytes 8192000 | tf_op jit(solution)/shard_map/pallas_call | solution.py:106
  (94 shorter events, 32.5 us)
Async XLA Ops:
  0.6 19.7 %copy-start.2 = (f32[2,2,8,5120]{3,2,1,0:T(8,128)S(1)}, f32[2,2,8,5120]{3,2,1,0:T(8,128)}, u32[]{:S(2)}) copy-start(f32[2,2,8,5120]{3,2,1,0:T(8,128)} %x_ref.1) | copy-start | bytes 1966084
  0.6 28.1 %copy-start.19 = (s32[16]{0:T(128)S(1)}, s32[16]{0:T(128)}, u32[]{:S(2)}) copy-start(s32[16]{0:T(128)} %param.15) | copy-start | bytes 196
  3.2 75.8 %collective-permute-start.2 = (f32[4,5120]{1,0:T(4,128)}, f32[4,5120]{1,0:T(4,128)S(1)}, u32[]{:S(2)}, u32[]{:S(2)}) collective-permute-start(f32[4,5120]{1,0:T(4,128)} %reshape_squeeze.8), channel_id=1, source_target_pairs={{0,1},{1,2},{2,3},{3,4},{4,5},{5,6},{6,7},{7,8},{8,9},{9,10},{10,1... | collective-permute-start | bytes 245768 | tf_op jit(solution)/shard_map/ppermute | solution.py:21
  16.0 27.9 %collective-permute-start = (f32[2,2,1,5120]{3,2,1,0:T(1,128)S(1)}, f32[2,2,1,5120]{3,2,1,0:T(1,128)S(1)}, u32[]{:S(2)}, u32[]{:S(2)}) collective-permute-start(f32[2,2,1,5120]{3,2,1,0:T(1,128)S(1)} %get-tuple-element.58), channel_id=1, source_target_pairs={{0,1},{1,2},{2,3},{3,4},{4,5},{5,6},{6,7},{7,8},{8,9},{9,10},{10,1... | collective-permute-start | bytes 245768 | tf_op jit(solution)/shard_map/ppermute | solution.py:21
  17.9 31.2 %collective-permute-start.1 = (f32[2,2,1,5120]{3,2,1,0:T(1,128)S(1)}, f32[2,2,1,5120]{3,2,1,0:T(1,128)S(1)}, u32[]{:S(2)}, u32[]{:S(2)}) collective-permute-start(f32[2,2,1,5120]{3,2,1,0:T(1,128)S(1)} %get-tuple-element.59), channel_id=1, source_target_pairs={{1,0},{2,1},{3,2},{4,3},{5,4},{6,5},{7,6},{8,7},{9,8},{10,9},{11,1... | collective-permute-start | bytes 245768 | tf_op jit(solution)/shard_map/ppermute | solution.py:21
  21.2 28.5 %collective-permute-start.4 = (f32[16,5120]{1,0:T(8,128)}, f32[16,5120]{1,0:T(8,128)}, u32[]{:S(2)}, u32[]{:S(2)}) collective-permute-start(f32[16,5120]{1,0:T(8,128)} %get-tuple-element.54), channel_id=1, source_target_pairs={{0,16},{16,32},{32,48},{48,64},{64,80},{80,96},{96,112},{1,17},{17... | collective-permute-start | bytes 983048 | tf_op jit(solution)/shard_map/ppermute | solution.py:21
  24.4 26.8 %collective-permute-start.5 = (f32[16,5120]{1,0:T(8,128)}, f32[16,5120]{1,0:T(8,128)}, u32[]{:S(2)}, u32[]{:S(2)}) collective-permute-start(f32[16,5120]{1,0:T(8,128)} %get-tuple-element.55), channel_id=1, source_target_pairs={{16,0},{32,16},{48,32},{64,48},{80,64},{96,80},{112,96},{17,1},{33... | collective-permute-start | bytes 983048 | tf_op jit(solution)/shard_map/ppermute | solution.py:21
  31.9 9.8 %copy-start.17 = (f32[2,3]{1,0:T(2,128)S(1)}, f32[2,3]{1,0:T(2,128)}, u32[]{:S(2)}) copy-start(f32[2,3]{1,0:T(2,128)} %param.14) | copy-start | bytes 76
  31.9 9.9 %copy-start.18 = (f32[2,3,2]{1,2,0:T(2,128)S(1)}, f32[2,3,2]{1,2,0:T(2,128)}, u32[]{:S(2)}) copy-start(f32[2,3,2]{1,2,0:T(2,128)} %param.13) | copy-start | bytes 148
  31.9 36.8 %all-to-all-start = ((f32[8,16,5120]{2,1,0:T(8,128)}), f32[8,16,5120]{2,1,0:T(8,128)}, u32[]{:S(2)}, u32[]{:S(2)}) async-start(f32[8,16,5120]{2,1,0:T(8,128)} %broadcast_select_fusion), calls=%async_computation | async-start | bytes 5242880 | tf_op jit(solution)/shard_map/all_to_all | solution.py:181
  43.9 35.1 %collective-permute-start.3 = (f32[4,5120]{1,0:T(4,128)}, f32[4,5120]{1,0:T(4,128)S(1)}, u32[]{:S(2)}, u32[]{:S(2)}) collective-permute-start(f32[4,5120]{1,0:T(4,128)} %reshape_squeeze.9), channel_id=1, source_target_pairs={{1,0},{2,1},{3,2},{4,3},{5,4},{6,5},{7,6},{8,7},{9,8},{10,9},{11,1... | collective-permute-start | bytes 245768 | tf_op jit(solution)/shard_map/ppermute | solution.py:21
  49.5 37.0 %copy-start.3 = (f32[2,2,8,5120]{3,2,1,0:T(8,128)S(1)}, f32[2,2,8,5120]{3,2,1,0:T(8,128)}, u32[]{:S(2)}) copy-start(f32[2,2,8,5120]{3,2,1,0:T(8,128)} %v_ref.1) | copy-start | bytes 1966084
  49.7 36.8 %copy-start = (f32[5,2,8,5120]{3,2,1,0:T(8,128)}, f32[5,2,8,5120]{3,2,1,0:T(8,128)S(1)}, u32[]{:S(2)}) copy-start(f32[5,2,8,5120]{3,2,1,0:T(8,128)S(1)} %bitcast_dynamic-update-slice_fusion.k_ref) | copy-start | bytes 4915204
  72.1 14.4 %collective-permute-start.6 = (f32[8,5120]{1,0:T(8,128)}, f32[8,5120]{1,0:T(8,128)S(1)}, u32[]{:S(2)}, u32[]{:S(2)}) collective-permute-start(f32[8,5120]{1,0:T(8,128)} %concatenate.25), channel_id=1, source_target_pairs={{1,0},{2,1},{3,2},{4,3},{5,4},{6,5},{7,6},{8,7},{9,8},{10,9},{11,1... | collective-permute-start | bytes 491528 | tf_op jit(solution)/shard_map/ppermute | solution.py:21
  95.0 27.5 %collective-permute-start.9 = (f32[16,5120]{1,0:T(8,128)}, f32[16,5120]{1,0:T(8,128)S(1)}, u32[]{:S(2)}, u32[]{:S(2)}) collective-permute-start(f32[16,5120]{1,0:T(8,128)} %get-tuple-element.23), channel_id=1, source_target_pairs={{0,16},{16,32},{32,48},{48,64},{64,80},{80,96},{96,112},{1,17},{17... | collective-permute-start | bytes 983048 | tf_op jit(solution)/shard_map/ppermute | solution.py:21
  96.9 7.4 %copy-start.16 = (f32[4,5120]{1,0:T(4,128)S(1)}, f32[4,5120]{1,0:T(4,128)}, u32[]{:S(2)}) copy-start(f32[4,5120]{1,0:T(4,128)} %copy-done.15) | copy-start | bytes 245764
  97.0 11.9 %copy-start.14 = (f32[16,5120]{1,0:T(8,128)S(1)}, f32[16,5120]{1,0:T(8,128)}, u32[]{:S(2)}) copy-start(f32[16,5120]{1,0:T(8,128)} %copy-done.13) | copy-start | bytes 983044
  97.0 51.9 %all-to-all-start.1 = ((f32[8,16,5120]{2,1,0:T(8,128)}), f32[8,16,5120]{2,1,0:T(8,128)}, u32[]{:S(2)}, u32[]{:S(2)}) async-start(f32[8,16,5120]{2,1,0:T(8,128)} %get-tuple-element.20), calls=%async_computation.1 | async-start | bytes 5242880 | tf_op jit(solution)/shard_map/all_to_all | solution.py:181
  104.4 52.7 %copy-start.5 = (f32[2,2,8,5120]{3,2,1,0:T(8,128)S(1)}, f32[2,2,8,5120]{3,2,1,0:T(8,128)}, u32[]{:S(2)}) copy-start(f32[2,2,8,5120]{3,2,1,0:T(8,128)} %copy-done.4) | copy-start | bytes 1966084
  104.4 52.7 %copy-start.7 = (f32[2,2,8,5120]{3,2,1,0:T(8,128)S(1)}, f32[2,2,8,5120]{3,2,1,0:T(8,128)}, u32[]{:S(2)}) copy-start(f32[2,2,8,5120]{3,2,1,0:T(8,128)} %copy-done.6) | copy-start | bytes 1966084
  104.4 49.5 %collective-permute-start.7 = (f32[4,5120]{1,0:T(4,128)S(1)}, f32[4,5120]{1,0:T(4,128)S(1)}, u32[]{:S(2)}, u32[]{:S(2)}) collective-permute-start(f32[4,5120]{1,0:T(4,128)S(1)} %copy-done.16), channel_id=1, source_target_pairs={{0,1},{1,2},{2,3},{3,4},{4,5},{5,6},{6,7},{7,8},{8,9},{9,10},{10,1... | collective-permute-start | bytes 245768 | tf_op jit(solution)/shard_map/ppermute | solution.py:21
  106.9 47.0 %collective-permute-start.8 = (f32[4,5120]{1,0:T(4,128)S(1)}, f32[4,5120]{1,0:T(4,128)S(1)}, u32[]{:S(2)}, u32[]{:S(2)}) collective-permute-start(f32[4,5120]{1,0:T(4,128)S(1)} %get-tuple-element.22), channel_id=1, source_target_pairs={{1,0},{2,1},{3,2},{4,3},{5,4},{6,5},{7,6},{8,7},{9,8},{10,9},{11,1... | collective-permute-start | bytes 245768 | tf_op jit(solution)/shard_map/ppermute | solution.py:21
  108.9 39.2 %collective-permute-start.10 = (f32[16,5120]{1,0:T(8,128)S(1)}, f32[16,5120]{1,0:T(8,128)S(1)}, u32[]{:S(2)}, u32[]{:S(2)}) collective-permute-start(f32[16,5120]{1,0:T(8,128)S(1)} %copy-done.14), channel_id=1, source_target_pairs={{16,0},{32,16},{48,32},{64,48},{80,64},{96,80},{112,96},{17,1},{33... | collective-permute-start | bytes 983048 | tf_op jit(solution)/shard_map/ppermute | solution.py:21
  150.3 6.8 %collective-permute-start.11 = (f32[8,5120]{1,0:T(8,128)S(1)}, f32[8,5120]{1,0:T(8,128)S(1)}, u32[]{:S(2)}, u32[]{:S(2)}) collective-permute-start(f32[8,5120]{1,0:T(8,128)S(1)} %concatenate.26), channel_id=1, source_target_pairs={{1,0},{2,1},{3,2},{4,3},{5,4},{6,5},{7,6},{8,7},{9,8},{10,9},{11,1... | collective-permute-start | bytes 491528 | tf_op jit(solution)/shard_map/ppermute | solution.py:21
  163.1 27.5 %collective-permute-start.14 = (f32[16,5120]{1,0:T(8,128)}, f32[16,5120]{1,0:T(8,128)}, u32[]{:S(2)}, u32[]{:S(2)}) collective-permute-start(f32[16,5120]{1,0:T(8,128)} %get-tuple-element.30), channel_id=1, source_target_pairs={{0,16},{16,32},{32,48},{48,64},{64,80},{80,96},{96,112},{1,17},{17... | collective-permute-start | bytes 983048 | tf_op jit(solution)/shard_map/ppermute | solution.py:21
  165.0 54.1 %all-to-all-start.2 = ((f32[8,16,5120]{2,1,0:T(8,128)}), f32[8,16,5120]{2,1,0:T(8,128)}, u32[]{:S(2)}, u32[]{:S(2)}) async-start(f32[8,16,5120]{2,1,0:T(8,128)} %get-tuple-element.27), calls=%async_computation.2 | async-start | bytes 5242880 | tf_op jit(solution)/shard_map/all_to_all | solution.py:181
  173.0 56.7 %copy-start.1 = (f32[5,2,8,5120]{3,2,1,0:T(8,128)S(1)}, f32[5,2,8,5120]{3,2,1,0:T(8,128)}, u32[]{:S(2)}) copy-start(f32[5,2,8,5120]{3,2,1,0:T(8,128)} %copy-done) | copy-start | bytes 4915204
  173.0 53.3 %collective-permute-start.12 = (f32[4,5120]{1,0:T(4,128)}, f32[4,5120]{1,0:T(4,128)S(1)}, u32[]{:S(2)}, u32[]{:S(2)}) collective-permute-start(f32[4,5120]{1,0:T(4,128)} %get-tuple-element.28), channel_id=1, source_target_pairs={{0,1},{1,2},{2,3},{3,4},{4,5},{5,6},{6,7},{7,8},{8,9},{9,10},{10,1... | collective-permute-start | bytes 245768 | tf_op jit(solution)/shard_map/ppermute | solution.py:21
  175.4 50.9 %collective-permute-start.13 = (f32[4,5120]{1,0:T(4,128)S(1)}, f32[4,5120]{1,0:T(4,128)S(1)}, u32[]{:S(2)}, u32[]{:S(2)}) collective-permute-start(f32[4,5120]{1,0:T(4,128)S(1)} %get-tuple-element.29), channel_id=1, source_target_pairs={{1,0},{2,1},{3,2},{4,3},{5,4},{6,5},{7,6},{8,7},{9,8},{10,9},{11,1... | collective-permute-start | bytes 245768 | tf_op jit(solution)/shard_map/ppermute | solution.py:21
  177.4 40.3 %collective-permute-start.15 = (f32[16,5120]{1,0:T(8,128)}, f32[16,5120]{1,0:T(8,128)S(1)}, u32[]{:S(2)}, u32[]{:S(2)}) collective-permute-start(f32[16,5120]{1,0:T(8,128)} %copy-done.12), channel_id=1, source_target_pairs={{16,0},{32,16},{48,32},{64,48},{80,64},{96,80},{112,96},{17,1},{33... | collective-permute-start | bytes 983048 | tf_op jit(solution)/shard_map/ppermute | solution.py:21
  222.7 7.0 %copy-start.9 = (f32[16,5120]{1,0:T(8,128)S(1)}, f32[16,5120]{1,0:T(8,128)}, u32[]{:S(2)}) copy-start(f32[16,5120]{1,0:T(8,128)} %copy-done.8) | copy-start | bytes 983044
  222.7 7.0 %collective-permute-start.16 = (f32[8,5120]{1,0:T(8,128)}, f32[8,5120]{1,0:T(8,128)S(1)}, u32[]{:S(2)}, u32[]{:S(2)}) collective-permute-start(f32[8,5120]{1,0:T(8,128)} %concatenate.27), channel_id=1, source_target_pairs={{1,0},{2,1},{3,2},{4,3},{5,4},{6,5},{7,6},{8,7},{9,8},{10,9},{11,1... | collective-permute-start | bytes 491528 | tf_op jit(solution)/shard_map/ppermute | solution.py:21
  (8 other events, 12.0 us)

commit v10 on v8

--- a/solution.py
+++ b/solution.py
@@ -165,11 +165,8 @@
 
     field = disp
     velocity = vel
-    send = field[0][None]
-    for l in range(1, local_count):
-        send = jnp.where((send_sel == l)[:, None, None, None], field[l][None], send)
     plane = ncomp * disp.shape[2]
-    send = send.reshape(block_count, plane, cols)
+    send = jnp.take(field.reshape(local_count, plane, cols), send_sel, axis=0, mode="clip")
     last_face = field[-1].reshape(plane, cols)
     first_face = field[0].reshape(plane, cols)
     top_rows = field[:, :, 0].reshape(local_count * ncomp, cols)

time: 236 us -> 242 us (1.025)
  the two profiles are of different devices: /device:TPU:97 before, /device:TPU:105 now
where the time goes in v10:
time: 242 us; the launch traced here: 240 us
  waiting for transfers between devices  109 us (45%)
  starting transfers between devices  71.3 us (29%)
  local copies, waits for them, and re-layouts  31.2 us (13%)
  Pallas kernels  15.9 us (7%)
  other arithmetic  8 us (3%)
  between operations  4.93 us (2%)
    ppermute x17, waiting for transfers between devices, shift_rows(): return lax.ppermute(block, axis, pairs)  109 us
    ppermute x17, starting transfers between devices, shift_rows(): return lax.ppermute(block, axis, pairs)  47.2 us
    all_to_all x3, starting transfers between devices, body(): recv = lax.all_to_all(send, 'gz', 0, 0, tiled=True)  24.1 us
    pallas_call x3, Pallas kernels, update(): pl.pallas_call(update_kernel, out_shape=(jax.ShapeDtypeStruct(x.shape, x....  15.9 us
    unnamed x49, local copies, waits for them, and re-layouts  6.54 us
    another operation x1, other arithmetic, body(): stiff = jnp.stack([kappa, alive])  6.27 us
    squeeze x3, local copies, waits for them, and re-layouts, body(): lax.dynamic_slice(recv, (src_block[l], c * rows, 0), (1, 1, cols))[0]  4.92 us
  transfers between devices with their start and end apart: 20, of which 7 were waited for; matrix products, arithmetic and copies ran while one was open for 13% of the time, Pallas kernels for 0%

profile of v10, /device:TPU:105, one launch (start us, length us, event | category | flops | bytes accessed | tf_op | source)
XLA Modules:
  0.0 240.0 jit_solution(17767190747831136703)
XLA Ops:
  3.2 3.8 %collective-permute-start.2 = (f32[4,5120]{1,0:T(4,128)}, f32[4,5120]{1,0:T(4,128)S(1)}, u32[]{:S(2)}, u32[]{:S(2)}) collective-permute-start(f32[4,5120]{1,0:T(4,128)} %reshape_squeeze.12), channel_id=1, source_target_pairs={{0,1},{1,2},{2,3},{3,4},{4,5},{5,6},{6,7},{7,8},{8,9},{9,10},{10,1... | collective-permute-start | bytes 245768 | tf_op jit(solution)/shard_map/ppermute | solution.py:21
  7.7 1.9 collective-permute-start.3
  12.2 6.3 %multiply_bitcast_fusion = f32[1,2,8,5120]{3,2,1,0:T(8,128)S(1)} fusion(s32[2,8,5120]{2,1,0:T(8,128)} %param.10, f32[]{:T(128)} %bitcast.7, f32[]{:T(128)} %bitcast.6, f32[]{:T(128)} %bitcast.5, f32[]{:T(128)} %bitcast.4, f32[]{:T(128)} %bitcast.3, f32[]{:T(128)} %bitcast.2, f32[]{:T(128)} %bitcast.1, f32[]{:T(128)} %bitcast, s32[2,8,5120]{2,1,0:T(8,128)} %param.11), kind=kLoop, calls=%fused_computation.18 | loop fusion | flops 1474560 | bytes 983072 | tf_op jit(solution)/shard_map/stack | solution.py:131
  18.6 3.6 %collective-permute-start = (f32[2,2,1,5120]{3,2,1,0:T(1,128)S(1)}, f32[2,2,1,5120]{3,2,1,0:T(1,128)S(1)}, u32[]{:S(2)}, u32[]{:S(2)}) collective-permute-start(f32[2,2,1,5120]{3,2,1,0:T(1,128)S(1)} %get-tuple-element.58), channel_id=1, source_target_pairs={{0,1},{1,2},{2,3},{3,4},{4,5},{5,6},{6,7},{7,8},{8,9},{9,10},{10,1... | collective-permute-start | bytes 245768 | tf_op jit(solution)/shard_map/ppermute | solution.py:21
  22.3 1.9 collective-permute-start.1
  25.1 2.2 collective-permute-start.5
  27.5 2.2 gather_fusion
  29.7 7.3 %all-to-all-start = ((f32[8,16,5120]{2,1,0:T(8,128)}), f32[8,16,5120]{2,1,0:T(8,128)}, u32[]{:S(2)}, u32[]{:S(2)}) async-start(f32[8,16,5120]{2,1,0:T(8,128)} %gather_fusion), calls=%async_computation | async-start | bytes 5242880 | tf_op jit(solution)/shard_map/all_to_all | solution.py:175
  41.9 3.1 %collective-permute-start.4 = (f32[16,5120]{1,0:T(8,128)}, f32[16,5120]{1,0:T(8,128)S(1)}, u32[]{:S(2)}, u32[]{:S(2)}) collective-permute-start(f32[16,5120]{1,0:T(8,128)} %get-tuple-element.55), channel_id=1, source_target_pairs={{0,16},{16,32},{32,48},{48,64},{64,80},{80,96},{96,112},{1,17},{17... | collective-permute-start | bytes 983048 | tf_op jit(solution)/shard_map/ppermute | solution.py:21
  47.0 27.4 %collective-permute-done.4.prevf_ref = f32[16,5120]{1,0:T(8,128)S(1)} collective-permute-done((f32[16,5120]{1,0:T(8,128)}, f32[16,5120]{1,0:T(8,128)S(1)}, u32[]{:S(2)}, u32[]{:S(2)}) %collective-permute-start.4) | collective-permute-done | bytes 327712 | tf_op jit(solution)/shard_map/ppermute | solution.py:21
  78.6 4.0 %collective-permute-start.6 = (f32[8,5120]{1,0:T(8,128)}, f32[8,5120]{1,0:T(8,128)S(1)}, u32[]{:S(2)}, u32[]{:S(2)}) collective-permute-start(f32[8,5120]{1,0:T(8,128)} %concatenate.25), channel_id=1, source_target_pairs={{1,0},{2,1},{3,2},{4,3},{5,4},{6,5},{7,6},{8,7},{9,8},{10,9},{11,1... | collective-permute-start | bytes 491528 | tf_op jit(solution)/shard_map/ppermute | solution.py:21
  83.8 2.5 %collective-permute-done.6.below_ref = f32[8,5120]{1,0:T(8,128)S(1)} collective-permute-done((f32[8,5120]{1,0:T(8,128)}, f32[8,5120]{1,0:T(8,128)S(1)}, u32[]{:S(2)}, u32[]{:S(2)}) %collective-permute-start.6) | collective-permute-done | bytes 163872 | tf_op jit(solution)/shard_map/ppermute | solution.py:21
  86.3 5.3 %shard_map.95 = (f32[2,2,8,5120]{3,2,1,0:T(8,128)S(1)}, f32[2,2,8,5120]{3,2,1,0:T(8,128)S(1)}, f32[8,16,5120]{2,1,0:T(8,128)}, f32[16,5120]{1,0:T(8,128)}, f32[1...) custom-call(f32[2,9]{1,0:T(2,128)S(1)} %pad_maximum_fusion.8.scal_ref, s32[8]{0:T(128)S(1)} %fusion.6.sel_ref, ...), custom_call_target="tpu_custom_call" | custom-call | flops 13107200 | bytes 8192000 | tf_op jit(solution)/shard_map/pallas_call | solution.py:103
  94.7 6.4 %collective-permute-start.9 = (f32[16,5120]{1,0:T(8,128)}, f32[16,5120]{1,0:T(8,128)S(1)}, u32[]{:S(2)}, u32[]{:S(2)}) collective-permute-start(f32[16,5120]{1,0:T(8,128)} %get-tuple-element.23), channel_id=1, source_target_pairs={{0,16},{16,32},{32,48},{48,64},{64,80},{80,96},{96,112},{1,17},{17... | collective-permute-start | bytes 983048 | tf_op jit(solution)/shard_map/ppermute | solution.py:21
  101.1 8.8 %all-to-all-start.1 = ((f32[8,16,5120]{2,1,0:T(8,128)}), f32[8,16,5120]{2,1,0:T(8,128)}, u32[]{:S(2)}, u32[]{:S(2)}) async-start(f32[8,16,5120]{2,1,0:T(8,128)} %get-tuple-element.20), calls=%async_computation.1 | async-start | bytes 5242880 | tf_op jit(solution)/shard_map/all_to_all | solution.py:175
  109.9 2.8 %collective-permute-start.7 = (f32[4,5120]{1,0:T(4,128)S(1)}, f32[4,5120]{1,0:T(4,128)S(1)}, u32[]{:S(2)}, u32[]{:S(2)}) collective-permute-start(f32[4,5120]{1,0:T(4,128)S(1)} %copy-done.18), channel_id=1, source_target_pairs={{0,1},{1,2},{2,3},{3,4},{4,5},{5,6},{6,7},{7,8},{8,9},{9,10},{10,1... | collective-permute-start | bytes 245768 | tf_op jit(solution)/shard_map/ppermute | solution.py:21
  112.7 1.9 collective-permute-start.8
  114.7 1.9 collective-permute-start.10
  116.7 36.9 %collective-permute-done.10.nextf_ref = f32[16,5120]{1,0:T(8,128)S(1)} collective-permute-done((f32[16,5120]{1,0:T(8,128)S(1)}, f32[16,5120]{1,0:T(8,128)S(1)}, u32[]{:S(2)}, u32[]{:S(2)}) %collective-permute-start.10) | collective-permute-done | bytes 327712 | tf_op jit(solution)/shard_map/ppermute | solution.py:21
  155.1 2.9 %collective-permute-start.11 = (f32[8,5120]{1,0:T(8,128)S(1)}, f32[8,5120]{1,0:T(8,128)S(1)}, u32[]{:S(2)}, u32[]{:S(2)}) collective-permute-start(f32[8,5120]{1,0:T(8,128)S(1)} %concatenate.26), channel_id=1, source_target_pairs={{1,0},{2,1},{3,2},{4,3},{5,4},{6,5},{7,6},{8,7},{9,8},{10,9},{11,1... | collective-permute-start | bytes 491528 | tf_op jit(solution)/shard_map/ppermute | solution.py:21
  159.2 2.5 %collective-permute-done.11.below_ref = f32[8,5120]{1,0:T(8,128)S(1)} collective-permute-done((f32[8,5120]{1,0:T(8,128)S(1)}, f32[8,5120]{1,0:T(8,128)S(1)}, u32[]{:S(2)}, u32[]{:S(2)}) %collective-permute-start.11) | collective-permute-done | bytes 163872 | tf_op jit(solution)/shard_map/ppermute | solution.py:21
  162.7 5.2 %shard_map.96 = (f32[2,2,8,5120]{3,2,1,0:T(8,128)S(1)}, f32[2,2,8,5120]{3,2,1,0:T(8,128)S(1)}, f32[8,16,5120]{2,1,0:T(8,128)}, f32[16,5120]{1,0:T(8,128)}, f32[1...) custom-call(f32[2,9]{1,0:T(2,128)S(1)} %pad_maximum_fusion.8.scal_ref, s32[8]{0:T(128)S(1)} %fusion.6.sel_ref, ...), custom_call_target="tpu_custom_call" | custom-call | flops 13107200 | bytes 8192000 | tf_op jit(solution)/shard_map/pallas_call | solution.py:103
  168.7 1.9 collective-permute-start.14
  170.6 8.0 %all-to-all-start.2 = ((f32[8,16,5120]{2,1,0:T(8,128)}), f32[8,16,5120]{2,1,0:T(8,128)}, u32[]{:S(2)}, u32[]{:S(2)}) async-start(f32[8,16,5120]{2,1,0:T(8,128)} %get-tuple-element.27), calls=%async_computation.2 | async-start | bytes 5242880 | tf_op jit(solution)/shard_map/all_to_all | solution.py:175
  178.6 2.4 %collective-permute-start.12 = (f32[4,5120]{1,0:T(4,128)}, f32[4,5120]{1,0:T(4,128)S(1)}, u32[]{:S(2)}, u32[]{:S(2)}) collective-permute-start(f32[4,5120]{1,0:T(4,128)} %get-tuple-element.28), channel_id=1, source_target_pairs={{0,1},{1,2},{2,3},{3,4},{4,5},{5,6},{6,7},{7,8},{8,9},{9,10},{10,1... | collective-permute-start | bytes 245768 | tf_op jit(solution)/shard_map/ppermute | solution.py:21
  181.0 2.0 collective-permute-start.13
  183.0 2.1 collective-permute-start.15
  185.1 11.1 %collective-permute-done.14.prevf_ref = f32[16,5120]{1,0:T(8,128)} collective-permute-done((f32[16,5120]{1,0:T(8,128)}, f32[16,5120]{1,0:T(8,128)}, u32[]{:S(2)}, u32[]{:S(2)}) %collective-permute-start.14) | collective-permute-done | bytes 327712 | tf_op jit(solution)/shard_map/ppermute | solution.py:21
  197.8 25.1 %collective-permute-done.15.nextf_ref = f32[16,5120]{1,0:T(8,128)S(1)} collective-permute-done((f32[16,5120]{1,0:T(8,128)}, f32[16,5120]{1,0:T(8,128)S(1)}, u32[]{:S(2)}, u32[]{:S(2)}) %collective-permute-start.15) | collective-permute-done | bytes 327712 | tf_op jit(solution)/shard_map/ppermute | solution.py:21
  227.8 2.4 %collective-permute-start.16 = (f32[8,5120]{1,0:T(8,128)}, f32[8,5120]{1,0:T(8,128)S(1)}, u32[]{:S(2)}, u32[]{:S(2)}) collective-permute-start(f32[8,5120]{1,0:T(8,128)} %concatenate.27), channel_id=1, source_target_pairs={{1,0},{2,1},{3,2},{4,3},{5,4},{6,5},{7,6},{8,7},{9,8},{10,9},{11,1... | collective-permute-start | bytes 491528 | tf_op jit(solution)/shard_map/ppermute | solution.py:21
  231.4 3.3 %collective-permute-done.16.below_ref = f32[8,5120]{1,0:T(8,128)S(1)} collective-permute-done((f32[8,5120]{1,0:T(8,128)}, f32[8,5120]{1,0:T(8,128)S(1)}, u32[]{:S(2)}, u32[]{:S(2)}) %collective-permute-start.16) | collective-permute-done | bytes 163872 | tf_op jit(solution)/shard_map/ppermute | solution.py:21
  234.7 5.3 %shard_map.97 = (f32[2,2,8,5120]{3,2,1,0:T(8,128)}, f32[2,2,8,5120]{3,2,1,0:T(8,128)}, f32[8,16,5120]{2,1,0:T(8,128)}, f32[16,5120]{1,0:T(8,128)}, f32[16,5120]{...) custom-call(f32[2,9]{1,0:T(2,128)S(1)} %pad_maximum_fusion.8.scal_ref, s32[8]{0:T(128)S(1)} %fusion.6.sel_ref, ...), custom_call_target="tpu_custom_call" | custom-call | flops 13107200 | bytes 8192000 | tf_op jit(solution)/shard_map/pallas_call | solution.py:103
  (98 shorter events, 30.7 us)
Async XLA Ops:
  0.6 23.6 %copy-start = (f32[2,2,8,5120]{3,2,1,0:T(8,128)S(1)}, f32[2,2,8,5120]{3,2,1,0:T(8,128)}, u32[]{:S(2)}) copy-start(f32[2,2,8,5120]{3,2,1,0:T(8,128)} %x_ref.1) | copy-start | bytes 1966084
  0.6 26.6 %copy-start.21 = (s32[16]{0:T(128)S(1)}, s32[16]{0:T(128)}, u32[]{:S(2)}) copy-start(s32[16]{0:T(128)} %param.15) | copy-start | bytes 196
  3.2 80.6 %collective-permute-start.2 = (f32[4,5120]{1,0:T(4,128)}, f32[4,5120]{1,0:T(4,128)S(1)}, u32[]{:S(2)}, u32[]{:S(2)}) collective-permute-start(f32[4,5120]{1,0:T(4,128)} %reshape_squeeze.12), channel_id=1, source_target_pairs={{0,1},{1,2},{2,3},{3,4},{4,5},{5,6},{6,7},{7,8},{8,9},{9,10},{10,1... | collective-permute-start | bytes 245768 | tf_op jit(solution)/shard_map/ppermute | solution.py:21
  7.7 76.1 %collective-permute-start.3 = (f32[4,5120]{1,0:T(4,128)}, f32[4,5120]{1,0:T(4,128)S(1)}, u32[]{:S(2)}, u32[]{:S(2)}) collective-permute-start(f32[4,5120]{1,0:T(4,128)} %reshape_squeeze.13), channel_id=1, source_target_pairs={{1,0},{2,1},{3,2},{4,3},{5,4},{6,5},{7,6},{8,7},{9,8},{10,9},{11,1... | collective-permute-start | bytes 245768 | tf_op jit(solution)/shard_map/ppermute | solution.py:21
  18.6 23.3 %collective-permute-start = (f32[2,2,1,5120]{3,2,1,0:T(1,128)S(1)}, f32[2,2,1,5120]{3,2,1,0:T(1,128)S(1)}, u32[]{:S(2)}, u32[]{:S(2)}) collective-permute-start(f32[2,2,1,5120]{3,2,1,0:T(1,128)S(1)} %get-tuple-element.58), channel_id=1, source_target_pairs={{0,1},{1,2},{2,3},{3,4},{4,5},{5,6},{6,7},{7,8},{8,9},{9,10},{10,1... | collective-permute-start | bytes 245768 | tf_op jit(solution)/shard_map/ppermute | solution.py:21
  22.3 22.7 %collective-permute-start.1 = (f32[2,2,1,5120]{3,2,1,0:T(1,128)S(1)}, f32[2,2,1,5120]{3,2,1,0:T(1,128)S(1)}, u32[]{:S(2)}, u32[]{:S(2)}) collective-permute-start(f32[2,2,1,5120]{3,2,1,0:T(1,128)S(1)} %get-tuple-element.59), channel_id=1, source_target_pairs={{1,0},{2,1},{3,2},{4,3},{5,4},{6,5},{7,6},{8,7},{9,8},{10,9},{11,1... | collective-permute-start | bytes 245768 | tf_op jit(solution)/shard_map/ppermute | solution.py:21
  25.1 20.5 %collective-permute-start.5 = (f32[16,5120]{1,0:T(8,128)}, f32[16,5120]{1,0:T(8,128)}, u32[]{:S(2)}, u32[]{:S(2)}) collective-permute-start(f32[16,5120]{1,0:T(8,128)} %get-tuple-element.54), channel_id=1, source_target_pairs={{16,0},{32,16},{48,32},{64,48},{80,64},{96,80},{112,96},{17,1},{33... | collective-permute-start | bytes 983048 | tf_op jit(solution)/shard_map/ppermute | solution.py:21
  29.7 10.6 %copy-start.19 = (f32[2,3]{1,0:T(2,128)S(1)}, f32[2,3]{1,0:T(2,128)}, u32[]{:S(2)}) copy-start(f32[2,3]{1,0:T(2,128)} %param.14) | copy-start | bytes 76
  29.7 10.6 %copy-start.20 = (f32[2,3,2]{1,2,0:T(2,128)S(1)}, f32[2,3,2]{1,2,0:T(2,128)}, u32[]{:S(2)}) copy-start(f32[2,3,2]{1,2,0:T(2,128)} %param.13) | copy-start | bytes 148
  29.7 45.4 %all-to-all-start = ((f32[8,16,5120]{2,1,0:T(8,128)}), f32[8,16,5120]{2,1,0:T(8,128)}, u32[]{:S(2)}, u32[]{:S(2)}) async-start(f32[8,16,5120]{2,1,0:T(8,128)} %gather_fusion), calls=%async_computation | async-start | bytes 5242880 | tf_op jit(solution)/shard_map/all_to_all | solution.py:175
  41.9 32.5 %collective-permute-start.4 = (f32[16,5120]{1,0:T(8,128)}, f32[16,5120]{1,0:T(8,128)S(1)}, u32[]{:S(2)}, u32[]{:S(2)}) collective-permute-start(f32[16,5120]{1,0:T(8,128)} %get-tuple-element.55), channel_id=1, source_target_pairs={{0,16},{16,32},{32,48},{48,64},{64,80},{80,96},{96,112},{1,17},{17... | collective-permute-start | bytes 983048 | tf_op jit(solution)/shard_map/ppermute | solution.py:21
  45.3 41.0 %copy-start.3 = (f32[2,2,8,5120]{3,2,1,0:T(8,128)S(1)}, f32[2,2,8,5120]{3,2,1,0:T(8,128)}, u32[]{:S(2)}) copy-start(f32[2,2,8,5120]{3,2,1,0:T(8,128)} %v_ref.1) | copy-start | bytes 1966084
  45.6 40.7 %copy-start.1 = (f32[5,2,8,5120]{3,2,1,0:T(8,128)}, f32[5,2,8,5120]{3,2,1,0:T(8,128)S(1)}, u32[]{:S(2)}) copy-start(f32[5,2,8,5120]{3,2,1,0:T(8,128)S(1)} %bitcast_dynamic-update-slice_fusion.k_ref) | copy-start | bytes 4915204
  78.6 7.7 %collective-permute-start.6 = (f32[8,5120]{1,0:T(8,128)}, f32[8,5120]{1,0:T(8,128)S(1)}, u32[]{:S(2)}, u32[]{:S(2)}) collective-permute-start(f32[8,5120]{1,0:T(8,128)} %concatenate.25), channel_id=1, source_target_pairs={{1,0},{2,1},{3,2},{4,3},{5,4},{6,5},{7,6},{8,7},{9,8},{10,9},{11,1... | collective-permute-start | bytes 491528 | tf_op jit(solution)/shard_map/ppermute | solution.py:21
  94.7 21.9 %collective-permute-start.9 = (f32[16,5120]{1,0:T(8,128)}, f32[16,5120]{1,0:T(8,128)S(1)}, u32[]{:S(2)}, u32[]{:S(2)}) collective-permute-start(f32[16,5120]{1,0:T(8,128)} %get-tuple-element.23), channel_id=1, source_target_pairs={{0,16},{16,32},{32,48},{48,64},{64,80},{80,96},{96,112},{1,17},{17... | collective-permute-start | bytes 983048 | tf_op jit(solution)/shard_map/ppermute | solution.py:21
  101.1 8.8 %copy-start.18 = (f32[4,5120]{1,0:T(4,128)S(1)}, f32[4,5120]{1,0:T(4,128)}, u32[]{:S(2)}) copy-start(f32[4,5120]{1,0:T(4,128)} %copy-done.17) | copy-start | bytes 245764
  101.1 13.6 %copy-start.16 = (f32[16,5120]{1,0:T(8,128)S(1)}, f32[16,5120]{1,0:T(8,128)}, u32[]{:S(2)}) copy-start(f32[16,5120]{1,0:T(8,128)} %copy-done.15) | copy-start | bytes 983044
  101.1 52.4 %all-to-all-start.1 = ((f32[8,16,5120]{2,1,0:T(8,128)}), f32[8,16,5120]{2,1,0:T(8,128)}, u32[]{:S(2)}, u32[]{:S(2)}) async-start(f32[8,16,5120]{2,1,0:T(8,128)} %get-tuple-element.20), calls=%async_computation.1 | async-start | bytes 5242880 | tf_op jit(solution)/shard_map/all_to_all | solution.py:175
  109.9 51.8 %copy-start.5 = (f32[2,2,8,5120]{3,2,1,0:T(8,128)S(1)}, f32[2,2,8,5120]{3,2,1,0:T(8,128)}, u32[]{:S(2)}) copy-start(f32[2,2,8,5120]{3,2,1,0:T(8,128)} %copy-done.4) | copy-start | bytes 1966084
  109.9 51.8 %copy-start.7 = (f32[2,2,8,5120]{3,2,1,0:T(8,128)S(1)}, f32[2,2,8,5120]{3,2,1,0:T(8,128)}, u32[]{:S(2)}) copy-start(f32[2,2,8,5120]{3,2,1,0:T(8,128)} %copy-done.6) | copy-start | bytes 1966084
  109.9 49.3 %collective-permute-start.7 = (f32[4,5120]{1,0:T(4,128)S(1)}, f32[4,5120]{1,0:T(4,128)S(1)}, u32[]{:S(2)}, u32[]{:S(2)}) collective-permute-start(f32[4,5120]{1,0:T(4,128)S(1)} %copy-done.18), channel_id=1, source_target_pairs={{0,1},{1,2},{2,3},{3,4},{4,5},{5,6},{6,7},{7,8},{8,9},{9,10},{10,1... | collective-permute-start | bytes 245768 | tf_op jit(solution)/shard_map/ppermute | solution.py:21
  112.7 46.4 %collective-permute-start.8 = (f32[4,5120]{1,0:T(4,128)S(1)}, f32[4,5120]{1,0:T(4,128)S(1)}, u32[]{:S(2)}, u32[]{:S(2)}) collective-permute-start(f32[4,5120]{1,0:T(4,128)S(1)} %get-tuple-element.22), channel_id=1, source_target_pairs={{1,0},{2,1},{3,2},{4,3},{5,4},{6,5},{7,6},{8,7},{9,8},{10,9},{11,1... | collective-permute-start | bytes 245768 | tf_op jit(solution)/shard_map/ppermute | solution.py:21
  114.7 38.8 %collective-permute-start.10 = (f32[16,5120]{1,0:T(8,128)S(1)}, f32[16,5120]{1,0:T(8,128)S(1)}, u32[]{:S(2)}, u32[]{:S(2)}) collective-permute-start(f32[16,5120]{1,0:T(8,128)S(1)} %copy-done.16), channel_id=1, source_target_pairs={{16,0},{32,16},{48,32},{64,48},{80,64},{96,80},{112,96},{17,1},{33... | collective-permute-start | bytes 983048 | tf_op jit(solution)/shard_map/ppermute | solution.py:21
  153.5 8.2 %copy-start.12 = (f32[16,5120]{1,0:T(8,128)}, f32[16,5120]{1,0:T(8,128)S(1)}, u32[]{:S(2)}) copy-start(f32[16,5120]{1,0:T(8,128)S(1)} %collective-permute-done.10.nextf_ref) | copy-start | bytes 983044
  155.1 6.6 %collective-permute-start.11 = (f32[8,5120]{1,0:T(8,128)S(1)}, f32[8,5120]{1,0:T(8,128)S(1)}, u32[]{:S(2)}, u32[]{:S(2)}) collective-permute-start(f32[8,5120]{1,0:T(8,128)S(1)} %concatenate.26), channel_id=1, source_target_pairs={{1,0},{2,1},{3,2},{4,3},{5,4},{6,5},{7,6},{8,7},{9,8},{10,9},{11,1... | collective-permute-start | bytes 491528 | tf_op jit(solution)/shard_map/ppermute | solution.py:21
  168.7 27.5 %collective-permute-start.14 = (f32[16,5120]{1,0:T(8,128)}, f32[16,5120]{1,0:T(8,128)}, u32[]{:S(2)}, u32[]{:S(2)}) collective-permute-start(f32[16,5120]{1,0:T(8,128)} %get-tuple-element.30), channel_id=1, source_target_pairs={{0,16},{16,32},{32,48},{48,64},{64,80},{80,96},{96,112},{1,17},{17... | collective-permute-start | bytes 983048 | tf_op jit(solution)/shard_map/ppermute | solution.py:21
  170.6 53.6 %all-to-all-start.2 = ((f32[8,16,5120]{2,1,0:T(8,128)}), f32[8,16,5120]{2,1,0:T(8,128)}, u32[]{:S(2)}, u32[]{:S(2)}) async-start(f32[8,16,5120]{2,1,0:T(8,128)} %get-tuple-element.27), calls=%async_computation.2 | async-start | bytes 5242880 | tf_op jit(solution)/shard_map/all_to_all | solution.py:175
  178.6 56.2 %copy-start.2 = (f32[5,2,8,5120]{3,2,1,0:T(8,128)S(1)}, f32[5,2,8,5120]{3,2,1,0:T(8,128)}, u32[]{:S(2)}) copy-start(f32[5,2,8,5120]{3,2,1,0:T(8,128)} %copy-done.1) | copy-start | bytes 4915204
  178.6 52.8 %collective-permute-start.12 = (f32[4,5120]{1,0:T(4,128)}, f32[4,5120]{1,0:T(4,128)S(1)}, u32[]{:S(2)}, u32[]{:S(2)}) collective-permute-start(f32[4,5120]{1,0:T(4,128)} %get-tuple-element.28), channel_id=1, source_target_pairs={{0,1},{1,2},{2,3},{3,4},{4,5},{5,6},{6,7},{7,8},{8,9},{9,10},{10,1... | collective-permute-start | bytes 245768 | tf_op jit(solution)/shard_map/ppermute | solution.py:21
  181.0 50.4 %collective-permute-start.13 = (f32[4,5120]{1,0:T(4,128)S(1)}, f32[4,5120]{1,0:T(4,128)S(1)}, u32[]{:S(2)}, u32[]{:S(2)}) collective-permute-start(f32[4,5120]{1,0:T(4,128)S(1)} %get-tuple-element.29), channel_id=1, source_target_pairs={{1,0},{2,1},{3,2},{4,3},{5,4},{6,5},{7,6},{8,7},{9,8},{10,9},{11,1... | collective-permute-start | bytes 245768 | tf_op jit(solution)/shard_map/ppermute | solution.py:21
  183.0 39.8 %collective-permute-start.15 = (f32[16,5120]{1,0:T(8,128)}, f32[16,5120]{1,0:T(8,128)S(1)}, u32[]{:S(2)}, u32[]{:S(2)}) collective-permute-start(f32[16,5120]{1,0:T(8,128)} %copy-done.14), channel_id=1, source_target_pairs={{16,0},{32,16},{48,32},{64,48},{80,64},{96,80},{112,96},{17,1},{33... | collective-permute-start | bytes 983048 | tf_op jit(solution)/shard_map/ppermute | solution.py:21
  227.8 7.0 %collective-permute-start.16 = (f32[8,5120]{1,0:T(8,128)}, f32[8,5120]{1,0:T(8,128)S(1)}, u32[]{:S(2)}, u32[]{:S(2)}) collective-permute-start(f32[8,5120]{1,0:T(8,128)} %concatenate.27), channel_id=1, source_target_pairs={{1,0},{2,1},{3,2},{4,3},{5,4},{6,5},{7,6},{8,7},{9,8},{10,9},{11,1... | collective-permute-start | bytes 491528 | tf_op jit(solution)/shard_map/ppermute | solution.py:21
  (10 other events, 20.8 us)

commit v11 on v10

--- a/solution.py
+++ b/solution.py
@@ -118,6 +118,24 @@
     )(scal, sel, x, v, kst, alive, part, up, down, prevf, nextf, below)
 
 
+def send_kernel(sel_ref, x_ref, send_ref):
+    ncomp, R = x_ref.shape[1], x_ref.shape[2]
+    for d in range(send_ref.shape[0]):
+        for c in range(ncomp):
+            send_ref[d, pl.ds(c * R, R), :] = x_ref[sel_ref[d], c]
+
+
+def first_send(sel, x):
+    nb = sel.shape[0]
+    return pl.pallas_call(
+        send_kernel,
+        out_shape=jax.ShapeDtypeStruct((nb, x.shape[1] * x.shape[2], x.shape[3]), x.dtype),
+        in_specs=[pl.BlockSpec(memory_space=pltpu.SMEM), pl.BlockSpec(memory_space=pltpu.VMEM)],
+        out_specs=pl.BlockSpec(memory_space=pltpu.VMEM),
+        cost_estimate=pl.CostEstimate(flops=0, bytes_accessed=4 * (x.size + nb * x[0].size), transcendentals=0),
+    )(sel, x)
+
+
 def body(disp, vel, stiff_class, valid, class_table, warp, spring_z, skip_partner):
     local_count = disp.shape[0]
     block_count = lax.axis_size("gz")
@@ -166,7 +184,7 @@
     field = disp
     velocity = vel
     plane = ncomp * disp.shape[2]
-    send = jnp.take(field.reshape(local_count, plane, cols), send_sel, axis=0, mode="clip")
+    send = first_send(send_sel, field)
     last_face = field[-1].reshape(plane, cols)
     first_face = field[0].reshape(plane, cols)
     top_rows = field[:, :, 0].reshape(local_count * ncomp, cols)

time: 242 us -> 239 us (0.988)
  local copies, waits for them, and re-layouts: 31.2 us -> 27.5 us
    pallas_call x0 -> x1, Pallas kernels: none -> 2.77 us  [first_send(): pl.pallas_call(send_kernel, out_shape=jax.ShapeDtypeStruct((nb, x.shape[1...]
  transfers between devices with their start and end apart: 20 -> 20, of which waited for: 7 -> 7; matrix products, arithmetic and copies ran while one was open for 13% -> 12% of each run, Pallas kernels for 0% -> 1%
where the time goes in v11:
time: 239 us; the launch traced here: 238 us
  waiting for transfers between devices  109 us (46%)
  starting transfers between devices  71.1 us (30%)
  local copies, waits for them, and re-layouts  27.5 us (12%)
  Pallas kernels  17.9 us (7%)
  other arithmetic  7.52 us (3%)
  between operations  4.98 us (2%)
    ppermute x17, waiting for transfers between devices, shift_rows(): return lax.ppermute(block, axis, pairs)  109 us
    ppermute x17, starting transfers between devices, shift_rows(): return lax.ppermute(block, axis, pairs)  47.1 us
    all_to_all x3, starting transfers between devices, body(): recv = lax.all_to_all(send, 'gz', 0, 0, tiled=True)  24.1 us
    pallas_call x3, Pallas kernels, update(): pl.pallas_call(update_kernel, out_shape=(jax.ShapeDtypeStruct(x.shape, x....  15.2 us
    another operation x1, other arithmetic, body(): stiff = jnp.stack([kappa, alive])  5.2 us
    squeeze x3, local copies, waits for them, and re-layouts, body(): lax.dynamic_slice(recv, (src_block[l], c * rows, 0), (1, 1, cols))[0]  4.92 us
    unnamed x49, local copies, waits for them, and re-layouts  4.89 us
  transfers between devices with their start and end apart: 20, of which 7 were waited for; matrix products, arithmetic and copies ran while one was open for 12% of the time, Pallas kernels for 1%

profile of v11, /device:TPU:105, one launch (start us, length us, event | category | flops | bytes accessed | tf_op | source)
XLA Modules:
  0.0 237.8 jit_solution(8518319618373192494)
XLA Ops:
  3.2 3.8 %collective-permute-start.2 = (f32[4,5120]{1,0:T(4,128)}, f32[4,5120]{1,0:T(4,128)S(1)}, u32[]{:S(2)}, u32[]{:S(2)}) collective-permute-start(f32[4,5120]{1,0:T(4,128)} %reshape_squeeze.12), channel_id=1, source_target_pairs={{0,1},{1,2},{2,3},{3,4},{4,5},{5,6},{6,7},{7,8},{8,9},{9,10},{10,1... | collective-permute-start | bytes 245768 | tf_op jit(solution)/shard_map/ppermute | solution.py:21
  7.7 1.9 collective-permute-start.3
  12.3 5.2 %multiply_bitcast_fusion = f32[1,2,8,5120]{3,2,1,0:T(8,128)S(1)} fusion(s32[2,8,5120]{2,1,0:T(8,128)S(1)} %copy-done.18, f32[]{:T(128)} %bitcast.7, f32[]{:T(128)} %bitcast.6, f32[]{:T(128)} %bitcast.5, f32[]{:T(128)} %bitcast.4, f32[]{:T(128)} %bitcast.3, f32[]{:T(128)} %bitcast.2, f32[]{:T(128)} %bitcast.1, f32[]{:T(128)} %bitcast, ...), kind=kLoop, calls=%fused_computation.17 | loop fusion | flops 1474560 | bytes 983072 | tf_op jit(solution)/shard_map/stack | solution.py:149
  17.6 3.6 %collective-permute-start = (f32[2,2,1,5120]{3,2,1,0:T(1,128)S(1)}, f32[2,2,1,5120]{3,2,1,0:T(1,128)S(1)}, u32[]{:S(2)}, u32[]{:S(2)}) collective-permute-start(f32[2,2,1,5120]{3,2,1,0:T(1,128)S(1)} %get-tuple-element.58), channel_id=1, source_target_pairs={{0,1},{1,2},{2,3},{3,4},{4,5},{5,6},{6,7},{7,8},{8,9},{9,10},{10,1... | collective-permute-start | bytes 245768 | tf_op jit(solution)/shard_map/ppermute | solution.py:21
  21.3 1.9 collective-permute-start.1
  24.1 2.2 collective-permute-start.5
  27.1 2.8 %shard_map.95 = f32[8,16,5120]{2,1,0:T(8,128)} custom-call(s32[8]{0:T(128)} %fusion.6.sel_ref, f32[2,2,8,5120]{3,2,1,0:T(8,128)} %x_ref.3), custom_call_target="tpu_custom_call" | custom-call | bytes 3276800 | tf_op jit(solution)/shard_map/pallas_call | solution.py:130
  29.8 7.3 %all-to-all-start = ((f32[8,16,5120]{2,1,0:T(8,128)}), f32[8,16,5120]{2,1,0:T(8,128)}, u32[]{:S(2)}, u32[]{:S(2)}) async-start(f32[8,16,5120]{2,1,0:T(8,128)} %shard_map.95), calls=%async_computation | async-start | bytes 5242880 | tf_op jit(solution)/shard_map/all_to_all | solution.py:193
  42.0 3.1 %collective-permute-start.4 = (f32[16,5120]{1,0:T(8,128)}, f32[16,5120]{1,0:T(8,128)S(1)}, u32[]{:S(2)}, u32[]{:S(2)}) collective-permute-start(f32[16,5120]{1,0:T(8,128)} %get-tuple-element.55), channel_id=1, source_target_pairs={{0,16},{16,32},{32,48},{48,64},{64,80},{80,96},{96,112},{1,17},{17... | collective-permute-start | bytes 983048 | tf_op jit(solution)/shard_map/ppermute | solution.py:21
  47.3 27.2 %collective-permute-done.4.prevf_ref = f32[16,5120]{1,0:T(8,128)S(1)} collective-permute-done((f32[16,5120]{1,0:T(8,128)}, f32[16,5120]{1,0:T(8,128)S(1)}, u32[]{:S(2)}, u32[]{:S(2)}) %collective-permute-start.4) | collective-permute-done | bytes 327712 | tf_op jit(solution)/shard_map/ppermute | solution.py:21
  78.7 4.0 %collective-permute-start.6 = (f32[8,5120]{1,0:T(8,128)}, f32[8,5120]{1,0:T(8,128)S(1)}, u32[]{:S(2)}, u32[]{:S(2)}) collective-permute-start(f32[8,5120]{1,0:T(8,128)} %concatenate.25), channel_id=1, source_target_pairs={{1,0},{2,1},{3,2},{4,3},{5,4},{6,5},{7,6},{8,7},{9,8},{10,9},{11,1... | collective-permute-start | bytes 491528 | tf_op jit(solution)/shard_map/ppermute | solution.py:21
  83.9 2.5 %collective-permute-done.6.below_ref = f32[8,5120]{1,0:T(8,128)S(1)} collective-permute-done((f32[8,5120]{1,0:T(8,128)}, f32[8,5120]{1,0:T(8,128)S(1)}, u32[]{:S(2)}, u32[]{:S(2)}) %collective-permute-start.6) | collective-permute-done | bytes 163872 | tf_op jit(solution)/shard_map/ppermute | solution.py:21
  86.4 5.1 %shard_map.96 = (f32[2,2,8,5120]{3,2,1,0:T(8,128)S(1)}, f32[2,2,8,5120]{3,2,1,0:T(8,128)S(1)}, f32[8,16,5120]{2,1,0:T(8,128)}, f32[16,5120]{1,0:T(8,128)}, f32[1...) custom-call(f32[2,9]{1,0:T(2,128)S(1)} %pad_maximum_fusion.8.scal_ref, s32[8]{0:T(128)S(1)} %copy-done.11, ...), custom_call_target="tpu_custom_call" | custom-call | flops 13107200 | bytes 8192000 | tf_op jit(solution)/shard_map/pallas_call | solution.py:103
  92.9 6.4 %collective-permute-start.9 = (f32[16,5120]{1,0:T(8,128)}, f32[16,5120]{1,0:T(8,128)S(1)}, u32[]{:S(2)}, u32[]{:S(2)}) collective-permute-start(f32[16,5120]{1,0:T(8,128)} %get-tuple-element.23), channel_id=1, source_target_pairs={{0,16},{16,32},{32,48},{48,64},{64,80},{80,96},{96,112},{1,17},{17... | collective-permute-start | bytes 983048 | tf_op jit(solution)/shard_map/ppermute | solution.py:21
  99.3 8.8 %all-to-all-start.1 = ((f32[8,16,5120]{2,1,0:T(8,128)}), f32[8,16,5120]{2,1,0:T(8,128)}, u32[]{:S(2)}, u32[]{:S(2)}) async-start(f32[8,16,5120]{2,1,0:T(8,128)} %get-tuple-element.20), calls=%async_computation.1 | async-start | bytes 5242880 | tf_op jit(solution)/shard_map/all_to_all | solution.py:193
  108.1 2.7 %collective-permute-start.7 = (f32[4,5120]{1,0:T(4,128)S(1)}, f32[4,5120]{1,0:T(4,128)S(1)}, u32[]{:S(2)}, u32[]{:S(2)}) collective-permute-start(f32[4,5120]{1,0:T(4,128)S(1)} %copy-done.16), channel_id=1, source_target_pairs={{0,1},{1,2},{2,3},{3,4},{4,5},{5,6},{6,7},{7,8},{8,9},{9,10},{10,1... | collective-permute-start | bytes 245768 | tf_op jit(solution)/shard_map/ppermute | solution.py:21
  110.8 1.9 collective-permute-start.8
  112.8 1.9 collective-permute-start.10
  114.7 37.0 %collective-permute-done.10.nextf_ref = f32[16,5120]{1,0:T(8,128)S(1)} collective-permute-done((f32[16,5120]{1,0:T(8,128)S(1)}, f32[16,5120]{1,0:T(8,128)S(1)}, u32[]{:S(2)}, u32[]{:S(2)}) %collective-permute-start.10) | collective-permute-done | bytes 327712 | tf_op jit(solution)/shard_map/ppermute | solution.py:21
  153.3 2.9 %collective-permute-start.11 = (f32[8,5120]{1,0:T(8,128)S(1)}, f32[8,5120]{1,0:T(8,128)S(1)}, u32[]{:S(2)}, u32[]{:S(2)}) collective-permute-start(f32[8,5120]{1,0:T(8,128)S(1)} %concatenate.26), channel_id=1, source_target_pairs={{1,0},{2,1},{3,2},{4,3},{5,4},{6,5},{7,6},{8,7},{9,8},{10,9},{11,1... | collective-permute-start | bytes 491528 | tf_op jit(solution)/shard_map/ppermute | solution.py:21
  157.4 2.5 %collective-permute-done.11.below_ref = f32[8,5120]{1,0:T(8,128)S(1)} collective-permute-done((f32[8,5120]{1,0:T(8,128)S(1)}, f32[8,5120]{1,0:T(8,128)S(1)}, u32[]{:S(2)}, u32[]{:S(2)}) %collective-permute-start.11) | collective-permute-done | bytes 163872 | tf_op jit(solution)/shard_map/ppermute | solution.py:21
  160.9 5.0 %shard_map.97 = (f32[2,2,8,5120]{3,2,1,0:T(8,128)S(1)}, f32[2,2,8,5120]{3,2,1,0:T(8,128)S(1)}, f32[8,16,5120]{2,1,0:T(8,128)}, f32[16,5120]{1,0:T(8,128)}, f32[1...) custom-call(f32[2,9]{1,0:T(2,128)S(1)} %pad_maximum_fusion.8.scal_ref, s32[8]{0:T(128)S(1)} %copy-done.11, ...), custom_call_target="tpu_custom_call" | custom-call | flops 13107200 | bytes 8192000 | tf_op jit(solution)/shard_map/pallas_call | solution.py:103
  166.7 1.9 collective-permute-start.14
  168.6 8.0 %all-to-all-start.2 = ((f32[8,16,5120]{2,1,0:T(8,128)}), f32[8,16,5120]{2,1,0:T(8,128)}, u32[]{:S(2)}, u32[]{:S(2)}) async-start(f32[8,16,5120]{2,1,0:T(8,128)} %get-tuple-element.27), calls=%async_computation.2 | async-start | bytes 5242880 | tf_op jit(solution)/shard_map/all_to_all | solution.py:193
  176.5 2.3 collective-permute-start.12
  178.8 2.0 collective-permute-start.13
  180.9 2.2 collective-permute-start.15
  183.1 11.1 %collective-permute-done.14.prevf_ref = f32[16,5120]{1,0:T(8,128)} collective-permute-done((f32[16,5120]{1,0:T(8,128)}, f32[16,5120]{1,0:T(8,128)}, u32[]{:S(2)}, u32[]{:S(2)}) %collective-permute-start.14) | collective-permute-done | bytes 327712 | tf_op jit(solution)/shard_map/ppermute | solution.py:21
  195.7 25.1 %collective-permute-done.15.nextf_ref = f32[16,5120]{1,0:T(8,128)S(1)} collective-permute-done((f32[16,5120]{1,0:T(8,128)}, f32[16,5120]{1,0:T(8,128)S(1)}, u32[]{:S(2)}, u32[]{:S(2)}) %collective-permute-start.15) | collective-permute-done | bytes 327712 | tf_op jit(solution)/shard_map/ppermute | solution.py:21
  225.8 2.4 %collective-permute-start.16 = (f32[8,5120]{1,0:T(8,128)}, f32[8,5120]{1,0:T(8,128)S(1)}, u32[]{:S(2)}, u32[]{:S(2)}) collective-permute-start(f32[8,5120]{1,0:T(8,128)} %concatenate.27), channel_id=1, source_target_pairs={{1,0},{2,1},{3,2},{4,3},{5,4},{6,5},{7,6},{8,7},{9,8},{10,9},{11,1... | collective-permute-start | bytes 491528 | tf_op jit(solution)/shard_map/ppermute | solution.py:21
  229.4 3.3 %collective-permute-done.16.below_ref = f32[8,5120]{1,0:T(8,128)S(1)} collective-permute-done((f32[8,5120]{1,0:T(8,128)}, f32[8,5120]{1,0:T(8,128)S(1)}, u32[]{:S(2)}, u32[]{:S(2)}) %collective-permute-start.16) | collective-permute-done | bytes 163872 | tf_op jit(solution)/shard_map/ppermute | solution.py:21
  232.7 5.0 %shard_map.98 = (f32[2,2,8,5120]{3,2,1,0:T(8,128)}, f32[2,2,8,5120]{3,2,1,0:T(8,128)}, f32[8,16,5120]{2,1,0:T(8,128)}, f32[16,5120]{1,0:T(8,128)}, f32[16,5120]{...) custom-call(f32[2,9]{1,0:T(2,128)S(1)} %pad_maximum_fusion.8.scal_ref, s32[8]{0:T(128)S(1)} %copy-done.11, ...), custom_call_target="tpu_custom_call" | custom-call | flops 13107200 | bytes 8192000 | tf_op jit(solution)/shard_map/pallas_call | solution.py:103
  (97 shorter events, 29.8 us)
Async XLA Ops:
  0.6 11.6 %copy-start.17 = (s32[2,8,5120]{2,1,0:T(8,128)S(1)}, s32[2,8,5120]{2,1,0:T(8,128)}, u32[]{:S(2)}) copy-start(s32[2,8,5120]{2,1,0:T(8,128)} %param.11) | copy-start | bytes 983044
  0.6 11.6 %copy-start.18 = (s32[2,8,5120]{2,1,0:T(8,128)S(1)}, s32[2,8,5120]{2,1,0:T(8,128)}, u32[]{:S(2)}) copy-start(s32[2,8,5120]{2,1,0:T(8,128)} %param.10) | copy-start | bytes 983044
  2.5 20.7 %copy-start.2 = (f32[2,2,8,5120]{3,2,1,0:T(8,128)S(1)}, f32[2,2,8,5120]{3,2,1,0:T(8,128)}, u32[]{:S(2)}) copy-start(f32[2,2,8,5120]{3,2,1,0:T(8,128)} %x_ref.3) | copy-start | bytes 1966084
  3.2 80.7 %collective-permute-start.2 = (f32[4,5120]{1,0:T(4,128)}, f32[4,5120]{1,0:T(4,128)S(1)}, u32[]{:S(2)}, u32[]{:S(2)}) collective-permute-start(f32[4,5120]{1,0:T(4,128)} %reshape_squeeze.12), channel_id=1, source_target_pairs={{0,1},{1,2},{2,3},{3,4},{4,5},{5,6},{6,7},{7,8},{8,9},{9,10},{10,1... | collective-permute-start | bytes 245768 | tf_op jit(solution)/shard_map/ppermute | solution.py:21
  7.7 76.2 %collective-permute-start.3 = (f32[4,5120]{1,0:T(4,128)}, f32[4,5120]{1,0:T(4,128)S(1)}, u32[]{:S(2)}, u32[]{:S(2)}) collective-permute-start(f32[4,5120]{1,0:T(4,128)} %reshape_squeeze.13), channel_id=1, source_target_pairs={{1,0},{2,1},{3,2},{4,3},{5,4},{6,5},{7,6},{8,7},{9,8},{10,9},{11,1... | collective-permute-start | bytes 245768 | tf_op jit(solution)/shard_map/ppermute | solution.py:21
  12.3 14.0 %copy-start.21 = (s32[16]{0:T(128)S(1)}, s32[16]{0:T(128)}, u32[]{:S(2)}) copy-start(s32[16]{0:T(128)} %param.15) | copy-start | bytes 196
  17.6 24.4 %collective-permute-start = (f32[2,2,1,5120]{3,2,1,0:T(1,128)S(1)}, f32[2,2,1,5120]{3,2,1,0:T(1,128)S(1)}, u32[]{:S(2)}, u32[]{:S(2)}) collective-permute-start(f32[2,2,1,5120]{3,2,1,0:T(1,128)S(1)} %get-tuple-element.58), channel_id=1, source_target_pairs={{0,1},{1,2},{2,3},{3,4},{4,5},{5,6},{6,7},{7,8},{8,9},{9,10},{10,1... | collective-permute-start | bytes 245768 | tf_op jit(solution)/shard_map/ppermute | solution.py:21
  21.3 23.8 %collective-permute-start.1 = (f32[2,2,1,5120]{3,2,1,0:T(1,128)S(1)}, f32[2,2,1,5120]{3,2,1,0:T(1,128)S(1)}, u32[]{:S(2)}, u32[]{:S(2)}) collective-permute-start(f32[2,2,1,5120]{3,2,1,0:T(1,128)S(1)} %get-tuple-element.59), channel_id=1, source_target_pairs={{1,0},{2,1},{3,2},{4,3},{5,4},{6,5},{7,6},{8,7},{9,8},{10,9},{11,1... | collective-permute-start | bytes 245768 | tf_op jit(solution)/shard_map/ppermute | solution.py:21
  24.1 21.7 %collective-permute-start.5 = (f32[16,5120]{1,0:T(8,128)}, f32[16,5120]{1,0:T(8,128)}, u32[]{:S(2)}, u32[]{:S(2)}) collective-permute-start(f32[16,5120]{1,0:T(8,128)} %get-tuple-element.54), channel_id=1, source_target_pairs={{16,0},{32,16},{48,32},{64,48},{80,64},{96,80},{112,96},{17,1},{33... | collective-permute-start | bytes 983048 | tf_op jit(solution)/shard_map/ppermute | solution.py:21
  29.8 10.6 %copy-start.19 = (f32[2,3]{1,0:T(2,128)S(1)}, f32[2,3]{1,0:T(2,128)}, u32[]{:S(2)}) copy-start(f32[2,3]{1,0:T(2,128)} %param.14) | copy-start | bytes 76
  29.8 10.6 %copy-start.20 = (f32[2,3,2]{1,2,0:T(2,128)S(1)}, f32[2,3,2]{1,2,0:T(2,128)}, u32[]{:S(2)}) copy-start(f32[2,3,2]{1,2,0:T(2,128)} %param.13) | copy-start | bytes 148
  29.8 45.4 %all-to-all-start = ((f32[8,16,5120]{2,1,0:T(8,128)}), f32[8,16,5120]{2,1,0:T(8,128)}, u32[]{:S(2)}, u32[]{:S(2)}) async-start(f32[8,16,5120]{2,1,0:T(8,128)} %shard_map.95), calls=%async_computation | async-start | bytes 5242880 | tf_op jit(solution)/shard_map/all_to_all | solution.py:193
  42.0 32.5 %collective-permute-start.4 = (f32[16,5120]{1,0:T(8,128)}, f32[16,5120]{1,0:T(8,128)S(1)}, u32[]{:S(2)}, u32[]{:S(2)}) collective-permute-start(f32[16,5120]{1,0:T(8,128)} %get-tuple-element.55), channel_id=1, source_target_pairs={{0,16},{16,32},{32,48},{48,64},{64,80},{80,96},{96,112},{1,17},{17... | collective-permute-start | bytes 983048 | tf_op jit(solution)/shard_map/ppermute | solution.py:21
  45.7 38.2 %copy-start = (f32[5,2,8,5120]{3,2,1,0:T(8,128)}, f32[5,2,8,5120]{3,2,1,0:T(8,128)S(1)}, u32[]{:S(2)}) copy-start(f32[5,2,8,5120]{3,2,1,0:T(8,128)S(1)} %bitcast_dynamic-update-slice_fusion.k_ref) | copy-start | bytes 4915204
  45.7 40.7 %copy-start.3 = (f32[2,2,8,5120]{3,2,1,0:T(8,128)S(1)}, f32[2,2,8,5120]{3,2,1,0:T(8,128)}, u32[]{:S(2)}) copy-start(f32[2,2,8,5120]{3,2,1,0:T(8,128)} %x_ref.3) | copy-start | bytes 1966084
  45.7 40.7 %copy-start.4 = (f32[2,2,8,5120]{3,2,1,0:T(8,128)S(1)}, f32[2,2,8,5120]{3,2,1,0:T(8,128)}, u32[]{:S(2)}) copy-start(f32[2,2,8,5120]{3,2,1,0:T(8,128)} %v_ref.1) | copy-start | bytes 1966084
  45.7 40.7 %copy-start.11 = (s32[8]{0:T(128)S(1)}, s32[8]{0:T(128)}, u32[]{:S(2)}) copy-start(s32[8]{0:T(128)} %fusion.6.sel_ref) | copy-start | bytes 100
  78.7 7.7 %collective-permute-start.6 = (f32[8,5120]{1,0:T(8,128)}, f32[8,5120]{1,0:T(8,128)S(1)}, u32[]{:S(2)}, u32[]{:S(2)}) collective-permute-start(f32[8,5120]{1,0:T(8,128)} %concatenate.25), channel_id=1, source_target_pairs={{1,0},{2,1},{3,2},{4,3},{5,4},{6,5},{7,6},{8,7},{9,8},{10,9},{11,1... | collective-permute-start | bytes 491528 | tf_op jit(solution)/shard_map/ppermute | solution.py:21
  92.9 21.8 %collective-permute-start.9 = (f32[16,5120]{1,0:T(8,128)}, f32[16,5120]{1,0:T(8,128)S(1)}, u32[]{:S(2)}, u32[]{:S(2)}) collective-permute-start(f32[16,5120]{1,0:T(8,128)} %get-tuple-element.23), channel_id=1, source_target_pairs={{0,16},{16,32},{32,48},{48,64},{64,80},{80,96},{96,112},{1,17},{17... | collective-permute-start | bytes 983048 | tf_op jit(solution)/shard_map/ppermute | solution.py:21
  99.3 13.4 %copy-start.14 = (f32[16,5120]{1,0:T(8,128)S(1)}, f32[16,5120]{1,0:T(8,128)}, u32[]{:S(2)}) copy-start(f32[16,5120]{1,0:T(8,128)} %copy-done.13) | copy-start | bytes 983044
  99.3 52.4 %all-to-all-start.1 = ((f32[8,16,5120]{2,1,0:T(8,128)}), f32[8,16,5120]{2,1,0:T(8,128)}, u32[]{:S(2)}, u32[]{:S(2)}) async-start(f32[8,16,5120]{2,1,0:T(8,128)} %get-tuple-element.20), calls=%async_computation.1 | async-start | bytes 5242880 | tf_op jit(solution)/shard_map/all_to_all | solution.py:193
  108.1 49.3 %collective-permute-start.7 = (f32[4,5120]{1,0:T(4,128)S(1)}, f32[4,5120]{1,0:T(4,128)S(1)}, u32[]{:S(2)}, u32[]{:S(2)}) collective-permute-start(f32[4,5120]{1,0:T(4,128)S(1)} %copy-done.16), channel_id=1, source_target_pairs={{0,1},{1,2},{2,3},{3,4},{4,5},{5,6},{6,7},{7,8},{8,9},{9,10},{10,1... | collective-permute-start | bytes 245768 | tf_op jit(solution)/shard_map/ppermute | solution.py:21
  110.8 46.6 %collective-permute-start.8 = (f32[4,5120]{1,0:T(4,128)S(1)}, f32[4,5120]{1,0:T(4,128)S(1)}, u32[]{:S(2)}, u32[]{:S(2)}) collective-permute-start(f32[4,5120]{1,0:T(4,128)S(1)} %get-tuple-element.22), channel_id=1, source_target_pairs={{1,0},{2,1},{3,2},{4,3},{5,4},{6,5},{7,6},{8,7},{9,8},{10,9},{11,1... | collective-permute-start | bytes 245768 | tf_op jit(solution)/shard_map/ppermute | solution.py:21
  112.8 39.0 %collective-permute-start.10 = (f32[16,5120]{1,0:T(8,128)S(1)}, f32[16,5120]{1,0:T(8,128)S(1)}, u32[]{:S(2)}, u32[]{:S(2)}) collective-permute-start(f32[16,5120]{1,0:T(8,128)S(1)} %copy-done.14), channel_id=1, source_target_pairs={{16,0},{32,16},{48,32},{64,48},{80,64},{96,80},{112,96},{17,1},{33... | collective-permute-start | bytes 983048 | tf_op jit(solution)/shard_map/ppermute | solution.py:21
  153.3 6.6 %collective-permute-start.11 = (f32[8,5120]{1,0:T(8,128)S(1)}, f32[8,5120]{1,0:T(8,128)S(1)}, u32[]{:S(2)}, u32[]{:S(2)}) collective-permute-start(f32[8,5120]{1,0:T(8,128)S(1)} %concatenate.26), channel_id=1, source_target_pairs={{1,0},{2,1},{3,2},{4,3},{5,4},{6,5},{7,6},{8,7},{9,8},{10,9},{11,1... | collective-permute-start | bytes 491528 | tf_op jit(solution)/shard_map/ppermute | solution.py:21
  166.7 27.5 %collective-permute-start.14 = (f32[16,5120]{1,0:T(8,128)}, f32[16,5120]{1,0:T(8,128)}, u32[]{:S(2)}, u32[]{:S(2)}) collective-permute-start(f32[16,5120]{1,0:T(8,128)} %get-tuple-element.30), channel_id=1, source_target_pairs={{0,16},{16,32},{32,48},{48,64},{64,80},{80,96},{96,112},{1,17},{17... | collective-permute-start | bytes 983048 | tf_op jit(solution)/shard_map/ppermute | solution.py:21
  168.6 53.6 %all-to-all-start.2 = ((f32[8,16,5120]{2,1,0:T(8,128)}), f32[8,16,5120]{2,1,0:T(8,128)}, u32[]{:S(2)}, u32[]{:S(2)}) async-start(f32[8,16,5120]{2,1,0:T(8,128)} %get-tuple-element.27), calls=%async_computation.2 | async-start | bytes 5242880 | tf_op jit(solution)/shard_map/all_to_all | solution.py:193
  176.5 52.8 %collective-permute-start.12 = (f32[4,5120]{1,0:T(4,128)}, f32[4,5120]{1,0:T(4,128)S(1)}, u32[]{:S(2)}, u32[]{:S(2)}) collective-permute-start(f32[4,5120]{1,0:T(4,128)} %get-tuple-element.28), channel_id=1, source_target_pairs={{0,1},{1,2},{2,3},{3,4},{4,5},{5,6},{6,7},{7,8},{8,9},{9,10},{10,1... | collective-permute-start | bytes 245768 | tf_op jit(solution)/shard_map/ppermute | solution.py:21
  178.8 50.5 %collective-permute-start.13 = (f32[4,5120]{1,0:T(4,128)S(1)}, f32[4,5120]{1,0:T(4,128)S(1)}, u32[]{:S(2)}, u32[]{:S(2)}) collective-permute-start(f32[4,5120]{1,0:T(4,128)S(1)} %get-tuple-element.29), channel_id=1, source_target_pairs={{1,0},{2,1},{3,2},{4,3},{5,4},{6,5},{7,6},{8,7},{9,8},{10,9},{11,1... | collective-permute-start | bytes 245768 | tf_op jit(solution)/shard_map/ppermute | solution.py:21
  180.9 51.9 %copy-start.1 = (f32[5,2,8,5120]{3,2,1,0:T(8,128)S(1)}, f32[5,2,8,5120]{3,2,1,0:T(8,128)}, u32[]{:S(2)}) copy-start(f32[5,2,8,5120]{3,2,1,0:T(8,128)} %copy-done) | copy-start | bytes 4915204
  180.9 40.0 %collective-permute-start.15 = (f32[16,5120]{1,0:T(8,128)}, f32[16,5120]{1,0:T(8,128)S(1)}, u32[]{:S(2)}, u32[]{:S(2)}) collective-permute-start(f32[16,5120]{1,0:T(8,128)} %copy-done.12), channel_id=1, source_target_pairs={{16,0},{32,16},{48,32},{64,48},{80,64},{96,80},{112,96},{17,1},{33... | collective-permute-start | bytes 983048 | tf_op jit(solution)/shard_map/ppermute | solution.py:21
  225.8 7.0 %collective-permute-start.16 = (f32[8,5120]{1,0:T(8,128)}, f32[8,5120]{1,0:T(8,128)S(1)}, u32[]{:S(2)}, u32[]{:S(2)}) collective-permute-start(f32[8,5120]{1,0:T(8,128)} %concatenate.27), channel_id=1, source_target_pairs={{1,0},{2,1},{3,2},{4,3},{5,4},{6,5},{7,6},{8,7},{9,8},{10,9},{11,1... | collective-permute-start | bytes 491528 | tf_op jit(solution)/shard_map/ppermute | solution.py:21
  (10 other events, 36.2 us)

commit v12 on v11

--- a/solution.py
+++ b/solution.py
@@ -30,8 +30,9 @@
 
 
 def update_kernel(scal_ref, sel_ref, x_ref, v_ref, k_ref, alive_ref, part_ref, up_ref, down_ref,
-                  prevf_ref, nextf_ref, below_ref, xo_ref, vo_ref, send_ref, lastf_ref, firstf_ref,
-                  top_ref, bot_ref):
+                  prevf_ref, nextf_ref, below_ref, xo_ref, vo_ref, send_ref=None, lastf_ref=None,
+                  firstf_ref=None, top_ref=None, bot_ref=None):
+    tail = send_ref is None
     L, ncomp, R, C = x_ref.shape
     rows = lax.broadcasted_iota(jnp.int32, (R, C), 0)
     cols = lax.broadcasted_iota(jnp.int32, (R, C), 1)
@@ -84,18 +85,22 @@
             vo_ref[l, c] = vel
             new = x + STEP * vel
             xo_ref[l, c] = new
+            if tail:
+                continue
             if l == L - 1:
                 lastf_ref[pl.ds(c * R, R), :] = new
             if l == 0:
                 firstf_ref[pl.ds(c * R, R), :] = new
             top_ref[pl.ds(l * ncomp + c, 1), :] = new[0:1]
             bot_ref[pl.ds(l * ncomp + c, 1), :] = new[R - 1 : R]
+    if tail:
+        return
     for d in range(send_ref.shape[0]):
         for c in range(ncomp):
             send_ref[d, pl.ds(c * R, R), :] = xo_ref[sel_ref[d], c]
 
 
-def update(scal, sel, x, v, kst, alive, part, up, down, prevf, nextf, below):
+def update(tail, scal, sel, x, v, kst, alive, part, up, down, prevf, nextf, below):
     nb = sel.shape[0]
     vmem = pl.BlockSpec(memory_space=pltpu.VMEM)
     smem = pl.BlockSpec(memory_space=pltpu.SMEM)
@@ -105,6 +110,11 @@
         out_shape=(
             jax.ShapeDtypeStruct(x.shape, x.dtype),
             jax.ShapeDtypeStruct(x.shape, x.dtype),
+        )
+        if tail
+        else (
+            jax.ShapeDtypeStruct(x.shape, x.dtype),
+            jax.ShapeDtypeStruct(x.shape, x.dtype),
             jax.ShapeDtypeStruct((nb, x.shape[1] * x.shape[2], x.shape[3]), x.dtype),
             jax.ShapeDtypeStruct((x.shape[1] * x.shape[2], x.shape[3]), x.dtype),
             jax.ShapeDtypeStruct((x.shape[1] * x.shape[2], x.shape[3]), x.dtype),
@@ -112,7 +122,7 @@
             jax.ShapeDtypeStruct((x.shape[0] * x.shape[1], x.shape[3]), x.dtype),
         ),
         in_specs=[smem, smem] + [vmem] * 10,
-        out_specs=[vmem] * 7,
+        out_specs=[vmem] * (2 if tail else 7),
         compiler_params=pltpu.CompilerParams(vmem_limit_bytes=48 * 1024 * 1024),
         cost_estimate=pl.CostEstimate(flops=80 * x.size, bytes_accessed=moved, transcendentals=0),
     )(scal, sel, x, v, kst, alive, part, up, down, prevf, nextf, below)
@@ -189,7 +199,7 @@
     first_face = field[0].reshape(plane, cols)
     top_rows = field[:, :, 0].reshape(local_count * ncomp, cols)
     bot_rows = field[:, :, -1].reshape(local_count * ncomp, cols)
-    for _ in range(ITERS):
+    for step in range(ITERS):
       recv = lax.all_to_all(send, "gz", 0, 0, tiled=True)
       partner8 = jnp.stack(
           [lax.dynamic_index_in_dim(recv, src_block[l], 0, keepdims=False) for l in range(local_count)]
@@ -208,7 +218,8 @@
       ]
       firsts = jnp.concatenate(heads, axis=0)
       below = shift_rows(firsts, "tile", False)
-      field, velocity, send, last_face, first_face, top_rows, bot_rows = update(
+      outs = update(
+          step == ITERS - 1,
           scal,
           send_sel,
           field,
@@ -222,6 +233,10 @@
           next_face,
           below,
       )
+      if step == ITERS - 1:
+          field, velocity = outs
+      else:
+          field, velocity, send, last_face, first_face, top_rows, bot_rows = outs
     return (field, velocity)
 
 

time: 239 us -> 238 us (level)
  no operation moved by 1% of the time
where the time goes in v12:
time: 238 us; the launch traced here: 237 us
  waiting for transfers between devices  109 us (46%)
  starting transfers between devices  71.2 us (30%)
  local copies, waits for them, and re-layouts  27.5 us (12%)
  Pallas kernels  16.8 us (7%)
  other arithmetic  7.55 us (3%)
  between operations  5.1 us (2%)
    ppermute x17, waiting for transfers between devices, shift_rows(): return lax.ppermute(block, axis, pairs)  109 us
    ppermute x17, starting transfers between devices, shift_rows(): return lax.ppermute(block, axis, pairs)  47.1 us
    all_to_all x3, starting transfers between devices, body(): recv = lax.all_to_all(send, 'gz', 0, 0, tiled=True)  24.1 us
    pallas_call x3, Pallas kernels, update(): pl.pallas_call(update_kernel, out_shape=(jax.ShapeDtypeStruct(x.shape, x....  14 us
    another operation x1, other arithmetic, body(): stiff = jnp.stack([kappa, alive])  5.28 us
    squeeze x3, local copies, waits for them, and re-layouts, body(): lax.dynamic_slice(recv, (src_block[l], c * rows, 0), (1, 1, cols))[0]  4.95 us
    unnamed x49, local copies, waits for them, and re-layouts  4.9 us
  transfers between devices with their start and end apart: 20, of which 7 were waited for; matrix products, arithmetic and copies ran while one was open for 12% of the time, Pallas kernels for 1%

profile of v12, /device:TPU:105, one launch (start us, length us, event | category | flops | bytes accessed | tf_op | source)
XLA Modules:
  0.0 236.7 jit_solution(6196783619060956191)
XLA Ops:
  3.2 3.8 %collective-permute-start.2 = (f32[4,5120]{1,0:T(4,128)}, f32[4,5120]{1,0:T(4,128)S(1)}, u32[]{:S(2)}, u32[]{:S(2)}) collective-permute-start(f32[4,5120]{1,0:T(4,128)} %reshape_squeeze.12), channel_id=1, source_target_pairs={{0,1},{1,2},{2,3},{3,4},{4,5},{5,6},{6,7},{7,8},{8,9},{9,10},{10,1... | collective-permute-start | bytes 245768 | tf_op jit(solution)/shard_map/ppermute | solution.py:21
  7.7 1.9 collective-permute-start.3
  12.3 5.3 %multiply_bitcast_fusion = f32[1,2,8,5120]{3,2,1,0:T(8,128)S(1)} fusion(s32[2,8,5120]{2,1,0:T(8,128)S(1)} %copy-done.18, f32[]{:T(128)} %bitcast.7, f32[]{:T(128)} %bitcast.6, f32[]{:T(128)} %bitcast.5, f32[]{:T(128)} %bitcast.4, f32[]{:T(128)} %bitcast.3, f32[]{:T(128)} %bitcast.2, f32[]{:T(128)} %bitcast.1, f32[]{:T(128)} %bitcast, ...), kind=kLoop, calls=%fused_computation.17 | loop fusion | flops 1474560 | bytes 983072 | tf_op jit(solution)/shard_map/stack | solution.py:159
  17.7 3.6 %collective-permute-start = (f32[2,2,1,5120]{3,2,1,0:T(1,128)S(1)}, f32[2,2,1,5120]{3,2,1,0:T(1,128)S(1)}, u32[]{:S(2)}, u32[]{:S(2)}) collective-permute-start(f32[2,2,1,5120]{3,2,1,0:T(1,128)S(1)} %get-tuple-element.54), channel_id=1, source_target_pairs={{0,1},{1,2},{2,3},{3,4},{4,5},{5,6},{6,7},{7,8},{8,9},{9,10},{10,1... | collective-permute-start | bytes 245768 | tf_op jit(solution)/shard_map/ppermute | solution.py:21
  21.3 1.9 collective-permute-start.1
  24.2 2.2 collective-permute-start.5
  27.1 2.8 %shard_map.95 = f32[8,16,5120]{2,1,0:T(8,128)} custom-call(s32[8]{0:T(128)} %fusion.6.sel_ref, f32[2,2,8,5120]{3,2,1,0:T(8,128)} %x_ref.3), custom_call_target="tpu_custom_call" | custom-call | bytes 3276800 | tf_op jit(solution)/shard_map/pallas_call | solution.py:140
  29.9 7.3 %all-to-all-start = ((f32[8,16,5120]{2,1,0:T(8,128)}), f32[8,16,5120]{2,1,0:T(8,128)}, u32[]{:S(2)}, u32[]{:S(2)}) async-start(f32[8,16,5120]{2,1,0:T(8,128)} %shard_map.95), calls=%async_computation | async-start | bytes 5242880 | tf_op jit(solution)/shard_map/all_to_all | solution.py:203
  42.1 3.1 %collective-permute-start.4 = (f32[16,5120]{1,0:T(8,128)}, f32[16,5120]{1,0:T(8,128)S(1)}, u32[]{:S(2)}, u32[]{:S(2)}) collective-permute-start(f32[16,5120]{1,0:T(8,128)} %get-tuple-element.51), channel_id=1, source_target_pairs={{0,16},{16,32},{32,48},{48,64},{64,80},{80,96},{96,112},{1,17},{17... | collective-permute-start | bytes 983048 | tf_op jit(solution)/shard_map/ppermute | solution.py:21
  47.5 27.1 %collective-permute-done.4.prevf_ref = f32[16,5120]{1,0:T(8,128)S(1)} collective-permute-done((f32[16,5120]{1,0:T(8,128)}, f32[16,5120]{1,0:T(8,128)S(1)}, u32[]{:S(2)}, u32[]{:S(2)}) %collective-permute-start.4) | collective-permute-done | bytes 327712 | tf_op jit(solution)/shard_map/ppermute | solution.py:21
  78.8 4.0 %collective-permute-start.6 = (f32[8,5120]{1,0:T(8,128)}, f32[8,5120]{1,0:T(8,128)S(1)}, u32[]{:S(2)}, u32[]{:S(2)}) collective-permute-start(f32[8,5120]{1,0:T(8,128)} %concatenate.25), channel_id=1, source_target_pairs={{1,0},{2,1},{3,2},{4,3},{5,4},{6,5},{7,6},{8,7},{9,8},{10,9},{11,1... | collective-permute-start | bytes 491528 | tf_op jit(solution)/shard_map/ppermute | solution.py:21
  84.0 2.5 %collective-permute-done.6.below_ref = f32[8,5120]{1,0:T(8,128)S(1)} collective-permute-done((f32[8,5120]{1,0:T(8,128)}, f32[8,5120]{1,0:T(8,128)S(1)}, u32[]{:S(2)}, u32[]{:S(2)}) %collective-permute-start.6) | collective-permute-done | bytes 163872 | tf_op jit(solution)/shard_map/ppermute | solution.py:21
  86.5 5.1 %shard_map.96 = (f32[2,2,8,5120]{3,2,1,0:T(8,128)S(1)}, f32[2,2,8,5120]{3,2,1,0:T(8,128)S(1)}, f32[8,16,5120]{2,1,0:T(8,128)}, f32[16,5120]{1,0:T(8,128)}, f32[1...) custom-call(f32[2,9]{1,0:T(2,128)S(1)} %pad_maximum_fusion.8.scal_ref, s32[8]{0:T(128)S(1)} %copy-done.11, ...), custom_call_target="tpu_custom_call" | custom-call | flops 13107200 | bytes 8192000 | tf_op jit(solution)/shard_map/pallas_call | solution.py:108
  93.0 6.4 %collective-permute-start.9 = (f32[16,5120]{1,0:T(8,128)}, f32[16,5120]{1,0:T(8,128)S(1)}, u32[]{:S(2)}, u32[]{:S(2)}) collective-permute-start(f32[16,5120]{1,0:T(8,128)} %get-tuple-element.21), channel_id=1, source_target_pairs={{0,16},{16,32},{32,48},{48,64},{64,80},{80,96},{96,112},{1,17},{17... | collective-permute-start | bytes 983048 | tf_op jit(solution)/shard_map/ppermute | solution.py:21
  99.4 8.8 %all-to-all-start.1 = ((f32[8,16,5120]{2,1,0:T(8,128)}), f32[8,16,5120]{2,1,0:T(8,128)}, u32[]{:S(2)}, u32[]{:S(2)}) async-start(f32[8,16,5120]{2,1,0:T(8,128)} %get-tuple-element.18), calls=%async_computation.1 | async-start | bytes 5242880 | tf_op jit(solution)/shard_map/all_to_all | solution.py:203
  108.2 2.7 %collective-permute-start.7 = (f32[4,5120]{1,0:T(4,128)S(1)}, f32[4,5120]{1,0:T(4,128)S(1)}, u32[]{:S(2)}, u32[]{:S(2)}) collective-permute-start(f32[4,5120]{1,0:T(4,128)S(1)} %copy-done.16), channel_id=1, source_target_pairs={{0,1},{1,2},{2,3},{3,4},{4,5},{5,6},{6,7},{7,8},{8,9},{9,10},{10,1... | collective-permute-start | bytes 245768 | tf_op jit(solution)/shard_map/ppermute | solution.py:21
  110.9 1.9 collective-permute-start.8
  112.8 1.9 collective-permute-start.10
  114.8 37.0 %collective-permute-done.10.nextf_ref = f32[16,5120]{1,0:T(8,128)S(1)} collective-permute-done((f32[16,5120]{1,0:T(8,128)S(1)}, f32[16,5120]{1,0:T(8,128)S(1)}, u32[]{:S(2)}, u32[]{:S(2)}) %collective-permute-start.10) | collective-permute-done | bytes 327712 | tf_op jit(solution)/shard_map/ppermute | solution.py:21
  153.4 2.9 %collective-permute-start.11 = (f32[8,5120]{1,0:T(8,128)S(1)}, f32[8,5120]{1,0:T(8,128)S(1)}, u32[]{:S(2)}, u32[]{:S(2)}) collective-permute-start(f32[8,5120]{1,0:T(8,128)S(1)} %concatenate.26), channel_id=1, source_target_pairs={{1,0},{2,1},{3,2},{4,3},{5,4},{6,5},{7,6},{8,7},{9,8},{10,9},{11,1... | collective-permute-start | bytes 491528 | tf_op jit(solution)/shard_map/ppermute | solution.py:21
  157.5 2.5 %collective-permute-done.11.below_ref = f32[8,5120]{1,0:T(8,128)S(1)} collective-permute-done((f32[8,5120]{1,0:T(8,128)S(1)}, f32[8,5120]{1,0:T(8,128)S(1)}, u32[]{:S(2)}, u32[]{:S(2)}) %collective-permute-start.11) | collective-permute-done | bytes 163872 | tf_op jit(solution)/shard_map/ppermute | solution.py:21
  161.0 5.0 %shard_map.97 = (f32[2,2,8,5120]{3,2,1,0:T(8,128)S(1)}, f32[2,2,8,5120]{3,2,1,0:T(8,128)S(1)}, f32[8,16,5120]{2,1,0:T(8,128)}, f32[16,5120]{1,0:T(8,128)}, f32[1...) custom-call(f32[2,9]{1,0:T(2,128)S(1)} %pad_maximum_fusion.8.scal_ref, s32[8]{0:T(128)S(1)} %copy-done.11, ...), custom_call_target="tpu_custom_call" | custom-call | flops 13107200 | bytes 8192000 | tf_op jit(solution)/shard_map/pallas_call | solution.py:108
  166.7 1.9 collective-permute-start.14
  168.6 8.0 %all-to-all-start.2 = ((f32[8,16,5120]{2,1,0:T(8,128)}), f32[8,16,5120]{2,1,0:T(8,128)}, u32[]{:S(2)}, u32[]{:S(2)}) async-start(f32[8,16,5120]{2,1,0:T(8,128)} %get-tuple-element.25), calls=%async_computation.2 | async-start | bytes 5242880 | tf_op jit(solution)/shard_map/all_to_all | solution.py:203
  176.6 2.3 collective-permute-start.12
  178.9 2.0 collective-permute-start.13
  181.0 2.2 collective-permute-start.15
  183.2 11.1 %collective-permute-done.14.prevf_ref = f32[16,5120]{1,0:T(8,128)} collective-permute-done((f32[16,5120]{1,0:T(8,128)}, f32[16,5120]{1,0:T(8,128)}, u32[]{:S(2)}, u32[]{:S(2)}) %collective-permute-start.14) | collective-permute-done | bytes 327712 | tf_op jit(solution)/shard_map/ppermute | solution.py:21
  195.8 25.1 %collective-permute-done.15.nextf_ref = f32[16,5120]{1,0:T(8,128)S(1)} collective-permute-done((f32[16,5120]{1,0:T(8,128)}, f32[16,5120]{1,0:T(8,128)S(1)}, u32[]{:S(2)}, u32[]{:S(2)}) %collective-permute-start.15) | collective-permute-done | bytes 327712 | tf_op jit(solution)/shard_map/ppermute | solution.py:21
  225.8 2.4 %collective-permute-start.16 = (f32[8,5120]{1,0:T(8,128)}, f32[8,5120]{1,0:T(8,128)S(1)}, u32[]{:S(2)}, u32[]{:S(2)}) collective-permute-start(f32[8,5120]{1,0:T(8,128)} %concatenate.27), channel_id=1, source_target_pairs={{1,0},{2,1},{3,2},{4,3},{5,4},{6,5},{7,6},{8,7},{9,8},{10,9},{11,1... | collective-permute-start | bytes 491528 | tf_op jit(solution)/shard_map/ppermute | solution.py:21
  229.5 3.3 %collective-permute-done.16.below_ref = f32[8,5120]{1,0:T(8,128)S(1)} collective-permute-done((f32[8,5120]{1,0:T(8,128)}, f32[8,5120]{1,0:T(8,128)S(1)}, u32[]{:S(2)}, u32[]{:S(2)}) %collective-permute-start.16) | collective-permute-done | bytes 163872 | tf_op jit(solution)/shard_map/ppermute | solution.py:21
  232.8 3.9 %shard_map.98 = (f32[2,2,8,5120]{3,2,1,0:T(8,128)}, f32[2,2,8,5120]{3,2,1,0:T(8,128)}) custom-call(f32[2,9]{1,0:T(2,128)S(1)} %pad_maximum_fusion.8.scal_ref, s32[8]{0:T(128)S(1)} %copy-done.11, f32[2,2,8,5120]{3,2,1,0:T(8,128)S(1)} %get-tuple-element.23.x_ref, f32[2,2,8,5120]{3,2,1,0:T(8,128)S(1)} %get-tuple-element.24.v_ref, ...), custom_call_target="tpu_custom_call" | custom-call | flops 13107200 | bytes 8192000 | tf_op jit(solution)/shard_map/pallas_call | solution.py:108
  (97 shorter events, 29.8 us)
Async XLA Ops:
  0.6 11.7 %copy-start.17 = (s32[2,8,5120]{2,1,0:T(8,128)S(1)}, s32[2,8,5120]{2,1,0:T(8,128)}, u32[]{:S(2)}) copy-start(s32[2,8,5120]{2,1,0:T(8,128)} %param.11) | copy-start | bytes 983044
  0.6 11.7 %copy-start.18 = (s32[2,8,5120]{2,1,0:T(8,128)S(1)}, s32[2,8,5120]{2,1,0:T(8,128)}, u32[]{:S(2)}) copy-start(s32[2,8,5120]{2,1,0:T(8,128)} %param.10) | copy-start | bytes 983044
  2.5 20.8 %copy-start.2 = (f32[2,2,8,5120]{3,2,1,0:T(8,128)S(1)}, f32[2,2,8,5120]{3,2,1,0:T(8,128)}, u32[]{:S(2)}) copy-start(f32[2,2,8,5120]{3,2,1,0:T(8,128)} %x_ref.3) | copy-start | bytes 1966084
  3.2 80.8 %collective-permute-start.2 = (f32[4,5120]{1,0:T(4,128)}, f32[4,5120]{1,0:T(4,128)S(1)}, u32[]{:S(2)}, u32[]{:S(2)}) collective-permute-start(f32[4,5120]{1,0:T(4,128)} %reshape_squeeze.12), channel_id=1, source_target_pairs={{0,1},{1,2},{2,3},{3,4},{4,5},{5,6},{6,7},{7,8},{8,9},{9,10},{10,1... | collective-permute-start | bytes 245768 | tf_op jit(solution)/shard_map/ppermute | solution.py:21
  7.7 76.3 %collective-permute-start.3 = (f32[4,5120]{1,0:T(4,128)}, f32[4,5120]{1,0:T(4,128)S(1)}, u32[]{:S(2)}, u32[]{:S(2)}) collective-permute-start(f32[4,5120]{1,0:T(4,128)} %reshape_squeeze.13), channel_id=1, source_target_pairs={{1,0},{2,1},{3,2},{4,3},{5,4},{6,5},{7,6},{8,7},{9,8},{10,9},{11,1... | collective-permute-start | bytes 245768 | tf_op jit(solution)/shard_map/ppermute | solution.py:21
  12.3 14.1 %copy-start.21 = (s32[16]{0:T(128)S(1)}, s32[16]{0:T(128)}, u32[]{:S(2)}) copy-start(s32[16]{0:T(128)} %param.15) | copy-start | bytes 196
  17.7 24.4 %collective-permute-start = (f32[2,2,1,5120]{3,2,1,0:T(1,128)S(1)}, f32[2,2,1,5120]{3,2,1,0:T(1,128)S(1)}, u32[]{:S(2)}, u32[]{:S(2)}) collective-permute-start(f32[2,2,1,5120]{3,2,1,0:T(1,128)S(1)} %get-tuple-element.54), channel_id=1, source_target_pairs={{0,1},{1,2},{2,3},{3,4},{4,5},{5,6},{6,7},{7,8},{8,9},{9,10},{10,1... | collective-permute-start | bytes 245768 | tf_op jit(solution)/shard_map/ppermute | solution.py:21
  21.3 23.9 %collective-permute-start.1 = (f32[2,2,1,5120]{3,2,1,0:T(1,128)S(1)}, f32[2,2,1,5120]{3,2,1,0:T(1,128)S(1)}, u32[]{:S(2)}, u32[]{:S(2)}) collective-permute-start(f32[2,2,1,5120]{3,2,1,0:T(1,128)S(1)} %get-tuple-element.55), channel_id=1, source_target_pairs={{1,0},{2,1},{3,2},{4,3},{5,4},{6,5},{7,6},{8,7},{9,8},{10,9},{11,1... | collective-permute-start | bytes 245768 | tf_op jit(solution)/shard_map/ppermute | solution.py:21
  24.2 21.7 %collective-permute-start.5 = (f32[16,5120]{1,0:T(8,128)}, f32[16,5120]{1,0:T(8,128)}, u32[]{:S(2)}, u32[]{:S(2)}) collective-permute-start(f32[16,5120]{1,0:T(8,128)} %get-tuple-element.50), channel_id=1, source_target_pairs={{16,0},{32,16},{48,32},{64,48},{80,64},{96,80},{112,96},{17,1},{33... | collective-permute-start | bytes 983048 | tf_op jit(solution)/shard_map/ppermute | solution.py:21
  29.9 10.6 %copy-start.19 = (f32[2,3]{1,0:T(2,128)S(1)}, f32[2,3]{1,0:T(2,128)}, u32[]{:S(2)}) copy-start(f32[2,3]{1,0:T(2,128)} %param.14) | copy-start | bytes 76
  29.9 10.7 %copy-start.20 = (f32[2,3,2]{1,2,0:T(2,128)S(1)}, f32[2,3,2]{1,2,0:T(2,128)}, u32[]{:S(2)}) copy-start(f32[2,3,2]{1,2,0:T(2,128)} %param.13) | copy-start | bytes 148
  29.9 45.4 %all-to-all-start = ((f32[8,16,5120]{2,1,0:T(8,128)}), f32[8,16,5120]{2,1,0:T(8,128)}, u32[]{:S(2)}, u32[]{:S(2)}) async-start(f32[8,16,5120]{2,1,0:T(8,128)} %shard_map.95), calls=%async_computation | async-start | bytes 5242880 | tf_op jit(solution)/shard_map/all_to_all | solution.py:203
  42.1 32.4 %collective-permute-start.4 = (f32[16,5120]{1,0:T(8,128)}, f32[16,5120]{1,0:T(8,128)S(1)}, u32[]{:S(2)}, u32[]{:S(2)}) collective-permute-start(f32[16,5120]{1,0:T(8,128)} %get-tuple-element.51), channel_id=1, source_target_pairs={{0,16},{16,32},{32,48},{48,64},{64,80},{80,96},{96,112},{1,17},{17... | collective-permute-start | bytes 983048 | tf_op jit(solution)/shard_map/ppermute | solution.py:21
  45.8 38.2 %copy-start = (f32[5,2,8,5120]{3,2,1,0:T(8,128)}, f32[5,2,8,5120]{3,2,1,0:T(8,128)S(1)}, u32[]{:S(2)}) copy-start(f32[5,2,8,5120]{3,2,1,0:T(8,128)S(1)} %bitcast_dynamic-update-slice_fusion.k_ref) | copy-start | bytes 4915204
  45.8 40.7 %copy-start.3 = (f32[2,2,8,5120]{3,2,1,0:T(8,128)S(1)}, f32[2,2,8,5120]{3,2,1,0:T(8,128)}, u32[]{:S(2)}) copy-start(f32[2,2,8,5120]{3,2,1,0:T(8,128)} %x_ref.3) | copy-start | bytes 1966084
  45.8 40.6 %copy-start.4 = (f32[2,2,8,5120]{3,2,1,0:T(8,128)S(1)}, f32[2,2,8,5120]{3,2,1,0:T(8,128)}, u32[]{:S(2)}) copy-start(f32[2,2,8,5120]{3,2,1,0:T(8,128)} %v_ref.1) | copy-start | bytes 1966084
  45.9 40.6 %copy-start.11 = (s32[8]{0:T(128)S(1)}, s32[8]{0:T(128)}, u32[]{:S(2)}) copy-start(s32[8]{0:T(128)} %fusion.6.sel_ref) | copy-start | bytes 100
  78.8 7.7 %collective-permute-start.6 = (f32[8,5120]{1,0:T(8,128)}, f32[8,5120]{1,0:T(8,128)S(1)}, u32[]{:S(2)}, u32[]{:S(2)}) collective-permute-start(f32[8,5120]{1,0:T(8,128)} %concatenate.25), channel_id=1, source_target_pairs={{1,0},{2,1},{3,2},{4,3},{5,4},{6,5},{7,6},{8,7},{9,8},{10,9},{11,1... | collective-permute-start | bytes 491528 | tf_op jit(solution)/shard_map/ppermute | solution.py:21
  93.0 21.8 %collective-permute-start.9 = (f32[16,5120]{1,0:T(8,128)}, f32[16,5120]{1,0:T(8,128)S(1)}, u32[]{:S(2)}, u32[]{:S(2)}) collective-permute-start(f32[16,5120]{1,0:T(8,128)} %get-tuple-element.21), channel_id=1, source_target_pairs={{0,16},{16,32},{32,48},{48,64},{64,80},{80,96},{96,112},{1,17},{17... | collective-permute-start | bytes 983048 | tf_op jit(solution)/shard_map/ppermute | solution.py:21
  99.4 13.4 %copy-start.14 = (f32[16,5120]{1,0:T(8,128)S(1)}, f32[16,5120]{1,0:T(8,128)}, u32[]{:S(2)}) copy-start(f32[16,5120]{1,0:T(8,128)} %copy-done.13) | copy-start | bytes 983044
  99.4 52.4 %all-to-all-start.1 = ((f32[8,16,5120]{2,1,0:T(8,128)}), f32[8,16,5120]{2,1,0:T(8,128)}, u32[]{:S(2)}, u32[]{:S(2)}) async-start(f32[8,16,5120]{2,1,0:T(8,128)} %get-tuple-element.18), calls=%async_computation.1 | async-start | bytes 5242880 | tf_op jit(solution)/shard_map/all_to_all | solution.py:203
  108.2 49.3 %collective-permute-start.7 = (f32[4,5120]{1,0:T(4,128)S(1)}, f32[4,5120]{1,0:T(4,128)S(1)}, u32[]{:S(2)}, u32[]{:S(2)}) collective-permute-start(f32[4,5120]{1,0:T(4,128)S(1)} %copy-done.16), channel_id=1, source_target_pairs={{0,1},{1,2},{2,3},{3,4},{4,5},{5,6},{6,7},{7,8},{8,9},{9,10},{10,1... | collective-permute-start | bytes 245768 | tf_op jit(solution)/shard_map/ppermute | solution.py:21
  110.9 46.6 %collective-permute-start.8 = (f32[4,5120]{1,0:T(4,128)S(1)}, f32[4,5120]{1,0:T(4,128)S(1)}, u32[]{:S(2)}, u32[]{:S(2)}) collective-permute-start(f32[4,5120]{1,0:T(4,128)S(1)} %get-tuple-element.20), channel_id=1, source_target_pairs={{1,0},{2,1},{3,2},{4,3},{5,4},{6,5},{7,6},{8,7},{9,8},{10,9},{11,1... | collective-permute-start | bytes 245768 | tf_op jit(solution)/shard_map/ppermute | solution.py:21
  112.8 39.0 %collective-permute-start.10 = (f32[16,5120]{1,0:T(8,128)S(1)}, f32[16,5120]{1,0:T(8,128)S(1)}, u32[]{:S(2)}, u32[]{:S(2)}) collective-permute-start(f32[16,5120]{1,0:T(8,128)S(1)} %copy-done.14), channel_id=1, source_target_pairs={{16,0},{32,16},{48,32},{64,48},{80,64},{96,80},{112,96},{17,1},{33... | collective-permute-start | bytes 983048 | tf_op jit(solution)/shard_map/ppermute | solution.py:21
  153.4 6.6 %collective-permute-start.11 = (f32[8,5120]{1,0:T(8,128)S(1)}, f32[8,5120]{1,0:T(8,128)S(1)}, u32[]{:S(2)}, u32[]{:S(2)}) collective-permute-start(f32[8,5120]{1,0:T(8,128)S(1)} %concatenate.26), channel_id=1, source_target_pairs={{1,0},{2,1},{3,2},{4,3},{5,4},{6,5},{7,6},{8,7},{9,8},{10,9},{11,1... | collective-permute-start | bytes 491528 | tf_op jit(solution)/shard_map/ppermute | solution.py:21
  166.7 27.5 %collective-permute-start.14 = (f32[16,5120]{1,0:T(8,128)}, f32[16,5120]{1,0:T(8,128)}, u32[]{:S(2)}, u32[]{:S(2)}) collective-permute-start(f32[16,5120]{1,0:T(8,128)} %get-tuple-element.28), channel_id=1, source_target_pairs={{0,16},{16,32},{32,48},{48,64},{64,80},{80,96},{96,112},{1,17},{17... | collective-permute-start | bytes 983048 | tf_op jit(solution)/shard_map/ppermute | solution.py:21
  168.6 53.7 %all-to-all-start.2 = ((f32[8,16,5120]{2,1,0:T(8,128)}), f32[8,16,5120]{2,1,0:T(8,128)}, u32[]{:S(2)}, u32[]{:S(2)}) async-start(f32[8,16,5120]{2,1,0:T(8,128)} %get-tuple-element.25), calls=%async_computation.2 | async-start | bytes 5242880 | tf_op jit(solution)/shard_map/all_to_all | solution.py:203
  176.6 52.8 %collective-permute-start.12 = (f32[4,5120]{1,0:T(4,128)}, f32[4,5120]{1,0:T(4,128)S(1)}, u32[]{:S(2)}, u32[]{:S(2)}) collective-permute-start(f32[4,5120]{1,0:T(4,128)} %get-tuple-element.26), channel_id=1, source_target_pairs={{0,1},{1,2},{2,3},{3,4},{4,5},{5,6},{6,7},{7,8},{8,9},{9,10},{10,1... | collective-permute-start | bytes 245768 | tf_op jit(solution)/shard_map/ppermute | solution.py:21
  178.9 50.5 %collective-permute-start.13 = (f32[4,5120]{1,0:T(4,128)S(1)}, f32[4,5120]{1,0:T(4,128)S(1)}, u32[]{:S(2)}, u32[]{:S(2)}) collective-permute-start(f32[4,5120]{1,0:T(4,128)S(1)} %get-tuple-element.27), channel_id=1, source_target_pairs={{1,0},{2,1},{3,2},{4,3},{5,4},{6,5},{7,6},{8,7},{9,8},{10,9},{11,1... | collective-permute-start | bytes 245768 | tf_op jit(solution)/shard_map/ppermute | solution.py:21
  180.9 51.9 %copy-start.1 = (f32[5,2,8,5120]{3,2,1,0:T(8,128)S(1)}, f32[5,2,8,5120]{3,2,1,0:T(8,128)}, u32[]{:S(2)}) copy-start(f32[5,2,8,5120]{3,2,1,0:T(8,128)} %copy-done) | copy-start | bytes 4915204
  181.0 40.0 %collective-permute-start.15 = (f32[16,5120]{1,0:T(8,128)}, f32[16,5120]{1,0:T(8,128)S(1)}, u32[]{:S(2)}, u32[]{:S(2)}) collective-permute-start(f32[16,5120]{1,0:T(8,128)} %copy-done.12), channel_id=1, source_target_pairs={{16,0},{32,16},{48,32},{64,48},{80,64},{96,80},{112,96},{17,1},{33... | collective-permute-start | bytes 983048 | tf_op jit(solution)/shard_map/ppermute | solution.py:21
  225.8 7.0 %collective-permute-start.16 = (f32[8,5120]{1,0:T(8,128)}, f32[8,5120]{1,0:T(8,128)S(1)}, u32[]{:S(2)}, u32[]{:S(2)}) collective-permute-start(f32[8,5120]{1,0:T(8,128)} %concatenate.27), channel_id=1, source_target_pairs={{1,0},{2,1},{3,2},{4,3},{5,4},{6,5},{7,6},{8,7},{9,8},{10,9},{11,1... | collective-permute-start | bytes 491528 | tf_op jit(solution)/shard_map/ppermute | solution.py:21
  (10 other events, 36.2 us)
